TPU v7x, 256 devices: a whole 4x4x8 slice. The times are simulated.
256 devices in a mesh: seq: 4 (over y), head: 64 (over x, z, core).
Axes of the slice: x: 4, y: 4, z: 8, core: 2. Of those that a mesh axis runs over, the one named last changes fastest.
Arguments:
- pre_x: bfloat16 [4096, 8192], P('seq', 'head'), may hold values from -6 to 6
- pre_bc: bfloat16 [4096, 256], P('seq'), may hold values from -6 to 6
- conv_x: float32 [4, 8192], P(None, 'head'), may hold values from -3 to 3
- conv_bc: float32 [4, 256], replicated, may hold values from -3 to 3
- log_decay: float32 [128, 4096], P('head', 'seq'), may hold values from -1.5 to 0
- lengths: int32 [4], replicated, may hold values from 1 to 2048, 4096 in all
- grad_out: bfloat16 [4096, 8192], P('seq', 'head'), may hold values from -0.3125 to 0.3125
Outputs:
- grad_pre_x: float32 [4096, 8192], P('seq', 'head')
- grad_pre_bc: float32 [4096, 256], P(('seq', 'head'))
- grad_log_decay: float32 [128, 4096], P('head', 'seq')
Inputs may be any that keep to these rules, and one draw needn't show every extreme that they name: `lengths`: the 4 counts sum to 4096.
All inputs are finite; a program needn't handle non-finite values.
Results may differ from a plain program's by a relative error of at most 0.0003.
Values may be sent and summed in bfloat16 or wider, within the bound.
A program may use at most 64 MiB of HBM per device.

v0:
```python
import jax
import jax.numpy as jnp
from jax import lax
from jax.sharding import PartitionSpec as P

P_SIZE = 64
N = 128
K = 4
BLOCK = 256


precise = lax.Precision.HIGHEST


def shifted(value, axis, steps):
    count = lax.axis_size(axis)
    initial, last = (max(0, -steps), min(count, count - steps))
    return lax.ppermute(value, axis, [(source, source + steps) for source in range(initial, last)])


def entering(value, axis, join, neutral, backward):
    count, mine = (lax.axis_size(axis), lax.axis_index(axis))
    pieces = jax.tree.map(lambda part: lax.all_gather(part, axis), value)
    if backward:
        pieces = jax.tree.map(lambda part: part[::-1], pieces)
        mine = count - 1 - mine
    total = jax.tree.map(
        lambda part, zero: jnp.full_like(part, 0) + jnp.asarray(zero, part.dtype), value, neutral
    )

    def hop(position, total):
        longer = join(total, jax.tree.map(lambda part: part[position], pieces))
        return jax.tree.map(lambda new, old: jnp.where(position < mine, new, old), longer, total)

    return lax.fori_loop(0, count - 1, hop, total)


def matmul(left, right):
    return jnp.dot(left, right, precision=precise, preferred_element_type=jnp.float32)


def note_index(positions, lengths):
    starts = jnp.cumsum(lengths) - lengths
    hits = (positions[:, None] >= starts[None, :]).astype(jnp.int32)
    return jnp.sum(hits, axis=1) - 1


def block_edges(log_block, note_block, note_before):
    cumul = jnp.cumsum(log_block)
    entry = jnp.exp(cumul) * (note_block == note_before)
    leave = jnp.exp(cumul[-1] - cumul) * (note_block == note_block[-1])
    through = jnp.exp(cumul[-1]) * (note_block[-1] == note_before)
    return (cumul, entry, leave, through)


def block_forward(state, x_block, b_block, c_block, log_block, note_block, note_before):
    cumul, entry, leave, through = block_edges(log_block, note_block, note_before)
    length = note_block.shape[0]
    lower = jnp.arange(length)[:, None] >= jnp.arange(length)[None, :]
    linked = lower & (note_block[:, None] == note_block[None, :])
    decay_matrix = jnp.exp(jnp.where(linked, cumul[:, None] - cumul[None, :], 0.0)) * linked
    scores = matmul(c_block, b_block.T) * decay_matrix
    output = matmul(scores, x_block) + entry[:, None] * matmul(c_block, state.T)
    updated = through * state + matmul((x_block * leave[:, None]).T, b_block)
    return (output, updated)


def head_forward(state, x_head, b_blocks, c_blocks, log_head, note_blocks, befores):

    def head_advance(carry, block):
        output, updated = block_forward(carry, *block)
        return (updated, output)

    final, outputs = lax.scan(
        head_advance, state, (x_head, b_blocks, c_blocks, log_head, note_blocks, befores)
    )
    return (outputs, final)


def conv_forward(extended, weights, note_ext):
    width = weights.shape[0]
    count = extended.shape[0] - width + 1
    result = jnp.zeros((count, extended.shape[1]), jnp.float32)
    for k in range(width):
        linked = note_ext[k : k + count] == note_ext[width - 1 : width - 1 + count]
        result = result + weights[k][None, :] * extended[k : k + count] * linked[:, None]
    return result


def conv_backward(extended, weights, note_ext):
    width = weights.shape[0]
    count = extended.shape[0] - width + 1
    result = jnp.zeros((count, extended.shape[1]), jnp.float32)
    for k in range(width):
        lag = width - 1 - k
        linked = note_ext[lag : lag + count] == note_ext[:count]
        result = result + weights[k][None, :] * extended[lag : lag + count] * linked[:, None]
    return result


def silu_slope(values):
    sigma = jax.nn.sigmoid(values)
    return sigma * (1.0 + values * (1.0 - sigma))


def chain_combine(earlier, later):
    return (earlier[0] * later[0], later[0][:, None, None] * earlier[1] + later[1])


def local(pre_x, pre_bc, conv_x, conv_bc, log_decay, lengths, grad_out):
    tok_rows = pre_x.shape[0]
    head_count = log_decay.shape[0]
    rim_width = K - 1
    block_count = tok_rows // BLOCK
    seq_start = lax.axis_index("seq") * tok_rows
    positions = seq_start + jnp.arange(-rim_width, tok_rows + rim_width)
    note_all = note_index(positions, lengths)
    note_ids = note_all[rim_width : rim_width + tok_rows]
    before_x, before_bc = shifted(
        (pre_x[tok_rows - rim_width :], pre_bc[tok_rows - rim_width :]), "seq", 1
    )
    u_x = conv_forward(
        jnp.concatenate([before_x, pre_x]).astype(jnp.float32),
        conv_x,
        note_all[: tok_rows + rim_width],
    )
    u_bc = conv_forward(
        jnp.concatenate([before_bc, pre_bc]).astype(jnp.float32),
        conv_bc,
        note_all[: tok_rows + rim_width],
    )
    v_x = jax.nn.silu(u_x)
    v_bc = jax.nn.silu(u_bc)
    x_heads = v_x.reshape(block_count, BLOCK, head_count, P_SIZE).transpose(2, 0, 1, 3)
    b_blocks = v_bc[:, :N].reshape(block_count, BLOCK, N)
    c_blocks = v_bc[:, N:].reshape(block_count, BLOCK, N)
    log_blocks = log_decay.reshape(head_count, block_count, BLOCK)
    grad_heads = (
        grad_out.astype(jnp.float32)
        .reshape(block_count, BLOCK, head_count, P_SIZE)
        .transpose(2, 0, 1, 3)
    )
    note_blocks = note_ids.reshape(block_count, BLOCK)
    befores = jnp.concatenate([note_all[rim_width - 1 : rim_width], note_blocks[:-1, -1]])

    def state_only(x_head, log_head):

        def state_advance(carry, block):
            x_block, b_block, log_block, note_block, note_before = block
            _, _, leave, through = block_edges(log_block, note_block, note_before)
            state, keep = carry
            return (
                (through * state + matmul((x_block * leave[:, None]).T, b_block), keep * through),
                None,
            )

        start = (jnp.zeros((P_SIZE, N), jnp.float32), jnp.ones((), jnp.float32))
        final, _ = lax.scan(
            state_advance, start, (x_head, b_blocks, log_head, note_blocks, befores)
        )
        return final

    def adjoint_only(grad_head, log_head):

        def retreat(carry, block):
            grad_block, c_block, log_block, note_block, note_before = block
            _, entry, _, through = block_edges(log_block, note_block, note_before)
            return (through * carry + matmul((grad_block * entry[:, None]).T, c_block), None)

        final, _ = lax.scan(
            retreat,
            jnp.zeros((P_SIZE, N), jnp.float32),
            (grad_head, c_blocks, log_head, note_blocks, befores),
            reverse=True,
        )
        return final

    local_state, local_keep = jax.vmap(state_only)(x_heads, log_blocks)
    local_adjoint = jax.vmap(adjoint_only)(grad_heads, log_blocks)
    identity = (
        jnp.ones((head_count,), jnp.float32),
        jnp.zeros((head_count, P_SIZE, N), jnp.float32),
    )
    _, state_in = entering((local_keep, local_state), "seq", chain_combine, identity, False)
    _, adjoint_in = entering((local_keep, local_adjoint), "seq", chain_combine, identity, True)

    def local_forward(x_all, b_all, c_all, log_all):

        def one_head(state, x_head, log_head):
            return head_forward(state, x_head, b_all, c_all, log_head, note_blocks, befores)

        return jax.vmap(one_head)(state_in, x_all, log_all)

    _, pull = jax.vjp(local_forward, x_heads, b_blocks, c_blocks, log_blocks)
    grad_x_heads, grad_b, grad_c, grad_log = pull((grad_heads, adjoint_in))
    grad_log_decay = grad_log.reshape(head_count, tok_rows)
    grad_v_x = grad_x_heads.transpose(1, 2, 0, 3).reshape(tok_rows, head_count * P_SIZE)
    grad_v_bc = jnp.concatenate([grad_b.reshape(tok_rows, N), grad_c.reshape(tok_rows, N)], axis=1)
    grad_u_x = grad_v_x * silu_slope(u_x)
    share_rows = tok_rows // lax.axis_size("head")
    row_start = lax.axis_index("head") * share_rows
    summed = lax.psum(grad_v_bc, "head")
    grad_u_bc = summed * silu_slope(u_bc)
    after_x, after_bc = shifted((grad_u_x[:rim_width], grad_u_bc[:rim_width]), "seq", -1)
    grad_pre_x = conv_backward(jnp.concatenate([grad_u_x, after_x]), conv_x, note_all[rim_width:])
    whole_bc = conv_backward(jnp.concatenate([grad_u_bc, after_bc]), conv_bc, note_all[rim_width:])
    grad_pre_bc = lax.dynamic_slice_in_dim(whole_bc, row_start, share_rows, 0)
    return (grad_pre_x, grad_pre_bc, grad_log_decay)


def solution(mesh):
    placed = (
        P("seq", "head"),
        P("seq", None),
        P(None, "head"),
        P(),
        P("head", "seq"),
        P(),
        P("seq", "head"),
    )
    return jax.shard_map(
        local,
        mesh=mesh,
        in_specs=placed,
        out_specs=(P("seq", "head"), P(("seq", "head"), None), P("head", "seq")),
        check_vma=False,
    )
```

profile of v0, /device:TPU:8, one launch (start us, length us, event | category | flops | bytes accessed | tf_op | source)
XLA Modules:
  0.0 437.9 jit_solution(13618500489905147454)
XLA Ops:
  7.9 3.5 collective-permute-start.1
  12.2 3.2 collective-permute-start
  24.5 1.4 fusion.119
  26.3 1.8 fusion.101
  28.8 18.5 %while.133 = (s32[]{:T(128)}, f32[2,64,128]{2,1,0:T(8,128)S(1)}, f32[2]{0:T(128)S(1)}, f32[4,2,256]{2,1,0:T(2,128)S(1)}, s32[4,256]{1,0:T(4,128)S(1)}, /*index=5...) while((s32[]{:T(128)}, f32[2,64,128]{2,1,0:T(8,128)S(1)}, ...), condition=%wide.region_5.6_spmd.clone, body=%wide.region_2.5_spmd.clone.sunk | while | flops 50480656 | bytes 424810 | solution.py:158
  47.6 8.4 %all-reduce.2 = f32[8]{0:T(128)S(1)} all-reduce(f32[8]{0:T(128)S(1)} %dynamic-update-slice), channel_id=2, replica_groups=mesh['seq'=4,'head'=64] {'seq'}, use_global_device_ids=true, to_apply=%add.2 | all-reduce | flops 8 | bytes 64
  56.1 11.0 %all-gather.2 = f32[8,64,128]{2,1,0:T(8,128)S(1)} all-gather(f32[2,64,128]{2,1,0:T(8,128)S(1)} %get-tuple-element.1220), channel_id=4, replica_groups=mesh['seq'=4,'head'=64] {'seq'}, dimensions={0}, use_global_device_ids=true | all-gather | bytes 327680 | tf_op jit(solution)/shard_map/all_gather | solution.py:23
  68.1 55.7 %while.132 = (s32[]{:T(128)}, f32[2,64,128]{2,1,0:T(8,128)S(1)}, f32[4,2,256]{2,1,0:T(2,128)S(1)}, f32[4,1,256]{2,1,0:T(1,128)S(1)}, f32[4,2,256]{2,1,0:T(2,128)...) while((s32[]{:T(128)}, f32[2,64,128]{2,1,0:T(8,128)S(1)}, ...), condition=%wide.region_17.18_spmd.clone.clone, body=%wide.region_14.17_spmd.clone.clone.sunk | while | flops 202543632 | bytes 5584979 | solution.py:74
  71.6 1.3 multiply_dynamic-update-slice_fusion.2
  78.5 1.3 dynamic_update_slice.251
  85.5 1.3 multiply_dynamic-update-slice_fusion.2
  92.4 1.3 dynamic_update_slice.251
  99.5 1.3 multiply_dynamic-update-slice_fusion.2
  106.2 1.3 dynamic_update_slice.251
  113.3 1.3 multiply_dynamic-update-slice_fusion.2
  120.2 1.3 dynamic_update_slice.251
  124.3 18.6 %while.134 = (s32[]{:T(128)}, f32[2,64,128]{2,1,0:T(8,128)S(1)}, f32[4,2,256]{2,1,0:T(2,128)S(1)}, s32[4,256]{1,0:T(4,128)S(1)}, s32[4]{0:T(128)S(1)}, /*index=5...) while((s32[]{:T(128)}, f32[2,64,128]{2,1,0:T(8,128)S(1)}, ...), condition=%wide.region_9.10_spmd.clone, body=%wide.region_6.9_spmd.clone.sunk | while | flops 50480144 | bytes 425292 | solution.py:170
  142.9 12.4 %all-gather.1 = f32[8,64,128]{2,1,0:T(8,128)S(1)} all-gather(f32[2,64,128]{2,1,0:T(8,128)S(1)} %get-tuple-element.1218), channel_id=3, replica_groups=mesh['seq'=4,'head'=64] {'seq'}, dimensions={0}, use_global_device_ids=true | all-gather | bytes 327680 | tf_op jit(solution)/shard_map/all_gather | solution.py:23
  155.3 2.3 while.135
  160.2 71.9 %while.131 = (s32[]{:T(128)}, f32[2,64,128]{2,1,0:T(8,128)S(1)}, f32[4,2,256,64]{2,3,1,0:T(8,128)}, f32[4,256,128]{2,1,0:T(8,128)}, f32[4,256,128]{2,1,0:T(8,128...) while((s32[]{:T(128)}, f32[2,64,128]{2,1,0:T(8,128)S(1)}, ...), condition=%wide.region_28.29_spmd, body=%wide.region_18.28_spmd.sunk | while | flops 605426688 | bytes 8532093 | solution.py:74
  161.3 2.0 fusion.202
  167.2 2.5 reduce-window.94
  170.6 2.0 fusion.204
  172.5 1.3 convolution_bitcast_fusion.5
  175.1 2.2 fusion.201
  179.2 2.0 fusion.202
  185.2 2.5 reduce-window.94
  188.5 1.9 fusion.204
  190.5 1.3 convolution_bitcast_fusion.5
  193.0 2.2 fusion.201
  197.2 2.0 fusion.202
  203.1 2.5 reduce-window.94
  206.4 1.9 fusion.204
  208.4 1.3 convolution_bitcast_fusion.5
  209.7 1.3 fusion.203
  210.9 2.2 fusion.201
  215.1 2.0 fusion.202
  221.0 2.5 reduce-window.94
  224.4 1.9 fusion.204
  226.4 1.3 convolution_bitcast_fusion.5
  228.9 2.2 fusion.201
  232.1 2.3 pad_maximum_fusion
  235.7 4.4 %collective-permute-start.2 = (f32[3,128]{0,1:T(8,128)S(1)}, f32[3,128]{0,1:T(8,128)S(1)}, u32[]{:S(2)}, u32[]{:S(2)}) collective-permute-start(f32[3,128]{0,1:T(8,128)S(1)} %slice.326), channel_id=1, source_target_pairs={{64,0},{128,64},{192,128},{65,1},{129,65},{193,129},{66,2},{130,66... | collective-permute-start | bytes 4616 | tf_op jit(solution)/shard_map/ppermute | solution.py:18
  240.3 1.7 collective-permute-done.2
  243.6 179.5 %all-reduce.5.cloned.1.call-done = f32[1024,256]{1,0:T(8,128)} async-done(((f32[1024,256]{1,0:T(8,128)}), f32[1024,256]{1,0:T(8,128)}) %all-reduce.5.cloned.1.call-update) | async-done | bytes 1048592 | tf_op jit(solution)/shard_map/psum | solution.py:202
  423.1 1.6 multiply_multiply_fusion
  424.7 2.4 collective-permute-start.3
  427.3 2.9 collective-permute-done.3
  (471 shorter events, 119.3 us)
Async XLA Ops:
  7.2 15.9 %copy-start.8 = (u32[256]{0:T(256)S(1)}, u32[256]{0:T(256)}, u32[]{:S(2)}) copy-start(u32[256]{0:T(256)} %constant.306) | copy-start | bytes 3076
  7.2 415.9 %all-reduce.5.cloned.1.call-start = ((), (), s32[]{:S(2)}) async-start(), calls=%async_computation | async-start | bytes 2097152 | tf_op jit(solution)/shard_map/psum | solution.py:202
  7.9 18.3 %collective-permute-start.1 = (bf16[3,256]{1,0:T(4,128)(2,1)S(1)}, bf16[3,256]{1,0:T(4,128)(2,1)S(1)}, u32[]{:S(2)}, u32[]{:S(2)}) collective-permute-start(bf16[3,256]{1,0:T(4,128)(2,1)S(1)} %slice.266), channel_id=1, source_target_pairs={{0,64},{64,128},{128,192},{1,65},{65,129},{129,193},{2,66},{66,130... | collective-permute-start | bytes 4616 | tf_op jit(solution)/shard_map/ppermute | solution.py:18
  12.2 12.1 %collective-permute-start = (bf16[3,128]{0,1:T(8,128)(2,1)S(1)}, bf16[3,128]{0,1:T(8,128)(2,1)S(1)}, u32[]{:S(2)}, u32[]{:S(2)}) collective-permute-start(bf16[3,128]{0,1:T(8,128)(2,1)S(1)} %copy.62), channel_id=1, source_target_pairs={{0,64},{64,128},{128,192},{1,65},{65,129},{129,193},{2,66},{66,130... | collective-permute-start | bytes 2312 | tf_op jit(solution)/shard_map/ppermute | solution.py:18
  20.7 5.2 %copy-start.6 = (f32[128]{0:T(128)}, f32[128]{0:T(128)S(1)}, u32[]{:S(2)}) copy-start(f32[128]{0:T(128)S(1)} %get-tuple-element.1930) | copy-start | bytes 1540
  24.5 1.7 copy-start.3
  28.1 0.7 copy-start.4
  123.7 0.6 copy-start.9
  155.3 4.9 %copy-start.10 = (f32[4]{0:T(128)S(1)}, f32[4]{0:T(128)}, u32[]{:S(2)}) copy-start(f32[4]{0:T(128)} %copy-done.9) | copy-start | bytes 52
  232.1 2.7 copy-start.5
  232.1 2.4 copy-start.2
  234.4 1.0 copy-start.1
  234.4 7.6 %copy-start.7 = (f32[128]{0:T(128)S(1)}, f32[128]{0:T(128)}, u32[]{:S(2)}) copy-start(f32[128]{0:T(128)} %copy-done.6) | copy-start | bytes 1540
  234.9 188.2 %copy-start = (f32[1024,256]{1,0:T(8,128)S(1)}, f32[1024,256]{1,0:T(8,128)}, u32[]{:S(2)}) copy-start(f32[1024,256]{1,0:T(8,128)} %get-tuple-element.1887) | copy-start | bytes 3145732
  235.7 6.3 %collective-permute-start.2 = (f32[3,128]{0,1:T(8,128)S(1)}, f32[3,128]{0,1:T(8,128)S(1)}, u32[]{:S(2)}, u32[]{:S(2)}) collective-permute-start(f32[3,128]{0,1:T(8,128)S(1)} %slice.326), channel_id=1, source_target_pairs={{64,0},{128,64},{192,128},{65,1},{129,65},{193,129},{66,2},{130,66... | collective-permute-start | bytes 4616 | tf_op jit(solution)/shard_map/ppermute | solution.py:18
  424.7 5.5 %collective-permute-start.3 = (f32[3,256]{1,0:T(4,128)S(1)}, f32[3,256]{1,0:T(4,128)S(1)}, u32[]{:S(2)}, u32[]{:S(2)}) collective-permute-start(f32[3,256]{1,0:T(4,128)S(1)} %slice.334), channel_id=1, source_target_pairs={{64,0},{128,64},{192,128},{65,1},{129,65},{193,129},{66,2},{130,66... | collective-permute-start | bytes 9224 | tf_op jit(solution)/shard_map/ppermute | solution.py:18
Sparse Core Ops, SparseCore 0:
  234.5 188.4 all-reduce.4
where the time goes:
time: 440 us; the launch traced here: 438 us
  waiting for transfers between devices  184 us (42%)
  other arithmetic  66.9 us (15%)
  local copies, waits for them, and re-layouts  62.9 us (14%)
  matrix products  47.6 us (11%)
  blocking collectives  31.9 us (7%)
  loops' own time  15.8 us (4%)
  between operations  15.1 us (3%)
  starting transfers between devices  13.6 us (3%)
    psum x1, waiting for transfers between devices, local(): summed = lax.psum(grad_v_bc, 'head')  179 us
    dot_general x48, matrix products, matmul(): jnp.dot(left, right, precision=precise, preferred_element_type=jnp.float32)  46.4 us
    all_gather x2, blocking collectives, entering(): pieces = jax.tree.map(lambda part: lax.all_gather(part, axis), value)  23.5 us
    another operation x53, other arithmetic  21.8 us
    dynamic_update_slice x32, other arithmetic, head_forward(): lax.scan(head_advance, state, (x_head, b_blocks, c_blocks, log_head, note...  19.2 us
    dynamic_update_slice x32, local copies, waits for them, and re-layouts, head_forward(): lax.scan(head_advance, state, (x_head, b_blocks, c_blocks, log_head, note...  13.6 us
    ppermute x4, starting transfers between devices, shifted(): lax.ppermute(value, axis, [(source, source + steps) for source in range(i...  13.5 us
  transfers between devices with their start and end apart: 5, of which 3 were waited for; matrix products, arithmetic and copies ran while one was open for 3% of the time, Pallas kernels for 0%

commit v1 on v0

--- a/solution.py
+++ b/solution.py
@@ -197,14 +197,11 @@
     grad_v_x = grad_x_heads.transpose(1, 2, 0, 3).reshape(tok_rows, head_count * P_SIZE)
     grad_v_bc = jnp.concatenate([grad_b.reshape(tok_rows, N), grad_c.reshape(tok_rows, N)], axis=1)
     grad_u_x = grad_v_x * silu_slope(u_x)
-    share_rows = tok_rows // lax.axis_size("head")
-    row_start = lax.axis_index("head") * share_rows
-    summed = lax.psum(grad_v_bc, "head")
-    grad_u_bc = summed * silu_slope(u_bc)
+    grad_u_bc = grad_v_bc * silu_slope(u_bc)
     after_x, after_bc = shifted((grad_u_x[:rim_width], grad_u_bc[:rim_width]), "seq", -1)
     grad_pre_x = conv_backward(jnp.concatenate([grad_u_x, after_x]), conv_x, note_all[rim_width:])
     whole_bc = conv_backward(jnp.concatenate([grad_u_bc, after_bc]), conv_bc, note_all[rim_width:])
-    grad_pre_bc = lax.dynamic_slice_in_dim(whole_bc, row_start, share_rows, 0)
+    grad_pre_bc = lax.psum_scatter(whole_bc, "head", scatter_dimension=0, tiled=True)
     return (grad_pre_x, grad_pre_bc, grad_log_decay)
 
 

time: 440 us -> 386 us (0.88)
  waiting for transfers between devices: 184 us -> 137 us
  local copies, waits for them, and re-layouts: 62.9 us -> 51.8 us
    psum x1 -> x0, waiting for transfers between devices: 179 us -> none  [local(): summed = lax.psum(grad_v_bc, 'head')]
    reduce_scatter x0 -> x1, waiting for transfers between devices: none -> 134 us  [local(): lax.psum_scatter(whole_bc, 'head', scatter_dimension=0, tiled=True)]
where the time goes in v1:
time: 386 us; the launch traced here: 384 us
  waiting for transfers between devices  137 us (35%)
  other arithmetic  65.5 us (17%)
  local copies, waits for them, and re-layouts  51.8 us (13%)
  matrix products  50.9 us (13%)
  blocking collectives  31.9 us (8%)
  loops' own time  16.1 us (4%)
  starting transfers between devices  15.6 us (4%)
  between operations  15.1 us (4%)
    reduce_scatter x1, waiting for transfers between devices, local(): lax.psum_scatter(whole_bc, 'head', scatter_dimension=0, tiled=True)  134 us
    dot_general x48, matrix products, matmul(): jnp.dot(left, right, precision=precise, preferred_element_type=jnp.float32)  49.8 us
    all_gather x2, blocking collectives, entering(): pieces = jax.tree.map(lambda part: lax.all_gather(part, axis), value)  22.5 us
    another operation x53, other arithmetic  21.8 us
    dynamic_update_slice x32, other arithmetic, head_forward(): lax.scan(head_advance, state, (x_head, b_blocks, c_blocks, log_head, note...  16.8 us
    ppermute x4, starting transfers between devices, shifted(): lax.ppermute(value, axis, [(source, source + steps) for source in range(i...  15.5 us
    dynamic_update_slice x32, local copies, waits for them, and re-layouts, head_forward(): lax.scan(head_advance, state, (x_head, b_blocks, c_blocks, log_head, note...  11.1 us
    unnamed x1, blocking collectives  9.47 us
  transfers between devices with their start and end apart: 5, of which 3 were waited for; matrix products, arithmetic and copies ran while one was open for 3% of the time, Pallas kernels for 0%

profile of v1, /device:TPU:8, one launch (start us, length us, event | category | flops | bytes accessed | tf_op | source)
XLA Modules:
  0.0 383.7 jit_solution(7631072621133922212)
XLA Ops:
  7.9 3.5 collective-permute-start.1
  12.2 3.2 collective-permute-start
  24.4 1.3 fusion.130
  27.3 1.8 fusion.112
  29.8 19.1 %while.133 = (s32[]{:T(128)}, f32[2,64,128]{2,1,0:T(8,128)S(1)}, f32[2]{0:T(128)S(1)}, f32[4,2,256]{2,1,0:T(2,128)S(1)}, s32[4,256]{1,0:T(4,128)S(1)}, /*index=5...) while((s32[]{:T(128)}, f32[2,64,128]{2,1,0:T(8,128)S(1)}, ...), condition=%wide.region_5.6_spmd.clone, body=%wide.region_2.5_spmd.clone.sunk | while | flops 50480656 | bytes 424810 | solution.py:158
  49.2 11.2 %all-gather.2 = f32[8,64,128]{2,1,0:T(8,128)S(1)} all-gather(f32[2,64,128]{2,1,0:T(8,128)S(1)} %get-tuple-element.1220), channel_id=4, replica_groups=mesh['seq'=4,'head'=64] {'seq'}, dimensions={0}, use_global_device_ids=true | all-gather | bytes 327680 | tf_op jit(solution)/shard_map/all_gather | solution.py:23
  60.4 9.5 %all-reduce.2 = f32[8]{0:T(128)S(1)} all-reduce(f32[8]{0:T(128)S(1)} %dynamic-update-slice), channel_id=2, replica_groups=mesh['seq'=4,'head'=64] {'seq'}, use_global_device_ids=true, to_apply=%add.2 | all-reduce | flops 8 | bytes 64
  70.3 50.7 %while.132 = (s32[]{:T(128)}, f32[2,64,128]{2,1,0:T(8,128)S(1)}, f32[4,2,256]{2,1,0:T(2,128)S(1)}, f32[4,1,256]{2,1,0:T(1,128)S(1)}, f32[4,2,256]{2,1,0:T(2,128)...) while((s32[]{:T(128)}, f32[2,64,128]{2,1,0:T(8,128)S(1)}, ...), condition=%wide.region_17.18_spmd.clone.clone, body=%wide.region_14.17_spmd.clone.clone.sunk | while | flops 202543632 | bytes 5584975 | solution.py:74
  73.9 1.3 multiply_dynamic-update-slice_fusion.2
  86.5 1.3 multiply_dynamic-update-slice_fusion.2
  99.2 1.3 multiply_dynamic-update-slice_fusion.2
  111.9 1.3 multiply_dynamic-update-slice_fusion.2
  121.0 19.3 %while.134 = (s32[]{:T(128)}, f32[2,64,128]{2,1,0:T(8,128)S(1)}, f32[4,2,256]{2,1,0:T(2,128)S(1)}, s32[4,256]{1,0:T(4,128)S(1)}, s32[4]{0:T(128)S(1)}, /*index=5...) while((s32[]{:T(128)}, f32[2,64,128]{2,1,0:T(8,128)S(1)}, ...), condition=%wide.region_9.10_spmd.clone, body=%wide.region_6.9_spmd.clone.sunk | while | flops 50480144 | bytes 425292 | solution.py:170
  140.3 11.2 %all-gather.1 = f32[8,64,128]{2,1,0:T(8,128)S(1)} all-gather(f32[2,64,128]{2,1,0:T(8,128)S(1)} %get-tuple-element.1218), channel_id=3, replica_groups=mesh['seq'=4,'head'=64] {'seq'}, dimensions={0}, use_global_device_ids=true | all-gather | bytes 327680 | tf_op jit(solution)/shard_map/all_gather | solution.py:23
  154.4 69.9 %while.131 = (s32[]{:T(128)}, f32[2,64,128]{2,1,0:T(8,128)S(1)}, f32[4,2,256,64]{2,3,1,0:T(8,128)}, f32[4,256,128]{2,1,0:T(8,128)}, f32[4,256,128]{2,1,0:T(8,128...) while((s32[]{:T(128)}, f32[2,64,128]{2,1,0:T(8,128)S(1)}, ...), condition=%wide.region_28.29_spmd, body=%wide.region_18.28_spmd.sunk | while | flops 605426688 | bytes 8532093 | solution.py:74
  155.5 2.0 fusion.205
  160.7 2.5 reduce-window.94
  163.7 1.2 convolution_bitcast_fusion.6
  164.9 2.0 fusion.207
  166.9 1.3 convolution_bitcast_fusion.5
  168.2 1.2 fusion.206
  169.4 2.2 fusion.204
  173.0 2.0 fusion.205
  178.2 2.5 reduce-window.94
  182.4 1.9 fusion.207
  184.4 1.3 convolution_bitcast_fusion.5
  185.7 1.2 fusion.206
  186.9 2.2 fusion.204
  190.4 2.0 fusion.205
  195.7 2.5 reduce-window.94
  198.6 1.2 convolution_bitcast_fusion.6
  199.9 1.9 fusion.207
  201.8 1.3 convolution_bitcast_fusion.5
  203.1 1.2 fusion.206
  204.4 2.2 fusion.204
  207.9 2.0 fusion.205
  213.2 2.5 reduce-window.94
  217.4 1.9 fusion.207
  219.3 1.3 convolution_bitcast_fusion.5
  220.6 1.2 fusion.206
  221.8 2.2 fusion.204
  224.3 1.9 maximum_multiply_fusion
  226.3 4.7 %collective-permute-start.3 = (f32[3,256]{1,0:T(4,128)S(1)}, f32[3,256]{1,0:T(4,128)S(1)}, u32[]{:S(2)}, u32[]{:S(2)}) collective-permute-start(f32[3,256]{1,0:T(4,128)S(1)} %slice.334), channel_id=1, source_target_pairs={{64,0},{128,64},{192,128},{65,1},{129,65},{193,129},{66,2},{130,66... | collective-permute-start | bytes 9224 | tf_op jit(solution)/shard_map/ppermute | solution.py:18
  231.0 1.3 collective-permute-done.3
  232.3 2.1 fusion.100
  235.6 4.2 %collective-permute-start.2 = (f32[3,128]{0,1:T(8,128)S(1)}, f32[3,128]{0,1:T(8,128)S(1)}, u32[]{:S(2)}, u32[]{:S(2)}) collective-permute-start(f32[3,128]{0,1:T(8,128)S(1)} %slice.326), channel_id=1, source_target_pairs={{64,0},{128,64},{192,128},{65,1},{129,65},{193,129},{66,2},{130,66... | collective-permute-start | bytes 4616 | tf_op jit(solution)/shard_map/ppermute | solution.py:18
  239.8 2.0 collective-permute-done.2
  243.4 133.5 %reduce-scatter.2.cloned.1.call-done = f32[16,256]{1,0:T(8,128)} async-done(((f32[1024,256]{1,0:T(8,128)}), f32[16,256]{1,0:T(8,128)}) %reduce-scatter.2.cloned.1.call-update) | async-done | bytes 16400 | tf_op jit(solution)/shard_map/reduce_scatter | solution.py:204
  (453 shorter events, 109.3 us)
Async XLA Ops:
  7.2 15.9 %copy-start.4 = (u32[256]{0:T(256)S(1)}, u32[256]{0:T(256)}, u32[]{:S(2)}) copy-start(u32[256]{0:T(256)} %constant.301) | copy-start | bytes 3076
  7.2 369.7 %reduce-scatter.2.cloned.1.call-start = ((), (), s32[]{:S(2)}) async-start(), calls=%async_computation.1 | async-start | bytes 1064960 | tf_op jit(solution)/shard_map/reduce_scatter | solution.py:204
  7.9 18.2 %collective-permute-start.1 = (bf16[3,256]{1,0:T(4,128)(2,1)S(1)}, bf16[3,256]{1,0:T(4,128)(2,1)S(1)}, u32[]{:S(2)}, u32[]{:S(2)}) collective-permute-start(bf16[3,256]{1,0:T(4,128)(2,1)S(1)} %slice.266), channel_id=1, source_target_pairs={{0,64},{64,128},{128,192},{1,65},{65,129},{129,193},{2,66},{66,130... | collective-permute-start | bytes 4616 | tf_op jit(solution)/shard_map/ppermute | solution.py:18
  12.2 12.1 %collective-permute-start = (bf16[3,128]{0,1:T(8,128)(2,1)S(1)}, bf16[3,128]{0,1:T(8,128)(2,1)S(1)}, u32[]{:S(2)}, u32[]{:S(2)}) collective-permute-start(bf16[3,128]{0,1:T(8,128)(2,1)S(1)} %copy.62), channel_id=1, source_target_pairs={{0,64},{64,128},{128,192},{1,65},{65,129},{129,193},{2,66},{66,130... | collective-permute-start | bytes 2312 | tf_op jit(solution)/shard_map/ppermute | solution.py:18
  29.1 0.7 copy-start.2
  224.3 10.0 %copy-start.3 = (f32[4,2,256]{2,1,0:T(2,128)}, f32[4,2,256]{2,1,0:T(2,128)S(1)}, u32[]{:S(2)}) copy-start(f32[4,2,256]{2,1,0:T(2,128)S(1)} %get-tuple-element.1245) | copy-start | bytes 24580
  226.3 8.1 %copy-start.1 = (f32[4,2,256,64]{2,3,1,0:T(8,128)S(1)}, f32[4,2,256,64]{2,3,1,0:T(8,128)}, u32[]{:S(2)}) copy-start(f32[4,2,256,64]{2,3,1,0:T(8,128)} %get-tuple-element.1242) | copy-start | bytes 1572868
  226.3 6.0 %collective-permute-start.3 = (f32[3,256]{1,0:T(4,128)S(1)}, f32[3,256]{1,0:T(4,128)S(1)}, u32[]{:S(2)}, u32[]{:S(2)}) collective-permute-start(f32[3,256]{1,0:T(4,128)S(1)} %slice.334), channel_id=1, source_target_pairs={{64,0},{128,64},{192,128},{65,1},{129,65},{193,129},{66,2},{130,66... | collective-permute-start | bytes 9224 | tf_op jit(solution)/shard_map/ppermute | solution.py:18
  234.4 1.0 copy-start
  235.6 6.2 %collective-permute-start.2 = (f32[3,128]{0,1:T(8,128)S(1)}, f32[3,128]{0,1:T(8,128)S(1)}, u32[]{:S(2)}, u32[]{:S(2)}) collective-permute-start(f32[3,128]{0,1:T(8,128)S(1)} %slice.326), channel_id=1, source_target_pairs={{64,0},{128,64},{192,128},{65,1},{129,65},{193,129},{66,2},{130,66... | collective-permute-start | bytes 4616 | tf_op jit(solution)/shard_map/ppermute | solution.py:18
Sparse Core Ops, SparseCore 0:
  234.5 142.3 reduce-scatter.1

commit v2 on v1

--- a/solution.py
+++ b/solution.py
@@ -201,7 +201,9 @@
     after_x, after_bc = shifted((grad_u_x[:rim_width], grad_u_bc[:rim_width]), "seq", -1)
     grad_pre_x = conv_backward(jnp.concatenate([grad_u_x, after_x]), conv_x, note_all[rim_width:])
     whole_bc = conv_backward(jnp.concatenate([grad_u_bc, after_bc]), conv_bc, note_all[rim_width:])
-    grad_pre_bc = lax.psum_scatter(whole_bc, "head", scatter_dimension=0, tiled=True)
+    head_size = lax.axis_size("head")
+    pieces = whole_bc.reshape(head_size, tok_rows // head_size, whole_bc.shape[1])
+    grad_pre_bc = lax.all_to_all(pieces, "head", 0, 0, tiled=False).sum(0)
     return (grad_pre_x, grad_pre_bc, grad_log_decay)
 
 

time: 386 us -> 274 us (0.71)
  waiting for transfers between devices: 137 us -> 23 us
  between operations: 15.1 us -> 1.68 us
  starting transfers between devices: 15.6 us -> 27.5 us
    reduce_scatter x1 -> x0, waiting for transfers between devices: 134 us -> none  [local(): lax.psum_scatter(whole_bc, 'head', scatter_dimension=0, tiled=True)]
    all_to_all x0 -> x1, waiting for transfers between devices: none -> 19.7 us  [local(): grad_pre_bc = lax.all_to_all(pieces, 'head', 0, 0, tiled=False).sum(0)]
    all_to_all x0 -> x1, starting transfers between devices: none -> 12.1 us  [local(): grad_pre_bc = lax.all_to_all(pieces, 'head', 0, 0, tiled=False).sum(0)]
  transfers between devices with their start and end apart: 5 -> 5, of which waited for: 3 -> 3; matrix products, arithmetic and copies ran while one was open for 3% -> 5% of each run, Pallas kernels for 0% -> 0%
where the time goes in v2:
time: 274 us; the launch traced here: 269 us
  other arithmetic  66.2 us (24%)
  local copies, waits for them, and re-layouts  51.3 us (19%)
  matrix products  50.9 us (19%)
  blocking collectives  31.9 us (12%)
  starting transfers between devices  27.5 us (10%)
  waiting for transfers between devices  23 us (8%)
  loops' own time  16.1 us (6%)
    dot_general x48, matrix products, matmul(): jnp.dot(left, right, precision=precise, preferred_element_type=jnp.float32)  49.8 us
    all_gather x2, blocking collectives, entering(): pieces = jax.tree.map(lambda part: lax.all_gather(part, axis), value)  22.5 us
    another operation x53, other arithmetic  21.8 us
    all_to_all x1, waiting for transfers between devices, local(): grad_pre_bc = lax.all_to_all(pieces, 'head', 0, 0, tiled=False).sum(0)  19.7 us
    dynamic_update_slice x32, other arithmetic, head_forward(): lax.scan(head_advance, state, (x_head, b_blocks, c_blocks, log_head, note...  16.8 us
    ppermute x4, starting transfers between devices, shifted(): lax.ppermute(value, axis, [(source, source + steps) for source in range(i...  15.4 us
    all_to_all x1, starting transfers between devices, local(): grad_pre_bc = lax.all_to_all(pieces, 'head', 0, 0, tiled=False).sum(0)  12.1 us
    dynamic_update_slice x32, local copies, waits for them, and re-layouts, head_forward(): lax.scan(head_advance, state, (x_head, b_blocks, c_blocks, log_head, note...  11.1 us
  transfers between devices with their start and end apart: 5, of which 3 were waited for; matrix products, arithmetic and copies ran while one was open for 5% of the time, Pallas kernels for 0%

profile of v2, /device:TPU:8, one launch (start us, length us, event | category | flops | bytes accessed | tf_op | source)
XLA Modules:
  0.0 268.6 jit_solution(10583746927824137356)
XLA Ops:
  1.3 3.5 %collective-permute-start.1 = (bf16[3,256]{1,0:T(4,128)(2,1)S(1)}, bf16[3,256]{1,0:T(4,128)(2,1)S(1)}, u32[]{:S(2)}, u32[]{:S(2)}) collective-permute-start(bf16[3,256]{1,0:T(4,128)(2,1)S(1)} %slice.266), channel_id=1, source_target_pairs={{0,64},{64,128},{128,192},{1,65},{65,129},{129,193},{2,66},{66,130... | collective-permute-start | bytes 4616 | tf_op jit(solution)/shard_map/ppermute | solution.py:18
  5.6 3.2 %collective-permute-start = (bf16[3,128]{0,1:T(8,128)(2,1)S(1)}, bf16[3,128]{0,1:T(8,128)(2,1)S(1)}, u32[]{:S(2)}, u32[]{:S(2)}) collective-permute-start(bf16[3,128]{0,1:T(8,128)(2,1)S(1)} %copy.62), channel_id=1, source_target_pairs={{0,64},{64,128},{128,192},{1,65},{65,129},{129,193},{2,66},{66,130... | collective-permute-start | bytes 2312 | tf_op jit(solution)/shard_map/ppermute | solution.py:18
  17.9 1.3 fusion.130
  20.7 1.8 fusion.112
  23.3 19.1 %while.133 = (s32[]{:T(128)}, f32[2,64,128]{2,1,0:T(8,128)S(1)}, f32[2]{0:T(128)S(1)}, f32[4,2,256]{2,1,0:T(2,128)S(1)}, s32[4,256]{1,0:T(4,128)S(1)}, /*index=5...) while((s32[]{:T(128)}, f32[2,64,128]{2,1,0:T(8,128)S(1)}, ...), condition=%wide.region_5.6_spmd.clone, body=%wide.region_2.5_spmd.clone.sunk | while | flops 50480656 | bytes 424810 | solution.py:158
  42.6 11.2 %all-gather.2 = f32[8,64,128]{2,1,0:T(8,128)S(1)} all-gather(f32[2,64,128]{2,1,0:T(8,128)S(1)} %get-tuple-element.1220), channel_id=4, replica_groups=mesh['seq'=4,'head'=64] {'seq'}, dimensions={0}, use_global_device_ids=true | all-gather | bytes 327680 | tf_op jit(solution)/shard_map/all_gather | solution.py:23
  53.8 9.5 %all-reduce.2 = f32[8]{0:T(128)S(1)} all-reduce(f32[8]{0:T(128)S(1)} %dynamic-update-slice), channel_id=2, replica_groups=mesh['seq'=4,'head'=64] {'seq'}, use_global_device_ids=true, to_apply=%add.2 | all-reduce | flops 8 | bytes 64
  63.8 50.7 %while.132 = (s32[]{:T(128)}, f32[2,64,128]{2,1,0:T(8,128)S(1)}, f32[4,2,256]{2,1,0:T(2,128)S(1)}, f32[4,1,256]{2,1,0:T(1,128)S(1)}, f32[4,2,256]{2,1,0:T(2,128)...) while((s32[]{:T(128)}, f32[2,64,128]{2,1,0:T(8,128)S(1)}, ...), condition=%wide.region_17.18_spmd.clone.clone, body=%wide.region_14.17_spmd.clone.clone.sunk | while | flops 202543632 | bytes 5584975 | solution.py:74
  67.3 1.3 multiply_dynamic-update-slice_fusion.2
  79.9 1.3 multiply_dynamic-update-slice_fusion.2
  92.6 1.3 multiply_dynamic-update-slice_fusion.2
  105.3 1.3 multiply_dynamic-update-slice_fusion.2
  114.5 19.3 %while.134 = (s32[]{:T(128)}, f32[2,64,128]{2,1,0:T(8,128)S(1)}, f32[4,2,256]{2,1,0:T(2,128)S(1)}, s32[4,256]{1,0:T(4,128)S(1)}, s32[4]{0:T(128)S(1)}, /*index=5...) while((s32[]{:T(128)}, f32[2,64,128]{2,1,0:T(8,128)S(1)}, ...), condition=%wide.region_9.10_spmd.clone, body=%wide.region_6.9_spmd.clone.sunk | while | flops 50480144 | bytes 425292 | solution.py:170
  133.8 11.2 %all-gather.1 = f32[8,64,128]{2,1,0:T(8,128)S(1)} all-gather(f32[2,64,128]{2,1,0:T(8,128)S(1)} %get-tuple-element.1218), channel_id=3, replica_groups=mesh['seq'=4,'head'=64] {'seq'}, dimensions={0}, use_global_device_ids=true | all-gather | bytes 327680 | tf_op jit(solution)/shard_map/all_gather | solution.py:23
  147.8 69.9 %while.131 = (s32[]{:T(128)}, f32[2,64,128]{2,1,0:T(8,128)S(1)}, f32[4,2,256,64]{2,3,1,0:T(8,128)}, f32[4,256,128]{2,1,0:T(8,128)}, f32[4,256,128]{2,1,0:T(8,128...) while((s32[]{:T(128)}, f32[2,64,128]{2,1,0:T(8,128)S(1)}, ...), condition=%wide.region_28.29_spmd, body=%wide.region_18.28_spmd.sunk | while | flops 605426688 | bytes 8532093 | solution.py:74
  148.9 2.0 fusion.205
  154.2 2.5 reduce-window.94
  157.1 1.2 convolution_bitcast_fusion.6
  158.4 2.0 fusion.207
  160.3 1.3 convolution_bitcast_fusion.5
  161.6 1.2 fusion.206
  162.9 2.2 fusion.204
  166.4 2.0 fusion.205
  171.6 2.5 reduce-window.94
  175.9 1.9 fusion.207
  177.8 1.3 convolution_bitcast_fusion.5
  179.1 1.2 fusion.206
  180.3 2.2 fusion.204
  183.9 2.0 fusion.205
  189.1 2.5 reduce-window.94
  193.3 1.9 fusion.207
  195.2 1.3 convolution_bitcast_fusion.5
  196.5 1.2 fusion.206
  197.8 2.2 fusion.204
  201.3 2.0 fusion.205
  206.6 2.5 reduce-window.94
  210.8 1.9 fusion.207
  212.7 1.3 convolution_bitcast_fusion.5
  214.0 1.2 fusion.206
  215.3 2.2 fusion.204
  217.8 1.9 maximum_multiply_fusion
  219.7 4.6 %collective-permute-start.3 = (f32[3,256]{1,0:T(4,128)S(1)}, f32[3,256]{1,0:T(4,128)S(1)}, u32[]{:S(2)}, u32[]{:S(2)}) collective-permute-start(f32[3,256]{1,0:T(4,128)S(1)} %slice.334), channel_id=1, source_target_pairs={{64,0},{128,64},{192,128},{65,1},{129,65},{193,129},{66,2},{130,66... | collective-permute-start | bytes 9224 | tf_op jit(solution)/shard_map/ppermute | solution.py:18
  224.3 1.3 collective-permute-done.3
  225.6 2.1 fusion.100
  227.7 12.1 %all-to-all-start = ((f32[64,16,256]{2,1,0:T(8,128)}), f32[64,16,256]{2,1,0:T(8,128)S(1)}, u32[]{:S(2)}, u32[]{:S(2)}) async-start(f32[64,16,256]{2,1,0:T(8,128)} %bitcast.58), calls=%async_computation | async-start | bytes 2097152 | tf_op jit(solution)/shard_map/all_to_all | solution.py:206
  240.4 4.2 %collective-permute-start.2 = (f32[3,128]{0,1:T(8,128)S(1)}, f32[3,128]{0,1:T(8,128)S(1)}, u32[]{:S(2)}, u32[]{:S(2)}) collective-permute-start(f32[3,128]{0,1:T(8,128)S(1)} %slice.326), channel_id=1, source_target_pairs={{64,0},{128,64},{192,128},{65,1},{129,65},{193,129},{66,2},{130,66... | collective-permute-start | bytes 4616 | tf_op jit(solution)/shard_map/ppermute | solution.py:18
  244.6 2.0 collective-permute-done.2
  248.2 19.7 %all-to-all-done = f32[64,16,256]{2,1,0:T(8,128)S(1)} async-done(((f32[64,16,256]{2,1,0:T(8,128)}), f32[64,16,256]{2,1,0:T(8,128)S(1)}, u32[]{:S(2)}, u32[]{:S(2)}) %all-to-all-start) | async-done | bytes 1048608 | tf_op jit(solution)/shard_map/all_to_all | solution.py:206
  (453 shorter events, 110.6 us)
Async XLA Ops:
  0.6 15.8 %copy-start.4 = (u32[256]{0:T(256)S(1)}, u32[256]{0:T(256)}, u32[]{:S(2)}) copy-start(u32[256]{0:T(256)} %constant.301) | copy-start | bytes 3076
  1.3 18.2 %collective-permute-start.1 = (bf16[3,256]{1,0:T(4,128)(2,1)S(1)}, bf16[3,256]{1,0:T(4,128)(2,1)S(1)}, u32[]{:S(2)}, u32[]{:S(2)}) collective-permute-start(bf16[3,256]{1,0:T(4,128)(2,1)S(1)} %slice.266), channel_id=1, source_target_pairs={{0,64},{64,128},{128,192},{1,65},{65,129},{129,193},{2,66},{66,130... | collective-permute-start | bytes 4616 | tf_op jit(solution)/shard_map/ppermute | solution.py:18
  5.6 12.1 %collective-permute-start = (bf16[3,128]{0,1:T(8,128)(2,1)S(1)}, bf16[3,128]{0,1:T(8,128)(2,1)S(1)}, u32[]{:S(2)}, u32[]{:S(2)}) collective-permute-start(bf16[3,128]{0,1:T(8,128)(2,1)S(1)} %copy.62), channel_id=1, source_target_pairs={{0,64},{64,128},{128,192},{1,65},{65,129},{129,193},{2,66},{66,130... | collective-permute-start | bytes 2312 | tf_op jit(solution)/shard_map/ppermute | solution.py:18
  22.6 0.7 copy-start.2
  217.7 9.9 %copy-start.3 = (f32[4,2,256]{2,1,0:T(2,128)}, f32[4,2,256]{2,1,0:T(2,128)S(1)}, u32[]{:S(2)}) copy-start(f32[4,2,256]{2,1,0:T(2,128)S(1)} %get-tuple-element.1245) | copy-start | bytes 24580
  219.7 5.9 %collective-permute-start.3 = (f32[3,256]{1,0:T(4,128)S(1)}, f32[3,256]{1,0:T(4,128)S(1)}, u32[]{:S(2)}, u32[]{:S(2)}) collective-permute-start(f32[3,256]{1,0:T(4,128)S(1)} %slice.334), channel_id=1, source_target_pairs={{64,0},{128,64},{192,128},{65,1},{129,65},{193,129},{66,2},{130,66... | collective-permute-start | bytes 9224 | tf_op jit(solution)/shard_map/ppermute | solution.py:18
  225.6 14.1 %copy-start.1 = (f32[4,2,256,64]{2,3,1,0:T(8,128)S(1)}, f32[4,2,256,64]{2,3,1,0:T(8,128)}, u32[]{:S(2)}) copy-start(f32[4,2,256,64]{2,3,1,0:T(8,128)} %get-tuple-element.1242) | copy-start | bytes 1572868
  227.7 12.5 %copy-start = (f32[1024,128]{0,1:T(8,128)S(1)}, f32[1024,128]{0,1:T(8,128)}, u32[]{:S(2)}) copy-start(f32[1024,128]{0,1:T(8,128)} %get-tuple-element.1889) | copy-start | bytes 1572868
  227.7 40.3 %all-to-all-start = ((f32[64,16,256]{2,1,0:T(8,128)}), f32[64,16,256]{2,1,0:T(8,128)S(1)}, u32[]{:S(2)}, u32[]{:S(2)}) async-start(f32[64,16,256]{2,1,0:T(8,128)} %bitcast.58), calls=%async_computation | async-start | bytes 2097152 | tf_op jit(solution)/shard_map/all_to_all | solution.py:206
  240.4 6.2 %collective-permute-start.2 = (f32[3,128]{0,1:T(8,128)S(1)}, f32[3,128]{0,1:T(8,128)S(1)}, u32[]{:S(2)}, u32[]{:S(2)}) collective-permute-start(f32[3,128]{0,1:T(8,128)S(1)} %slice.326), channel_id=1, source_target_pairs={{64,0},{128,64},{192,128},{65,1},{129,65},{193,129},{66,2},{130,66... | collective-permute-start | bytes 4616 | tf_op jit(solution)/shard_map/ppermute | solution.py:18

commit v3 on v2

--- a/solution.py
+++ b/solution.py
@@ -105,6 +105,46 @@
 
 def chain_combine(earlier, later):
     return (earlier[0] * later[0], later[0][:, None, None] * earlier[1] + later[1])
+
+
+def chain_in(value, keep, axis, direction):
+    count = lax.axis_size(axis)
+    packed = jnp.concatenate(
+        [value.reshape(value.shape[0], -1), jnp.broadcast_to(keep[:, None], (keep.shape[0], 128))], axis=1
+    )
+    total = jnp.zeros_like(value)
+    scale = jnp.ones_like(keep)
+    for distance in range(1, count):
+        arrived = shifted(packed, axis, direction * distance)
+        part = arrived[:, : value[0].size].reshape(value.shape)
+        total = total + scale[:, None, None] * part
+        scale = scale * arrived[:, value[0].size]
+    return total
+
+
+def einsum(spec, *operands):
+    return jnp.einsum(spec, *operands, precision=precise, preferred_element_type=jnp.float32)
+
+
+def block_forward_all(state, x_all, b_all, c_all, log_all, note_blocks, befores):
+    cumul = jnp.cumsum(log_all, axis=-1)
+    entry = jnp.exp(cumul) * (note_blocks == befores[:, None])
+    leave = jnp.exp(cumul[..., -1:] - cumul) * (note_blocks == note_blocks[:, -1:])
+    through = jnp.exp(cumul[..., -1]) * (note_blocks[:, -1] == befores)
+    length = note_blocks.shape[1]
+    lower = jnp.arange(length)[:, None] >= jnp.arange(length)[None, :]
+    linked = lower & (note_blocks[:, :, None] == note_blocks[:, None, :])
+    differences = cumul[..., :, None] - cumul[..., None, :]
+    decay_matrix = jnp.exp(jnp.where(linked, differences, 0.0)) * linked
+    scores = einsum("bin,bjn->bij", c_all, b_all) * decay_matrix
+    output = einsum("hbij,hbjp->hbip", scores, x_all)
+    chunk = einsum("hbjp,bjn->hbpn", x_all * leave[..., None], b_all)
+    starts = []
+    for block in range(note_blocks.shape[0]):
+        starts.append(state)
+        state = through[:, block, None, None] * state + chunk[:, block]
+    output = output + entry[..., None] * einsum("bin,hbpn->hbip", c_all, jnp.stack(starts, axis=1))
+    return (output, state)
 
 
 def local(pre_x, pre_bc, conv_x, conv_bc, log_decay, lengths, grad_out):
@@ -143,53 +183,29 @@
     note_blocks = note_ids.reshape(block_count, BLOCK)
     befores = jnp.concatenate([note_all[rim_width - 1 : rim_width], note_blocks[:-1, -1]])
 
-    def state_only(x_head, log_head):
-
-        def state_advance(carry, block):
-            x_block, b_block, log_block, note_block, note_before = block
-            _, _, leave, through = block_edges(log_block, note_block, note_before)
-            state, keep = carry
-            return (
-                (through * state + matmul((x_block * leave[:, None]).T, b_block), keep * through),
-                None,
-            )
-
-        start = (jnp.zeros((P_SIZE, N), jnp.float32), jnp.ones((), jnp.float32))
-        final, _ = lax.scan(
-            state_advance, start, (x_head, b_blocks, log_head, note_blocks, befores)
+    note_before = note_all[rim_width - 1]
+    log_rows = log_decay.astype(jnp.float32)
+    x_rows = v_x.reshape(tok_rows, head_count, P_SIZE)
+    g_rows = grad_out.astype(jnp.float32).reshape(tok_rows, head_count, P_SIZE)
+    shard_cumul = jnp.cumsum(log_rows, axis=-1)
+    keep = jnp.exp(shard_cumul[:, -1]) * (note_ids[-1] == note_before)
+    leave_rows = jnp.exp(shard_cumul[:, -1:] - shard_cumul) * (note_ids == note_ids[-1])
+    entry_rows = jnp.exp(shard_cumul) * (note_ids == note_before)
+    local_state = jnp.einsum(
+        "thp,ht,tn->hpn", x_rows, leave_rows, v_bc[:, :N], precision=precise,
+        preferred_element_type=jnp.float32,
+    )
+    local_adjoint = jnp.einsum(
+        "thp,ht,tn->hpn", g_rows, entry_rows, v_bc[:, N:], precision=precise,
+        preferred_element_type=jnp.float32,
+    )
+    state_in = chain_in(local_state, keep, "seq", 1)
+    adjoint_in = chain_in(local_adjoint, keep, "seq", -1)
+
+    def local_forward(x_all, b_all, c_all, log_all):
+        return block_forward_all(
+            state_in, x_all, b_all, c_all, log_all, note_blocks, befores
         )
-        return final
-
-    def adjoint_only(grad_head, log_head):
-
-        def retreat(carry, block):
-            grad_block, c_block, log_block, note_block, note_before = block
-            _, entry, _, through = block_edges(log_block, note_block, note_before)
-            return (through * carry + matmul((grad_block * entry[:, None]).T, c_block), None)
-
-        final, _ = lax.scan(
-            retreat,
-            jnp.zeros((P_SIZE, N), jnp.float32),
-            (grad_head, c_blocks, log_head, note_blocks, befores),
-            reverse=True,
-        )
-        return final
-
-    local_state, local_keep = jax.vmap(state_only)(x_heads, log_blocks)
-    local_adjoint = jax.vmap(adjoint_only)(grad_heads, log_blocks)
-    identity = (
-        jnp.ones((head_count,), jnp.float32),
-        jnp.zeros((head_count, P_SIZE, N), jnp.float32),
-    )
-    _, state_in = entering((local_keep, local_state), "seq", chain_combine, identity, False)
-    _, adjoint_in = entering((local_keep, local_adjoint), "seq", chain_combine, identity, True)
-
-    def local_forward(x_all, b_all, c_all, log_all):
-
-        def one_head(state, x_head, log_head):
-            return head_forward(state, x_head, b_all, c_all, log_head, note_blocks, befores)
-
-        return jax.vmap(one_head)(state_in, x_all, log_all)
 
     _, pull = jax.vjp(local_forward, x_heads, b_blocks, c_blocks, log_blocks)
     grad_x_heads, grad_b, grad_c, grad_log = pull((grad_heads, adjoint_in))

time: 274 us -> 128 us (0.47); the launches traced: 269 us -> 126 us
  other arithmetic: 66.2 us -> 33.7 us
  blocking collectives: 31.9 us -> 0 us
  matrix products: 50.9 us -> 20.7 us
  local copies, waits for them, and re-layouts: 51.3 us -> 21.7 us
  waiting for transfers between devices: 23 us -> 2.27 us
  starting transfers between devices: 27.5 us -> 45.1 us
  loops' own time: 16.1 us -> 0 us
    dot_general x48 -> x13, matrix products: 49.8 us -> 20.7 us  [the longest x11 19.3 us: einsum(): jnp.einsum(spec, *operands, precision=precise, preferred_element_type=jnp...]
    all_gather x2 -> x0, blocking collectives: 22.5 us -> none  [entering(): pieces = jax.tree.map(lambda part: lax.all_gather(part, axis), value)]
    all_to_all x1, waiting for transfers between devices: 19.7 us -> 0.01 us  [local(): grad_pre_bc = lax.all_to_all(pieces, 'head', 0, 0, tiled=False).sum(0)]
    ppermute x4 -> x10, starting transfers between devices: 15.4 us -> 32.9 us  [shifted(): lax.ppermute(value, axis, [(source, source + steps) for source in range(i...]
    dynamic_update_slice x32 -> x0, other arithmetic: 16.8 us -> none  [head_forward(): lax.scan(head_advance, state, (x_head, b_blocks, c_blocks, log_head, note...]
    another operation x6 -> x0, loops' own time: 16.1 us -> none  [the longest x2 5.54 us: head_forward(): lax.scan(head_advance, state, (x_head, b_blocks, c_blocks, log_head, note...]
    dynamic_update_slice x32 -> x0, local copies, waits for them, and re-layouts: 11.1 us -> none  [head_forward(): lax.scan(head_advance, state, (x_head, b_blocks, c_blocks, log_head, note...]
    dynamic_slice x32 -> x0, local copies, waits for them, and re-layouts: 9.91 us -> none  [the longest x24 7.54 us: state_only(): lax.scan(state_advance, start, (x_head, b_blocks, log_head, note_blocks,...]
  transfers between devices with their start and end apart: 5 -> 11, of which waited for: 3 -> 1; matrix products, arithmetic and copies ran while one was open for 5% -> 48% of each run, Pallas kernels for 0% -> 0%
where the time goes in v3:
time: 128 us; the launch traced here: 126 us
  starting transfers between devices  45.1 us (35%)
  other arithmetic  33.7 us (26%)
  local copies, waits for them, and re-layouts  21.7 us (17%)
  matrix products  20.7 us (16%)
  between operations  3.01 us (2%)
  waiting for transfers between devices  2.27 us (2%)
    ppermute x10, starting transfers between devices, shifted(): lax.ppermute(value, axis, [(source, source + steps) for source in range(i...  32.9 us
    dot_general x11, matrix products, einsum(): jnp.einsum(spec, *operands, precision=precise, preferred_element_type=jnp...  19.3 us
    another operation x9, other arithmetic  14.3 us
    all_to_all x1, starting transfers between devices, local(): grad_pre_bc = lax.all_to_all(pieces, 'head', 0, 0, tiled=False).sum(0)  12.2 us
    broadcast_in_dim x4, local copies, waits for them, and re-layouts, block_forward_all(): state = through[:, block, None, None] * state + chunk[:, block]  5.01 us
    add x2, other arithmetic, conv_backward(): result + weights[k][None, :] * extended[lag:lag + count] * linked[:, None]  3.64 us
    reduce_sum x2, other arithmetic, block_forward_all(): state = through[:, block, None, None] * state + chunk[:, block]  2.94 us
  transfers between devices with their start and end apart: 11, of which 1 were waited for; matrix products, arithmetic and copies ran while one was open for 48% of the time, Pallas kernels for 0%

profile of v3, /device:TPU:8, one launch (start us, length us, event | category | flops | bytes accessed | tf_op | source)
XLA Modules:
  0.0 126.4 jit_solution(14978747202610313103)
XLA Ops:
  0.7 0.7 slice.252
  1.4 3.5 %collective-permute-start = (bf16[3,256]{1,0:T(4,128)(2,1)S(1)}, bf16[3,256]{1,0:T(4,128)(2,1)S(1)}, u32[]{:S(2)}, u32[]{:S(2)}) collective-permute-start(bf16[3,256]{1,0:T(4,128)(2,1)S(1)} %slice.252), channel_id=1, source_target_pairs={{0,64},{64,128},{128,192},{1,65},{65,129},{129,193},{2,66},{66,130... | collective-permute-start | bytes 4616 | tf_op jit(solution)/shard_map/ppermute | solution.py:18
  5.7 3.2 %collective-permute-start.4 = (bf16[3,128]{0,1:T(8,128)(2,1)S(1)}, bf16[3,128]{0,1:T(8,128)(2,1)S(1)}, u32[]{:S(2)}, u32[]{:S(2)}) collective-permute-start(bf16[3,128]{0,1:T(8,128)(2,1)S(1)} %copy.231), channel_id=1, source_target_pairs={{0,64},{64,128},{128,192},{1,65},{65,129},{129,193},{2,66},{66,130... | collective-permute-start | bytes 2312 | tf_op jit(solution)/shard_map/ppermute | solution.py:18
  8.9 0.8 reduce-window.34
  11.1 2.0 %compare_convert_fusion = (f32[1024]{0:T(1024)S(1)}, f32[1024]{0:T(1024)S(1)}, f32[1024]{0:T(1024)}, f32[1024]{0:T(1024)}, f32[1024]{0:T(1024)}, /*index=5*/f32[...) fusion(s32[]{:T(128)} %bitcast.11, s32[1030]{0:T(1024)S(1)} %broadcast_add_fusion.2, s32[]{:T(128)} %bitcast.3), kind=kLoop, calls=%fused_computation.209 | loop fusion | flops 16384 | bytes 61448 | tf_op jit(solution)/shard_map/convert_element_type | solution.py:192
  14.9 0.8 fusion.127
  15.7 0.8 slice_bitcast_fusion.12
  16.6 0.7 reshape.469
  19.2 0.7 compare_convert_fusion.4
  20.0 2.4 %reduce-window.42 = f32[2,4,2,128]{3,2,1,0:T(2,128)S(1)} reduce-window(f32[2,4,2,128]{3,2,1,0:T(2,128)S(1)} %reshape.469, f32[]{:T(128)} %constant.34.clone.1), window={size=1x1x1x128 pad=0_0x0_0x0_0x127_0}, to_apply=%region_4.5 | reduce-window | flops 260096 | bytes 16388 | tf_op jit(solution)/shard_map/reduce-window.3
  23.0 1.0 compare_and_fusion
  24.7 0.8 slice_reduce_fusion.8
  27.2 1.2 maximum_convert_fusion
  28.3 1.0 fusion.35
  31.0 1.3 %collective-permute-start.2 = (f32[2,8320]{1,0:T(2,128)S(1)}, f32[2,8320]{1,0:T(2,128)S(1)}, u32[]{:S(2)}, u32[]{:S(2)}) collective-permute-start(f32[2,8320]{1,0:T(2,128)S(1)} %get-tuple-element.83), channel_id=1, source_target_pairs={{128,0},{192,64},{129,1},{193,65},{130,2},{194,66},{131,3},{195,67... | collective-permute-start | bytes 199688 | tf_op jit(solution)/shard_map/ppermute | solution.py:18
  32.3 2.6 %collective-permute-start.1 = (f32[2,8320]{1,0:T(2,128)S(1)}, f32[2,8320]{1,0:T(2,128)S(1)}, u32[]{:S(2)}, u32[]{:S(2)}) collective-permute-start(f32[2,8320]{1,0:T(2,128)S(1)} %get-tuple-element.83), channel_id=1, source_target_pairs={{64,0},{128,64},{192,128},{65,1},{129,65},{193,129},{66,2},{130,66... | collective-permute-start | bytes 199688 | tf_op jit(solution)/shard_map/ppermute | solution.py:18
  35.0 5.4 %collective-permute-start.7 = (f32[2,8320]{1,0:T(2,128)S(1)}, f32[2,8320]{1,0:T(2,128)S(1)}, u32[]{:S(2)}, u32[]{:S(2)}) collective-permute-start(f32[2,8320]{1,0:T(2,128)S(1)} %get-tuple-element.82), channel_id=1, source_target_pairs={{0,128},{64,192},{1,129},{65,193},{2,130},{66,194},{3,131},{67,195... | collective-permute-start | bytes 199688 | tf_op jit(solution)/shard_map/ppermute | solution.py:18
  40.4 1.9 %collective-permute-start.6 = (f32[2,8320]{1,0:T(2,128)S(1)}, f32[2,8320]{1,0:T(2,128)S(1)}, u32[]{:S(2)}, u32[]{:S(2)}) collective-permute-start(f32[2,8320]{1,0:T(2,128)S(1)} %get-tuple-element.82), channel_id=1, source_target_pairs={{0,64},{64,128},{128,192},{1,65},{65,129},{129,193},{2,66},{66,130... | collective-permute-start | bytes 199688 | tf_op jit(solution)/shard_map/ppermute | solution.py:18
  43.1 1.0 fusion.128
  44.1 0.7 convolution_bitcast_fusion.3
  44.9 4.4 %fusion.16 = (f32[2,4,256]{2,1,0:T(4,128)}, f32[2,4,256]{2,1,0:T(4,128)}, f32[4,256,256]{1,2,0:T(8,128)S(1)}, f32[2,4,256,256]{2,3,1,0:T(8,128)}) fusion(f32[4,256,256]{1,2,0:T(8,128)S(1)} %get-tuple-element.53, f32[2,4,256]{2,1,0:T(4,128)S(1)} %reduce_window_sum.72, f32[4,256,256]{1,2,0:T(8,128)S(1)} %fusion.128, pred[4,256,256]{1,2,0:T(8,128)(4,1)S(1)} %copy-done.16, ...), kind=kOutput, calls=%fused_computation.22 | convolution fusion | flops 408678400 | bytes 6316032 | tf_op jit(solution)/shard_map/transpose(jvp(hbij,hbjp->hbip))/dot_general | solution.py:126
  50.0 0.8 collective-permute-start.3
  51.7 1.0 fusion.88
  52.8 1.0 convolution_bitcast_fusion.2
  53.9 1.1 convolution_add_fusion.1
  55.1 1.0 convolution_bitcast_fusion.1
  56.1 1.9 %convolution_add_fusion = f32[4,256,128]{2,1,0:T(8,128)S(1)} fusion(f32[4,256,128]{2,1,0:T(8,128)S(1)} %convolution_bitcast_fusion.1, f32[4,256,256]{1,2,0:T(8,128)S(1)} %get-tuple-element.20, f32[4,256,128]{2,1,0:T(8,128)S(1)} %bitcast.328), kind=kOutput, calls=%fused_computation.13 | convolution fusion | flops 402784256 | bytes 2621440 | tf_op jit(solution)/shard_map/transpose(jvp(bin,bjn->bij))/dot_general | solution.py:126
  59.0 10.3 %collective-permute-start.9 = (f32[3,256]{1,0:T(4,128)}, f32[3,256]{1,0:T(4,128)}, u32[]{:S(2)}, u32[]{:S(2)}) collective-permute-start(f32[3,256]{1,0:T(4,128)} %slice.354), channel_id=1, source_target_pairs={{64,0},{128,64},{192,128},{65,1},{129,65},{193,129},{66,2},{130,66... | collective-permute-start | bytes 9224 | tf_op jit(solution)/shard_map/ppermute | solution.py:18
  69.3 1.3 %mul.857 = f32[4,2,128]{2,1,0:T(2,128)} reshape(f32[4,256]{1,0:T(4,128)} %copy-done.22) | data formatting | bytes 8192 | tf_op jit(solution)/shard_map/jvp()/mul | solution.py:132
  70.6 1.3 %copy.226 = f32[4,256,2]{1,2,0:T(2,128)} copy(f32[4,256,2]{1,0,2:T(4,128)} %bitcast.344) | data formatting | bytes 16384 | tf_op jit(solution)/shard_map/transpose(jvp())/mul | solution.py:141
  71.9 3.0 %fusion.23 = f32[1024,256]{1,0:T(8,128)} fusion(f32[3,256]{1,0:T(4,128)} %collective-permute-done.9, f32[1024,256]{1,0:T(8,128)S(1)} %maximum_multiply_fusion, f32[1024]{0:T(1024)} %get-tuple-element.62, f32[1024]{0:T(1024)} %get-tuple-element.63, f32[1024]{0:T(1024)} %get-tuple-element.64, f32[256]{0:T(256)} %bitcast.353, f32[256]{0:T(256)} %bitcast.355, ...), kind=kLoop, calls=%fused_computation.33 | loop fusion | flops 3407872 | bytes 2116608 | tf_op jit(solution)/shard_map/add | solution.py:97
  74.9 12.2 %all-to-all-start = ((f32[64,16,256]{2,1,0:T(8,128)}), f32[64,16,256]{2,1,0:T(8,128)S(1)}, u32[]{:S(2)}, u32[]{:S(2)}) async-start(f32[64,16,256]{2,1,0:T(8,128)} %bitcast.337), calls=%async_computation | async-start | bytes 2097152 | tf_op jit(solution)/shard_map/all_to_all | solution.py:222
  87.1 2.0 %fusion.98 = (f32[2]{0:T(128)}, f32[2]{0:T(128)}, f32[2]{0:T(128)}) fusion(f32[2,4,64,128]{3,2,0,1:T(8,128)} %copy-done.1, f32[2]{0:T(128)} %get-tuple-element.25, f32[2]{0:T(128)} %get-tuple-element.24, f32[2]{0:T(128)} %get-tuple-element.26, f32[2,4,64,128]{3,2,0,1:T(8,128)} %copy-done, f32[1,2,64,128]{3,1,2,0:T(2,128)} %copy-done.10, f32[2]{0:T(128)} %copy-done.40, ...), kind=kLoop, calls=%fused_computation.153 | loop fusion | flops 393210 | bytes 720984 | tf_op jit(solution)/shard_map/transpose(jvp())/reduce_sum | solution.py:145
  89.1 1.2 copy.239
  90.3 1.3 copy.240
  91.5 1.3 %copy.241 = f32[2,1]{1,0:T(2,128)} copy(f32[2,1]{0,1:T(1,128)} %bitcast.362) | data formatting | bytes 16 | tf_op jit(solution)/shard_map/transpose(jvp())/broadcast_in_dim | solution.py:145
  92.8 1.2 copy.238
  94.1 1.4 %multiply_bitcast_fusion.1 = f32[2,4,1]{1,0,2:T(2,128)} fusion(f32[2,1]{1,0:T(2,128)} %copy.241, f32[2,1]{1,0:T(2,128)} %copy.240, f32[2,1]{1,0:T(2,128)} %copy.239, f32[2,1]{1,0:T(2,128)} %copy.238, f32[2,4]{1,0:T(2,128)} %copy-done.26, f32[4]{0:T(128)} %copy-done.38), kind=kLoop, calls=%fused_computation.220 | loop fusion | flops 40 | bytes 112 | tf_op jit(solution)/shard_map/transpose(jvp())/broadcast_in_dim | solution.py:133
  95.4 1.4 %copy.242 = f32[2,4,1]{2,1,0:T(4,128)} copy(f32[2,4,1]{1,0,2:T(2,128)} %multiply_bitcast_fusion.1) | data formatting | bytes 64 | tf_op jit(solution)/shard_map/transpose(jvp())/broadcast_in_dim | solution.py:133
  96.8 3.0 %fusion.58 = (f32[2,4,256]{2,0,1:T(2,128)}, f32[4,2,64,256]{3,2,1,0:T(8,128)}) fusion(f32[4,256,2,64]{1,0,3,2:T(4,128)S(1)} %reshape.477, f32[4,256,128,1]{2,1,3,0:T(8,128)S(1)} %bitcast.329, f32[2,1,64,128]{3,2,0,1:T(8,128)} %copy-done.4, f32[2,1,64,128]{3,2,0,1:T(8,128)} %copy-done.5, f32[2,1,64,128]{3,2,0,1:T(8,128)} %copy-done.6, ...), kind=kOutput, calls=%fused_computation.87 | convolution fusion | flops 201783296 | bytes 1843200 | tf_op jit(solution)/shard_map/transpose(jvp(hbjp,bjn->hbpn))/dot_general | solution.py:126
  100.5 0.9 fusion.106
  101.5 1.5 %fusion.17 = f32[2,4,256]{2,0,1:T(2,128)S(1)} fusion(f32[4,256,128,1]{2,1,3,0:T(8,128)S(1)} %bitcast.333, bf16[4,256,2,64]{1,0,3,2:T(4,128)(2,1)S(1)} %reshape.472, f32[2,1,64,128]{3,2,0,1:T(8,128)S(1)} %get-tuple-element.47, f32[2,1,64,128]{3,2,0,1:T(8,128)S(1)} %get-tuple-element.48, f32[2,1,64,128]{3,2,0,1:T(8,128)} %copy-done.2, ...), kind=kOutput, calls=%fused_computation.23 | convolution fusion | flops 201914368 | bytes 1056768 | tf_op jit(solution)/shard_map/jvp(bin,hbpn->hbip)/dot_general | solution.py:126
  103.0 0.8 fusion.101
  103.8 10.1 %reduce-window.44 = f32[2,4,2,128]{3,2,1,0:T(2,128)S(1)} reduce-window(f32[2,4,2,128]{3,2,1,0:T(2,128)S(1)} %reshape.493, f32[]{:T(128)} %constant.34.clone.1), window={size=1x1x1x128 pad=0_0x0_0x0_0x0_127}, to_apply=%region_17.18 | reduce-window | flops 260096 | bytes 16388 | tf_op jit(solution)/shard_map/reduce-window.5
  114.2 3.0 %fusion.11 = f32[4,256,2,64]{1,3,2,0:T(8,128)S(1)} fusion(f32[2,4,256,256]{2,3,1,0:T(8,128)} %get-tuple-element.42, f32[4,2,64,256]{3,2,1,0:T(8,128)} %get-tuple-element.85, bf16[2,4,256,64]{2,1,3,0:T(4,128)(2,1)S(1)} %bitcast.335, f32[4,256,2]{1,2,0:T(2,128)} %copy.226), kind=kOutput, calls=%fused_computation.19 | convolution fusion | flops 402915328 | bytes 3416064 | tf_op jit(solution)/shard_map/transpose(jvp(hbij,hbjp->hbip))/dot_general | solution.py:126
  117.9 3.2 %collective-permute-start.5 = (f32[3,128]{0,1:T(8,128)S(1)}, f32[3,128]{0,1:T(8,128)S(1)}, u32[]{:S(2)}, u32[]{:S(2)}) collective-permute-start(f32[3,128]{0,1:T(8,128)S(1)} %slice.338), channel_id=1, source_target_pairs={{64,0},{128,64},{192,128},{65,1},{129,65},{193,129},{66,2},{130,66... | collective-permute-start | bytes 4616 | tf_op jit(solution)/shard_map/ppermute | solution.py:18
  121.8 2.2 %collective-permute-done.5 = f32[3,128]{0,1:T(8,128)S(1)} collective-permute-done((f32[3,128]{0,1:T(8,128)S(1)}, f32[3,128]{0,1:T(8,128)S(1)}, u32[]{:S(2)}, u32[]{:S(2)}) %collective-permute-start.5) | collective-permute-done | bytes 1568 | tf_op jit(solution)/shard_map/ppermute | solution.py:18
  124.7 1.0 copy.249
  (189 shorter events, 16.0 us)
Async XLA Ops:
  0.6 24.9 %copy-start.14 = (bf16[1024,128]{1,0:T(8,128)(2,1)S(1)}, bf16[1024,128]{1,0:T(8,128)(2,1)}, u32[]{:S(2)}) copy-start(bf16[1024,128]{1,0:T(8,128)(2,1)} %param.7) | copy-start | bytes 786436
  0.6 25.0 %copy-start.15 = (bf16[1024,128]{1,0:T(8,128)(2,1)S(1)}, bf16[1024,128]{1,0:T(8,128)(2,1)}, u32[]{:S(2)}) copy-start(bf16[1024,128]{1,0:T(8,128)(2,1)} %param.13) | copy-start | bytes 786436
  1.4 25.7 %collective-permute-start = (bf16[3,256]{1,0:T(4,128)(2,1)S(1)}, bf16[3,256]{1,0:T(4,128)(2,1)S(1)}, u32[]{:S(2)}, u32[]{:S(2)}) collective-permute-start(bf16[3,256]{1,0:T(4,128)(2,1)S(1)} %slice.252), channel_id=1, source_target_pairs={{0,64},{64,128},{128,192},{1,65},{65,129},{129,193},{2,66},{66,130... | collective-permute-start | bytes 4616 | tf_op jit(solution)/shard_map/ppermute | solution.py:18
  5.7 20.4 %collective-permute-start.4 = (bf16[3,128]{0,1:T(8,128)(2,1)S(1)}, bf16[3,128]{0,1:T(8,128)(2,1)S(1)}, u32[]{:S(2)}, u32[]{:S(2)}) collective-permute-start(bf16[3,128]{0,1:T(8,128)(2,1)S(1)} %copy.231), channel_id=1, source_target_pairs={{0,64},{64,128},{128,192},{1,65},{65,129},{129,193},{2,66},{66,130... | collective-permute-start | bytes 2312 | tf_op jit(solution)/shard_map/ppermute | solution.py:18
  15.7 12.6 %copy-start.31 = (f32[1,256]{1,0:T(1,128)}, f32[1,256]{1,0:T(1,128)S(1)}, u32[]{:S(2)}) copy-start(f32[1,256]{1,0:T(1,128)S(1)} %get-tuple-element.74) | copy-start | bytes 3076
  15.7 12.6 %copy-start.32 = (f32[1,256]{1,0:T(1,128)}, f32[1,256]{1,0:T(1,128)S(1)}, u32[]{:S(2)}) copy-start(f32[1,256]{1,0:T(1,128)S(1)} %get-tuple-element.75) | copy-start | bytes 3076
  15.7 12.6 %copy-start.33 = (f32[1,256]{1,0:T(1,128)}, f32[1,256]{1,0:T(1,128)S(1)}, u32[]{:S(2)}) copy-start(f32[1,256]{1,0:T(1,128)S(1)} %get-tuple-element.76) | copy-start | bytes 3076
  15.7 12.6 %copy-start.34 = (f32[1,256]{1,0:T(1,128)}, f32[1,256]{1,0:T(1,128)S(1)}, u32[]{:S(2)}) copy-start(f32[1,256]{1,0:T(1,128)S(1)} %get-tuple-element.77) | copy-start | bytes 3076
  16.6 9.7 %copy-start.42 = (f32[128]{0:T(128)}, f32[128]{0:T(128)S(1)}, u32[]{:S(2)}) copy-start(f32[128]{0:T(128)S(1)} %get-tuple-element.78) | copy-start | bytes 1540
  16.6 9.7 %copy-start.44 = (f32[128]{0:T(128)}, f32[128]{0:T(128)S(1)}, u32[]{:S(2)}) copy-start(f32[128]{0:T(128)S(1)} %get-tuple-element.79) | copy-start | bytes 1540
  16.6 9.7 %copy-start.46 = (f32[128]{0:T(128)}, f32[128]{0:T(128)S(1)}, u32[]{:S(2)}) copy-start(f32[128]{0:T(128)S(1)} %get-tuple-element.80) | copy-start | bytes 1540
  16.6 9.7 %copy-start.48 = (f32[128]{0:T(128)}, f32[128]{0:T(128)S(1)}, u32[]{:S(2)}) copy-start(f32[128]{0:T(128)S(1)} %get-tuple-element.81) | copy-start | bytes 1540
  19.9 4.8 %copy-start.38 = (f32[4]{0:T(128)}, f32[4]{0:T(128)S(1)}, u32[]{:S(2)}) copy-start(f32[4]{0:T(128)S(1)} %get-tuple-element.38) | copy-start | bytes 52
  20.0 6.9 %copy-start.22 = (f32[4,256]{1,0:T(4,128)}, f32[4,256]{1,0:T(4,128)S(1)}, u32[]{:S(2)}) copy-start(f32[4,256]{1,0:T(4,128)S(1)} %get-tuple-element.72) | copy-start | bytes 12292
  20.0 6.9 %copy-start.27 = (f32[4,256]{1,0:T(4,128)}, f32[4,256]{1,0:T(4,128)S(1)}, u32[]{:S(2)}) copy-start(f32[4,256]{1,0:T(4,128)S(1)} %get-tuple-element.73) | copy-start | bytes 12292
  23.0 3.9 %copy-start.26 = (f32[2,4]{1,0:T(2,128)}, f32[2,4]{1,0:T(2,128)S(1)}, u32[]{:S(2)}) copy-start(f32[2,4]{1,0:T(2,128)S(1)} %slice_reduce_fusion.1) | copy-start | bytes 100
  25.9 18.3 %copy-start.19 = (f32[2,4,256]{2,0,1:T(2,128)}, f32[2,4,256]{2,0,1:T(2,128)S(1)}, u32[]{:S(2)}) copy-start(f32[2,4,256]{2,0,1:T(2,128)S(1)} %copy.234) | copy-start | bytes 24580
  25.9 23.4 %copy-start.17 = (f32[4,2,256]{2,1,0:T(2,128)}, f32[4,2,256]{2,1,0:T(2,128)S(1)}, u32[]{:S(2)}) copy-start(f32[4,2,256]{2,1,0:T(2,128)S(1)} %copy.223) | copy-start | bytes 24580
  31.0 20.4 %collective-permute-start.2 = (f32[2,8320]{1,0:T(2,128)S(1)}, f32[2,8320]{1,0:T(2,128)S(1)}, u32[]{:S(2)}, u32[]{:S(2)}) collective-permute-start(f32[2,8320]{1,0:T(2,128)S(1)} %get-tuple-element.83), channel_id=1, source_target_pairs={{128,0},{192,64},{129,1},{193,65},{130,2},{194,66},{131,3},{195,67... | collective-permute-start | bytes 199688 | tf_op jit(solution)/shard_map/ppermute | solution.py:18
  32.3 19.2 %collective-permute-start.1 = (f32[2,8320]{1,0:T(2,128)S(1)}, f32[2,8320]{1,0:T(2,128)S(1)}, u32[]{:S(2)}, u32[]{:S(2)}) collective-permute-start(f32[2,8320]{1,0:T(2,128)S(1)} %get-tuple-element.83), channel_id=1, source_target_pairs={{64,0},{128,64},{192,128},{65,1},{129,65},{193,129},{66,2},{130,66... | collective-permute-start | bytes 199688 | tf_op jit(solution)/shard_map/ppermute | solution.py:18
  35.0 15.1 %collective-permute-start.7 = (f32[2,8320]{1,0:T(2,128)S(1)}, f32[2,8320]{1,0:T(2,128)S(1)}, u32[]{:S(2)}, u32[]{:S(2)}) collective-permute-start(f32[2,8320]{1,0:T(2,128)S(1)} %get-tuple-element.82), channel_id=1, source_target_pairs={{0,128},{64,192},{1,129},{65,193},{2,130},{66,194},{3,131},{67,195... | collective-permute-start | bytes 199688 | tf_op jit(solution)/shard_map/ppermute | solution.py:18
  40.4 10.6 %collective-permute-start.6 = (f32[2,8320]{1,0:T(2,128)S(1)}, f32[2,8320]{1,0:T(2,128)S(1)}, u32[]{:S(2)}, u32[]{:S(2)}) collective-permute-start(f32[2,8320]{1,0:T(2,128)S(1)} %get-tuple-element.82), channel_id=1, source_target_pairs={{0,64},{64,128},{128,192},{1,65},{65,129},{129,193},{2,66},{66,130... | collective-permute-start | bytes 199688 | tf_op jit(solution)/shard_map/ppermute | solution.py:18
  42.3 8.8 %collective-permute-start.8 = (f32[2,8320]{1,0:T(2,128)S(1)}, f32[2,8320]{1,0:T(2,128)S(1)}, u32[]{:S(2)}, u32[]{:S(2)}) collective-permute-start(f32[2,8320]{1,0:T(2,128)S(1)} %get-tuple-element.82), channel_id=1, source_target_pairs={{0,192},{1,193},{2,194},{3,195},{4,196},{5,197},{6,198},{7,199},{8... | collective-permute-start | bytes 199688 | tf_op jit(solution)/shard_map/ppermute | solution.py:18
  44.8 6.4 %copy-start.1 = (f32[2,4,64,128]{3,2,0,1:T(8,128)}, f32[2,4,64,128]{3,2,0,1:T(8,128)S(1)}, u32[]{:S(2)}) copy-start(f32[2,4,64,128]{3,2,0,1:T(8,128)S(1)} %convolution_bitcast_fusion.3) | copy-start | bytes 786436
  44.9 6.4 %copy-start.29 = (f32[2]{0:T(128)S(1)}, f32[2]{0:T(128)}, u32[]{:S(2)}) copy-start(f32[2]{0:T(128)} %get-tuple-element.25) | copy-start | bytes 28
  44.9 6.4 %copy-start.30 = (f32[2]{0:T(128)S(1)}, f32[2]{0:T(128)}, u32[]{:S(2)}) copy-start(f32[2]{0:T(128)} %get-tuple-element.26) | copy-start | bytes 28
  44.9 6.4 %copy-start.35 = (f32[2]{0:T(128)S(1)}, f32[2]{0:T(128)}, u32[]{:S(2)}) copy-start(f32[2]{0:T(128)} %get-tuple-element.24) | copy-start | bytes 28
  49.3 3.4 %copy-start.41 = (f32[2]{0:T(128)S(1)}, f32[2]{0:T(128)}, u32[]{:S(2)}) copy-start(f32[2]{0:T(128)} %get-tuple-element.27) | copy-start | bytes 28
  49.3 3.5 %copy-start.20 = (f32[2,4,256]{2,0,1:T(2,128)S(1)}, f32[2,4,256]{2,0,1:T(2,128)}, u32[]{:S(2)}) copy-start(f32[2,4,256]{2,0,1:T(2,128)} %copy-done.19) | copy-start | bytes 24580
  50.0 3.9 %copy-start = (f32[2,4,64,128]{3,2,0,1:T(8,128)}, f32[2,4,64,128]{3,2,0,1:T(8,128)S(1)}, u32[]{:S(2)}) copy-start(f32[2,4,64,128]{3,2,0,1:T(8,128)S(1)} %convolution_bitcast_fusion.4) | copy-start | bytes 786436
  50.0 1.6 %collective-permute-start.3 = (f32[2,8320]{1,0:T(2,128)S(1)}, f32[2,8320]{1,0:T(2,128)S(1)}, u32[]{:S(2)}, u32[]{:S(2)}) collective-permute-start(f32[2,8320]{1,0:T(2,128)S(1)} %get-tuple-element.83), channel_id=1, source_target_pairs={{192,0},{193,1},{194,2},{195,3},{196,4},{197,5},{198,6},{199,7},{2... | collective-permute-start | bytes 199688 | tf_op jit(solution)/shard_map/ppermute | solution.py:18
  51.2 3.8 %copy-start.36 = (f32[2]{0:T(128)}, f32[2]{0:T(128)S(1)}, u32[]{:S(2)}) copy-start(f32[2]{0:T(128)S(1)} %slice_reduce_fusion.5) | copy-start | bytes 28
  51.2 3.8 %copy-start.37 = (f32[2]{0:T(128)}, f32[2]{0:T(128)S(1)}, u32[]{:S(2)}) copy-start(f32[2]{0:T(128)S(1)} %mul.793) | copy-start | bytes 28
  51.4 3.7 %copy-start.2 = (f32[2,1,64,128]{3,2,0,1:T(8,128)}, f32[2,1,64,128]{3,2,0,1:T(8,128)S(1)}, u32[]{:S(2)}) copy-start(f32[2,1,64,128]{3,2,0,1:T(8,128)S(1)} %get-tuple-element.49) | copy-start | bytes 196612
  51.4 3.7 %copy-start.3 = (f32[2,1,64,128]{3,2,0,1:T(8,128)}, f32[2,1,64,128]{3,2,0,1:T(8,128)S(1)}, u32[]{:S(2)}) copy-start(f32[2,1,64,128]{3,2,0,1:T(8,128)S(1)} %get-tuple-element.50) | copy-start | bytes 196612
  51.6 3.4 %copy-start.39 = (f32[2]{0:T(128)}, f32[2]{0:T(128)S(1)}, u32[]{:S(2)}) copy-start(f32[2]{0:T(128)S(1)} %slice_reduce_fusion.7) | copy-start | bytes 28
  51.6 3.4 %copy-start.40 = (f32[2]{0:T(128)}, f32[2]{0:T(128)S(1)}, u32[]{:S(2)}) copy-start(f32[2]{0:T(128)S(1)} %mul.727) | copy-start | bytes 28
  52.8 3.3 %copy-start.4 = (f32[2,1,64,128]{3,2,0,1:T(8,128)}, f32[2,1,64,128]{3,2,0,1:T(8,128)S(1)}, u32[]{:S(2)}) copy-start(f32[2,1,64,128]{3,2,0,1:T(8,128)S(1)} %get-tuple-element.34) | copy-start | bytes 196612
  59.0 12.9 %collective-permute-start.9 = (f32[3,256]{1,0:T(4,128)}, f32[3,256]{1,0:T(4,128)}, u32[]{:S(2)}, u32[]{:S(2)}) collective-permute-start(f32[3,256]{1,0:T(4,128)} %slice.354), channel_id=1, source_target_pairs={{64,0},{128,64},{192,128},{65,1},{129,65},{193,129},{66,2},{130,66... | collective-permute-start | bytes 9224 | tf_op jit(solution)/shard_map/ppermute | solution.py:18
  74.9 50.8 %all-to-all-start = ((f32[64,16,256]{2,1,0:T(8,128)}), f32[64,16,256]{2,1,0:T(8,128)S(1)}, u32[]{:S(2)}, u32[]{:S(2)}) async-start(f32[64,16,256]{2,1,0:T(8,128)} %bitcast.337), calls=%async_computation | async-start | bytes 2097152 | tf_op jit(solution)/shard_map/all_to_all | solution.py:222
  117.1 6.9 %copy-start.23 = (f32[1024]{0:T(1024)S(1)}, f32[1024]{0:T(1024)}, u32[]{:S(2)}) copy-start(f32[1024]{0:T(1024)} %get-tuple-element.62) | copy-start | bytes 12292
  117.2 6.9 %copy-start.24 = (f32[1024]{0:T(1024)S(1)}, f32[1024]{0:T(1024)}, u32[]{:S(2)}) copy-start(f32[1024]{0:T(1024)} %get-tuple-element.63) | copy-start | bytes 12292
  117.2 6.9 %copy-start.25 = (f32[1024]{0:T(1024)S(1)}, f32[1024]{0:T(1024)}, u32[]{:S(2)}) copy-start(f32[1024]{0:T(1024)} %get-tuple-element.64) | copy-start | bytes 12292
  117.2 6.9 %copy-start.43 = (f32[128]{0:T(128)S(1)}, f32[128]{0:T(128)}, u32[]{:S(2)}) copy-start(f32[128]{0:T(128)} %copy-done.42) | copy-start | bytes 1540
  117.2 6.9 %copy-start.45 = (f32[128]{0:T(128)S(1)}, f32[128]{0:T(128)}, u32[]{:S(2)}) copy-start(f32[128]{0:T(128)} %copy-done.44) | copy-start | bytes 1540
  117.2 6.9 %copy-start.47 = (f32[128]{0:T(128)S(1)}, f32[128]{0:T(128)}, u32[]{:S(2)}) copy-start(f32[128]{0:T(128)} %copy-done.46) | copy-start | bytes 1540
  117.2 6.9 %copy-start.49 = (f32[128]{0:T(128)S(1)}, f32[128]{0:T(128)}, u32[]{:S(2)}) copy-start(f32[128]{0:T(128)} %copy-done.48) | copy-start | bytes 1540
  117.9 6.2 %collective-permute-start.5 = (f32[3,128]{0,1:T(8,128)S(1)}, f32[3,128]{0,1:T(8,128)S(1)}, u32[]{:S(2)}, u32[]{:S(2)}) collective-permute-start(f32[3,128]{0,1:T(8,128)S(1)} %slice.338), channel_id=1, source_target_pairs={{64,0},{128,64},{192,128},{65,1},{129,65},{193,129},{66,2},{130,66... | collective-permute-start | bytes 4616 | tf_op jit(solution)/shard_map/ppermute | solution.py:18
  (14 other events, 30.5 us)

commit v4 on v3

--- a/solution.py
+++ b/solution.py
@@ -122,12 +122,18 @@
     return total
 
 
+def running_sum(values):
+    length = values.shape[-1]
+    upper = (jnp.arange(length)[:, None] <= jnp.arange(length)[None, :]).astype(values.dtype)
+    return jnp.dot(values, upper, precision=precise, preferred_element_type=jnp.float32)
+
+
 def einsum(spec, *operands):
     return jnp.einsum(spec, *operands, precision=precise, preferred_element_type=jnp.float32)
 
 
 def block_forward_all(state, x_all, b_all, c_all, log_all, note_blocks, befores):
-    cumul = jnp.cumsum(log_all, axis=-1)
+    cumul = running_sum(log_all)
     entry = jnp.exp(cumul) * (note_blocks == befores[:, None])
     leave = jnp.exp(cumul[..., -1:] - cumul) * (note_blocks == note_blocks[:, -1:])
     through = jnp.exp(cumul[..., -1]) * (note_blocks[:, -1] == befores)
@@ -156,9 +162,10 @@
     positions = seq_start + jnp.arange(-rim_width, tok_rows + rim_width)
     note_all = note_index(positions, lengths)
     note_ids = note_all[rim_width : rim_width + tok_rows]
-    before_x, before_bc = shifted(
-        (pre_x[tok_rows - rim_width :], pre_bc[tok_rows - rim_width :]), "seq", 1
-    )
+    before_both = shifted(
+        jnp.concatenate([pre_x[tok_rows - rim_width :], pre_bc[tok_rows - rim_width :]], axis=1), "seq", 1
+    )
+    before_x, before_bc = before_both[:, : pre_x.shape[1]], before_both[:, pre_x.shape[1] :]
     u_x = conv_forward(
         jnp.concatenate([before_x, pre_x]).astype(jnp.float32),
         conv_x,
@@ -187,7 +194,7 @@
     log_rows = log_decay.astype(jnp.float32)
     x_rows = v_x.reshape(tok_rows, head_count, P_SIZE)
     g_rows = grad_out.astype(jnp.float32).reshape(tok_rows, head_count, P_SIZE)
-    shard_cumul = jnp.cumsum(log_rows, axis=-1)
+    shard_cumul = running_sum(log_rows)
     keep = jnp.exp(shard_cumul[:, -1]) * (note_ids[-1] == note_before)
     leave_rows = jnp.exp(shard_cumul[:, -1:] - shard_cumul) * (note_ids == note_ids[-1])
     entry_rows = jnp.exp(shard_cumul) * (note_ids == note_before)
@@ -214,7 +221,8 @@
     grad_v_bc = jnp.concatenate([grad_b.reshape(tok_rows, N), grad_c.reshape(tok_rows, N)], axis=1)
     grad_u_x = grad_v_x * silu_slope(u_x)
     grad_u_bc = grad_v_bc * silu_slope(u_bc)
-    after_x, after_bc = shifted((grad_u_x[:rim_width], grad_u_bc[:rim_width]), "seq", -1)
+    after_both = shifted(jnp.concatenate([grad_u_x[:rim_width], grad_u_bc[:rim_width]], axis=1), "seq", -1)
+    after_x, after_bc = after_both[:, : grad_u_x.shape[1]], after_both[:, grad_u_x.shape[1] :]
     grad_pre_x = conv_backward(jnp.concatenate([grad_u_x, after_x]), conv_x, note_all[rim_width:])
     whole_bc = conv_backward(jnp.concatenate([grad_u_bc, after_bc]), conv_bc, note_all[rim_width:])
     head_size = lax.axis_size("head")

time: 128 us -> 126 us (0.984)
  the two profiles are of different devices: /device:TPU:8 before, /device:TPU:1 now
where the time goes in v4:
time: 126 us; the launch traced here: 125 us
  starting transfers between devices  32.3 us (26%)
  waiting for transfers between devices  24 us (19%)
  local copies, waits for them, and re-layouts  23.2 us (18%)
  other arithmetic  22.5 us (18%)
  matrix products  19.6 us (16%)
  between operations  3.32 us (3%)
    ppermute x8, starting transfers between devices, shifted(): lax.ppermute(value, axis, [(source, source + steps) for source in range(i...  17.4 us
    all_to_all x1, waiting for transfers between devices, local(): grad_pre_bc = lax.all_to_all(pieces, 'head', 0, 0, tiled=False).sum(0)  16.5 us
    dot_general x11, matrix products, einsum(): jnp.einsum(spec, *operands, precision=precise, preferred_element_type=jnp...  15.8 us
    all_to_all x1, starting transfers between devices, local(): grad_pre_bc = lax.all_to_all(pieces, 'head', 0, 0, tiled=False).sum(0)  14.9 us
    ppermute x8, waiting for transfers between devices, shifted(): lax.ppermute(value, axis, [(source, source + steps) for source in range(i...  7.52 us
    unnamed x192, local copies, waits for them, and re-layouts  5.86 us
    reshape x2, local copies, waits for them, and re-layouts, local(): grad_x_heads.transpose(1, 2, 0, 3).reshape(tok_rows, head_count * P_SIZE)  3.98 us
    reduce_sum x2, other arithmetic, block_forward_all(): state = through[:, block, None, None] * state + chunk[:, block]  3.43 us
  transfers between devices with their start and end apart: 9, of which 4 were waited for; matrix products, arithmetic and copies ran while one was open for 32% of the time, Pallas kernels for 0%

profile of v4, /device:TPU:1, one launch (start us, length us, event | category | flops | bytes accessed | tf_op | source)
XLA Modules:
  0.0 124.9 jit_solution(5793200847759271631)
XLA Ops:
  0.7 0.7 slice.245
  2.1 4.0 %collective-permute-start = (bf16[3,384]{1,0:T(4,128)(2,1)S(1)}, bf16[3,384]{1,0:T(4,128)(2,1)S(1)}, u32[]{:S(2)}, u32[]{:S(2)}) collective-permute-start(bf16[3,384]{1,0:T(4,128)(2,1)S(1)} %pad_maximum_fusion.8), channel_id=1, source_target_pairs={{0,64},{64,128},{128,192},{1,65},{65,129},{129,193},{2,66},{66,130... | collective-permute-start | bytes 6920 | tf_op jit(solution)/shard_map/ppermute | solution.py:18
  6.1 0.8 reduce-window.9
  8.3 2.0 %fusion.122 = (f32[1024]{0:T(1024)S(1)}, f32[1024]{0:T(1024)S(1)}, f32[1024]{0:T(1024)S(1)}, f32[1024]{0:T(1024)}, f32[1024]{0:T(1024)}, /*index=5*/f32[1024]{0:T(1024)S(1)}, f32[1024]{0:T(1024)S(1)}, f32[1024]{0:T(1024)S(1)}) fusion(s32[1030]{0:T(1024)S(1)} %broadcast_add_fusion, s32[]{:T(128)} %bitcast.4, s32[]{:T(128)} %bitcast.12), kind=kLoop, calls=%fused_computation.210 | loop fusion | flops 16384 | bytes 61448 | tf_op jit(solution)/shard_map/convert_element_type | solution.py:97
  12.0 1.4 %fusion.19 = f32[2,1024]{1,0:T(2,128)S(1)} fusion(f32[2,1024]{1,0:T(2,128)} %param.11), kind=kOutput, calls=%fused_computation.30 | convolution fusion | flops 26214400 | bytes 16384 | tf_op jit(solution)/shard_map/dot_general | solution.py:128
  13.5 0.7 compare_convert_fusion.4
  14.7 1.4 %compare_and_fusion = (pred[4,256,256]{1,2,0:T(8,128)(4,1)}, f32[4,256,256]{1,2,0:T(8,128)}) fusion(s32[4,256]{1,0:T(4,128)S(1)} %reshape.387, pred[256,256]{0,1:T(8,128)(4,1)S(1)} %iota_compare_fusion.4), kind=kLoop, calls=%fused_computation.57 | loop fusion | flops 786432 | bytes 1380352 | tf_op jit(solution)/shard_map/jvp()/and | solution.py:142
  17.7 0.8 slice_reduce_fusion.10
  19.0 1.8 %fusion.37 = (f32[1024,256]{1,0:T(8,128)S(1)}, f32[1024,256]{1,0:T(8,128)}) fusion(f32[1027,256]{1,0:T(8,128)S(1)} %maximum_convert_fusion, f32[256]{0:T(256)S(1)} %bitcast.347, f32[1024]{0:T(1024)S(1)} %get-tuple-element.47, f32[256]{0:T(256)S(1)} %bitcast.349, f32[1024]{0:T(1024)S(1)} %get-tuple-element.48, f32[256]{0:T(256)S(1)} %bitcast.345, ...), kind=kLoop, calls=%fused_computation.56 | loop fusion | flops 3670016 | bytes 6307840 | tf_op jit(solution)/shard_map/jit(silu)/mul | solution.py:180
  21.7 1.3 %collective-permute-start.1 = (f32[2,8320]{1,0:T(2,128)S(1)}, f32[2,8320]{1,0:T(2,128)S(1)}, u32[]{:S(2)}, u32[]{:S(2)}) collective-permute-start(f32[2,8320]{1,0:T(2,128)S(1)} %pad_maximum_fusion.6), channel_id=1, source_target_pairs={{64,0},{128,64},{192,128},{65,1},{129,65},{193,129},{66,2},{130,66... | collective-permute-start | bytes 199688 | tf_op jit(solution)/shard_map/ppermute | solution.py:18
  23.0 1.3 %collective-permute-start.2 = (f32[2,8320]{1,0:T(2,128)S(1)}, f32[2,8320]{1,0:T(2,128)S(1)}, u32[]{:S(2)}, u32[]{:S(2)}) collective-permute-start(f32[2,8320]{1,0:T(2,128)S(1)} %pad_maximum_fusion.6), channel_id=1, source_target_pairs={{128,0},{192,64},{129,1},{193,65},{130,2},{194,66},{131,3},{195,67... | collective-permute-start | bytes 199688 | tf_op jit(solution)/shard_map/ppermute | solution.py:18
  24.3 1.3 %collective-permute-start.3 = (f32[2,8320]{1,0:T(2,128)S(1)}, f32[2,8320]{1,0:T(2,128)S(1)}, u32[]{:S(2)}, u32[]{:S(2)}) collective-permute-start(f32[2,8320]{1,0:T(2,128)S(1)} %pad_maximum_fusion.6), channel_id=1, source_target_pairs={{192,0},{193,1},{194,2},{195,3},{196,4},{197,5},{198,6},{199,7},{2... | collective-permute-start | bytes 199688 | tf_op jit(solution)/shard_map/ppermute | solution.py:18
  25.7 1.0 fusion.143
  27.7 1.9 %collective-permute-done.2 = f32[2,8320]{1,0:T(2,128)S(1)} collective-permute-done((f32[2,8320]{1,0:T(2,128)S(1)}, f32[2,8320]{1,0:T(2,128)S(1)}, u32[]{:S(2)}, u32[]{:S(2)}) %collective-permute-start.2) | collective-permute-done | bytes 66592 | tf_op jit(solution)/shard_map/ppermute | solution.py:18
  29.8 2.5 %collective-permute-done.3 = f32[2,8320]{1,0:T(2,128)S(1)} collective-permute-done((f32[2,8320]{1,0:T(2,128)S(1)}, f32[2,8320]{1,0:T(2,128)S(1)}, u32[]{:S(2)}, u32[]{:S(2)}) %collective-permute-start.3) | collective-permute-done | bytes 66592 | tf_op jit(solution)/shard_map/ppermute | solution.py:18
  33.8 2.5 %fusion.12 = f32[4,256,2,64]{1,3,2,0:T(8,128)} fusion(f32[4,2,64,256]{3,2,1,0:T(8,128)S(1)} %fusion.68, bf16[2,4,256,64]{2,1,3,0:T(4,128)(2,1)S(1)} %bitcast.331, f32[4,256,2]{1,2,0:T(2,128)S(1)} %copy.188, f32[4,256,256]{1,2,0:T(8,128)S(1)} %copy-done.8, f32[2,4,256]{2,1,0:T(4,128)S(1)} %bitcast.340, f32[4,256,256]{1,2,0:T(8,128)S(1)} %fusion.143, ...), kind=kOutput, calls=%fused_computation.21 | convolution fusion | flops 405012480 | bytes 3686400 | tf_op jit(solution)/shard_map/transpose(jvp(hbij,hbjp->hbip))/dot_general | solution.py:132
  36.3 2.2 %copy.217 = f32[4,256,2,64]{3,2,1,0:T(2,128)} copy(f32[4,256,2,64]{1,3,2,0:T(8,128)} %fusion.12) | data formatting | bytes 1048576 | tf_op jit(solution)/shard_map/reshape | solution.py:220
  38.5 1.8 %reshape.418 = f32[1024,128]{1,0:T(8,128)S(1)} reshape(f32[4,256,2,64]{3,2,1,0:T(2,128)} %copy.217) | data formatting | bytes 1048576 | tf_op jit(solution)/shard_map/reshape | solution.py:220
  40.3 2.0 %multiply_multiply_fusion = (f32[1024,128]{1,0:T(8,128)}, f32[1024,128]{1,0:T(8,128)S(1)}) fusion(f32[1024,128]{1,0:T(8,128)S(1)} %reshape.418, f32[1027,128]{1,0:T(8,128)S(1)} %maximum_convert_fusion.1, f32[128]{0:T(128)} %get-tuple-element.62, f32[1024]{0:T(1024)} %copy-done.48, f32[128]{0:T(128)} %get-tuple-element.63, f32[1024]{0:T(1024)} %copy-done.49, ...), kind=kLoop, calls=%fused_computation.97 | loop fusion | flops 2359296 | bytes 3684352 | tf_op jit(solution)/shard_map/mul | solution.py:222
  42.7 1.4 %convolution_bitcast_fusion.5 = f32[1,2,64,128]{3,2,1,0:T(8,128)S(1)} fusion(f32[2,1024,64]{1,2,0:T(8,128)S(1)} %bitcast.336, f32[2,1024]{1,0:T(2,128)} %get-tuple-element.50, f32[1024,256]{1,0:T(8,128)S(1)} %get-tuple-element.27), kind=kOutput, calls=%fused_computation.28 | convolution fusion | flops 201457664 | bytes 1122304 | tf_op jit(solution)/shard_map/thp,ht,tn->hpn/dot_general | solution.py:201
  44.7 1.9 %collective-permute-start.5 = (f32[2,8320]{1,0:T(2,128)}, f32[2,8320]{1,0:T(2,128)}, u32[]{:S(2)}, u32[]{:S(2)}) collective-permute-start(f32[2,8320]{1,0:T(2,128)} %pad_maximum_fusion.5), channel_id=1, source_target_pairs={{0,128},{64,192},{1,129},{65,193},{2,130},{66,194},{3,131},{67,195... | collective-permute-start | bytes 199688 | tf_op jit(solution)/shard_map/ppermute | solution.py:18
  46.7 4.4 %collective-permute-start.4 = (f32[2,8320]{1,0:T(2,128)}, f32[2,8320]{1,0:T(2,128)}, u32[]{:S(2)}, u32[]{:S(2)}) collective-permute-start(f32[2,8320]{1,0:T(2,128)} %pad_maximum_fusion.5), channel_id=1, source_target_pairs={{0,64},{64,128},{128,192},{1,65},{65,129},{129,193},{2,66},{66,130... | collective-permute-start | bytes 199688 | tf_op jit(solution)/shard_map/ppermute | solution.py:18
  51.1 1.9 %collective-permute-start.6 = (f32[2,8320]{1,0:T(2,128)}, f32[2,8320]{1,0:T(2,128)}, u32[]{:S(2)}, u32[]{:S(2)}) collective-permute-start(f32[2,8320]{1,0:T(2,128)} %pad_maximum_fusion.5), channel_id=1, source_target_pairs={{0,192},{1,193},{2,194},{3,195},{4,196},{5,197},{6,198},{7,199},{8... | collective-permute-start | bytes 199688 | tf_op jit(solution)/shard_map/ppermute | solution.py:18
  54.1 1.2 copy.220
  56.0 1.4 %fusion.125 = (f32[2,4]{1,0:T(2,128)}, f32[2,4,256]{2,1,0:T(4,128)S(1)}) fusion(f32[2,4]{1,0:T(2,128)} %copy-done.53, f32[4,256]{1,0:T(4,128)S(1)} %copy-done.46, f32[2,4,256]{2,0,1:T(2,128)S(1)} %fusion.60, f32[256,2,4]{0,2,1:T(4,128)S(1)} %copy-done.40), kind=kLoop, calls=%fused_computation.231 | loop fusion | flops 10232 | bytes 28736 | tf_op jit(solution)/shard_map/transpose(jvp())/reduce_sum | solution.py:138
  57.4 4.6 %fusion.17 = (f32[2,4,256]{2,1,0:T(4,128)}, f32[2,4,256]{2,1,0:T(4,128)}, f32[4,256,256]{1,2,0:T(8,128)S(1)}) fusion(f32[4,256,256]{1,2,0:T(8,128)S(1)} %copy-done.9, f32[2,4,256]{2,1,0:T(4,128)S(1)} %bitcast.341, f32[4,256,256]{1,2,0:T(8,128)} %copy-done.10, pred[4,256,256]{1,2,0:T(8,128)(4,1)} %get-tuple-element.38, ...), kind=kOutput, calls=%fused_computation.24 | convolution fusion | flops 408154112 | bytes 4218880 | tf_op jit(solution)/shard_map/transpose(jvp(hbij,hbjp->hbip))/dot_general | solution.py:132
  62.1 1.0 convolution_bitcast_fusion.2
  63.1 1.1 convolution_add_fusion.1
  65.2 0.8 slice_bitcast_fusion.4
  66.1 0.8 slice_reduce_fusion.3
  66.9 0.8 slice_bitcast_fusion.5
  67.7 0.8 slice_reduce_fusion.4
  68.5 0.8 slice_bitcast_fusion.3
  69.4 0.7 slice_bitcast_fusion.2
  70.8 1.0 convolution_bitcast_fusion.1
  71.8 1.8 %convolution_add_fusion = f32[4,256,128]{2,1,0:T(8,128)S(1)} fusion(f32[4,256,128]{2,1,0:T(8,128)S(1)} %convolution_bitcast_fusion.1, f32[4,256,256]{1,2,0:T(8,128)S(1)} %get-tuple-element.5, f32[4,256,128]{2,1,0:T(8,128)S(1)} %bitcast.330), kind=kOutput, calls=%fused_computation.15 | convolution fusion | flops 402784256 | bytes 2621440 | tf_op jit(solution)/shard_map/transpose(jvp(bin,bjn->bij))/dot_general | solution.py:132
  74.2 1.3 %collective-permute-start.7 = (f32[3,384]{1,0:T(4,128)S(1)}, f32[3,384]{1,0:T(4,128)S(1)}, u32[]{:S(2)}, u32[]{:S(2)}) collective-permute-start(f32[3,384]{1,0:T(4,128)S(1)} %pad_maximum_fusion.7), channel_id=1, source_target_pairs={{64,0},{128,64},{192,128},{65,1},{129,65},{193,129},{66,2},{130,66... | collective-permute-start | bytes 13832 | tf_op jit(solution)/shard_map/ppermute | solution.py:18
  75.5 3.1 %collective-permute-done.7 = f32[3,384]{1,0:T(4,128)S(1)} collective-permute-done((f32[3,384]{1,0:T(4,128)S(1)}, f32[3,384]{1,0:T(4,128)S(1)}, u32[]{:S(2)}, u32[]{:S(2)}) %collective-permute-start.7) | collective-permute-done | bytes 4640 | tf_op jit(solution)/shard_map/ppermute | solution.py:18
  78.6 2.1 %fusion.25 = f32[1024,256]{1,0:T(8,128)} fusion(f32[3,256]{1,0:T(4,128)S(1)} %slice.347, f32[1024,256]{1,0:T(8,128)S(1)} %maximum_multiply_fusion, f32[1024]{0:T(1024)S(1)} %copy-done.42, f32[1024]{0:T(1024)S(1)} %copy-done.43, f32[1024]{0:T(1024)S(1)} %get-tuple-element.42, f32[256]{0:T(256)S(1)} %bitcast.348, f32[256]{0:T(256)S(1)} %bitcast.350, ...), kind=kLoop, calls=%fused_computation.37 | loop fusion | flops 3407872 | bytes 2116608 | tf_op jit(solution)/shard_map/add | solution.py:97
  80.8 14.9 %all-to-all-start = ((f32[64,16,256]{2,1,0:T(8,128)}), f32[64,16,256]{2,1,0:T(8,128)S(1)}, u32[]{:S(2)}, u32[]{:S(2)}) async-start(f32[64,16,256]{2,1,0:T(8,128)} %bitcast.48), calls=%async_computation | async-start | bytes 2097152 | tf_op jit(solution)/shard_map/all_to_all | solution.py:230
  95.7 1.4 %copy.207 = f32[2,4,1]{2,1,0:T(4,128)} copy(f32[2,4,1]{1,0,2:T(2,128)} %bitcast.352) | data formatting | bytes 64 | tf_op jit(solution)/shard_map/transpose(jvp())/reshape | solution.py:138
  97.0 2.0 %fusion.91 = f32[2]{0:T(128)} fusion(f32[1,2,64,128]{3,2,1,0:T(8,128)} %get-tuple-element.32, f32[1,2,64,128]{3,2,1,0:T(8,128)} %get-tuple-element.37, f32[1,2,64,128]{3,2,1,0:T(8,128)} %get-tuple-element.31, f32[2,8320]{1,0:T(2,128)} %collective-permute-done.6, f32[2,8320]{1,0:T(2,128)} %collective-permute-done.5, f32[2,8320]{1,0:T(2,128)} %collective-permute-done.4, ...), kind=kLoop, calls=%fused_computation.134 | loop fusion | flops 262142 | bytes 589888 | tf_op jit(solution)/shard_map/transpose(jvp())/reduce_sum | solution.py:151
  99.0 1.2 copy.201
  100.3 1.4 %fusion.101 = (f32[2]{0:T(128)}, f32[2]{0:T(128)}, f32[2]{0:T(128)}) fusion(f32[2,4,64,128]{3,2,0,1:T(8,128)S(1)} %copy-done.7, f32[2]{0:T(128)} %get-tuple-element.13, f32[2]{0:T(128)} %get-tuple-element.12, f32[2]{0:T(128)} %get-tuple-element.14, f32[2,4,64,128]{3,2,0,1:T(8,128)S(1)} %copy-done.5, f32[1,2,64,128]{3,1,2,0:T(2,128)S(1)} %copy-done.24, ...), kind=kLoop, calls=%fused_computation.155 | loop fusion | flops 393210 | bytes 720984 | tf_op jit(solution)/shard_map/transpose(jvp())/reduce_sum | solution.py:151
  102.5 0.7 copy.203
  103.9 0.8 multiply_bitcast_fusion
  106.4 1.3 %fusion.46 = f32[1024,128]{1,0:T(8,128)} fusion(f32[3,128]{1,0:T(4,128)S(1)} %slice-done, f32[1024,128]{1,0:T(8,128)S(1)} %copy-done.1, f32[1024]{0:T(1024)S(1)} %copy-done.42, f32[1024]{0:T(1024)S(1)} %copy-done.44, f32[1024]{0:T(1024)S(1)} %get-tuple-element.42, f32[128]{0:T(128)S(1)} %copy-done.80, f32[128]{0:T(128)S(1)} %copy-done.81, ...), kind=kLoop, calls=%fused_computation.69 | loop fusion | flops 1703936 | bytes 1064448 | tf_op jit(solution)/shard_map/add | solution.py:97
  107.7 16.5 %all-to-all-done = f32[64,16,256]{2,1,0:T(8,128)S(1)} async-done(((f32[64,16,256]{2,1,0:T(8,128)}), f32[64,16,256]{2,1,0:T(8,128)S(1)}, u32[]{:S(2)}, u32[]{:S(2)}) %all-to-all-start) | async-done | bytes 1048608 | tf_op jit(solution)/shard_map/all_to_all | solution.py:230
  (255 shorter events, 17.0 us)
Async XLA Ops:
  0.6 12.7 %copy-start.71 = (f32[2,1024]{1,0:T(2,128)S(1)}, f32[2,1024]{1,0:T(2,128)}, u32[]{:S(2)}) copy-start(f32[2,1024]{1,0:T(2,128)} %param.11) | copy-start | bytes 24580
  0.6 12.8 %copy-start.85 = (f32[4,256]{1,0:T(4,128)S(1)}, f32[4,256]{1,0:T(4,128)}, u32[]{:S(2)}) copy-start(f32[4,256]{1,0:T(4,128)} %param.10) | copy-start | bytes 12292
  2.1 16.8 %collective-permute-start = (bf16[3,384]{1,0:T(4,128)(2,1)S(1)}, bf16[3,384]{1,0:T(4,128)(2,1)S(1)}, u32[]{:S(2)}, u32[]{:S(2)}) collective-permute-start(bf16[3,384]{1,0:T(4,128)(2,1)S(1)} %pad_maximum_fusion.8), channel_id=1, source_target_pairs={{0,64},{64,128},{128,192},{1,65},{65,129},{129,193},{2,66},{66,130... | collective-permute-start | bytes 6920 | tf_op jit(solution)/shard_map/ppermute | solution.py:18
  10.2 8.7 %copy-start.48 = (f32[1024]{0:T(1024)}, f32[1024]{0:T(1024)S(1)}, u32[]{:S(2)}) copy-start(f32[1024]{0:T(1024)S(1)} %get-tuple-element.47) | copy-start | bytes 12292
  10.2 8.7 %copy-start.49 = (f32[1024]{0:T(1024)}, f32[1024]{0:T(1024)S(1)}, u32[]{:S(2)}) copy-start(f32[1024]{0:T(1024)S(1)} %get-tuple-element.48) | copy-start | bytes 12292
  10.2 8.7 %copy-start.50 = (f32[1024]{0:T(1024)}, f32[1024]{0:T(1024)S(1)}, u32[]{:S(2)}) copy-start(f32[1024]{0:T(1024)S(1)} %get-tuple-element.49) | copy-start | bytes 12292
  13.4 5.0 %copy-start.33 = (bf16[1024,128]{1,0:T(8,128)(2,1)S(1)}, bf16[1024,128]{1,0:T(8,128)(2,1)}, u32[]{:S(2)}) copy-start(bf16[1024,128]{1,0:T(8,128)(2,1)} %param.13) | copy-start | bytes 786436
  13.5 5.5 %copy-start.61 = (f32[1,256]{1,0:T(1,128)}, f32[1,256]{1,0:T(1,128)S(1)}, u32[]{:S(2)}) copy-start(f32[1,256]{1,0:T(1,128)S(1)} %get-tuple-element.56) | copy-start | bytes 3076
  13.5 5.5 %copy-start.63 = (f32[1,256]{1,0:T(1,128)}, f32[1,256]{1,0:T(1,128)S(1)}, u32[]{:S(2)}) copy-start(f32[1,256]{1,0:T(1,128)S(1)} %get-tuple-element.57) | copy-start | bytes 3076
  13.5 5.5 %copy-start.65 = (f32[1,256]{1,0:T(1,128)}, f32[1,256]{1,0:T(1,128)S(1)}, u32[]{:S(2)}) copy-start(f32[1,256]{1,0:T(1,128)S(1)} %get-tuple-element.58) | copy-start | bytes 3076
  13.5 5.5 %copy-start.67 = (f32[1,256]{1,0:T(1,128)}, f32[1,256]{1,0:T(1,128)S(1)}, u32[]{:S(2)}) copy-start(f32[1,256]{1,0:T(1,128)S(1)} %get-tuple-element.59) | copy-start | bytes 3076
  21.7 5.9 %collective-permute-start.1 = (f32[2,8320]{1,0:T(2,128)S(1)}, f32[2,8320]{1,0:T(2,128)S(1)}, u32[]{:S(2)}, u32[]{:S(2)}) collective-permute-start(f32[2,8320]{1,0:T(2,128)S(1)} %pad_maximum_fusion.6), channel_id=1, source_target_pairs={{64,0},{128,64},{192,128},{65,1},{129,65},{193,129},{66,2},{130,66... | collective-permute-start | bytes 199688 | tf_op jit(solution)/shard_map/ppermute | solution.py:18
  23.0 6.6 %collective-permute-start.2 = (f32[2,8320]{1,0:T(2,128)S(1)}, f32[2,8320]{1,0:T(2,128)S(1)}, u32[]{:S(2)}, u32[]{:S(2)}) collective-permute-start(f32[2,8320]{1,0:T(2,128)S(1)} %pad_maximum_fusion.6), channel_id=1, source_target_pairs={{128,0},{192,64},{129,1},{193,65},{130,2},{194,66},{131,3},{195,67... | collective-permute-start | bytes 199688 | tf_op jit(solution)/shard_map/ppermute | solution.py:18
  24.3 8.0 %collective-permute-start.3 = (f32[2,8320]{1,0:T(2,128)S(1)}, f32[2,8320]{1,0:T(2,128)S(1)}, u32[]{:S(2)}, u32[]{:S(2)}) collective-permute-start(f32[2,8320]{1,0:T(2,128)S(1)} %pad_maximum_fusion.6), channel_id=1, source_target_pairs={{192,0},{193,1},{194,2},{195,3},{196,4},{197,5},{198,6},{199,7},{2... | collective-permute-start | bytes 199688 | tf_op jit(solution)/shard_map/ppermute | solution.py:18
  26.7 7.1 %copy-start.10 = (f32[4,256,256]{1,2,0:T(8,128)}, f32[4,256,256]{1,2,0:T(8,128)S(1)}, u32[]{:S(2)}) copy-start(f32[4,256,256]{1,2,0:T(8,128)S(1)} %fusion.143) | copy-start | bytes 3145732
  26.7 5.6 %copy-start.55 = (f32[2]{0:T(128)S(1)}, f32[2]{0:T(128)}, u32[]{:S(2)}) copy-start(f32[2]{0:T(128)} %get-tuple-element.13) | copy-start | bytes 28
  26.7 5.6 %copy-start.58 = (f32[2]{0:T(128)S(1)}, f32[2]{0:T(128)}, u32[]{:S(2)}) copy-start(f32[2]{0:T(128)} %get-tuple-element.14) | copy-start | bytes 28
  26.7 5.6 %copy-start.77 = (f32[2]{0:T(128)S(1)}, f32[2]{0:T(128)}, u32[]{:S(2)}) copy-start(f32[2]{0:T(128)} %get-tuple-element.11) | copy-start | bytes 28
  27.5 5.0 %copy-start.4 = (f32[2,4,64,128]{3,2,0,1:T(8,128)}, f32[2,4,64,128]{3,2,0,1:T(8,128)S(1)}, u32[]{:S(2)}) copy-start(f32[2,4,64,128]{3,2,0,1:T(8,128)S(1)} %convolution_bitcast_fusion.4) | copy-start | bytes 786436
  27.6 6.1 %copy-start.35 = (f32[2,8320]{1,0:T(2,128)}, f32[2,8320]{1,0:T(2,128)S(1)}, u32[]{:S(2)}) copy-start(f32[2,8320]{1,0:T(2,128)S(1)} %collective-permute-done.1) | copy-start | bytes 199684
  27.6 4.9 %copy-start.19 = (f32[1,2,64,128]{3,1,2,0:T(2,128)}, f32[1,2,64,128]{3,1,2,0:T(2,128)S(1)}, u32[]{:S(2)}) copy-start(f32[1,2,64,128]{3,1,2,0:T(2,128)S(1)} %slice_bitcast_fusion.8) | copy-start | bytes 196612
  44.7 20.5 %collective-permute-start.5 = (f32[2,8320]{1,0:T(2,128)}, f32[2,8320]{1,0:T(2,128)}, u32[]{:S(2)}, u32[]{:S(2)}) collective-permute-start(f32[2,8320]{1,0:T(2,128)} %pad_maximum_fusion.5), channel_id=1, source_target_pairs={{0,128},{64,192},{1,129},{65,193},{2,130},{66,194},{3,131},{67,195... | collective-permute-start | bytes 199688 | tf_op jit(solution)/shard_map/ppermute | solution.py:18
  46.7 20.2 %collective-permute-start.4 = (f32[2,8320]{1,0:T(2,128)}, f32[2,8320]{1,0:T(2,128)}, u32[]{:S(2)}, u32[]{:S(2)}) collective-permute-start(f32[2,8320]{1,0:T(2,128)} %pad_maximum_fusion.5), channel_id=1, source_target_pairs={{0,64},{64,128},{128,192},{1,65},{65,129},{129,193},{2,66},{66,130... | collective-permute-start | bytes 199688 | tf_op jit(solution)/shard_map/ppermute | solution.py:18
  51.1 17.4 %collective-permute-start.6 = (f32[2,8320]{1,0:T(2,128)}, f32[2,8320]{1,0:T(2,128)}, u32[]{:S(2)}, u32[]{:S(2)}) collective-permute-start(f32[2,8320]{1,0:T(2,128)} %pad_maximum_fusion.5), channel_id=1, source_target_pairs={{0,192},{1,193},{2,194},{3,195},{4,196},{5,197},{6,198},{7,199},{8... | collective-permute-start | bytes 199688 | tf_op jit(solution)/shard_map/ppermute | solution.py:18
  64.2 5.2 %copy-start.56 = (f32[2]{0:T(128)S(1)}, f32[2]{0:T(128)}, u32[]{:S(2)}) copy-start(f32[2]{0:T(128)} %get-tuple-element.13) | copy-start | bytes 28
  64.2 5.2 %copy-start.59 = (f32[2]{0:T(128)S(1)}, f32[2]{0:T(128)}, u32[]{:S(2)}) copy-start(f32[2]{0:T(128)} %get-tuple-element.14) | copy-start | bytes 28
  64.2 5.2 %copy-start.69 = (f32[2]{0:T(128)S(1)}, f32[2]{0:T(128)}, u32[]{:S(2)}) copy-start(f32[2]{0:T(128)} %get-tuple-element.12) | copy-start | bytes 28
  64.9 5.2 %copy-start.6 = (f32[2,4,64,128]{3,2,0,1:T(8,128)}, f32[2,4,64,128]{3,2,0,1:T(8,128)S(1)}, u32[]{:S(2)}) copy-start(f32[2,4,64,128]{3,2,0,1:T(8,128)S(1)} %convolution_bitcast_fusion.3) | copy-start | bytes 786436
  73.7 4.9 %copy-start.42 = (f32[1024]{0:T(1024)S(1)}, f32[1024]{0:T(1024)}, u32[]{:S(2)}) copy-start(f32[1024]{0:T(1024)} %get-tuple-element.45) | copy-start | bytes 12292
  73.7 4.8 %copy-start.43 = (f32[1024]{0:T(1024)S(1)}, f32[1024]{0:T(1024)}, u32[]{:S(2)}) copy-start(f32[1024]{0:T(1024)} %get-tuple-element.46) | copy-start | bytes 12292
  73.7 4.8 %copy-start.62 = (f32[1,256]{1,0:T(1,128)S(1)}, f32[1,256]{1,0:T(1,128)}, u32[]{:S(2)}) copy-start(f32[1,256]{1,0:T(1,128)} %copy-done.61) | copy-start | bytes 3076
  73.7 4.8 %copy-start.64 = (f32[1,256]{1,0:T(1,128)S(1)}, f32[1,256]{1,0:T(1,128)}, u32[]{:S(2)}) copy-start(f32[1,256]{1,0:T(1,128)} %copy-done.63) | copy-start | bytes 3076
  73.7 4.8 %copy-start.66 = (f32[1,256]{1,0:T(1,128)S(1)}, f32[1,256]{1,0:T(1,128)}, u32[]{:S(2)}) copy-start(f32[1,256]{1,0:T(1,128)} %copy-done.65) | copy-start | bytes 3076
  74.2 4.4 %collective-permute-start.7 = (f32[3,384]{1,0:T(4,128)S(1)}, f32[3,384]{1,0:T(4,128)S(1)}, u32[]{:S(2)}, u32[]{:S(2)}) collective-permute-start(f32[3,384]{1,0:T(4,128)S(1)} %pad_maximum_fusion.7), channel_id=1, source_target_pairs={{64,0},{128,64},{192,128},{65,1},{129,65},{193,129},{66,2},{130,66... | collective-permute-start | bytes 13832 | tf_op jit(solution)/shard_map/ppermute | solution.py:18
  80.7 16.3 %copy-start.57 = (f32[2]{0:T(128)S(1)}, f32[2]{0:T(128)}, u32[]{:S(2)}) copy-start(f32[2]{0:T(128)} %get-tuple-element.13) | copy-start | bytes 28
  80.7 16.3 %copy-start.60 = (f32[2]{0:T(128)S(1)}, f32[2]{0:T(128)}, u32[]{:S(2)}) copy-start(f32[2]{0:T(128)} %get-tuple-element.14) | copy-start | bytes 28
  80.7 19.6 %copy-start.5 = (f32[2,4,64,128]{3,2,0,1:T(8,128)S(1)}, f32[2,4,64,128]{3,2,0,1:T(8,128)}, u32[]{:S(2)}) copy-start(f32[2,4,64,128]{3,2,0,1:T(8,128)} %copy-done.4) | copy-start | bytes 786436
  80.7 19.6 %copy-start.7 = (f32[2,4,64,128]{3,2,0,1:T(8,128)S(1)}, f32[2,4,64,128]{3,2,0,1:T(8,128)}, u32[]{:S(2)}) copy-start(f32[2,4,64,128]{3,2,0,1:T(8,128)} %copy-done.6) | copy-start | bytes 786436
  80.7 19.5 %copy-start.20 = (f32[1,2,64,128]{3,1,2,0:T(2,128)S(1)}, f32[1,2,64,128]{3,1,2,0:T(2,128)}, u32[]{:S(2)}) copy-start(f32[1,2,64,128]{3,1,2,0:T(2,128)} %copy-done.19) | copy-start | bytes 196612
  80.7 19.5 %copy-start.22 = (f32[1,2,64,128]{3,1,2,0:T(2,128)S(1)}, f32[1,2,64,128]{3,1,2,0:T(2,128)}, u32[]{:S(2)}) copy-start(f32[1,2,64,128]{3,1,2,0:T(2,128)} %copy-done.21) | copy-start | bytes 196612
  80.7 19.5 %copy-start.24 = (f32[1,2,64,128]{3,1,2,0:T(2,128)S(1)}, f32[1,2,64,128]{3,1,2,0:T(2,128)}, u32[]{:S(2)}) copy-start(f32[1,2,64,128]{3,1,2,0:T(2,128)} %copy-done.23) | copy-start | bytes 196612
  80.7 19.5 %copy-start.26 = (f32[1,2,64,128]{3,1,2,0:T(2,128)S(1)}, f32[1,2,64,128]{3,1,2,0:T(2,128)}, u32[]{:S(2)}) copy-start(f32[1,2,64,128]{3,1,2,0:T(2,128)} %copy-done.25) | copy-start | bytes 196612
  80.8 19.5 %copy-start.28 = (f32[1,2,64,128]{3,1,2,0:T(2,128)S(1)}, f32[1,2,64,128]{3,1,2,0:T(2,128)}, u32[]{:S(2)}) copy-start(f32[1,2,64,128]{3,1,2,0:T(2,128)} %copy-done.27) | copy-start | bytes 196612
  80.8 19.5 %copy-start.30 = (f32[1,2,64,128]{3,1,2,0:T(2,128)S(1)}, f32[1,2,64,128]{3,1,2,0:T(2,128)}, u32[]{:S(2)}) copy-start(f32[1,2,64,128]{3,1,2,0:T(2,128)} %copy-done.29) | copy-start | bytes 196612
  80.8 43.4 %all-to-all-start = ((f32[64,16,256]{2,1,0:T(8,128)}), f32[64,16,256]{2,1,0:T(8,128)S(1)}, u32[]{:S(2)}, u32[]{:S(2)}) async-start(f32[64,16,256]{2,1,0:T(8,128)} %bitcast.48), calls=%async_computation | async-start | bytes 2097152 | tf_op jit(solution)/shard_map/all_to_all | solution.py:230
  95.6 9.2 %copy-start.12 = (f32[2,1,64,128]{3,2,0,1:T(8,128)S(1)}, f32[2,1,64,128]{3,2,0,1:T(8,128)}, u32[]{:S(2)}) copy-start(f32[2,1,64,128]{3,2,0,1:T(8,128)} %copy-done.11) | copy-start | bytes 196612
  95.6 9.2 %copy-start.14 = (f32[2,1,64,128]{3,2,0,1:T(8,128)S(1)}, f32[2,1,64,128]{3,2,0,1:T(8,128)}, u32[]{:S(2)}) copy-start(f32[2,1,64,128]{3,2,0,1:T(8,128)} %copy-done.13) | copy-start | bytes 196612
  99.0 6.4 %copy-start.41 = (f32[256,2,4]{0,2,1:T(4,128)S(1)}, f32[256,2,4]{0,2,1:T(4,128)}, u32[]{:S(2)}) copy-start(f32[256,2,4]{0,2,1:T(4,128)} %copy-done.38) | copy-start | bytes 24580
  (53 other events, 158.7 us)

commit v5 on v4

--- a/solution.py
+++ b/solution.py
@@ -225,26 +225,35 @@
     after_x, after_bc = after_both[:, : grad_u_x.shape[1]], after_both[:, grad_u_x.shape[1] :]
     grad_pre_x = conv_backward(jnp.concatenate([grad_u_x, after_x]), conv_x, note_all[rim_width:])
     whole_bc = conv_backward(jnp.concatenate([grad_u_bc, after_bc]), conv_bc, note_all[rim_width:])
-    head_size = lax.axis_size("head")
-    pieces = whole_bc.reshape(head_size, tok_rows // head_size, whole_bc.shape[1])
-    grad_pre_bc = lax.all_to_all(pieces, "head", 0, 0, tiled=False).sum(0)
+    chips, cores = lax.axis_size("chip"), lax.axis_size("core")
+    pieces = whole_bc.reshape(chips, cores, tok_rows // (chips * cores), whole_bc.shape[1])
+    core = lax.axis_index("core")
+    mine = lax.dynamic_index_in_dim(pieces, core, 1, keepdims=False)
+    other = lax.dynamic_index_in_dim(pieces, 1 - core, 1, keepdims=False)
+    pair_sum = mine + lax.ppermute(other, "core", [(0, 1), (1, 0)])
+    grad_pre_bc = lax.all_to_all(pair_sum, "chip", 0, 0, tiled=False).sum(0)
     return (grad_pre_x, grad_pre_bc, grad_log_decay)
 
 
 def solution(mesh):
+    seq_size, head_size = mesh.shape["seq"], mesh.shape["head"]
+    split = jax.sharding.Mesh(
+        mesh.devices.reshape(seq_size, head_size // 2, 2), ("seq", "chip", "core")
+    )
+    head = ("chip", "core")
     placed = (
-        P("seq", "head"),
+        P("seq", head),
         P("seq", None),
-        P(None, "head"),
+        P(None, head),
         P(),
-        P("head", "seq"),
+        P(head, "seq"),
         P(),
-        P("seq", "head"),
+        P("seq", head),
     )
     return jax.shard_map(
         local,
-        mesh=mesh,
+        mesh=split,
         in_specs=placed,
-        out_specs=(P("seq", "head"), P(("seq", "head"), None), P("head", "seq")),
+        out_specs=(P("seq", head), P(("seq",) + head, None), P(head, "seq")),
         check_vma=False,
     )

time: 126 us -> 117 us (0.929)
  the two profiles are of different devices: /device:TPU:1 before, /device:TPU:32 now
where the time goes in v5:
time: 117 us; the launch traced here: 116 us
  starting transfers between devices  28 us (24%)
  waiting for transfers between devices  23.4 us (20%)
  other arithmetic  20.7 us (18%)
  local copies, waits for them, and re-layouts  20.6 us (18%)
  matrix products  19.6 us (17%)
  between operations  3.4 us (3%)
    ppermute x8, starting transfers between devices, shifted(): lax.ppermute(value, axis, [(source, source + steps) for source in range(i...  16.6 us
    dot_general x11, matrix products, einsum(): jnp.einsum(spec, *operands, precision=precise, preferred_element_type=jnp...  15.8 us
    all_to_all x1, waiting for transfers between devices, local(): grad_pre_bc = lax.all_to_all(pair_sum, 'chip', 0, 0, tiled=False).sum(0)  12.5 us
    all_to_all x1, starting transfers between devices, local(): grad_pre_bc = lax.all_to_all(pair_sum, 'chip', 0, 0, tiled=False).sum(0)  11.3 us
    ppermute x8, waiting for transfers between devices, shifted(): lax.ppermute(value, axis, [(source, source + steps) for source in range(i...  10.1 us
    unnamed x200, local copies, waits for them, and re-layouts  6.92 us
    reshape x2, local copies, waits for them, and re-layouts, local(): grad_x_heads.transpose(1, 2, 0, 3).reshape(tok_rows, head_count * P_SIZE)  3.98 us
    add x2, other arithmetic, conv_backward(): result + weights[k][None, :] * extended[lag:lag + count] * linked[:, None]  3.22 us
  transfers between devices with their start and end apart: 10, of which 6 were waited for; matrix products, arithmetic and copies ran while one was open for 29% of the time, Pallas kernels for 0%

profile of v5, /device:TPU:32, one launch (start us, length us, event | category | flops | bytes accessed | tf_op | source)
XLA Modules:
  0.0 115.7 jit_solution(14841054951400360895)
XLA Ops:
  0.7 0.7 slice.245
  1.4 0.7 slice.244
  2.1 3.5 %collective-permute-start = (bf16[3,384]{1,0:T(4,128)(2,1)S(1)}, bf16[3,384]{1,0:T(4,128)(2,1)S(1)}, u32[]{:S(2)}, u32[]{:S(2)}) collective-permute-start(bf16[3,384]{1,0:T(4,128)(2,1)S(1)} %pad_maximum_fusion.8), channel_id=1, source_target_pairs={{0,64},{64,128},{128,192},{1,65},{65,129},{129,193},{2,66},{66,130... | collective-permute-start | bytes 6920 | tf_op jit(solution)/shard_map/ppermute | solution.py:18
  5.6 0.8 reduce-window.9
  7.7 2.0 %fusion.122 = (f32[1024]{0:T(1024)S(1)}, f32[1024]{0:T(1024)S(1)}, f32[1024]{0:T(1024)S(1)}, f32[1024]{0:T(1024)}, f32[1024]{0:T(1024)}, /*index=5*/f32[1024]{0:T(1024)S(1)}, f32[1024]{0:T(1024)S(1)}, f32[1024]{0:T(1024)S(1)}) fusion(s32[1030]{0:T(1024)S(1)} %broadcast_add_fusion, s32[]{:T(128)} %bitcast.4, s32[]{:T(128)} %bitcast.12), kind=kLoop, calls=%fused_computation.212 | loop fusion | flops 16384 | bytes 61448 | tf_op jit(solution)/shard_map/convert_element_type | solution.py:97
  11.5 1.4 %fusion.19 = f32[2,1024]{1,0:T(2,128)S(1)} fusion(f32[2,1024]{1,0:T(2,128)} %param.11), kind=kOutput, calls=%fused_computation.30 | convolution fusion | flops 26214400 | bytes 16384 | tf_op jit(solution)/shard_map/dot_general | solution.py:128
  13.0 0.7 compare_convert_fusion.4
  14.1 1.4 %compare_and_fusion = (pred[4,256,256]{1,2,0:T(8,128)(4,1)}, f32[4,256,256]{1,2,0:T(8,128)}) fusion(s32[4,256]{1,0:T(4,128)S(1)} %reshape.387, pred[256,256]{0,1:T(8,128)(4,1)S(1)} %iota_compare_fusion.4), kind=kLoop, calls=%fused_computation.57 | loop fusion | flops 786432 | bytes 1380352 | tf_op jit(solution)/shard_map/jvp()/and | solution.py:142
  17.1 0.8 slice_reduce_fusion.10
  18.4 1.8 %fusion.37 = (f32[1024,256]{1,0:T(8,128)S(1)}, f32[1024,256]{1,0:T(8,128)}) fusion(f32[1027,256]{1,0:T(8,128)S(1)} %maximum_convert_fusion, f32[256]{0:T(256)S(1)} %bitcast.353, f32[1024]{0:T(1024)S(1)} %get-tuple-element.47, f32[256]{0:T(256)S(1)} %bitcast.355, f32[1024]{0:T(1024)S(1)} %get-tuple-element.48, f32[256]{0:T(256)S(1)} %bitcast.351, ...), kind=kLoop, calls=%fused_computation.56 | loop fusion | flops 3670016 | bytes 6307840 | tf_op jit(solution)/shard_map/jit(silu)/mul | solution.py:180
  21.1 1.3 %collective-permute-start.1 = (f32[2,8320]{1,0:T(2,128)S(1)}, f32[2,8320]{1,0:T(2,128)S(1)}, u32[]{:S(2)}, u32[]{:S(2)}) collective-permute-start(f32[2,8320]{1,0:T(2,128)S(1)} %pad_maximum_fusion.6), channel_id=1, source_target_pairs={{64,0},{128,64},{192,128},{65,1},{129,65},{193,129},{66,2},{130,66... | collective-permute-start | bytes 199688 | tf_op jit(solution)/shard_map/ppermute | solution.py:18
  22.4 1.3 %collective-permute-start.2 = (f32[2,8320]{1,0:T(2,128)S(1)}, f32[2,8320]{1,0:T(2,128)S(1)}, u32[]{:S(2)}, u32[]{:S(2)}) collective-permute-start(f32[2,8320]{1,0:T(2,128)S(1)} %pad_maximum_fusion.6), channel_id=1, source_target_pairs={{128,0},{192,64},{129,1},{193,65},{130,2},{194,66},{131,3},{195,67... | collective-permute-start | bytes 199688 | tf_op jit(solution)/shard_map/ppermute | solution.py:18
  23.7 1.3 %collective-permute-start.3 = (f32[2,8320]{1,0:T(2,128)S(1)}, f32[2,8320]{1,0:T(2,128)S(1)}, u32[]{:S(2)}, u32[]{:S(2)}) collective-permute-start(f32[2,8320]{1,0:T(2,128)S(1)} %pad_maximum_fusion.6), channel_id=1, source_target_pairs={{192,0},{193,1},{194,2},{195,3},{196,4},{197,5},{198,6},{199,7},{2... | collective-permute-start | bytes 199688 | tf_op jit(solution)/shard_map/ppermute | solution.py:18
  25.1 1.0 fusion.143
  26.2 0.7 convolution_bitcast_fusion.4
  27.4 2.8 %collective-permute-done.2 = f32[2,8320]{1,0:T(2,128)S(1)} collective-permute-done((f32[2,8320]{1,0:T(2,128)S(1)}, f32[2,8320]{1,0:T(2,128)S(1)}, u32[]{:S(2)}, u32[]{:S(2)}) %collective-permute-start.2) | collective-permute-done | bytes 66592 | tf_op jit(solution)/shard_map/ppermute | solution.py:18
  30.4 2.8 %collective-permute-done.3 = f32[2,8320]{1,0:T(2,128)S(1)} collective-permute-done((f32[2,8320]{1,0:T(2,128)S(1)}, f32[2,8320]{1,0:T(2,128)S(1)}, u32[]{:S(2)}, u32[]{:S(2)}) %collective-permute-start.3) | collective-permute-done | bytes 66592 | tf_op jit(solution)/shard_map/ppermute | solution.py:18
  34.6 2.5 %fusion.12 = f32[4,256,2,64]{1,3,2,0:T(8,128)} fusion(f32[4,2,64,256]{3,2,1,0:T(8,128)S(1)} %fusion.68, bf16[2,4,256,64]{2,1,3,0:T(4,128)(2,1)S(1)} %bitcast.337, f32[4,256,2]{1,2,0:T(2,128)S(1)} %copy.188, f32[4,256,256]{1,2,0:T(8,128)S(1)} %copy-done.8, f32[2,4,256]{2,1,0:T(4,128)S(1)} %bitcast.346, f32[4,256,256]{1,2,0:T(8,128)S(1)} %fusion.143, ...), kind=kOutput, calls=%fused_computation.21 | convolution fusion | flops 405012480 | bytes 3686400 | tf_op jit(solution)/shard_map/transpose(jvp(hbij,hbjp->hbip))/dot_general | solution.py:132
  37.2 2.2 %copy.217 = f32[4,256,2,64]{3,2,1,0:T(2,128)} copy(f32[4,256,2,64]{1,3,2,0:T(8,128)} %fusion.12) | data formatting | bytes 1048576 | tf_op jit(solution)/shard_map/reshape | solution.py:220
  39.3 1.8 %reshape.418 = f32[1024,128]{1,0:T(8,128)S(1)} reshape(f32[4,256,2,64]{3,2,1,0:T(2,128)} %copy.217) | data formatting | bytes 1048576 | tf_op jit(solution)/shard_map/reshape | solution.py:220
  41.2 2.0 %multiply_multiply_fusion = (f32[1024,128]{1,0:T(8,128)}, f32[1024,128]{1,0:T(8,128)S(1)}) fusion(f32[1024,128]{1,0:T(8,128)S(1)} %reshape.418, f32[1027,128]{1,0:T(8,128)S(1)} %maximum_convert_fusion.1, f32[128]{0:T(128)} %get-tuple-element.62, f32[1024]{0:T(1024)} %copy-done.47, f32[128]{0:T(128)} %get-tuple-element.63, f32[1024]{0:T(1024)} %copy-done.48, ...), kind=kLoop, calls=%fused_computation.99 | loop fusion | flops 2359296 | bytes 3684352 | tf_op jit(solution)/shard_map/mul | solution.py:222
  43.5 1.4 %convolution_bitcast_fusion.5 = f32[1,2,64,128]{3,2,1,0:T(8,128)S(1)} fusion(f32[2,1024,64]{1,2,0:T(8,128)S(1)} %bitcast.342, f32[2,1024]{1,0:T(2,128)} %get-tuple-element.50, f32[1024,256]{1,0:T(8,128)S(1)} %get-tuple-element.27), kind=kOutput, calls=%fused_computation.28 | convolution fusion | flops 201457664 | bytes 1122304 | tf_op jit(solution)/shard_map/thp,ht,tn->hpn/dot_general | solution.py:201
  45.6 1.9 %collective-permute-start.5 = (f32[2,8320]{1,0:T(2,128)}, f32[2,8320]{1,0:T(2,128)}, u32[]{:S(2)}, u32[]{:S(2)}) collective-permute-start(f32[2,8320]{1,0:T(2,128)} %pad_maximum_fusion.5), channel_id=1, source_target_pairs={{0,128},{64,192},{1,129},{65,193},{2,130},{66,194},{3,131},{67,195... | collective-permute-start | bytes 199688 | tf_op jit(solution)/shard_map/ppermute | solution.py:18
  47.5 4.1 %collective-permute-start.4 = (f32[2,8320]{1,0:T(2,128)}, f32[2,8320]{1,0:T(2,128)}, u32[]{:S(2)}, u32[]{:S(2)}) collective-permute-start(f32[2,8320]{1,0:T(2,128)} %pad_maximum_fusion.5), channel_id=1, source_target_pairs={{0,64},{64,128},{128,192},{1,65},{65,129},{129,193},{2,66},{66,130... | collective-permute-start | bytes 199688 | tf_op jit(solution)/shard_map/ppermute | solution.py:18
  51.6 1.9 %collective-permute-start.6 = (f32[2,8320]{1,0:T(2,128)}, f32[2,8320]{1,0:T(2,128)}, u32[]{:S(2)}, u32[]{:S(2)}) collective-permute-start(f32[2,8320]{1,0:T(2,128)} %pad_maximum_fusion.5), channel_id=1, source_target_pairs={{0,192},{1,193},{2,194},{3,195},{4,196},{5,197},{6,198},{7,199},{8... | collective-permute-start | bytes 199688 | tf_op jit(solution)/shard_map/ppermute | solution.py:18
  54.7 1.2 %copy.220 = f32[4,256,2,64]{1,3,0,2:T(8,128)} copy(f32[4,256,2,64]{3,2,1,0:T(2,128)S(1)} %reshape.419) | data formatting | bytes 1048576 | tf_op jit(solution)/shard_map/transpose | solution.py:181
  56.5 1.4 %fusion.125 = (f32[2,4]{1,0:T(2,128)}, f32[2,4,256]{2,1,0:T(4,128)S(1)}) fusion(f32[2,4]{1,0:T(2,128)} %copy-done.52, f32[4,256]{1,0:T(4,128)S(1)} %copy-done.45, f32[2,4,256]{2,0,1:T(2,128)S(1)} %fusion.60, f32[256,2,4]{0,2,1:T(4,128)S(1)} %copy-done.40), kind=kLoop, calls=%fused_computation.233 | loop fusion | flops 10232 | bytes 28736 | tf_op jit(solution)/shard_map/transpose(jvp())/reduce_sum | solution.py:138
  57.9 4.6 %fusion.17 = (f32[2,4,256]{2,1,0:T(4,128)}, f32[2,4,256]{2,1,0:T(4,128)}, f32[4,256,256]{1,2,0:T(8,128)S(1)}) fusion(f32[4,256,256]{1,2,0:T(8,128)S(1)} %copy-done.9, f32[2,4,256]{2,1,0:T(4,128)S(1)} %bitcast.347, f32[4,256,256]{1,2,0:T(8,128)} %copy-done.10, pred[4,256,256]{1,2,0:T(8,128)(4,1)} %get-tuple-element.38, ...), kind=kOutput, calls=%fused_computation.24 | convolution fusion | flops 408154112 | bytes 4218880 | tf_op jit(solution)/shard_map/transpose(jvp(hbij,hbjp->hbip))/dot_general | solution.py:132
  62.6 1.0 convolution_bitcast_fusion.2
  63.6 1.1 convolution_add_fusion.1
  64.7 0.7 convolution_bitcast_fusion.3
  65.7 0.8 slice_bitcast_fusion.4
  66.6 0.8 slice_reduce_fusion.3
  67.4 0.8 slice_bitcast_fusion.5
  68.2 0.8 slice_reduce_fusion.4
  69.0 0.8 slice_bitcast_fusion.3
  69.9 0.7 slice_bitcast_fusion.2
  71.2 1.0 convolution_bitcast_fusion.1
  72.3 1.8 %convolution_add_fusion = f32[4,256,128]{2,1,0:T(8,128)S(1)} fusion(f32[4,256,128]{2,1,0:T(8,128)S(1)} %convolution_bitcast_fusion.1, f32[4,256,256]{1,2,0:T(8,128)S(1)} %get-tuple-element.5, f32[4,256,128]{2,1,0:T(8,128)S(1)} %bitcast.334), kind=kOutput, calls=%fused_computation.15 | convolution fusion | flops 402784256 | bytes 2621440 | tf_op jit(solution)/shard_map/transpose(jvp(bin,bjn->bij))/dot_general | solution.py:132
  74.6 1.3 %collective-permute-start.7 = (f32[3,384]{1,0:T(4,128)S(1)}, f32[3,384]{1,0:T(4,128)S(1)}, u32[]{:S(2)}, u32[]{:S(2)}) collective-permute-start(f32[3,384]{1,0:T(4,128)S(1)} %pad_maximum_fusion.7), channel_id=1, source_target_pairs={{64,0},{128,64},{192,128},{65,1},{129,65},{193,129},{66,2},{130,66... | collective-permute-start | bytes 13832 | tf_op jit(solution)/shard_map/ppermute | solution.py:18
  75.9 4.2 %collective-permute-done.7 = f32[3,384]{1,0:T(4,128)S(1)} collective-permute-done((f32[3,384]{1,0:T(4,128)S(1)}, f32[3,384]{1,0:T(4,128)S(1)}, u32[]{:S(2)}, u32[]{:S(2)}) %collective-permute-start.7) | collective-permute-done | bytes 4640 | tf_op jit(solution)/shard_map/ppermute | solution.py:18
  80.7 1.9 %fusion.25 = f32[1024,256]{1,0:T(8,128)S(1)} fusion(f32[3,256]{1,0:T(4,128)S(1)} %slice.347, f32[1024,256]{1,0:T(8,128)S(1)} %maximum_multiply_fusion, f32[1024]{0:T(1024)S(1)} %copy-done.42, f32[1024]{0:T(1024)S(1)} %copy-done.43, f32[1024]{0:T(1024)S(1)} %get-tuple-element.42, f32[256]{0:T(256)} %bitcast.354, f32[256]{0:T(256)} %bitcast.356, ...), kind=kLoop, calls=%fused_computation.37 | loop fusion | flops 3407872 | bytes 2116608 | tf_op jit(solution)/shard_map/add | solution.py:97
  84.0 0.8 collective-permute-done.8
  84.7 0.9 bitcast_add_fusion
  85.8 11.3 %all-to-all-start = ((f32[32,16,256]{2,1,0:T(8,128)}), f32[32,16,256]{2,1,0:T(8,128)S(1)}, u32[]{:S(2)}, u32[]{:S(2)}) async-start(f32[32,16,256]{2,1,0:T(8,128)} %bitcast_add_fusion), calls=%async_computation | async-start | bytes 1048576 | tf_op jit(solution)/shard_map/all_to_all | solution.py:234
  97.1 1.5 %fusion.91 = f32[2]{0:T(128)S(1)} fusion(f32[1,2,64,128]{3,2,1,0:T(8,128)} %get-tuple-element.32, f32[1,2,64,128]{3,2,1,0:T(8,128)} %get-tuple-element.37, f32[1,2,64,128]{3,2,1,0:T(8,128)} %get-tuple-element.31, f32[2,8320]{1,0:T(2,128)} %collective-permute-done.6, f32[2,8320]{1,0:T(2,128)} %collective-permute-done.5, ...), kind=kLoop, calls=%fused_computation.136 | loop fusion | flops 262142 | bytes 589888 | tf_op jit(solution)/shard_map/transpose(jvp())/reduce_sum | solution.py:151
  101.3 1.3 %fusion.46 = f32[1024,128]{1,0:T(8,128)} fusion(f32[3,128]{1,0:T(4,128)S(1)} %slice-done, f32[1024,128]{1,0:T(8,128)S(1)} %copy-done.1, f32[1024]{0:T(1024)S(1)} %copy-done.42, f32[1024]{0:T(1024)S(1)} %copy-done.43, f32[1024]{0:T(1024)S(1)} %get-tuple-element.42, f32[128]{0:T(128)S(1)} %copy-done.83, f32[128]{0:T(128)S(1)} %copy-done.84, ...), kind=kLoop, calls=%fused_computation.69 | loop fusion | flops 1703936 | bytes 1064448 | tf_op jit(solution)/shard_map/add | solution.py:97
  102.6 12.5 %all-to-all-done = f32[32,16,256]{2,1,0:T(8,128)S(1)} async-done(((f32[32,16,256]{2,1,0:T(8,128)}), f32[32,16,256]{2,1,0:T(8,128)S(1)}, u32[]{:S(2)}, u32[]{:S(2)}) %all-to-all-start) | async-done | bytes 524320 | tf_op jit(solution)/shard_map/all_to_all | solution.py:234
  (267 shorter events, 16.4 us)
Async XLA Ops:
  0.6 12.2 %copy-start.68 = (f32[2,1024]{1,0:T(2,128)S(1)}, f32[2,1024]{1,0:T(2,128)}, u32[]{:S(2)}) copy-start(f32[2,1024]{1,0:T(2,128)} %param.11) | copy-start | bytes 24580
  0.6 12.2 %copy-start.89 = (f32[4,256]{1,0:T(4,128)S(1)}, f32[4,256]{1,0:T(4,128)}, u32[]{:S(2)}) copy-start(f32[4,256]{1,0:T(4,128)} %param.10) | copy-start | bytes 12292
  2.1 16.2 %collective-permute-start = (bf16[3,384]{1,0:T(4,128)(2,1)S(1)}, bf16[3,384]{1,0:T(4,128)(2,1)S(1)}, u32[]{:S(2)}, u32[]{:S(2)}) collective-permute-start(bf16[3,384]{1,0:T(4,128)(2,1)S(1)} %pad_maximum_fusion.8), channel_id=1, source_target_pairs={{0,64},{64,128},{128,192},{1,65},{65,129},{129,193},{2,66},{66,130... | collective-permute-start | bytes 6920 | tf_op jit(solution)/shard_map/ppermute | solution.py:18
  9.7 8.7 %copy-start.47 = (f32[1024]{0:T(1024)}, f32[1024]{0:T(1024)S(1)}, u32[]{:S(2)}) copy-start(f32[1024]{0:T(1024)S(1)} %get-tuple-element.47) | copy-start | bytes 12292
  9.7 8.7 %copy-start.48 = (f32[1024]{0:T(1024)}, f32[1024]{0:T(1024)S(1)}, u32[]{:S(2)}) copy-start(f32[1024]{0:T(1024)S(1)} %get-tuple-element.48) | copy-start | bytes 12292
  9.7 8.7 %copy-start.49 = (f32[1024]{0:T(1024)}, f32[1024]{0:T(1024)S(1)}, u32[]{:S(2)}) copy-start(f32[1024]{0:T(1024)S(1)} %get-tuple-element.49) | copy-start | bytes 12292
  12.9 5.5 %copy-start.61 = (f32[1,256]{1,0:T(1,128)}, f32[1,256]{1,0:T(1,128)S(1)}, u32[]{:S(2)}) copy-start(f32[1,256]{1,0:T(1,128)S(1)} %get-tuple-element.56) | copy-start | bytes 3076
  12.9 5.5 %copy-start.62 = (f32[1,256]{1,0:T(1,128)}, f32[1,256]{1,0:T(1,128)S(1)}, u32[]{:S(2)}) copy-start(f32[1,256]{1,0:T(1,128)S(1)} %get-tuple-element.57) | copy-start | bytes 3076
  21.1 6.2 %collective-permute-start.1 = (f32[2,8320]{1,0:T(2,128)S(1)}, f32[2,8320]{1,0:T(2,128)S(1)}, u32[]{:S(2)}, u32[]{:S(2)}) collective-permute-start(f32[2,8320]{1,0:T(2,128)S(1)} %pad_maximum_fusion.6), channel_id=1, source_target_pairs={{64,0},{128,64},{192,128},{65,1},{129,65},{193,129},{66,2},{130,66... | collective-permute-start | bytes 199688 | tf_op jit(solution)/shard_map/ppermute | solution.py:18
  22.4 7.8 %collective-permute-start.2 = (f32[2,8320]{1,0:T(2,128)S(1)}, f32[2,8320]{1,0:T(2,128)S(1)}, u32[]{:S(2)}, u32[]{:S(2)}) collective-permute-start(f32[2,8320]{1,0:T(2,128)S(1)} %pad_maximum_fusion.6), channel_id=1, source_target_pairs={{128,0},{192,64},{129,1},{193,65},{130,2},{194,66},{131,3},{195,67... | collective-permute-start | bytes 199688 | tf_op jit(solution)/shard_map/ppermute | solution.py:18
  23.7 9.5 %collective-permute-start.3 = (f32[2,8320]{1,0:T(2,128)S(1)}, f32[2,8320]{1,0:T(2,128)S(1)}, u32[]{:S(2)}, u32[]{:S(2)}) collective-permute-start(f32[2,8320]{1,0:T(2,128)S(1)} %pad_maximum_fusion.6), channel_id=1, source_target_pairs={{192,0},{193,1},{194,2},{195,3},{196,4},{197,5},{198,6},{199,7},{2... | collective-permute-start | bytes 199688 | tf_op jit(solution)/shard_map/ppermute | solution.py:18
  26.1 8.5 %copy-start.10 = (f32[4,256,256]{1,2,0:T(8,128)}, f32[4,256,256]{1,2,0:T(8,128)S(1)}, u32[]{:S(2)}) copy-start(f32[4,256,256]{1,2,0:T(8,128)S(1)} %fusion.143) | copy-start | bytes 3145732
  26.1 7.1 %copy-start.54 = (f32[2]{0:T(128)S(1)}, f32[2]{0:T(128)}, u32[]{:S(2)}) copy-start(f32[2]{0:T(128)} %get-tuple-element.13) | copy-start | bytes 28
  26.1 7.1 %copy-start.58 = (f32[2]{0:T(128)S(1)}, f32[2]{0:T(128)}, u32[]{:S(2)}) copy-start(f32[2]{0:T(128)} %get-tuple-element.14) | copy-start | bytes 28
  26.1 7.1 %copy-start.79 = (f32[2]{0:T(128)S(1)}, f32[2]{0:T(128)}, u32[]{:S(2)}) copy-start(f32[2]{0:T(128)} %get-tuple-element.11) | copy-start | bytes 28
  26.9 6.5 %copy-start.4 = (f32[2,4,64,128]{3,2,0,1:T(8,128)}, f32[2,4,64,128]{3,2,0,1:T(8,128)S(1)}, u32[]{:S(2)}) copy-start(f32[2,4,64,128]{3,2,0,1:T(8,128)S(1)} %convolution_bitcast_fusion.4) | copy-start | bytes 786436
  27.3 7.3 %copy-start.35 = (f32[2,8320]{1,0:T(2,128)}, f32[2,8320]{1,0:T(2,128)S(1)}, u32[]{:S(2)}) copy-start(f32[2,8320]{1,0:T(2,128)S(1)} %collective-permute-done.1) | copy-start | bytes 199684
  27.3 6.1 %copy-start.19 = (f32[1,2,64,128]{3,1,2,0:T(2,128)}, f32[1,2,64,128]{3,1,2,0:T(2,128)S(1)}, u32[]{:S(2)}) copy-start(f32[1,2,64,128]{3,1,2,0:T(2,128)S(1)} %slice_bitcast_fusion.8) | copy-start | bytes 196612
  27.4 6.0 %copy-start.75 = (f32[2]{0:T(128)}, f32[2]{0:T(128)S(1)}, u32[]{:S(2)}) copy-start(f32[2]{0:T(128)S(1)} %slice_reduce_fusion.6) | copy-start | bytes 28
  45.6 20.1 %collective-permute-start.5 = (f32[2,8320]{1,0:T(2,128)}, f32[2,8320]{1,0:T(2,128)}, u32[]{:S(2)}, u32[]{:S(2)}) collective-permute-start(f32[2,8320]{1,0:T(2,128)} %pad_maximum_fusion.5), channel_id=1, source_target_pairs={{0,128},{64,192},{1,129},{65,193},{2,130},{66,194},{3,131},{67,195... | collective-permute-start | bytes 199688 | tf_op jit(solution)/shard_map/ppermute | solution.py:18
  47.5 19.8 %collective-permute-start.4 = (f32[2,8320]{1,0:T(2,128)}, f32[2,8320]{1,0:T(2,128)}, u32[]{:S(2)}, u32[]{:S(2)}) collective-permute-start(f32[2,8320]{1,0:T(2,128)} %pad_maximum_fusion.5), channel_id=1, source_target_pairs={{0,64},{64,128},{128,192},{1,65},{65,129},{129,193},{2,66},{66,130... | collective-permute-start | bytes 199688 | tf_op jit(solution)/shard_map/ppermute | solution.py:18
  51.6 17.4 %collective-permute-start.6 = (f32[2,8320]{1,0:T(2,128)}, f32[2,8320]{1,0:T(2,128)}, u32[]{:S(2)}, u32[]{:S(2)}) collective-permute-start(f32[2,8320]{1,0:T(2,128)} %pad_maximum_fusion.5), channel_id=1, source_target_pairs={{0,192},{1,193},{2,194},{3,195},{4,196},{5,197},{6,198},{7,199},{8... | collective-permute-start | bytes 199688 | tf_op jit(solution)/shard_map/ppermute | solution.py:18
  74.2 6.5 %copy-start.42 = (f32[1024]{0:T(1024)S(1)}, f32[1024]{0:T(1024)}, u32[]{:S(2)}) copy-start(f32[1024]{0:T(1024)} %get-tuple-element.45) | copy-start | bytes 12292
  74.2 6.5 %copy-start.43 = (f32[1024]{0:T(1024)S(1)}, f32[1024]{0:T(1024)}, u32[]{:S(2)}) copy-start(f32[1024]{0:T(1024)} %get-tuple-element.46) | copy-start | bytes 12292
  74.6 5.5 %collective-permute-start.7 = (f32[3,384]{1,0:T(4,128)S(1)}, f32[3,384]{1,0:T(4,128)S(1)}, u32[]{:S(2)}, u32[]{:S(2)}) collective-permute-start(f32[3,384]{1,0:T(4,128)S(1)} %pad_maximum_fusion.7), channel_id=1, source_target_pairs={{64,0},{128,64},{192,128},{65,1},{129,65},{193,129},{66,2},{130,66... | collective-permute-start | bytes 13832 | tf_op jit(solution)/shard_map/ppermute | solution.py:18
  82.7 2.0 %collective-permute-start.8 = (f32[32,16,256]{2,1,0:T(8,128)S(1)}, f32[32,16,256]{2,1,0:T(8,128)S(1)}, u32[]{:S(2)}, u32[]{:S(2)}) collective-permute-start(f32[32,16,256]{2,1,0:T(8,128)S(1)} %dynamic-slice_bitcast_fusion), channel_id=1, source_target_pairs={{0,1},{1,0},{2,3},{3,2},{4,5},{5,4},{6,7},{7,6},{8,9},{9,8},{10,11... | collective-permute-start | bytes 1572872 | tf_op jit(solution)/shard_map/ppermute | solution.py:233
  84.0 13.2 %copy-start.56 = (f32[2]{0:T(128)S(1)}, f32[2]{0:T(128)}, u32[]{:S(2)}) copy-start(f32[2]{0:T(128)} %get-tuple-element.13) | copy-start | bytes 28
  85.6 13.2 %copy-start.5 = (f32[2,4,64,128]{3,2,0,1:T(8,128)S(1)}, f32[2,4,64,128]{3,2,0,1:T(8,128)}, u32[]{:S(2)}) copy-start(f32[2,4,64,128]{3,2,0,1:T(8,128)} %copy-done.4) | copy-start | bytes 786436
  85.6 13.2 %copy-start.7 = (f32[2,4,64,128]{3,2,0,1:T(8,128)S(1)}, f32[2,4,64,128]{3,2,0,1:T(8,128)}, u32[]{:S(2)}) copy-start(f32[2,4,64,128]{3,2,0,1:T(8,128)} %copy-done.6) | copy-start | bytes 786436
  85.6 13.2 %copy-start.20 = (f32[1,2,64,128]{3,1,2,0:T(2,128)S(1)}, f32[1,2,64,128]{3,1,2,0:T(2,128)}, u32[]{:S(2)}) copy-start(f32[1,2,64,128]{3,1,2,0:T(2,128)} %copy-done.19) | copy-start | bytes 196612
  85.6 13.2 %copy-start.22 = (f32[1,2,64,128]{3,1,2,0:T(2,128)S(1)}, f32[1,2,64,128]{3,1,2,0:T(2,128)}, u32[]{:S(2)}) copy-start(f32[1,2,64,128]{3,1,2,0:T(2,128)} %copy-done.21) | copy-start | bytes 196612
  85.6 13.2 %copy-start.24 = (f32[1,2,64,128]{3,1,2,0:T(2,128)S(1)}, f32[1,2,64,128]{3,1,2,0:T(2,128)}, u32[]{:S(2)}) copy-start(f32[1,2,64,128]{3,1,2,0:T(2,128)} %copy-done.23) | copy-start | bytes 196612
  85.6 13.2 %copy-start.26 = (f32[1,2,64,128]{3,1,2,0:T(2,128)S(1)}, f32[1,2,64,128]{3,1,2,0:T(2,128)}, u32[]{:S(2)}) copy-start(f32[1,2,64,128]{3,1,2,0:T(2,128)} %copy-done.25) | copy-start | bytes 196612
  85.6 13.2 %copy-start.28 = (f32[1,2,64,128]{3,1,2,0:T(2,128)S(1)}, f32[1,2,64,128]{3,1,2,0:T(2,128)}, u32[]{:S(2)}) copy-start(f32[1,2,64,128]{3,1,2,0:T(2,128)} %copy-done.27) | copy-start | bytes 196612
  85.7 13.2 %copy-start.30 = (f32[1,2,64,128]{3,1,2,0:T(2,128)S(1)}, f32[1,2,64,128]{3,1,2,0:T(2,128)}, u32[]{:S(2)}) copy-start(f32[1,2,64,128]{3,1,2,0:T(2,128)} %copy-done.29) | copy-start | bytes 196612
  85.7 13.2 %copy-start.57 = (f32[2]{0:T(128)S(1)}, f32[2]{0:T(128)}, u32[]{:S(2)}) copy-start(f32[2]{0:T(128)} %get-tuple-element.13) | copy-start | bytes 28
  85.7 13.2 %copy-start.60 = (f32[2]{0:T(128)S(1)}, f32[2]{0:T(128)}, u32[]{:S(2)}) copy-start(f32[2]{0:T(128)} %get-tuple-element.14) | copy-start | bytes 28
  85.7 13.2 %copy-start.66 = (f32[2]{0:T(128)S(1)}, f32[2]{0:T(128)}, u32[]{:S(2)}) copy-start(f32[2]{0:T(128)} %get-tuple-element.12) | copy-start | bytes 28
  85.7 13.2 %copy-start.70 = (f32[2]{0:T(128)S(1)}, f32[2]{0:T(128)}, u32[]{:S(2)}) copy-start(f32[2]{0:T(128)} %copy-done.69) | copy-start | bytes 28
  85.7 13.2 %copy-start.72 = (f32[2]{0:T(128)S(1)}, f32[2]{0:T(128)}, u32[]{:S(2)}) copy-start(f32[2]{0:T(128)} %copy-done.71) | copy-start | bytes 28
  85.7 13.2 %copy-start.76 = (f32[2]{0:T(128)S(1)}, f32[2]{0:T(128)}, u32[]{:S(2)}) copy-start(f32[2]{0:T(128)} %copy-done.75) | copy-start | bytes 28
  85.7 13.2 %copy-start.78 = (f32[2]{0:T(128)S(1)}, f32[2]{0:T(128)}, u32[]{:S(2)}) copy-start(f32[2]{0:T(128)} %copy-done.77) | copy-start | bytes 28
  85.7 13.2 %copy-start.80 = (f32[2]{0:T(128)S(1)}, f32[2]{0:T(128)}, u32[]{:S(2)}) copy-start(f32[2]{0:T(128)} %get-tuple-element.11) | copy-start | bytes 28
  85.7 13.7 %copy-start.53 = (f32[2,4]{1,0:T(2,128)S(1)}, f32[2,4]{1,0:T(2,128)}, u32[]{:S(2)}) copy-start(f32[2,4]{1,0:T(2,128)} %copy-done.52) | copy-start | bytes 100
  85.8 13.7 %copy-start.74 = (f32[4]{0:T(128)S(1)}, f32[4]{0:T(128)}, u32[]{:S(2)}) copy-start(f32[4]{0:T(128)} %copy-done.73) | copy-start | bytes 52
  85.8 13.9 %copy-start.12 = (f32[2,1,64,128]{3,2,0,1:T(8,128)S(1)}, f32[2,1,64,128]{3,2,0,1:T(8,128)}, u32[]{:S(2)}) copy-start(f32[2,1,64,128]{3,2,0,1:T(8,128)} %copy-done.11) | copy-start | bytes 196612
  85.8 13.9 %copy-start.14 = (f32[2,1,64,128]{3,2,0,1:T(8,128)S(1)}, f32[2,1,64,128]{3,2,0,1:T(8,128)}, u32[]{:S(2)}) copy-start(f32[2,1,64,128]{3,2,0,1:T(8,128)} %copy-done.13) | copy-start | bytes 196612
  85.8 29.3 %all-to-all-start = ((f32[32,16,256]{2,1,0:T(8,128)}), f32[32,16,256]{2,1,0:T(8,128)S(1)}, u32[]{:S(2)}, u32[]{:S(2)}) async-start(f32[32,16,256]{2,1,0:T(8,128)} %bitcast_add_fusion), calls=%async_computation | async-start | bytes 1048576 | tf_op jit(solution)/shard_map/all_to_all | solution.py:234
  (58 other events, 157.1 us)

commit v6 on v5

--- a/solution.py
+++ b/solution.py
@@ -1,7 +1,12 @@
+import functools
 import jax
 import jax.numpy as jnp
 from jax import lax
+from jax.experimental import pallas as pl
+from jax.experimental.pallas import tpu as pltpu
 from jax.sharding import PartitionSpec as P
+
+MESH = pl.DeviceIdType.MESH
 
 P_SIZE = 64
 N = 128
@@ -153,6 +158,71 @@
     return (output, state)
 
 
+def reduce_kernel(count, cores, pieces_ref, out_ref, landed, send_sems, recv_sems):
+    seq = lax.axis_index("seq")
+    me = lax.axis_index("chip") * cores + lax.axis_index("core")
+
+    def place(peer):
+        return (seq, peer // cores, peer % cores)
+
+    barrier = pltpu.get_barrier_semaphore()
+
+    def greet(step, carry):
+        peer = lax.rem(me + step, count)
+        pl.semaphore_signal(barrier, inc=1, device_id=place(peer), device_id_type=MESH)
+        return carry
+
+    lax.fori_loop(1, count, greet, 0)
+    pl.semaphore_wait(barrier, count - 1)
+
+    def outgoing(step):
+        peer = lax.rem(me + step, count)
+        return pltpu.make_async_remote_copy(
+            src_ref=pieces_ref.at[peer],
+            dst_ref=landed.at[count - 1 - step],
+            send_sem=send_sems.at[step - 1],
+            recv_sem=recv_sems.at[count - 1 - step],
+            device_id=place(peer),
+            device_id_type=MESH,
+        )
+
+    def send(step, carry):
+        outgoing(step).start()
+        return carry
+
+    lax.fori_loop(1, count, send, 0)
+
+    def finish(step, carry):
+        outgoing(step).wait_send()
+        outgoing(count - step).wait_recv()
+        return carry
+
+    lax.fori_loop(1, count, finish, 0)
+
+    def accumulate(slot, total):
+        return total + landed[slot]
+
+    out_ref[...] = lax.fori_loop(0, count - 1, accumulate, pieces_ref[me])
+
+
+def head_reduce(partial):
+    cores = lax.axis_size("core")
+    count = lax.axis_size("chip") * cores
+    rows, columns = partial.shape[0] // count, partial.shape[1]
+    return pl.pallas_call(
+        functools.partial(reduce_kernel, count, cores),
+        out_shape=jax.ShapeDtypeStruct((rows, columns), jnp.float32),
+        in_specs=[pl.BlockSpec(memory_space=pltpu.VMEM)],
+        out_specs=pl.BlockSpec(memory_space=pltpu.VMEM),
+        scratch_shapes=[
+            pltpu.VMEM((count - 1, rows, columns), jnp.float32),
+            pltpu.SemaphoreType.DMA((count - 1,)),
+            pltpu.SemaphoreType.DMA((count - 1,)),
+        ],
+        compiler_params=pltpu.CompilerParams(collective_id=0, has_side_effects=True),
+    )(partial.reshape(count, rows, columns))
+
+
 def local(pre_x, pre_bc, conv_x, conv_bc, log_decay, lengths, grad_out):
     tok_rows = pre_x.shape[0]
     head_count = log_decay.shape[0]
@@ -225,13 +295,7 @@
     after_x, after_bc = after_both[:, : grad_u_x.shape[1]], after_both[:, grad_u_x.shape[1] :]
     grad_pre_x = conv_backward(jnp.concatenate([grad_u_x, after_x]), conv_x, note_all[rim_width:])
     whole_bc = conv_backward(jnp.concatenate([grad_u_bc, after_bc]), conv_bc, note_all[rim_width:])
-    chips, cores = lax.axis_size("chip"), lax.axis_size("core")
-    pieces = whole_bc.reshape(chips, cores, tok_rows // (chips * cores), whole_bc.shape[1])
-    core = lax.axis_index("core")
-    mine = lax.dynamic_index_in_dim(pieces, core, 1, keepdims=False)
-    other = lax.dynamic_index_in_dim(pieces, 1 - core, 1, keepdims=False)
-    pair_sum = mine + lax.ppermute(other, "core", [(0, 1), (1, 0)])
-    grad_pre_bc = lax.all_to_all(pair_sum, "chip", 0, 0, tiled=False).sum(0)
+    grad_pre_bc = head_reduce(whole_bc)
     return (grad_pre_x, grad_pre_bc, grad_log_decay)
 
 

time: 117 us -> 131 us (1.12)
  the two profiles are of different devices: /device:TPU:32 before, /device:TPU:1 now
where the time goes in v6:
time: 131 us; the launch traced here: 130 us
  Pallas kernels  40.9 us (31%)
  matrix products  21.1 us (16%)
  other arithmetic  20.7 us (16%)
  local copies, waits for them, and re-layouts  20.6 us (16%)
  starting transfers between devices  17.4 us (13%)
  waiting for transfers between devices  6.59 us (5%)
  between operations  3.21 us (2%)
    pallas_call x1, Pallas kernels, head_reduce(): pl.pallas_call(functools.partial(reduce_kernel, count, cores), out_shape=...  40.9 us
    ppermute x8, starting transfers between devices, shifted(): lax.ppermute(value, axis, [(source, source + steps) for source in range(i...  17.4 us
    dot_general x11, matrix products, einsum(): jnp.einsum(spec, *operands, precision=precise, preferred_element_type=jnp...  17.3 us
    ppermute x8, waiting for transfers between devices, shifted(): lax.ppermute(value, axis, [(source, source + steps) for source in range(i...  6.59 us
    unnamed x183, local copies, waits for them, and re-layouts  5.68 us
    reshape x2, local copies, waits for them, and re-layouts, local(): grad_x_heads.transpose(1, 2, 0, 3).reshape(tok_rows, head_count * P_SIZE)  3.99 us
    add x2, other arithmetic, conv_backward(): result + weights[k][None, :] * extended[lag:lag + count] * linked[:, None]  3.36 us
    reduce_sum x2, other arithmetic, block_forward_all(): state = through[:, block, None, None] * state + chunk[:, block]  2.8 us
  transfers between devices with their start and end apart: 8, of which 3 were waited for; matrix products, arithmetic and copies ran while one was open for 24% of the time, Pallas kernels for 0%

profile of v6, /device:TPU:1, one launch (start us, length us, event | category | flops | bytes accessed | tf_op | source)
XLA Modules:
  0.0 130.4 jit_solution(5692372895272978644)
XLA Ops:
  0.7 0.7 slice.245
  1.4 0.7 slice.244
  2.1 4.0 %collective-permute-start = (bf16[3,384]{1,0:T(4,128)(2,1)S(1)}, bf16[3,384]{1,0:T(4,128)(2,1)S(1)}, u32[]{:S(2)}, u32[]{:S(2)}) collective-permute-start(bf16[3,384]{1,0:T(4,128)(2,1)S(1)} %pad_maximum_fusion.8), channel_id=1, source_target_pairs={{0,64},{64,128},{128,192},{1,65},{65,129},{129,193},{2,66},{66,130... | collective-permute-start | bytes 6920 | tf_op jit(solution)/shard_map/ppermute | solution.py:23
  6.1 0.8 reduce-window.9
  8.3 2.0 %fusion.122 = (f32[1024]{0:T(1024)S(1)}, f32[1024]{0:T(1024)S(1)}, f32[1024]{0:T(1024)S(1)}, f32[1024]{0:T(1024)}, f32[1024]{0:T(1024)}, /*index=5*/f32[1024]{0:T(1024)S(1)}, f32[1024]{0:T(1024)S(1)}, f32[1024]{0:T(1024)S(1)}) fusion(s32[1030]{0:T(1024)S(1)} %broadcast_add_fusion, s32[]{:T(128)} %bitcast.4, s32[]{:T(128)} %bitcast.12), kind=kLoop, calls=%fused_computation.210 | loop fusion | flops 16384 | bytes 61448 | tf_op jit(solution)/shard_map/convert_element_type | solution.py:102
  12.0 1.4 %fusion.19 = f32[2,1024]{1,0:T(2,128)S(1)} fusion(f32[2,1024]{1,0:T(2,128)} %param.11), kind=kOutput, calls=%fused_computation.30 | convolution fusion | flops 26214400 | bytes 16384 | tf_op jit(solution)/shard_map/dot_general | solution.py:133
  13.5 0.7 compare_convert_fusion.4
  14.7 1.3 %compare_and_fusion = (pred[4,256,256]{1,2,0:T(8,128)(4,1)}, f32[4,256,256]{1,2,0:T(8,128)}) fusion(s32[4,256]{1,0:T(4,128)S(1)} %reshape.387, pred[256,256]{0,1:T(8,128)(4,1)S(1)} %iota_compare_fusion.4), kind=kLoop, calls=%fused_computation.57 | loop fusion | flops 786432 | bytes 1380352 | tf_op jit(solution)/shard_map/jvp()/and | solution.py:147
  16.9 0.7 exponential_multiply_fusion
  18.9 1.8 %fusion.37 = (f32[1024,256]{1,0:T(8,128)S(1)}, f32[1024,256]{1,0:T(8,128)}) fusion(f32[1027,256]{1,0:T(8,128)S(1)} %maximum_convert_fusion, f32[256]{0:T(256)S(1)} %bitcast.348, f32[1024]{0:T(1024)S(1)} %get-tuple-element.47, f32[256]{0:T(256)S(1)} %bitcast.350, f32[1024]{0:T(1024)S(1)} %get-tuple-element.48, f32[256]{0:T(256)S(1)} %bitcast.346, ...), kind=kLoop, calls=%fused_computation.56 | loop fusion | flops 3670016 | bytes 6307840 | tf_op jit(solution)/shard_map/jit(silu)/mul | solution.py:250
  20.7 0.7 convolution_bitcast_fusion.6
  21.5 1.3 collective-permute-start.1
  22.8 1.3 collective-permute-start.2
  24.1 1.3 collective-permute-start.3
  25.5 1.0 fusion.143
  26.5 0.7 convolution_bitcast_fusion.4
  27.5 2.0 %collective-permute-done.2 = f32[2,8320]{1,0:T(2,128)S(1)} collective-permute-done((f32[2,8320]{1,0:T(2,128)S(1)}, f32[2,8320]{1,0:T(2,128)S(1)}, u32[]{:S(2)}, u32[]{:S(2)}) %collective-permute-start.2) | collective-permute-done | bytes 66592 | tf_op jit(solution)/shard_map/ppermute | solution.py:23
  29.6 2.5 %collective-permute-done.3 = f32[2,8320]{1,0:T(2,128)S(1)} collective-permute-done((f32[2,8320]{1,0:T(2,128)S(1)}, f32[2,8320]{1,0:T(2,128)S(1)}, u32[]{:S(2)}, u32[]{:S(2)}) %collective-permute-start.3) | collective-permute-done | bytes 66592 | tf_op jit(solution)/shard_map/ppermute | solution.py:23
  33.6 2.5 %fusion.12 = f32[4,256,2,64]{1,3,2,0:T(8,128)} fusion(f32[4,2,64,256]{3,2,1,0:T(8,128)S(1)} %fusion.68, bf16[2,4,256,64]{2,1,3,0:T(4,128)(2,1)S(1)} %bitcast.332, f32[4,256,2]{1,2,0:T(2,128)S(1)} %copy.188, f32[4,256,256]{1,2,0:T(8,128)S(1)} %copy-done.8, f32[2,4,256]{2,1,0:T(4,128)S(1)} %bitcast.341, f32[4,256,256]{1,2,0:T(8,128)S(1)} %fusion.143, ...), kind=kOutput, calls=%fused_computation.21 | convolution fusion | flops 405012480 | bytes 3686400 | tf_op jit(solution)/shard_map/transpose(jvp(hbij,hbjp->hbip))/dot_general | solution.py:137
  36.1 2.2 %copy.217 = f32[4,256,2,64]{3,2,1,0:T(2,128)} copy(f32[4,256,2,64]{1,3,2,0:T(8,128)} %fusion.12) | data formatting | bytes 1048576 | tf_op jit(solution)/shard_map/reshape | solution.py:290
  38.3 1.8 %reshape.418 = f32[1024,128]{1,0:T(8,128)S(1)} reshape(f32[4,256,2,64]{3,2,1,0:T(2,128)} %copy.217) | data formatting | bytes 1048576 | tf_op jit(solution)/shard_map/reshape | solution.py:290
  40.1 2.0 %multiply_multiply_fusion = (f32[1024,128]{1,0:T(8,128)}, f32[1024,128]{1,0:T(8,128)S(1)}) fusion(f32[1024,128]{1,0:T(8,128)S(1)} %reshape.418, f32[1027,128]{1,0:T(8,128)S(1)} %maximum_convert_fusion.1, f32[128]{0:T(128)} %get-tuple-element.62, f32[1024]{0:T(1024)} %copy-done.41, f32[128]{0:T(128)} %get-tuple-element.63, f32[1024]{0:T(1024)} %copy-done.42, ...), kind=kLoop, calls=%fused_computation.97 | loop fusion | flops 2359296 | bytes 3684352 | tf_op jit(solution)/shard_map/mul | solution.py:292
  42.5 1.4 %convolution_bitcast_fusion.5 = f32[1,2,64,128]{3,2,1,0:T(8,128)S(1)} fusion(f32[2,1024,64]{1,2,0:T(8,128)S(1)} %bitcast.337, f32[2,1024]{1,0:T(2,128)} %get-tuple-element.50, f32[1024,256]{1,0:T(8,128)S(1)} %get-tuple-element.27), kind=kOutput, calls=%fused_computation.28 | convolution fusion | flops 201457664 | bytes 1122304 | tf_op jit(solution)/shard_map/thp,ht,tn->hpn/dot_general | solution.py:271
  44.6 1.9 %collective-permute-start.5 = (f32[2,8320]{1,0:T(2,128)}, f32[2,8320]{1,0:T(2,128)}, u32[]{:S(2)}, u32[]{:S(2)}) collective-permute-start(f32[2,8320]{1,0:T(2,128)} %pad_maximum_fusion.5), channel_id=1, source_target_pairs={{0,128},{64,192},{1,129},{65,193},{2,130},{66,194},{3,131},{67,195... | collective-permute-start | bytes 199688 | tf_op jit(solution)/shard_map/ppermute | solution.py:23
  46.5 4.4 %collective-permute-start.4 = (f32[2,8320]{1,0:T(2,128)}, f32[2,8320]{1,0:T(2,128)}, u32[]{:S(2)}, u32[]{:S(2)}) collective-permute-start(f32[2,8320]{1,0:T(2,128)} %pad_maximum_fusion.5), channel_id=1, source_target_pairs={{0,64},{64,128},{128,192},{1,65},{65,129},{129,193},{2,66},{66,130... | collective-permute-start | bytes 199688 | tf_op jit(solution)/shard_map/ppermute | solution.py:23
  50.9 1.9 %collective-permute-start.6 = (f32[2,8320]{1,0:T(2,128)}, f32[2,8320]{1,0:T(2,128)}, u32[]{:S(2)}, u32[]{:S(2)}) collective-permute-start(f32[2,8320]{1,0:T(2,128)} %pad_maximum_fusion.5), channel_id=1, source_target_pairs={{0,192},{1,193},{2,194},{3,195},{4,196},{5,197},{6,198},{7,199},{8... | collective-permute-start | bytes 199688 | tf_op jit(solution)/shard_map/ppermute | solution.py:23
  53.9 1.2 copy.220
  55.8 1.4 %fusion.125 = (f32[2,4]{1,0:T(2,128)}, f32[2,4,256]{2,1,0:T(4,128)S(1)}) fusion(f32[2,4]{1,0:T(2,128)} %copy-done.46, f32[4,256]{1,0:T(4,128)S(1)} %copy-done.39, f32[2,4,256]{2,0,1:T(2,128)S(1)} %fusion.60, f32[256,2,4]{0,2,1:T(4,128)S(1)} %copy-done.34), kind=kLoop, calls=%fused_computation.231 | loop fusion | flops 10232 | bytes 28736 | tf_op jit(solution)/shard_map/transpose(jvp())/reduce_sum | solution.py:143
  57.2 4.6 %fusion.17 = (f32[2,4,256]{2,1,0:T(4,128)}, f32[2,4,256]{2,1,0:T(4,128)}, f32[4,256,256]{1,2,0:T(8,128)S(1)}) fusion(f32[4,256,256]{1,2,0:T(8,128)S(1)} %copy-done.9, f32[2,4,256]{2,1,0:T(4,128)S(1)} %bitcast.342, f32[4,256,256]{1,2,0:T(8,128)} %copy-done.10, pred[4,256,256]{1,2,0:T(8,128)(4,1)} %get-tuple-element.38, ...), kind=kOutput, calls=%fused_computation.24 | convolution fusion | flops 408154112 | bytes 4218880 | tf_op jit(solution)/shard_map/transpose(jvp(hbij,hbjp->hbip))/dot_general | solution.py:137
  61.8 1.0 convolution_bitcast_fusion.2
  62.9 1.9 %convolution_add_fusion.1 = f32[4,256,128]{2,1,0:T(8,128)} fusion(f32[4,256,128]{2,1,0:T(8,128)S(1)} %convolution_bitcast_fusion.2, f32[4,256,256]{1,2,0:T(8,128)S(1)} %get-tuple-element.5, f32[4,256,128]{2,1,0:T(8,128)S(1)} %bitcast.329), kind=kOutput, calls=%fused_computation.16 | convolution fusion | flops 402784256 | bytes 2621440 | tf_op jit(solution)/shard_map/transpose(jvp(bin,bjn->bij))/dot_general | solution.py:137
  64.7 1.4 %convolution_bitcast_fusion.3 = f32[2,4,64,128]{3,2,0,1:T(8,128)} fusion(f32[4,256,128,1]{2,1,3,0:T(8,128)S(1)} %bitcast.325, f32[4,256,2,64]{1,3,2,0:T(8,128)S(1)} %copy.195, f32[2,4,256]{2,0,1:T(2,128)S(1)} %copy.196), kind=kOutput, calls=%fused_computation.26 | convolution fusion | flops 201457664 | bytes 1318912 | tf_op jit(solution)/shard_map/jvp(hbjp,bjn->hbpn)/dot_general | solution.py:137
  66.1 1.4 %copy.207 = f32[2,4,1]{2,1,0:T(4,128)} copy(f32[2,4,1]{1,0,2:T(2,128)} %bitcast.353) | data formatting | bytes 64 | tf_op jit(solution)/shard_map/transpose(jvp())/reshape | solution.py:143
  68.1 0.8 slice_bitcast_fusion.4
  69.0 0.8 slice_reduce_fusion.3
  69.7 0.8 slice_bitcast_fusion.5
  70.6 0.8 slice_reduce_fusion.4
  71.4 0.8 slice_bitcast_fusion.3
  72.2 1.0 slice_bitcast_fusion.2
  73.3 1.5 %fusion.101 = (f32[2]{0:T(128)}, f32[2]{0:T(128)}, f32[2]{0:T(128)}) fusion(f32[2,4,64,128]{3,2,0,1:T(8,128)S(1)} %copy-done.7, f32[2]{0:T(128)S(1)} %copy-done.49, f32[2]{0:T(128)} %get-tuple-element.12, f32[2]{0:T(128)} %copy-done.50, f32[2,4,64,128]{3,2,0,1:T(8,128)S(1)} %copy-done.6, f32[1,2,64,128]{3,1,2,0:T(2,128)S(1)} %copy-done.20, f32[2]{0:T(128)} %copy-done.67, ...), kind=kLoop, calls=%fused_computation.155 | loop fusion | flops 393210 | bytes 720984 | tf_op jit(solution)/shard_map/transpose(jvp())/reduce_sum | solution.py:156
  75.5 1.0 convolution_bitcast_fusion.1
  76.6 1.3 fusion.91
  78.5 1.9 %convolution_add_fusion = f32[4,256,128]{2,1,0:T(8,128)S(1)} fusion(f32[4,256,128]{2,1,0:T(8,128)S(1)} %convolution_bitcast_fusion.1, f32[4,256,256]{1,2,0:T(8,128)S(1)} %get-tuple-element.5, f32[4,256,128]{2,1,0:T(8,128)S(1)} %bitcast.326), kind=kOutput, calls=%fused_computation.15 | convolution fusion | flops 402784256 | bytes 2621440 | tf_op jit(solution)/shard_map/transpose(jvp(bin,bjn->bij))/dot_general | solution.py:137
  81.1 1.3 collective-permute-start.7
  83.3 2.1 %collective-permute-done.7 = f32[3,384]{1,0:T(4,128)S(1)} collective-permute-done((f32[3,384]{1,0:T(4,128)S(1)}, f32[3,384]{1,0:T(4,128)S(1)}, u32[]{:S(2)}, u32[]{:S(2)}) %collective-permute-start.7) | collective-permute-done | bytes 4640 | tf_op jit(solution)/shard_map/ppermute | solution.py:23
  85.5 2.1 %fusion.25 = f32[1024,256]{1,0:T(8,128)} fusion(f32[3,256]{1,0:T(4,128)S(1)} %slice.347, f32[1024,256]{1,0:T(8,128)S(1)} %maximum_multiply_fusion, f32[1024]{0:T(1024)S(1)} %copy-done.36, f32[1024]{0:T(1024)S(1)} %copy-done.37, f32[1024]{0:T(1024)S(1)} %get-tuple-element.42, f32[256]{0:T(256)S(1)} %bitcast.349, f32[256]{0:T(256)S(1)} %bitcast.351, ...), kind=kLoop, calls=%fused_computation.37 | loop fusion | flops 3407872 | bytes 2116608 | tf_op jit(solution)/shard_map/add | solution.py:102
  87.6 40.9 %shard_map.94 = f32[16,256]{1,0:T(8,128)} custom-call(f32[64,16,256]{2,1,0:T(8,128)} %bitcast.331), custom_call_target="tpu_custom_call" | custom-call | tf_op jit(solution)/shard_map/pallas_call | solution.py:212
  128.5 1.3 fusion.46
  (243 shorter events, 13.0 us)
Async XLA Ops:
  0.6 12.7 %copy-start.61 = (f32[2,1024]{1,0:T(2,128)S(1)}, f32[2,1024]{1,0:T(2,128)}, u32[]{:S(2)}) copy-start(f32[2,1024]{1,0:T(2,128)} %param.11) | copy-start | bytes 24580
  0.6 12.8 %copy-start.77 = (f32[4,256]{1,0:T(4,128)S(1)}, f32[4,256]{1,0:T(4,128)}, u32[]{:S(2)}) copy-start(f32[4,256]{1,0:T(4,128)} %param.10) | copy-start | bytes 12292
  2.1 16.6 %collective-permute-start = (bf16[3,384]{1,0:T(4,128)(2,1)S(1)}, bf16[3,384]{1,0:T(4,128)(2,1)S(1)}, u32[]{:S(2)}, u32[]{:S(2)}) collective-permute-start(bf16[3,384]{1,0:T(4,128)(2,1)S(1)} %pad_maximum_fusion.8), channel_id=1, source_target_pairs={{0,64},{64,128},{128,192},{1,65},{65,129},{129,193},{2,66},{66,130... | collective-permute-start | bytes 6920 | tf_op jit(solution)/shard_map/ppermute | solution.py:23
  10.2 8.6 %copy-start.41 = (f32[1024]{0:T(1024)}, f32[1024]{0:T(1024)S(1)}, u32[]{:S(2)}) copy-start(f32[1024]{0:T(1024)S(1)} %get-tuple-element.47) | copy-start | bytes 12292
  10.2 8.6 %copy-start.42 = (f32[1024]{0:T(1024)}, f32[1024]{0:T(1024)S(1)}, u32[]{:S(2)}) copy-start(f32[1024]{0:T(1024)S(1)} %get-tuple-element.48) | copy-start | bytes 12292
  10.2 8.6 %copy-start.43 = (f32[1024]{0:T(1024)}, f32[1024]{0:T(1024)S(1)}, u32[]{:S(2)}) copy-start(f32[1024]{0:T(1024)S(1)} %get-tuple-element.49) | copy-start | bytes 12292
  13.4 4.9 %copy-start.23 = (bf16[1024,128]{1,0:T(8,128)(2,1)S(1)}, bf16[1024,128]{1,0:T(8,128)(2,1)}, u32[]{:S(2)}) copy-start(bf16[1024,128]{1,0:T(8,128)(2,1)} %param.13) | copy-start | bytes 786436
  13.5 5.4 %copy-start.52 = (f32[1,256]{1,0:T(1,128)}, f32[1,256]{1,0:T(1,128)S(1)}, u32[]{:S(2)}) copy-start(f32[1,256]{1,0:T(1,128)S(1)} %get-tuple-element.56) | copy-start | bytes 3076
  13.5 5.4 %copy-start.54 = (f32[1,256]{1,0:T(1,128)}, f32[1,256]{1,0:T(1,128)S(1)}, u32[]{:S(2)}) copy-start(f32[1,256]{1,0:T(1,128)S(1)} %get-tuple-element.57) | copy-start | bytes 3076
  13.5 5.4 %copy-start.56 = (f32[1,256]{1,0:T(1,128)}, f32[1,256]{1,0:T(1,128)S(1)}, u32[]{:S(2)}) copy-start(f32[1,256]{1,0:T(1,128)S(1)} %get-tuple-element.58) | copy-start | bytes 3076
  13.5 5.4 %copy-start.58 = (f32[1,256]{1,0:T(1,128)}, f32[1,256]{1,0:T(1,128)S(1)}, u32[]{:S(2)}) copy-start(f32[1,256]{1,0:T(1,128)S(1)} %get-tuple-element.59) | copy-start | bytes 3076
  14.7 4.0 %copy-start.21 = (bf16[1024,256]{1,0:T(8,128)(2,1)S(1)}, bf16[1024,256]{1,0:T(8,128)(2,1)}, u32[]{:S(2)}) copy-start(bf16[1024,256]{1,0:T(8,128)(2,1)} %param.8) | copy-start | bytes 1572868
  18.3 13.9 %copy-start.48 = (f32[2]{0:T(128)}, f32[2]{0:T(128)S(1)}, u32[]{:S(2)}) copy-start(f32[2]{0:T(128)S(1)} %get-tuple-element.13) | copy-start | bytes 28
  18.3 13.9 %copy-start.50 = (f32[2]{0:T(128)}, f32[2]{0:T(128)S(1)}, u32[]{:S(2)}) copy-start(f32[2]{0:T(128)S(1)} %get-tuple-element.14) | copy-start | bytes 28
  18.3 13.9 %copy-start.69 = (f32[2]{0:T(128)}, f32[2]{0:T(128)S(1)}, u32[]{:S(2)}) copy-start(f32[2]{0:T(128)S(1)} %get-tuple-element.11) | copy-start | bytes 28
  21.5 4.0 %copy-start.74 = (f32[2,128]{1,0:T(2,128)}, f32[2,128]{1,0:T(2,128)S(1)}, u32[]{:S(2)}) copy-start(f32[2,128]{1,0:T(2,128)S(1)} %broadcast_in_dim.22) | copy-start | bytes 3076
  21.5 5.8 %collective-permute-start.1 = (f32[2,8320]{1,0:T(2,128)S(1)}, f32[2,8320]{1,0:T(2,128)S(1)}, u32[]{:S(2)}, u32[]{:S(2)}) collective-permute-start(f32[2,8320]{1,0:T(2,128)S(1)} %pad_maximum_fusion.6), channel_id=1, source_target_pairs={{64,0},{128,64},{192,128},{65,1},{129,65},{193,129},{66,2},{130,66... | collective-permute-start | bytes 199688 | tf_op jit(solution)/shard_map/ppermute | solution.py:23
  22.8 6.6 %collective-permute-start.2 = (f32[2,8320]{1,0:T(2,128)S(1)}, f32[2,8320]{1,0:T(2,128)S(1)}, u32[]{:S(2)}, u32[]{:S(2)}) collective-permute-start(f32[2,8320]{1,0:T(2,128)S(1)} %pad_maximum_fusion.6), channel_id=1, source_target_pairs={{128,0},{192,64},{129,1},{193,65},{130,2},{194,66},{131,3},{195,67... | collective-permute-start | bytes 199688 | tf_op jit(solution)/shard_map/ppermute | solution.py:23
  24.1 8.0 %collective-permute-start.3 = (f32[2,8320]{1,0:T(2,128)S(1)}, f32[2,8320]{1,0:T(2,128)S(1)}, u32[]{:S(2)}, u32[]{:S(2)}) collective-permute-start(f32[2,8320]{1,0:T(2,128)S(1)} %pad_maximum_fusion.6), channel_id=1, source_target_pairs={{192,0},{193,1},{194,2},{195,3},{196,4},{197,5},{198,6},{199,7},{2... | collective-permute-start | bytes 199688 | tf_op jit(solution)/shard_map/ppermute | solution.py:23
  26.5 7.0 %copy-start.10 = (f32[4,256,256]{1,2,0:T(8,128)}, f32[4,256,256]{1,2,0:T(8,128)S(1)}, u32[]{:S(2)}) copy-start(f32[4,256,256]{1,2,0:T(8,128)S(1)} %fusion.143) | copy-start | bytes 3145732
  27.2 5.1 %copy-start.5 = (f32[2,4,64,128]{3,2,0,1:T(8,128)}, f32[2,4,64,128]{3,2,0,1:T(8,128)S(1)}, u32[]{:S(2)}) copy-start(f32[2,4,64,128]{3,2,0,1:T(8,128)S(1)} %convolution_bitcast_fusion.4) | copy-start | bytes 786436
  27.3 6.2 %copy-start.25 = (f32[2,8320]{1,0:T(2,128)}, f32[2,8320]{1,0:T(2,128)S(1)}, u32[]{:S(2)}) copy-start(f32[2,8320]{1,0:T(2,128)S(1)} %collective-permute-done.1) | copy-start | bytes 199684
  27.4 5.0 %copy-start.15 = (f32[1,2,64,128]{3,1,2,0:T(2,128)}, f32[1,2,64,128]{3,1,2,0:T(2,128)S(1)}, u32[]{:S(2)}) copy-start(f32[1,2,64,128]{3,1,2,0:T(2,128)S(1)} %slice_bitcast_fusion.8) | copy-start | bytes 196612
  27.5 4.8 %copy-start.65 = (f32[2]{0:T(128)}, f32[2]{0:T(128)S(1)}, u32[]{:S(2)}) copy-start(f32[2]{0:T(128)S(1)} %slice_reduce_fusion.6) | copy-start | bytes 28
  29.5 4.1 %copy-start.27 = (f32[2,8320]{1,0:T(2,128)}, f32[2,8320]{1,0:T(2,128)S(1)}, u32[]{:S(2)}) copy-start(f32[2,8320]{1,0:T(2,128)S(1)} %collective-permute-done.2) | copy-start | bytes 199684
  29.6 4.0 %copy-start.8 = (f32[4,256,256]{1,2,0:T(8,128)S(1)}, f32[4,256,256]{1,2,0:T(8,128)}, u32[]{:S(2)}) copy-start(f32[4,256,256]{1,2,0:T(8,128)} %get-tuple-element.39) | copy-start | bytes 3145732
  44.6 23.5 %collective-permute-start.5 = (f32[2,8320]{1,0:T(2,128)}, f32[2,8320]{1,0:T(2,128)}, u32[]{:S(2)}, u32[]{:S(2)}) collective-permute-start(f32[2,8320]{1,0:T(2,128)} %pad_maximum_fusion.5), channel_id=1, source_target_pairs={{0,128},{64,192},{1,129},{65,193},{2,130},{66,194},{3,131},{67,195... | collective-permute-start | bytes 199688 | tf_op jit(solution)/shard_map/ppermute | solution.py:23
  46.5 23.3 %collective-permute-start.4 = (f32[2,8320]{1,0:T(2,128)}, f32[2,8320]{1,0:T(2,128)}, u32[]{:S(2)}, u32[]{:S(2)}) collective-permute-start(f32[2,8320]{1,0:T(2,128)} %pad_maximum_fusion.5), channel_id=1, source_target_pairs={{0,64},{64,128},{128,192},{1,65},{65,129},{129,193},{2,66},{66,130... | collective-permute-start | bytes 199688 | tf_op jit(solution)/shard_map/ppermute | solution.py:23
  50.9 20.5 %collective-permute-start.6 = (f32[2,8320]{1,0:T(2,128)}, f32[2,8320]{1,0:T(2,128)}, u32[]{:S(2)}, u32[]{:S(2)}) collective-permute-start(f32[2,8320]{1,0:T(2,128)} %pad_maximum_fusion.5), channel_id=1, source_target_pairs={{0,192},{1,193},{2,194},{3,195},{4,196},{5,197},{6,198},{7,199},{8... | collective-permute-start | bytes 199688 | tf_op jit(solution)/shard_map/ppermute | solution.py:23
  57.2 4.7 %copy-start.12 = (f32[2,1,64,128]{3,2,0,1:T(8,128)S(1)}, f32[2,1,64,128]{3,2,0,1:T(8,128)}, u32[]{:S(2)}) copy-start(f32[2,1,64,128]{3,2,0,1:T(8,128)} %copy-done.11) | copy-start | bytes 196612
  57.2 4.6 %copy-start.14 = (f32[2,1,64,128]{3,2,0,1:T(8,128)S(1)}, f32[2,1,64,128]{3,2,0,1:T(8,128)}, u32[]{:S(2)}) copy-start(f32[2,1,64,128]{3,2,0,1:T(8,128)} %copy-done.13) | copy-start | bytes 196612
  64.7 7.5 %copy-start.49 = (f32[2]{0:T(128)S(1)}, f32[2]{0:T(128)}, u32[]{:S(2)}) copy-start(f32[2]{0:T(128)} %copy-done.48) | copy-start | bytes 28
  64.7 8.5 %copy-start.16 = (f32[1,2,64,128]{3,1,2,0:T(2,128)S(1)}, f32[1,2,64,128]{3,1,2,0:T(2,128)}, u32[]{:S(2)}) copy-start(f32[1,2,64,128]{3,1,2,0:T(2,128)} %copy-done.15) | copy-start | bytes 196612
  64.7 8.5 %copy-start.18 = (f32[1,2,64,128]{3,1,2,0:T(2,128)S(1)}, f32[1,2,64,128]{3,1,2,0:T(2,128)}, u32[]{:S(2)}) copy-start(f32[1,2,64,128]{3,1,2,0:T(2,128)} %copy-done.17) | copy-start | bytes 196612
  66.1 7.2 %copy-start.6 = (f32[2,4,64,128]{3,2,0,1:T(8,128)S(1)}, f32[2,4,64,128]{3,2,0,1:T(8,128)}, u32[]{:S(2)}) copy-start(f32[2,4,64,128]{3,2,0,1:T(8,128)} %copy-done.5) | copy-start | bytes 786436
  66.1 7.2 %copy-start.7 = (f32[2,4,64,128]{3,2,0,1:T(8,128)S(1)}, f32[2,4,64,128]{3,2,0,1:T(8,128)}, u32[]{:S(2)}) copy-start(f32[2,4,64,128]{3,2,0,1:T(8,128)} %convolution_bitcast_fusion.3) | copy-start | bytes 786436
  67.5 5.8 %copy-start.20 = (f32[1,2,64,128]{3,1,2,0:T(2,128)S(1)}, f32[1,2,64,128]{3,1,2,0:T(2,128)}, u32[]{:S(2)}) copy-start(f32[1,2,64,128]{3,1,2,0:T(2,128)} %copy-done.19) | copy-start | bytes 196612
  80.5 5.0 %copy-start.36 = (f32[1024]{0:T(1024)S(1)}, f32[1024]{0:T(1024)}, u32[]{:S(2)}) copy-start(f32[1024]{0:T(1024)} %get-tuple-element.45) | copy-start | bytes 12292
  80.5 5.0 %copy-start.37 = (f32[1024]{0:T(1024)S(1)}, f32[1024]{0:T(1024)}, u32[]{:S(2)}) copy-start(f32[1024]{0:T(1024)} %get-tuple-element.46) | copy-start | bytes 12292
  80.5 5.0 %copy-start.53 = (f32[1,256]{1,0:T(1,128)S(1)}, f32[1,256]{1,0:T(1,128)}, u32[]{:S(2)}) copy-start(f32[1,256]{1,0:T(1,128)} %copy-done.52) | copy-start | bytes 3076
  80.5 5.0 %copy-start.55 = (f32[1,256]{1,0:T(1,128)S(1)}, f32[1,256]{1,0:T(1,128)}, u32[]{:S(2)}) copy-start(f32[1,256]{1,0:T(1,128)} %copy-done.54) | copy-start | bytes 3076
  80.5 5.0 %copy-start.57 = (f32[1,256]{1,0:T(1,128)S(1)}, f32[1,256]{1,0:T(1,128)}, u32[]{:S(2)}) copy-start(f32[1,256]{1,0:T(1,128)} %copy-done.56) | copy-start | bytes 3076
  80.5 5.0 %copy-start.59 = (f32[1,256]{1,0:T(1,128)S(1)}, f32[1,256]{1,0:T(1,128)}, u32[]{:S(2)}) copy-start(f32[1,256]{1,0:T(1,128)} %copy-done.58) | copy-start | bytes 3076
  81.1 4.4 %collective-permute-start.7 = (f32[3,384]{1,0:T(4,128)S(1)}, f32[3,384]{1,0:T(4,128)S(1)}, u32[]{:S(2)}, u32[]{:S(2)}) collective-permute-start(f32[3,384]{1,0:T(4,128)S(1)} %pad_maximum_fusion.7), channel_id=1, source_target_pairs={{64,0},{128,64},{192,128},{65,1},{129,65},{193,129},{66,2},{130,66... | collective-permute-start | bytes 13832 | tf_op jit(solution)/shard_map/ppermute | solution.py:23
  87.6 40.9 %copy-start.70 = (f32[128]{0:T(128)S(1)}, f32[128]{0:T(128)}, u32[]{:S(2)}) copy-start(f32[128]{0:T(128)} %get-tuple-element.60) | copy-start | bytes 1540
  87.6 40.9 %copy-start.71 = (f32[128]{0:T(128)S(1)}, f32[128]{0:T(128)}, u32[]{:S(2)}) copy-start(f32[128]{0:T(128)} %get-tuple-element.61) | copy-start | bytes 1540
  87.6 40.9 %copy-start.72 = (f32[128]{0:T(128)S(1)}, f32[128]{0:T(128)}, u32[]{:S(2)}) copy-start(f32[128]{0:T(128)} %get-tuple-element.62) | copy-start | bytes 1540
  87.6 40.9 %copy-start.73 = (f32[128]{0:T(128)S(1)}, f32[128]{0:T(128)}, u32[]{:S(2)}) copy-start(f32[128]{0:T(128)} %get-tuple-element.63) | copy-start | bytes 1540
  (46 other events, 95.0 us)

commit v7 on v5

--- a/solution.py
+++ b/solution.py
@@ -126,6 +126,29 @@
     length = values.shape[-1]
     upper = (jnp.arange(length)[:, None] <= jnp.arange(length)[None, :]).astype(values.dtype)
     return jnp.dot(values, upper, precision=precise, preferred_element_type=jnp.float32)
+
+
+def chain_both(state, adjoint, keep, axis):
+    count, mine = lax.axis_size(axis), lax.axis_index(axis)
+    heads, size = state.shape[0], state[0].size
+    tail = jnp.broadcast_to(keep[:, None], (heads, 128))
+    later = jnp.concatenate([state.reshape(heads, size), tail], axis=1)
+    earlier = jnp.concatenate([adjoint.reshape(heads, size), tail], axis=1)
+    targets = jnp.arange(count)[:, None, None]
+    outgoing = jnp.where(targets > mine, later[None], jnp.where(targets < mine, earlier[None], 0.0))
+    arrived = lax.all_to_all(outgoing, axis, 0, 0, tiled=False)
+    parts = arrived[:, :, :size].reshape((count,) + state.shape)
+    keeps = arrived[:, :, size]
+    totals = []
+    for order in (range(count - 1, -1, -1), range(count)):
+        total = jnp.zeros_like(state)
+        scale = jnp.ones_like(keep)
+        for source in order:
+            near = (source < mine) if order.step < 0 else (source > mine)
+            total = total + jnp.where(near, scale, 0.0)[:, None, None] * parts[source]
+            scale = jnp.where(near, scale * keeps[source], scale)
+        totals.append(total)
+    return totals[0], totals[1]
 
 
 def einsum(spec, *operands):
@@ -206,8 +229,7 @@
         "thp,ht,tn->hpn", g_rows, entry_rows, v_bc[:, N:], precision=precise,
         preferred_element_type=jnp.float32,
     )
-    state_in = chain_in(local_state, keep, "seq", 1)
-    adjoint_in = chain_in(local_adjoint, keep, "seq", -1)
+    state_in, adjoint_in = chain_both(local_state, local_adjoint, keep, "seq")
 
     def local_forward(x_all, b_all, c_all, log_all):
         return block_forward_all(

time: 117 us -> 108 us (0.923)
  the two profiles are of different devices: /device:TPU:32 before, /device:TPU:8 now
where the time goes in v7:
time: 108 us; the launch traced here: 106 us
  local copies, waits for them, and re-layouts  24 us (22%)
  other arithmetic  23.5 us (22%)
  matrix products  22.2 us (21%)
  starting transfers between devices  21.3 us (20%)
  waiting for transfers between devices  12.2 us (11%)
  between operations  2.7 us (2%)
    dot_general x11, matrix products, einsum(): jnp.einsum(spec, *operands, precision=precise, preferred_element_type=jnp...  18.3 us
    all_to_all x1, starting transfers between devices, local(): grad_pre_bc = lax.all_to_all(pair_sum, 'chip', 0, 0, tiled=False).sum(0)  11.3 us
    all_to_all x1, waiting for transfers between devices, local(): grad_pre_bc = lax.all_to_all(pair_sum, 'chip', 0, 0, tiled=False).sum(0)  6.47 us
    ppermute x2, starting transfers between devices, shifted(): lax.ppermute(value, axis, [(source, source + steps) for source in range(i...  5.4 us
    all_to_all x1, starting transfers between devices, chain_both(): arrived = lax.all_to_all(outgoing, axis, 0, 0, tiled=False)  4.62 us
    unnamed x97, local copies, waits for them, and re-layouts  4.11 us
    ppermute x2, waiting for transfers between devices, shifted(): lax.ppermute(value, axis, [(source, source + steps) for source in range(i...  3.59 us
    add x2, other arithmetic, conv_backward(): result + weights[k][None, :] * extended[lag:lag + count] * linked[:, None]  3.25 us
  transfers between devices with their start and end apart: 5, of which 3 were waited for; matrix products, arithmetic and copies ran while one was open for 33% of the time, Pallas kernels for 0%

profile of v7, /device:TPU:8, one launch (start us, length us, event | category | flops | bytes accessed | tf_op | source)
XLA Modules:
  0.0 105.9 jit_solution(203130565790632677)
XLA Ops:
  0.6 0.7 slice.259
  2.1 3.5 %collective-permute-start = (bf16[3,384]{1,0:T(4,128)(2,1)S(1)}, bf16[3,384]{1,0:T(4,128)(2,1)S(1)}, u32[]{:S(2)}, u32[]{:S(2)}) collective-permute-start(bf16[3,384]{1,0:T(4,128)(2,1)S(1)} %pad_maximum_fusion.8), channel_id=1, source_target_pairs={{0,64},{64,128},{128,192},{1,65},{65,129},{129,193},{2,66},{66,130... | collective-permute-start | bytes 6920 | tf_op jit(solution)/shard_map/ppermute | solution.py:18
  5.6 0.8 reduce-window.9
  8.2 1.4 %fusion.19 = f32[2,1024]{1,0:T(2,128)S(1)} fusion(f32[2,1024]{1,0:T(2,128)} %param.11), kind=kOutput, calls=%fused_computation.30 | convolution fusion | flops 26214400 | bytes 16384 | tf_op jit(solution)/shard_map/dot_general | solution.py:128
  11.6 2.0 %fusion.122 = (f32[1024]{0:T(1024)}, f32[1024]{0:T(1024)S(1)}, f32[1024]{0:T(1024)S(1)}, f32[1024]{0:T(1024)}, f32[1024]{0:T(1024)}, /*index=5*/f32[1024]{0:T(1024)S(1)}, f32[1024]{0:T(1024)S(1)}, f32[1024]{0:T(1024)S(1)}) fusion(s32[1030]{0:T(1024)S(1)} %broadcast_add_fusion, s32[]{:T(128)} %bitcast.9, s32[]{:T(128)} %bitcast.15), kind=kLoop, calls=%fused_computation.214 | loop fusion | flops 16384 | bytes 61448 | tf_op jit(solution)/shard_map/convert_element_type | solution.py:97
  13.6 0.8 slice_bitcast_fusion.7
  14.5 0.8 fusion.145
  16.5 0.7 slice_reduce_fusion.8
  17.4 1.4 %compare_and_fusion = (pred[4,256,256]{1,2,0:T(8,128)(4,1)}, f32[4,256,256]{1,2,0:T(8,128)}) fusion(s32[4,256]{1,0:T(4,128)S(1)} %reshape.473, pred[256,256]{0,1:T(8,128)(4,1)S(1)} %iota_compare_fusion.4), kind=kLoop, calls=%fused_computation.57 | loop fusion | flops 786432 | bytes 1380352 | tf_op jit(solution)/shard_map/jvp()/and | solution.py:165
  20.7 1.3 %fusion.66 = (f32[1024,128]{1,0:T(8,128)S(1)}, f32[1024,128]{1,0:T(8,128)}) fusion(f32[1027,128]{1,0:T(8,128)S(1)} %maximum_convert_fusion.1, f32[128]{0:T(128)S(1)} %get-tuple-element.68, f32[1024]{0:T(1024)S(1)} %get-tuple-element.53, f32[128]{0:T(128)S(1)} %get-tuple-element.69, f32[1024]{0:T(1024)S(1)} %get-tuple-element.54, ...), kind=kLoop, calls=%fused_computation.101 | loop fusion | flops 1835008 | bytes 3160064 | tf_op jit(solution)/shard_map/jit(silu)/mul | solution.py:202
  22.0 1.0 copy.172
  24.1 1.2 %copy.208 = f32[4,256,2,64]{1,3,0,2:T(8,128)} copy(f32[4,256,2,64]{3,2,1,0:T(2,128)S(1)} %reshape.494) | data formatting | bytes 1048576 | tf_op jit(solution)/shard_map/transpose | solution.py:204
  25.5 1.0 fusion.37
  26.6 1.0 copy-done.3
  29.1 0.9 select_select_fusion
  30.0 4.6 %all-to-all-start = ((f32[4,2,8320]{2,1,0:T(2,128)}), f32[4,2,8320]{2,1,0:T(2,128)S(1)}, u32[]{:S(2)}, u32[]{:S(2)}) async-start(f32[4,2,8320]{2,1,0:T(2,128)} %select_select_fusion), calls=%async_computation | async-start | bytes 532480 | tf_op jit(solution)/shard_map/all_to_all | solution.py:139
  35.9 1.5 %squeeze.89 = f32[1,2,8192]{2,1,0:T(2,128)} reshape(f32[2,1,64,128]{3,2,0,1:T(8,128)} %get-tuple-element.41) | data formatting | bytes 131072 | tf_op jit(solution)/shard_map/jvp()/squeeze | solution.py:174
  38.7 1.0 fusion.146
  40.2 4.7 %fusion.17 = (f32[2,4,256]{2,1,0:T(4,128)}, f32[2,4,256]{2,1,0:T(4,128)}, f32[4,256,256]{1,2,0:T(8,128)}, f32[2,4,256,256]{2,3,1,0:T(8,128)}) fusion(f32[4,256,256]{1,2,0:T(8,128)S(1)} %copy-done.6, f32[2,4,256]{2,1,0:T(4,128)S(1)} %bitcast.344, f32[4,256,256]{1,2,0:T(8,128)S(1)} %fusion.146, pred[4,256,256]{1,2,0:T(8,128)(4,1)S(1)} %copy-done.17, ...), kind=kOutput, calls=%fused_computation.24 | convolution fusion | flops 408678400 | bytes 6316032 | tf_op jit(solution)/shard_map/transpose(jvp(hbij,hbjp->hbip))/dot_general | solution.py:155
  44.9 1.4 %convolution_bitcast_fusion.4 = f32[2,4,64,128]{3,2,0,1:T(8,128)} fusion(f32[4,256,128,1]{2,1,3,0:T(8,128)S(1)} %bitcast.332, f32[4,2,256]{2,1,0:T(2,128)S(1)} %copy-done.18, bf16[4,256,2,64]{1,0,3,2:T(4,128)(2,1)S(1)} %reshape.474), kind=kOutput, calls=%fused_computation.27 | convolution fusion | flops 201588736 | bytes 1056768 | tf_op jit(solution)/shard_map/transpose(jvp(bin,hbpn->hbip))/dot_general | solution.py:155
  46.5 1.9 %multiply_reduce_fusion.1 = (f32[2]{0:T(128)}, f32[1,2,64,128]{3,1,2,0:T(2,128)S(1)}) fusion(f32[1,2,8192]{2,1,0:T(2,128)} %squeeze.91, f32[1,2,8192]{2,1,0:T(2,128)} %squeeze.90, f32[1,2,8192]{2,1,0:T(2,128)} %squeeze.89, f32[4,2,8320]{2,1,0:T(2,128)S(1)} %all-to-all-done, f32[2]{0:T(128)S(1)} %get-tuple-element.72, f32[2]{0:T(128)S(1)} %get-tuple-element.73, ...), kind=kLoop, calls=%fused_computation.166 | loop fusion | flops 360446 | bytes 524376 | tf_op jit(solution)/shard_map/transpose(jvp())/reduce_sum | solution.py:174
  49.2 1.1 %multiply_add_fusion.3 = (f32[2,1,64,128]{3,2,0,1:T(8,128)S(1)}, f32[2,1,64,128]{3,2,0,1:T(8,128)S(1)}, f32[2,1,64,128]{3,2,0,1:T(8,128)S(1)}, f32[2,1,64,128]{3,2,0,1:T(8,128)S(1)}) fusion(f32[2,4,64,128]{3,2,0,1:T(8,128)} %convolution_bitcast_fusion.4, f32[2]{0:T(128)} %get-tuple-element.17, f32[2]{0:T(128)} %get-tuple-element.18, ...), kind=kLoop, calls=%fused_computation.170 | loop fusion | flops 212992 | bytes 720948 | tf_op jit(solution)/shard_map/transpose(jvp())/add_any | solution.py:174
  50.3 1.8 %convolution_bitcast_fusion.2 = f32[4,256,128]{2,1,0:T(8,128)S(1)} fusion(f32[4,256,2,64]{1,3,2,0:T(8,128)S(1)} %copy.184, f32[2,4,256]{2,0,1:T(2,128)} %copy-done.20, f32[2,1,64,128]{3,2,0,1:T(8,128)S(1)} %get-tuple-element.19, f32[2,1,64,128]{3,2,0,1:T(8,128)S(1)} %get-tuple-element.20, f32[2,1,64,128]{3,2,0,1:T(8,128)S(1)} %get-tuple-element.21, ...), kind=kOutput, calls=%fused_computation.20 | convolution fusion | flops 201654272 | bytes 1318912 | tf_op jit(solution)/shard_map/transpose(jvp(hbjp,bjn->hbpn))/dot_general | solution.py:155
  52.1 1.2 %fusion.60 = (f32[2,4,256]{2,0,1:T(2,128)}, f32[4,2,64,256]{3,2,1,0:T(8,128)S(1)}) fusion(f32[4,256,2,64]{1,3,2,0:T(8,128)S(1)} %copy.184, f32[4,256,128,1]{2,1,3,0:T(8,128)S(1)} %bitcast.329, f32[2,1,64,128]{3,2,0,1:T(8,128)S(1)} %get-tuple-element.19, f32[2,1,64,128]{3,2,0,1:T(8,128)S(1)} %get-tuple-element.20, ...), kind=kOutput, calls=%fused_computation.89 | convolution fusion | flops 201783296 | bytes 1843200 | tf_op jit(solution)/shard_map/transpose(jvp(hbjp,bjn->hbpn))/dot_general | solution.py:155
  53.4 1.0 convolution_bitcast_fusion.1
  54.5 1.8 %convolution_add_fusion = f32[4,256,128]{2,1,0:T(8,128)S(1)} fusion(f32[4,256,128]{2,1,0:T(8,128)S(1)} %convolution_bitcast_fusion.1, f32[4,256,256]{1,2,0:T(8,128)S(1)} %copy-done, f32[4,256,128]{2,1,0:T(8,128)S(1)} %bitcast.330), kind=kOutput, calls=%fused_computation.15 | convolution fusion | flops 402784256 | bytes 2621440 | tf_op jit(solution)/shard_map/transpose(jvp(bin,bjn->bij))/dot_general | solution.py:155
  56.3 1.1 %convolution_add_fusion.1 = f32[4,256,128]{2,1,0:T(8,128)S(1)} fusion(f32[4,256,128]{2,1,0:T(8,128)S(1)} %convolution_bitcast_fusion.2, f32[4,256,256]{1,2,0:T(8,128)S(1)} %copy-done, f32[4,256,128]{2,1,0:T(8,128)S(1)} %bitcast.333), kind=kOutput, calls=%fused_computation.16 | convolution fusion | flops 402784256 | bytes 2621440 | tf_op jit(solution)/shard_map/transpose(jvp(bin,bjn->bij))/dot_general | solution.py:155
  57.8 1.2 %copy-done.4 = f32[2,4,256,256]{2,3,1,0:T(8,128)S(1)} copy-done((f32[2,4,256,256]{2,3,1,0:T(8,128)S(1)}, f32[2,4,256,256]{2,3,1,0:T(8,128)}, u32[]{:S(2)}) %copy-start.4) | copy-done | bytes 2097176
  59.0 2.0 %fusion.12 = f32[4,256,2,64]{1,3,2,0:T(8,128)} fusion(f32[2,4,256,256]{2,3,1,0:T(8,128)S(1)} %copy-done.4, f32[4,2,64,256]{3,2,1,0:T(8,128)S(1)} %get-tuple-element.81, bf16[2,4,256,64]{2,1,3,0:T(4,128)(2,1)S(1)} %bitcast.336, f32[4,256,2]{1,2,0:T(2,128)S(1)} %copy-done.25), kind=kOutput, calls=%fused_computation.21 | convolution fusion | flops 402915328 | bytes 3416064 | tf_op jit(solution)/shard_map/transpose(jvp(hbij,hbjp->hbip))/dot_general | solution.py:155
  61.1 1.7 %copy.205 = f32[4,256,2,64]{3,2,1,0:T(2,128)S(1)} copy(f32[4,256,2,64]{1,3,2,0:T(8,128)} %fusion.12) | data formatting | bytes 1048576 | tf_op jit(solution)/shard_map/reshape | solution.py:242
  62.8 1.4 %reshape.493 = f32[1024,128]{1,0:T(8,128)} reshape(f32[4,256,2,64]{3,2,1,0:T(2,128)S(1)} %copy.205) | data formatting | bytes 1048576 | tf_op jit(solution)/shard_map/reshape | solution.py:242
  64.2 1.4 %multiply_multiply_fusion = f32[1024,128]{1,0:T(8,128)S(1)} fusion(f32[1024,128]{1,0:T(8,128)} %reshape.493, f32[1024,128]{1,0:T(8,128)} %get-tuple-element.30), kind=kLoop, calls=%fused_computation.98 | loop fusion | flops 1048576 | bytes 1572864 | tf_op jit(solution)/shard_map/mul | solution.py:244
  65.6 1.9 %collective-permute-start.1 = (f32[3,384]{1,0:T(4,128)S(1)}, f32[3,384]{1,0:T(4,128)S(1)}, u32[]{:S(2)}, u32[]{:S(2)}) collective-permute-start(f32[3,384]{1,0:T(4,128)S(1)} %pad_maximum_fusion.7), channel_id=1, source_target_pairs={{64,0},{128,64},{192,128},{65,1},{129,65},{193,129},{66,2},{130,66... | collective-permute-start | bytes 13832 | tf_op jit(solution)/shard_map/ppermute | solution.py:18
  67.5 3.6 %collective-permute-done.1 = f32[3,384]{1,0:T(4,128)S(1)} collective-permute-done((f32[3,384]{1,0:T(4,128)S(1)}, f32[3,384]{1,0:T(4,128)S(1)}, u32[]{:S(2)}, u32[]{:S(2)}) %collective-permute-start.1) | collective-permute-done | bytes 4640 | tf_op jit(solution)/shard_map/ppermute | solution.py:18
  71.7 1.3 %fusion.25 = f32[1024,256]{1,0:T(8,128)S(1)} fusion(f32[3,256]{1,0:T(4,128)S(1)} %slice.361, f32[1024,256]{1,0:T(8,128)S(1)} %maximum_multiply_fusion, f32[1024]{0:T(1024)S(1)} %copy-done.22, f32[1024]{0:T(1024)S(1)} %copy-done.23, f32[1024]{0:T(1024)S(1)} %copy-done.21, f32[256]{0:T(256)S(1)} %bitcast.351, f32[256]{0:T(256)S(1)} %bitcast.353, ...), kind=kLoop, calls=%fused_computation.37 | loop fusion | flops 3407872 | bytes 2116608 | tf_op jit(solution)/shard_map/add | solution.py:97
  73.1 0.9 dynamic-slice_bitcast_fusion
  73.9 2.1 %collective-permute-done.2 = f32[32,16,256]{2,1,0:T(8,128)S(1)} collective-permute-done((f32[32,16,256]{2,1,0:T(8,128)}, f32[32,16,256]{2,1,0:T(8,128)S(1)}, u32[]{:S(2)}, u32[]{:S(2)}) %collective-permute-start.2) | collective-permute-done | bytes 524320 | tf_op jit(solution)/shard_map/ppermute | solution.py:255
  76.0 0.9 bitcast_add_fusion
  76.9 11.3 %all-to-all-start.1 = ((f32[32,16,256]{2,1,0:T(8,128)}), f32[32,16,256]{2,1,0:T(8,128)S(1)}, u32[]{:S(2)}, u32[]{:S(2)}) async-start(f32[32,16,256]{2,1,0:T(8,128)} %bitcast_add_fusion), calls=%async_computation.1 | async-start | bytes 1048576 | tf_op jit(solution)/shard_map/all_to_all | solution.py:256
  88.2 1.0 fusion.89
  89.3 0.8 copy.189
  90.0 0.8 fusion.101
  91.1 0.8 multiply_bitcast_fusion
  92.0 0.9 fusion.127
  92.9 1.6 %fusion.18 = f32[2,4,256]{2,0,1:T(2,128)S(1)} fusion(f32[4,256,128,1]{2,1,3,0:T(8,128)S(1)} %bitcast.334, bf16[4,256,2,64]{1,0,3,2:T(4,128)(2,1)S(1)} %reshape.474, f32[2,1,64,128]{3,2,0,1:T(8,128)} %copy-done.9, f32[2,1,64,128]{3,2,0,1:T(8,128)} %copy-done.10, f32[2,1,64,128]{3,2,0,1:T(8,128)} %copy-done.11, f32[2,1,64,128]{3,2,0,1:T(8,128)} %copy-done.12), kind=kOutput, calls=%fused_computation.25 | convolution fusion | flops 201914368 | bytes 1056768 | tf_op jit(solution)/shard_map/jvp(bin,hbpn->hbip)/dot_general | solution.py:155
  94.5 1.0 convolution_bitcast_fusion.7
  96.8 2.0 %fusion.46 = f32[1024,128]{1,0:T(8,128)} fusion(f32[3,128]{1,0:T(4,128)S(1)} %slice.353, f32[1024,128]{1,0:T(8,128)S(1)} %copy-done.2, f32[1024]{0:T(1024)} %get-tuple-element.51, f32[1024]{0:T(1024)} %get-tuple-element.52, f32[1024]{0:T(1024)S(1)} %copy-done.21, f32[128]{0:T(128)} %copy-done.44, f32[128]{0:T(128)} %copy-done.45, f32[128]{0:T(128)} %copy-done.43, ...), kind=kLoop, calls=%fused_computation.69 | loop fusion | flops 1703936 | bytes 1064448 | tf_op jit(solution)/shard_map/add | solution.py:97
  98.8 6.5 %all-to-all-done.1 = f32[32,16,256]{2,1,0:T(8,128)S(1)} async-done(((f32[32,16,256]{2,1,0:T(8,128)}), f32[32,16,256]{2,1,0:T(8,128)S(1)}, u32[]{:S(2)}, u32[]{:S(2)}) %all-to-all-start.1) | async-done | bytes 524320 | tf_op jit(solution)/shard_map/all_to_all | solution.py:256
  (156 shorter events, 16.8 us)
Async XLA Ops:
  0.6 20.0 %copy-start.15 = (bf16[1024,128]{1,0:T(8,128)(2,1)S(1)}, bf16[1024,128]{1,0:T(8,128)(2,1)}, u32[]{:S(2)}) copy-start(bf16[1024,128]{1,0:T(8,128)(2,1)} %param.7) | copy-start | bytes 786436
  0.6 19.7 %copy-start.16 = (bf16[1024,128]{1,0:T(8,128)(2,1)S(1)}, bf16[1024,128]{1,0:T(8,128)(2,1)}, u32[]{:S(2)}) copy-start(bf16[1024,128]{1,0:T(8,128)(2,1)} %param.13) | copy-start | bytes 786436
  2.1 18.6 %collective-permute-start = (bf16[3,384]{1,0:T(4,128)(2,1)S(1)}, bf16[3,384]{1,0:T(4,128)(2,1)S(1)}, u32[]{:S(2)}, u32[]{:S(2)}) collective-permute-start(bf16[3,384]{1,0:T(4,128)(2,1)S(1)} %pad_maximum_fusion.8), channel_id=1, source_target_pairs={{0,64},{64,128},{128,192},{1,65},{65,129},{129,193},{2,66},{66,130... | collective-permute-start | bytes 6920 | tf_op jit(solution)/shard_map/ppermute | solution.py:18
  14.4 7.6 %copy-start.42 = (f32[128]{0:T(128)}, f32[128]{0:T(128)S(1)}, u32[]{:S(2)}) copy-start(f32[128]{0:T(128)S(1)} %get-tuple-element.66) | copy-start | bytes 1540
  14.4 7.6 %copy-start.43 = (f32[128]{0:T(128)}, f32[128]{0:T(128)S(1)}, u32[]{:S(2)}) copy-start(f32[128]{0:T(128)S(1)} %get-tuple-element.67) | copy-start | bytes 1540
  14.4 7.6 %copy-start.44 = (f32[128]{0:T(128)}, f32[128]{0:T(128)S(1)}, u32[]{:S(2)}) copy-start(f32[128]{0:T(128)S(1)} %get-tuple-element.68) | copy-start | bytes 1540
  14.5 7.6 %copy-start.45 = (f32[128]{0:T(128)}, f32[128]{0:T(128)S(1)}, u32[]{:S(2)}) copy-start(f32[128]{0:T(128)S(1)} %get-tuple-element.69) | copy-start | bytes 1540
  15.3 10.1 %copy-start.26 = (f32[1,256]{1,0:T(1,128)}, f32[1,256]{1,0:T(1,128)S(1)}, u32[]{:S(2)}) copy-start(f32[1,256]{1,0:T(1,128)S(1)} %get-tuple-element.62) | copy-start | bytes 3076
  15.3 10.1 %copy-start.28 = (f32[1,256]{1,0:T(1,128)}, f32[1,256]{1,0:T(1,128)S(1)}, u32[]{:S(2)}) copy-start(f32[1,256]{1,0:T(1,128)S(1)} %get-tuple-element.63) | copy-start | bytes 3076
  15.3 10.1 %copy-start.30 = (f32[1,256]{1,0:T(1,128)}, f32[1,256]{1,0:T(1,128)S(1)}, u32[]{:S(2)}) copy-start(f32[1,256]{1,0:T(1,128)S(1)} %get-tuple-element.64) | copy-start | bytes 3076
  15.3 10.1 %copy-start.32 = (f32[1,256]{1,0:T(1,128)}, f32[1,256]{1,0:T(1,128)S(1)}, u32[]{:S(2)}) copy-start(f32[1,256]{1,0:T(1,128)S(1)} %get-tuple-element.65) | copy-start | bytes 3076
  16.1 6.0 %copy-start.41 = (f32[4]{0:T(128)}, f32[4]{0:T(128)S(1)}, u32[]{:S(2)}) copy-start(f32[4]{0:T(128)S(1)} %get-tuple-element.27) | copy-start | bytes 52
  16.1 4.5 %copy-start.46 = (f32[4,256]{1,0:T(4,128)}, f32[4,256]{1,0:T(4,128)S(1)}, u32[]{:S(2)}) copy-start(f32[4,256]{1,0:T(4,128)S(1)} %get-tuple-element.61) | copy-start | bytes 12292
  16.5 5.5 %copy-start.24 = (f32[2,4]{1,0:T(2,128)}, f32[2,4]{1,0:T(2,128)S(1)}, u32[]{:S(2)}) copy-start(f32[2,4]{1,0:T(2,128)S(1)} %slice_reduce_fusion) | copy-start | bytes 100
  20.3 14.3 %copy-start.20 = (f32[2,4,256]{2,0,1:T(2,128)}, f32[2,4,256]{2,0,1:T(2,128)S(1)}, u32[]{:S(2)}) copy-start(f32[2,4,256]{2,0,1:T(2,128)S(1)} %copy.185) | copy-start | bytes 24580
  23.0 2.3 %copy-start.13 = (bf16[1024,256]{1,0:T(8,128)(2,1)S(1)}, bf16[1024,256]{1,0:T(8,128)(2,1)}, u32[]{:S(2)}) copy-start(bf16[1024,256]{1,0:T(8,128)(2,1)} %param.8) | copy-start | bytes 1572868
  30.0 16.3 %all-to-all-start = ((f32[4,2,8320]{2,1,0:T(2,128)}), f32[4,2,8320]{2,1,0:T(2,128)S(1)}, u32[]{:S(2)}, u32[]{:S(2)}) async-start(f32[4,2,8320]{2,1,0:T(2,128)} %select_select_fusion), calls=%async_computation | async-start | bytes 532480 | tf_op jit(solution)/shard_map/all_to_all | solution.py:139
  38.7 1.4 %copy-start.17 = (pred[4,256,256]{1,2,0:T(8,128)(4,1)S(1)}, pred[4,256,256]{1,2,0:T(8,128)(4,1)}, u32[]{:S(2)}) copy-start(pred[4,256,256]{1,2,0:T(8,128)(4,1)} %get-tuple-element.46) | copy-start | bytes 786436
  40.2 4.7 %copy-start.18 = (f32[4,2,256]{2,1,0:T(2,128)S(1)}, f32[4,2,256]{2,1,0:T(2,128)}, u32[]{:S(2)}) copy-start(f32[4,2,256]{2,1,0:T(2,128)} %copy.174) | copy-start | bytes 24580
  46.4 6.9 %copy-start.34 = (f32[2]{0:T(128)}, f32[2]{0:T(128)S(1)}, u32[]{:S(2)}) copy-start(f32[2]{0:T(128)S(1)} %get-tuple-element.70) | copy-start | bytes 28
  46.4 6.9 %copy-start.35 = (f32[2]{0:T(128)}, f32[2]{0:T(128)S(1)}, u32[]{:S(2)}) copy-start(f32[2]{0:T(128)S(1)} %get-tuple-element.71) | copy-start | bytes 28
  46.4 6.9 %copy-start.36 = (f32[2]{0:T(128)}, f32[2]{0:T(128)S(1)}, u32[]{:S(2)}) copy-start(f32[2]{0:T(128)S(1)} %get-tuple-element.72) | copy-start | bytes 28
  46.5 6.9 %copy-start.37 = (f32[2]{0:T(128)}, f32[2]{0:T(128)S(1)}, u32[]{:S(2)}) copy-start(f32[2]{0:T(128)S(1)} %get-tuple-element.73) | copy-start | bytes 28
  46.5 6.9 %copy-start.38 = (f32[2]{0:T(128)}, f32[2]{0:T(128)S(1)}, u32[]{:S(2)}) copy-start(f32[2]{0:T(128)S(1)} %get-tuple-element.76) | copy-start | bytes 28
  46.5 6.9 %copy-start.39 = (f32[2]{0:T(128)}, f32[2]{0:T(128)S(1)}, u32[]{:S(2)}) copy-start(f32[2]{0:T(128)S(1)} %get-tuple-element.77) | copy-start | bytes 28
  46.5 6.9 %copy-start.7 = (f32[1,2,64,128]{3,1,2,0:T(2,128)}, f32[1,2,64,128]{3,1,2,0:T(2,128)S(1)}, u32[]{:S(2)}) copy-start(f32[1,2,64,128]{3,1,2,0:T(2,128)S(1)} %get-tuple-element.40) | copy-start | bytes 196612
  48.4 5.0 %copy-start.8 = (f32[1,2,64,128]{3,1,2,0:T(2,128)}, f32[1,2,64,128]{3,1,2,0:T(2,128)S(1)}, u32[]{:S(2)}) copy-start(f32[1,2,64,128]{3,1,2,0:T(2,128)S(1)} %get-tuple-element.37) | copy-start | bytes 196612
  49.1 5.3 %copy-start.9 = (f32[2,1,64,128]{3,2,0,1:T(8,128)}, f32[2,1,64,128]{3,2,0,1:T(8,128)S(1)}, u32[]{:S(2)}) copy-start(f32[2,1,64,128]{3,2,0,1:T(8,128)S(1)} %get-tuple-element.23) | copy-start | bytes 196612
  49.2 5.3 %copy-start.10 = (f32[2,1,64,128]{3,2,0,1:T(8,128)}, f32[2,1,64,128]{3,2,0,1:T(8,128)S(1)}, u32[]{:S(2)}) copy-start(f32[2,1,64,128]{3,2,0,1:T(8,128)S(1)} %get-tuple-element.24) | copy-start | bytes 196612
  49.2 5.3 %copy-start.11 = (f32[2,1,64,128]{3,2,0,1:T(8,128)}, f32[2,1,64,128]{3,2,0,1:T(8,128)S(1)}, u32[]{:S(2)}) copy-start(f32[2,1,64,128]{3,2,0,1:T(8,128)S(1)} %get-tuple-element.25) | copy-start | bytes 196612
  49.2 5.3 %copy-start.12 = (f32[2,1,64,128]{3,2,0,1:T(8,128)}, f32[2,1,64,128]{3,2,0,1:T(8,128)S(1)}, u32[]{:S(2)}) copy-start(f32[2,1,64,128]{3,2,0,1:T(8,128)S(1)} %get-tuple-element.26) | copy-start | bytes 196612
  49.2 4.2 %copy-start.19 = (f32[4,2,256]{2,1,0:T(2,128)S(1)}, f32[4,2,256]{2,1,0:T(2,128)}, u32[]{:S(2)}) copy-start(f32[4,2,256]{2,1,0:T(2,128)} %copy.174) | copy-start | bytes 24580
  50.3 4.2 %copy-start = (f32[4,256,256]{1,2,0:T(8,128)S(1)}, f32[4,256,256]{1,2,0:T(8,128)}, u32[]{:S(2)}) copy-start(f32[4,256,256]{1,2,0:T(8,128)} %get-tuple-element.5) | copy-start | bytes 3145732
  57.4 1.6 %copy-start.4 = (f32[2,4,256,256]{2,3,1,0:T(8,128)S(1)}, f32[2,4,256,256]{2,3,1,0:T(8,128)}, u32[]{:S(2)}) copy-start(f32[2,4,256,256]{2,3,1,0:T(8,128)} %get-tuple-element.33) | copy-start | bytes 6291460
  57.4 1.6 %copy-start.25 = (f32[4,256,2]{1,2,0:T(2,128)S(1)}, f32[4,256,2]{1,2,0:T(2,128)}, u32[]{:S(2)}) copy-start(f32[4,256,2]{1,2,0:T(2,128)} %copy.177) | copy-start | bytes 24580
  61.0 10.7 %copy-start.21 = (f32[1024]{0:T(1024)S(1)}, f32[1024]{0:T(1024)}, u32[]{:S(2)}) copy-start(f32[1024]{0:T(1024)} %get-tuple-element.48) | copy-start | bytes 12292
  61.0 10.7 %copy-start.22 = (f32[1024]{0:T(1024)S(1)}, f32[1024]{0:T(1024)}, u32[]{:S(2)}) copy-start(f32[1024]{0:T(1024)} %get-tuple-element.51) | copy-start | bytes 12292
  61.0 10.7 %copy-start.23 = (f32[1024]{0:T(1024)S(1)}, f32[1024]{0:T(1024)}, u32[]{:S(2)}) copy-start(f32[1024]{0:T(1024)} %get-tuple-element.52) | copy-start | bytes 12292
  61.0 10.7 %copy-start.27 = (f32[1,256]{1,0:T(1,128)S(1)}, f32[1,256]{1,0:T(1,128)}, u32[]{:S(2)}) copy-start(f32[1,256]{1,0:T(1,128)} %copy-done.26) | copy-start | bytes 3076
  61.0 10.7 %copy-start.29 = (f32[1,256]{1,0:T(1,128)S(1)}, f32[1,256]{1,0:T(1,128)}, u32[]{:S(2)}) copy-start(f32[1,256]{1,0:T(1,128)} %copy-done.28) | copy-start | bytes 3076
  61.1 10.7 %copy-start.31 = (f32[1,256]{1,0:T(1,128)S(1)}, f32[1,256]{1,0:T(1,128)}, u32[]{:S(2)}) copy-start(f32[1,256]{1,0:T(1,128)} %copy-done.30) | copy-start | bytes 3076
  61.1 10.7 %copy-start.33 = (f32[1,256]{1,0:T(1,128)S(1)}, f32[1,256]{1,0:T(1,128)}, u32[]{:S(2)}) copy-start(f32[1,256]{1,0:T(1,128)} %copy-done.32) | copy-start | bytes 3076
  65.5 5.6 %copy-start.1 = (f32[1024,128]{1,0:T(8,128)}, f32[1024,128]{1,0:T(8,128)S(1)}, u32[]{:S(2)}) copy-start(f32[1024,128]{1,0:T(8,128)S(1)} %multiply_multiply_fusion) | copy-start | bytes 1572868
  65.6 5.5 %collective-permute-start.1 = (f32[3,384]{1,0:T(4,128)S(1)}, f32[3,384]{1,0:T(4,128)S(1)}, u32[]{:S(2)}, u32[]{:S(2)}) collective-permute-start(f32[3,384]{1,0:T(4,128)S(1)} %pad_maximum_fusion.7), channel_id=1, source_target_pairs={{64,0},{128,64},{192,128},{65,1},{129,65},{193,129},{66,2},{130,66... | collective-permute-start | bytes 13832 | tf_op jit(solution)/shard_map/ppermute | solution.py:18
  73.0 15.2 %copy-start.5 = (f32[2,4,64,128]{3,2,0,1:T(8,128)S(1)}, f32[2,4,64,128]{3,2,0,1:T(8,128)}, u32[]{:S(2)}) copy-start(f32[2,4,64,128]{3,2,0,1:T(8,128)} %convolution_bitcast_fusion.4) | copy-start | bytes 786436
  73.9 2.1 %collective-permute-start.2 = (f32[32,16,256]{2,1,0:T(8,128)}, f32[32,16,256]{2,1,0:T(8,128)S(1)}, u32[]{:S(2)}, u32[]{:S(2)}) collective-permute-start(f32[32,16,256]{2,1,0:T(8,128)} %dynamic-slice_bitcast_fusion), channel_id=1, source_target_pairs={{0,1},{1,0},{2,3},{3,2},{4,5},{5,4},{6,7},{7,6},{8,9},{9,8},{10,11... | collective-permute-start | bytes 1572872 | tf_op jit(solution)/shard_map/ppermute | solution.py:255
  73.9 22.9 %copy-start.2 = (f32[1024,128]{1,0:T(8,128)S(1)}, f32[1024,128]{1,0:T(8,128)}, u32[]{:S(2)}) copy-start(f32[1024,128]{1,0:T(8,128)} %copy-done.1) | copy-start | bytes 1572868
  76.9 28.4 %all-to-all-start.1 = ((f32[32,16,256]{2,1,0:T(8,128)}), f32[32,16,256]{2,1,0:T(8,128)S(1)}, u32[]{:S(2)}, u32[]{:S(2)}) async-start(f32[32,16,256]{2,1,0:T(8,128)} %bitcast_add_fusion), calls=%async_computation.1 | async-start | bytes 1048576 | tf_op jit(solution)/shard_map/all_to_all | solution.py:256
  (4 other events, 4.2 us)

commit v8 on v7

--- a/solution.py
+++ b/solution.py
@@ -152,7 +152,7 @@
 
 
 def einsum(spec, *operands):
-    return jnp.einsum(spec, *operands, precision=precise, preferred_element_type=jnp.float32)
+    return jnp.einsum(spec, *operands, precision=lax.Precision.HIGH, preferred_element_type=jnp.float32)
 
 
 def block_forward_all(state, x_all, b_all, c_all, log_all, note_blocks, befores):

time: 108 us -> 104 us (0.963)
  matrix products: 22.2 us -> 17.9 us
    dot_general x11, matrix products: 18.3 us -> 14 us  [einsum(): jnp.einsum(spec, *operands, precision=lax.Precision.HIGH, preferred_eleme...]
where the time goes in v8:
time: 104 us; the launch traced here: 102 us
  local copies, waits for them, and re-layouts  24.2 us (23%)
  other arithmetic  23.5 us (23%)
  starting transfers between devices  21.3 us (20%)
  matrix products  17.9 us (17%)
  waiting for transfers between devices  12.4 us (12%)
  between operations  2.7 us (3%)
    dot_general x11, matrix products, einsum(): jnp.einsum(spec, *operands, precision=lax.Precision.HIGH, preferred_eleme...  14 us
    all_to_all x1, starting transfers between devices, local(): grad_pre_bc = lax.all_to_all(pair_sum, 'chip', 0, 0, tiled=False).sum(0)  11.3 us
    all_to_all x1, waiting for transfers between devices, local(): grad_pre_bc = lax.all_to_all(pair_sum, 'chip', 0, 0, tiled=False).sum(0)  6.69 us
    ppermute x2, starting transfers between devices, shifted(): lax.ppermute(value, axis, [(source, source + steps) for source in range(i...  5.4 us
    all_to_all x1, starting transfers between devices, chain_both(): arrived = lax.all_to_all(outgoing, axis, 0, 0, tiled=False)  4.62 us
    unnamed x97, local copies, waits for them, and re-layouts  4.53 us
    ppermute x2, waiting for transfers between devices, shifted(): lax.ppermute(value, axis, [(source, source + steps) for source in range(i...  3.59 us
    add x2, other arithmetic, conv_backward(): result + weights[k][None, :] * extended[lag:lag + count] * linked[:, None]  3.25 us
  transfers between devices with their start and end apart: 5, of which 3 were waited for; matrix products, arithmetic and copies ran while one was open for 33% of the time, Pallas kernels for 0%

profile of v8, /device:TPU:8, one launch (start us, length us, event | category | flops | bytes accessed | tf_op | source)
XLA Modules:
  0.0 102.1 jit_solution(17527868710232167612)
XLA Ops:
  0.6 0.7 slice.259
  2.1 3.5 %collective-permute-start = (bf16[3,384]{1,0:T(4,128)(2,1)S(1)}, bf16[3,384]{1,0:T(4,128)(2,1)S(1)}, u32[]{:S(2)}, u32[]{:S(2)}) collective-permute-start(bf16[3,384]{1,0:T(4,128)(2,1)S(1)} %pad_maximum_fusion.8), channel_id=1, source_target_pairs={{0,64},{64,128},{128,192},{1,65},{65,129},{129,193},{2,66},{66,130... | collective-permute-start | bytes 6920 | tf_op jit(solution)/shard_map/ppermute | solution.py:18
  5.6 0.8 reduce-window.9
  8.2 1.4 %fusion.19 = f32[2,1024]{1,0:T(2,128)S(1)} fusion(f32[2,1024]{1,0:T(2,128)} %param.11), kind=kOutput, calls=%fused_computation.30 | convolution fusion | flops 26214400 | bytes 16384 | tf_op jit(solution)/shard_map/dot_general | solution.py:128
  9.6 0.7 reshape.472
  11.6 2.0 %fusion.122 = (f32[1024]{0:T(1024)}, f32[1024]{0:T(1024)S(1)}, f32[1024]{0:T(1024)S(1)}, f32[1024]{0:T(1024)}, f32[1024]{0:T(1024)}, /*index=5*/f32[1024]{0:T(1024)S(1)}, f32[1024]{0:T(1024)S(1)}, f32[1024]{0:T(1024)S(1)}) fusion(s32[1030]{0:T(1024)S(1)} %broadcast_add_fusion, s32[]{:T(128)} %bitcast.9, s32[]{:T(128)} %bitcast.15), kind=kLoop, calls=%fused_computation.214 | loop fusion | flops 16384 | bytes 61448 | tf_op jit(solution)/shard_map/convert_element_type | solution.py:97
  13.6 0.8 slice_bitcast_fusion.7
  14.5 0.8 fusion.145
  15.3 0.7 compare_convert_fusion.4
  16.5 0.7 slice_reduce_fusion.8
  17.4 1.4 %compare_and_fusion = (pred[4,256,256]{1,2,0:T(8,128)(4,1)}, f32[4,256,256]{1,2,0:T(8,128)}) fusion(s32[4,256]{1,0:T(4,128)S(1)} %reshape.473, pred[256,256]{0,1:T(8,128)(4,1)S(1)} %iota_compare_fusion.4), kind=kLoop, calls=%fused_computation.57 | loop fusion | flops 786432 | bytes 1380352 | tf_op jit(solution)/shard_map/jvp()/and | solution.py:165
  20.7 1.3 %fusion.66 = (f32[1024,128]{1,0:T(8,128)S(1)}, f32[1024,128]{1,0:T(8,128)}) fusion(f32[1027,128]{1,0:T(8,128)S(1)} %maximum_convert_fusion.1, f32[128]{0:T(128)S(1)} %get-tuple-element.68, f32[1024]{0:T(1024)S(1)} %get-tuple-element.53, f32[128]{0:T(128)S(1)} %get-tuple-element.69, f32[1024]{0:T(1024)S(1)} %get-tuple-element.54, ...), kind=kLoop, calls=%fused_computation.101 | loop fusion | flops 1835008 | bytes 3160064 | tf_op jit(solution)/shard_map/jit(silu)/mul | solution.py:202
  22.0 1.0 copy.172
  24.1 1.2 %copy.208 = f32[4,256,2,64]{1,3,0,2:T(8,128)} copy(f32[4,256,2,64]{3,2,1,0:T(2,128)S(1)} %reshape.494) | data formatting | bytes 1048576 | tf_op jit(solution)/shard_map/transpose | solution.py:204
  25.5 1.0 %fusion.37 = (f32[1024,256]{1,0:T(8,128)S(1)}, f32[1024,256]{1,0:T(8,128)S(1)}) fusion(f32[1027,256]{1,0:T(8,128)S(1)} %maximum_convert_fusion, f32[256]{0:T(256)S(1)} %bitcast.350, f32[1024]{0:T(1024)S(1)} %get-tuple-element.53, f32[256]{0:T(256)S(1)} %bitcast.352, f32[1024]{0:T(1024)S(1)} %get-tuple-element.54, f32[256]{0:T(256)S(1)} %bitcast.348, ...), kind=kLoop, calls=%fused_computation.56 | loop fusion | flops 3670016 | bytes 6307840 | tf_op jit(solution)/shard_map/jit(silu)/mul | solution.py:203
  26.6 1.0 copy-done.3
  29.1 0.9 select_select_fusion
  30.0 4.6 %all-to-all-start = ((f32[4,2,8320]{2,1,0:T(2,128)}), f32[4,2,8320]{2,1,0:T(2,128)S(1)}, u32[]{:S(2)}, u32[]{:S(2)}) async-start(f32[4,2,8320]{2,1,0:T(2,128)} %select_select_fusion), calls=%async_computation | async-start | bytes 532480 | tf_op jit(solution)/shard_map/all_to_all | solution.py:139
  35.6 1.5 %squeeze.89 = f32[1,2,8192]{2,1,0:T(2,128)} reshape(f32[2,1,64,128]{3,2,0,1:T(8,128)} %get-tuple-element.41) | data formatting | bytes 131072 | tf_op jit(solution)/shard_map/jvp()/squeeze | solution.py:174
  39.9 4.5 %fusion.17 = (f32[2,4,256]{2,1,0:T(4,128)}, f32[2,4,256]{2,1,0:T(4,128)}, f32[4,256,256]{1,2,0:T(8,128)}, f32[2,4,256,256]{2,3,1,0:T(8,128)}) fusion(f32[4,256,256]{1,2,0:T(8,128)S(1)} %copy-done.6, f32[2,4,256]{2,1,0:T(4,128)S(1)} %bitcast.344, f32[4,256,256]{1,2,0:T(8,128)S(1)} %fusion.146, pred[4,256,256]{1,2,0:T(8,128)(4,1)S(1)} %copy-done.17, ...), kind=kOutput, calls=%fused_computation.24 | convolution fusion | flops 207351808 | bytes 6316032 | tf_op jit(solution)/shard_map/transpose(jvp(hbij,hbjp->hbip))/dot_general | solution.py:155
  44.3 1.1 %convolution_bitcast_fusion.4 = f32[2,4,64,128]{3,2,0,1:T(8,128)} fusion(f32[4,256,128,1]{2,1,3,0:T(8,128)S(1)} %bitcast.332, f32[4,2,256]{2,1,0:T(2,128)S(1)} %copy-done.18, bf16[4,256,2,64]{1,0,3,2:T(4,128)(2,1)S(1)} %reshape.474), kind=kOutput, calls=%fused_computation.27 | convolution fusion | flops 100925440 | bytes 1056768 | tf_op jit(solution)/shard_map/transpose(jvp(bin,hbpn->hbip))/dot_general | solution.py:155
  45.7 1.9 %multiply_reduce_fusion.1 = (f32[2]{0:T(128)}, f32[1,2,64,128]{3,1,2,0:T(2,128)S(1)}) fusion(f32[1,2,8192]{2,1,0:T(2,128)} %squeeze.91, f32[1,2,8192]{2,1,0:T(2,128)} %squeeze.90, f32[1,2,8192]{2,1,0:T(2,128)} %squeeze.89, f32[4,2,8320]{2,1,0:T(2,128)S(1)} %all-to-all-done, f32[2]{0:T(128)S(1)} %get-tuple-element.72, f32[2]{0:T(128)S(1)} %get-tuple-element.73, ...), kind=kLoop, calls=%fused_computation.166 | loop fusion | flops 360446 | bytes 524376 | tf_op jit(solution)/shard_map/transpose(jvp())/reduce_sum | solution.py:174
  47.6 0.7 multiply_add_fusion
  48.4 1.1 %multiply_add_fusion.3 = (f32[2,1,64,128]{3,2,0,1:T(8,128)S(1)}, f32[2,1,64,128]{3,2,0,1:T(8,128)S(1)}, f32[2,1,64,128]{3,2,0,1:T(8,128)S(1)}, f32[2,1,64,128]{3,2,0,1:T(8,128)S(1)}) fusion(f32[2,4,64,128]{3,2,0,1:T(8,128)} %convolution_bitcast_fusion.4, f32[2]{0:T(128)} %get-tuple-element.17, f32[2]{0:T(128)} %get-tuple-element.18, ...), kind=kLoop, calls=%fused_computation.170 | loop fusion | flops 212992 | bytes 720948 | tf_op jit(solution)/shard_map/transpose(jvp())/add_any | solution.py:174
  49.5 1.4 %convolution_bitcast_fusion.2 = f32[4,256,128]{2,1,0:T(8,128)S(1)} fusion(f32[4,256,2,64]{1,3,2,0:T(8,128)S(1)} %copy.184, f32[2,4,256]{2,0,1:T(2,128)} %copy-done.20, f32[2,1,64,128]{3,2,0,1:T(8,128)S(1)} %get-tuple-element.19, f32[2,1,64,128]{3,2,0,1:T(8,128)S(1)} %get-tuple-element.20, f32[2,1,64,128]{3,2,0,1:T(8,128)S(1)} %get-tuple-element.21, ...), kind=kOutput, calls=%fused_computation.20 | convolution fusion | flops 100990976 | bytes 1318912 | tf_op jit(solution)/shard_map/transpose(jvp(hbjp,bjn->hbpn))/dot_general | solution.py:155
  50.9 1.0 fusion.60
  52.6 1.0 %convolution_add_fusion = f32[4,256,128]{2,1,0:T(8,128)S(1)} fusion(f32[4,256,128]{2,1,0:T(8,128)S(1)} %convolution_bitcast_fusion.1, f32[4,256,256]{1,2,0:T(8,128)S(1)} %copy-done, f32[4,256,128]{2,1,0:T(8,128)S(1)} %bitcast.330), kind=kOutput, calls=%fused_computation.15 | convolution fusion | flops 201457664 | bytes 2621440 | tf_op jit(solution)/shard_map/transpose(jvp(bin,bjn->bij))/dot_general | solution.py:155
  54.6 1.2 %copy-done.4 = f32[2,4,256,256]{2,3,1,0:T(8,128)S(1)} copy-done((f32[2,4,256,256]{2,3,1,0:T(8,128)S(1)}, f32[2,4,256,256]{2,3,1,0:T(8,128)}, u32[]{:S(2)}) %copy-start.4) | copy-done | bytes 2097176
  55.8 1.6 %fusion.12 = f32[4,256,2,64]{1,3,2,0:T(8,128)} fusion(f32[2,4,256,256]{2,3,1,0:T(8,128)S(1)} %copy-done.4, f32[4,2,64,256]{3,2,1,0:T(8,128)S(1)} %get-tuple-element.81, bf16[2,4,256,64]{2,1,3,0:T(4,128)(2,1)S(1)} %bitcast.336, f32[4,256,2]{1,2,0:T(2,128)S(1)} %copy-done.25), kind=kOutput, calls=%fused_computation.21 | convolution fusion | flops 201588736 | bytes 3416064 | tf_op jit(solution)/shard_map/transpose(jvp(hbij,hbjp->hbip))/dot_general | solution.py:155
  57.4 1.5 %copy.205 = f32[4,256,2,64]{3,2,1,0:T(2,128)S(1)} copy(f32[4,256,2,64]{1,3,2,0:T(8,128)} %fusion.12) | data formatting | bytes 1048576 | tf_op jit(solution)/shard_map/reshape | solution.py:242
  58.9 1.4 %reshape.493 = f32[1024,128]{1,0:T(8,128)} reshape(f32[4,256,2,64]{3,2,1,0:T(2,128)S(1)} %copy.205) | data formatting | bytes 1048576 | tf_op jit(solution)/shard_map/reshape | solution.py:242
  60.3 1.4 %multiply_multiply_fusion = f32[1024,128]{1,0:T(8,128)S(1)} fusion(f32[1024,128]{1,0:T(8,128)} %reshape.493, f32[1024,128]{1,0:T(8,128)} %get-tuple-element.30), kind=kLoop, calls=%fused_computation.98 | loop fusion | flops 1048576 | bytes 1572864 | tf_op jit(solution)/shard_map/mul | solution.py:244
  61.7 1.9 %collective-permute-start.1 = (f32[3,384]{1,0:T(4,128)S(1)}, f32[3,384]{1,0:T(4,128)S(1)}, u32[]{:S(2)}, u32[]{:S(2)}) collective-permute-start(f32[3,384]{1,0:T(4,128)S(1)} %pad_maximum_fusion.7), channel_id=1, source_target_pairs={{64,0},{128,64},{192,128},{65,1},{129,65},{193,129},{66,2},{130,66... | collective-permute-start | bytes 13832 | tf_op jit(solution)/shard_map/ppermute | solution.py:18
  63.7 3.6 %collective-permute-done.1 = f32[3,384]{1,0:T(4,128)S(1)} collective-permute-done((f32[3,384]{1,0:T(4,128)S(1)}, f32[3,384]{1,0:T(4,128)S(1)}, u32[]{:S(2)}, u32[]{:S(2)}) %collective-permute-start.1) | collective-permute-done | bytes 4640 | tf_op jit(solution)/shard_map/ppermute | solution.py:18
  67.9 1.3 %fusion.25 = f32[1024,256]{1,0:T(8,128)S(1)} fusion(f32[3,256]{1,0:T(4,128)S(1)} %slice.361, f32[1024,256]{1,0:T(8,128)S(1)} %maximum_multiply_fusion, f32[1024]{0:T(1024)S(1)} %copy-done.22, f32[1024]{0:T(1024)S(1)} %copy-done.23, f32[1024]{0:T(1024)S(1)} %copy-done.21, f32[256]{0:T(256)S(1)} %bitcast.351, f32[256]{0:T(256)S(1)} %bitcast.353, ...), kind=kLoop, calls=%fused_computation.37 | loop fusion | flops 3407872 | bytes 2116608 | tf_op jit(solution)/shard_map/add | solution.py:97
  69.2 0.9 dynamic-slice_bitcast_fusion
  70.1 2.1 %collective-permute-done.2 = f32[32,16,256]{2,1,0:T(8,128)S(1)} collective-permute-done((f32[32,16,256]{2,1,0:T(8,128)}, f32[32,16,256]{2,1,0:T(8,128)S(1)}, u32[]{:S(2)}, u32[]{:S(2)}) %collective-permute-start.2) | collective-permute-done | bytes 524320 | tf_op jit(solution)/shard_map/ppermute | solution.py:255
  72.2 0.9 bitcast_add_fusion
  73.1 11.3 %all-to-all-start.1 = ((f32[32,16,256]{2,1,0:T(8,128)}), f32[32,16,256]{2,1,0:T(8,128)S(1)}, u32[]{:S(2)}, u32[]{:S(2)}) async-start(f32[32,16,256]{2,1,0:T(8,128)} %bitcast_add_fusion), calls=%async_computation.1 | async-start | bytes 1048576 | tf_op jit(solution)/shard_map/all_to_all | solution.py:256
  84.4 1.0 fusion.89
  85.4 0.8 copy.189
  86.2 0.8 fusion.101
  87.3 0.8 multiply_bitcast_fusion
  88.1 0.9 fusion.127
  89.1 1.3 %fusion.18 = f32[2,4,256]{2,0,1:T(2,128)S(1)} fusion(f32[4,256,128,1]{2,1,3,0:T(8,128)S(1)} %bitcast.334, bf16[4,256,2,64]{1,0,3,2:T(4,128)(2,1)S(1)} %reshape.474, f32[2,1,64,128]{3,2,0,1:T(8,128)} %copy-done.9, f32[2,1,64,128]{3,2,0,1:T(8,128)} %copy-done.10, f32[2,1,64,128]{3,2,0,1:T(8,128)} %copy-done.11, f32[2,1,64,128]{3,2,0,1:T(8,128)} %copy-done.12), kind=kOutput, calls=%fused_computation.25 | convolution fusion | flops 101251072 | bytes 1056768 | tf_op jit(solution)/shard_map/jvp(bin,hbpn->hbip)/dot_general | solution.py:155
  90.4 1.0 convolution_bitcast_fusion.7
  92.8 2.0 %fusion.46 = f32[1024,128]{1,0:T(8,128)} fusion(f32[3,128]{1,0:T(4,128)S(1)} %slice.353, f32[1024,128]{1,0:T(8,128)S(1)} %copy-done.2, f32[1024]{0:T(1024)} %get-tuple-element.51, f32[1024]{0:T(1024)} %get-tuple-element.52, f32[1024]{0:T(1024)S(1)} %copy-done.21, f32[128]{0:T(128)} %copy-done.44, f32[128]{0:T(128)} %copy-done.45, f32[128]{0:T(128)} %copy-done.43, ...), kind=kLoop, calls=%fused_computation.69 | loop fusion | flops 1703936 | bytes 1064448 | tf_op jit(solution)/shard_map/add | solution.py:97
  94.7 6.7 %all-to-all-done.1 = f32[32,16,256]{2,1,0:T(8,128)S(1)} async-done(((f32[32,16,256]{2,1,0:T(8,128)}), f32[32,16,256]{2,1,0:T(8,128)S(1)}, u32[]{:S(2)}, u32[]{:S(2)}) %all-to-all-start.1) | async-done | bytes 524320 | tf_op jit(solution)/shard_map/all_to_all | solution.py:256
  (156 shorter events, 16.5 us)
Async XLA Ops:
  0.6 20.0 %copy-start.15 = (bf16[1024,128]{1,0:T(8,128)(2,1)S(1)}, bf16[1024,128]{1,0:T(8,128)(2,1)}, u32[]{:S(2)}) copy-start(bf16[1024,128]{1,0:T(8,128)(2,1)} %param.7) | copy-start | bytes 786436
  0.6 19.7 %copy-start.16 = (bf16[1024,128]{1,0:T(8,128)(2,1)S(1)}, bf16[1024,128]{1,0:T(8,128)(2,1)}, u32[]{:S(2)}) copy-start(bf16[1024,128]{1,0:T(8,128)(2,1)} %param.13) | copy-start | bytes 786436
  2.1 18.6 %collective-permute-start = (bf16[3,384]{1,0:T(4,128)(2,1)S(1)}, bf16[3,384]{1,0:T(4,128)(2,1)S(1)}, u32[]{:S(2)}, u32[]{:S(2)}) collective-permute-start(bf16[3,384]{1,0:T(4,128)(2,1)S(1)} %pad_maximum_fusion.8), channel_id=1, source_target_pairs={{0,64},{64,128},{128,192},{1,65},{65,129},{129,193},{2,66},{66,130... | collective-permute-start | bytes 6920 | tf_op jit(solution)/shard_map/ppermute | solution.py:18
  14.4 7.6 %copy-start.42 = (f32[128]{0:T(128)}, f32[128]{0:T(128)S(1)}, u32[]{:S(2)}) copy-start(f32[128]{0:T(128)S(1)} %get-tuple-element.66) | copy-start | bytes 1540
  14.4 7.6 %copy-start.43 = (f32[128]{0:T(128)}, f32[128]{0:T(128)S(1)}, u32[]{:S(2)}) copy-start(f32[128]{0:T(128)S(1)} %get-tuple-element.67) | copy-start | bytes 1540
  14.4 7.6 %copy-start.44 = (f32[128]{0:T(128)}, f32[128]{0:T(128)S(1)}, u32[]{:S(2)}) copy-start(f32[128]{0:T(128)S(1)} %get-tuple-element.68) | copy-start | bytes 1540
  14.5 7.6 %copy-start.45 = (f32[128]{0:T(128)}, f32[128]{0:T(128)S(1)}, u32[]{:S(2)}) copy-start(f32[128]{0:T(128)S(1)} %get-tuple-element.69) | copy-start | bytes 1540
  15.3 10.1 %copy-start.26 = (f32[1,256]{1,0:T(1,128)}, f32[1,256]{1,0:T(1,128)S(1)}, u32[]{:S(2)}) copy-start(f32[1,256]{1,0:T(1,128)S(1)} %get-tuple-element.62) | copy-start | bytes 3076
  15.3 10.1 %copy-start.28 = (f32[1,256]{1,0:T(1,128)}, f32[1,256]{1,0:T(1,128)S(1)}, u32[]{:S(2)}) copy-start(f32[1,256]{1,0:T(1,128)S(1)} %get-tuple-element.63) | copy-start | bytes 3076
  15.3 10.1 %copy-start.30 = (f32[1,256]{1,0:T(1,128)}, f32[1,256]{1,0:T(1,128)S(1)}, u32[]{:S(2)}) copy-start(f32[1,256]{1,0:T(1,128)S(1)} %get-tuple-element.64) | copy-start | bytes 3076
  15.3 10.1 %copy-start.32 = (f32[1,256]{1,0:T(1,128)}, f32[1,256]{1,0:T(1,128)S(1)}, u32[]{:S(2)}) copy-start(f32[1,256]{1,0:T(1,128)S(1)} %get-tuple-element.65) | copy-start | bytes 3076
  16.1 6.0 %copy-start.41 = (f32[4]{0:T(128)}, f32[4]{0:T(128)S(1)}, u32[]{:S(2)}) copy-start(f32[4]{0:T(128)S(1)} %get-tuple-element.27) | copy-start | bytes 52
  16.1 4.5 %copy-start.46 = (f32[4,256]{1,0:T(4,128)}, f32[4,256]{1,0:T(4,128)S(1)}, u32[]{:S(2)}) copy-start(f32[4,256]{1,0:T(4,128)S(1)} %get-tuple-element.61) | copy-start | bytes 12292
  16.5 5.5 %copy-start.24 = (f32[2,4]{1,0:T(2,128)}, f32[2,4]{1,0:T(2,128)S(1)}, u32[]{:S(2)}) copy-start(f32[2,4]{1,0:T(2,128)S(1)} %slice_reduce_fusion) | copy-start | bytes 100
  20.3 14.3 %copy-start.20 = (f32[2,4,256]{2,0,1:T(2,128)}, f32[2,4,256]{2,0,1:T(2,128)S(1)}, u32[]{:S(2)}) copy-start(f32[2,4,256]{2,0,1:T(2,128)S(1)} %copy.185) | copy-start | bytes 24580
  23.0 2.3 %copy-start.13 = (bf16[1024,256]{1,0:T(8,128)(2,1)S(1)}, bf16[1024,256]{1,0:T(8,128)(2,1)}, u32[]{:S(2)}) copy-start(bf16[1024,256]{1,0:T(8,128)(2,1)} %param.8) | copy-start | bytes 1572868
  30.0 15.4 %all-to-all-start = ((f32[4,2,8320]{2,1,0:T(2,128)}), f32[4,2,8320]{2,1,0:T(2,128)S(1)}, u32[]{:S(2)}, u32[]{:S(2)}) async-start(f32[4,2,8320]{2,1,0:T(2,128)} %select_select_fusion), calls=%async_computation | async-start | bytes 532480 | tf_op jit(solution)/shard_map/all_to_all | solution.py:139
  38.5 1.4 %copy-start.17 = (pred[4,256,256]{1,2,0:T(8,128)(4,1)S(1)}, pred[4,256,256]{1,2,0:T(8,128)(4,1)}, u32[]{:S(2)}) copy-start(pred[4,256,256]{1,2,0:T(8,128)(4,1)} %get-tuple-element.46) | copy-start | bytes 786436
  39.9 4.5 %copy-start.18 = (f32[4,2,256]{2,1,0:T(2,128)S(1)}, f32[4,2,256]{2,1,0:T(2,128)}, u32[]{:S(2)}) copy-start(f32[4,2,256]{2,1,0:T(2,128)} %copy.174) | copy-start | bytes 24580
  45.6 6.3 %copy-start.34 = (f32[2]{0:T(128)}, f32[2]{0:T(128)S(1)}, u32[]{:S(2)}) copy-start(f32[2]{0:T(128)S(1)} %get-tuple-element.70) | copy-start | bytes 28
  45.6 6.3 %copy-start.35 = (f32[2]{0:T(128)}, f32[2]{0:T(128)S(1)}, u32[]{:S(2)}) copy-start(f32[2]{0:T(128)S(1)} %get-tuple-element.71) | copy-start | bytes 28
  45.6 6.3 %copy-start.36 = (f32[2]{0:T(128)}, f32[2]{0:T(128)S(1)}, u32[]{:S(2)}) copy-start(f32[2]{0:T(128)S(1)} %get-tuple-element.72) | copy-start | bytes 28
  45.6 6.2 %copy-start.37 = (f32[2]{0:T(128)}, f32[2]{0:T(128)S(1)}, u32[]{:S(2)}) copy-start(f32[2]{0:T(128)S(1)} %get-tuple-element.73) | copy-start | bytes 28
  45.6 6.2 %copy-start.38 = (f32[2]{0:T(128)}, f32[2]{0:T(128)S(1)}, u32[]{:S(2)}) copy-start(f32[2]{0:T(128)S(1)} %get-tuple-element.76) | copy-start | bytes 28
  45.6 6.2 %copy-start.39 = (f32[2]{0:T(128)}, f32[2]{0:T(128)S(1)}, u32[]{:S(2)}) copy-start(f32[2]{0:T(128)S(1)} %get-tuple-element.77) | copy-start | bytes 28
  45.7 6.2 %copy-start.7 = (f32[1,2,64,128]{3,1,2,0:T(2,128)}, f32[1,2,64,128]{3,1,2,0:T(2,128)S(1)}, u32[]{:S(2)}) copy-start(f32[1,2,64,128]{3,1,2,0:T(2,128)S(1)} %get-tuple-element.40) | copy-start | bytes 196612
  47.6 4.3 %copy-start.8 = (f32[1,2,64,128]{3,1,2,0:T(2,128)}, f32[1,2,64,128]{3,1,2,0:T(2,128)S(1)}, u32[]{:S(2)}) copy-start(f32[1,2,64,128]{3,1,2,0:T(2,128)S(1)} %get-tuple-element.37) | copy-start | bytes 196612
  48.3 4.2 %copy-start.9 = (f32[2,1,64,128]{3,2,0,1:T(8,128)}, f32[2,1,64,128]{3,2,0,1:T(8,128)S(1)}, u32[]{:S(2)}) copy-start(f32[2,1,64,128]{3,2,0,1:T(8,128)S(1)} %get-tuple-element.23) | copy-start | bytes 196612
  48.3 4.2 %copy-start.10 = (f32[2,1,64,128]{3,2,0,1:T(8,128)}, f32[2,1,64,128]{3,2,0,1:T(8,128)S(1)}, u32[]{:S(2)}) copy-start(f32[2,1,64,128]{3,2,0,1:T(8,128)S(1)} %get-tuple-element.24) | copy-start | bytes 196612
  48.3 4.2 %copy-start.11 = (f32[2,1,64,128]{3,2,0,1:T(8,128)}, f32[2,1,64,128]{3,2,0,1:T(8,128)S(1)}, u32[]{:S(2)}) copy-start(f32[2,1,64,128]{3,2,0,1:T(8,128)S(1)} %get-tuple-element.25) | copy-start | bytes 196612
  48.3 4.2 %copy-start.12 = (f32[2,1,64,128]{3,2,0,1:T(8,128)}, f32[2,1,64,128]{3,2,0,1:T(8,128)S(1)}, u32[]{:S(2)}) copy-start(f32[2,1,64,128]{3,2,0,1:T(8,128)S(1)} %get-tuple-element.26) | copy-start | bytes 196612
  48.4 3.6 %copy-start.19 = (f32[4,2,256]{2,1,0:T(2,128)S(1)}, f32[4,2,256]{2,1,0:T(2,128)}, u32[]{:S(2)}) copy-start(f32[4,2,256]{2,1,0:T(2,128)} %copy.174) | copy-start | bytes 24580
  49.5 3.1 %copy-start = (f32[4,256,256]{1,2,0:T(8,128)S(1)}, f32[4,256,256]{1,2,0:T(8,128)}, u32[]{:S(2)}) copy-start(f32[4,256,256]{1,2,0:T(8,128)} %get-tuple-element.5) | copy-start | bytes 3145732
  54.2 1.6 %copy-start.4 = (f32[2,4,256,256]{2,3,1,0:T(8,128)S(1)}, f32[2,4,256,256]{2,3,1,0:T(8,128)}, u32[]{:S(2)}) copy-start(f32[2,4,256,256]{2,3,1,0:T(8,128)} %get-tuple-element.33) | copy-start | bytes 6291460
  54.2 1.6 %copy-start.25 = (f32[4,256,2]{1,2,0:T(2,128)S(1)}, f32[4,256,2]{1,2,0:T(2,128)}, u32[]{:S(2)}) copy-start(f32[4,256,2]{1,2,0:T(2,128)} %copy.177) | copy-start | bytes 24580
  57.4 10.5 %copy-start.21 = (f32[1024]{0:T(1024)S(1)}, f32[1024]{0:T(1024)}, u32[]{:S(2)}) copy-start(f32[1024]{0:T(1024)} %get-tuple-element.48) | copy-start | bytes 12292
  57.4 10.5 %copy-start.22 = (f32[1024]{0:T(1024)S(1)}, f32[1024]{0:T(1024)}, u32[]{:S(2)}) copy-start(f32[1024]{0:T(1024)} %get-tuple-element.51) | copy-start | bytes 12292
  57.4 10.5 %copy-start.23 = (f32[1024]{0:T(1024)S(1)}, f32[1024]{0:T(1024)}, u32[]{:S(2)}) copy-start(f32[1024]{0:T(1024)} %get-tuple-element.52) | copy-start | bytes 12292
  57.4 10.5 %copy-start.27 = (f32[1,256]{1,0:T(1,128)S(1)}, f32[1,256]{1,0:T(1,128)}, u32[]{:S(2)}) copy-start(f32[1,256]{1,0:T(1,128)} %copy-done.26) | copy-start | bytes 3076
  57.4 10.5 %copy-start.29 = (f32[1,256]{1,0:T(1,128)S(1)}, f32[1,256]{1,0:T(1,128)}, u32[]{:S(2)}) copy-start(f32[1,256]{1,0:T(1,128)} %copy-done.28) | copy-start | bytes 3076
  57.4 10.5 %copy-start.31 = (f32[1,256]{1,0:T(1,128)S(1)}, f32[1,256]{1,0:T(1,128)}, u32[]{:S(2)}) copy-start(f32[1,256]{1,0:T(1,128)} %copy-done.30) | copy-start | bytes 3076
  57.4 10.5 %copy-start.33 = (f32[1,256]{1,0:T(1,128)S(1)}, f32[1,256]{1,0:T(1,128)}, u32[]{:S(2)}) copy-start(f32[1,256]{1,0:T(1,128)} %copy-done.32) | copy-start | bytes 3076
  61.7 5.6 %copy-start.1 = (f32[1024,128]{1,0:T(8,128)}, f32[1024,128]{1,0:T(8,128)S(1)}, u32[]{:S(2)}) copy-start(f32[1024,128]{1,0:T(8,128)S(1)} %multiply_multiply_fusion) | copy-start | bytes 1572868
  61.7 5.5 %collective-permute-start.1 = (f32[3,384]{1,0:T(4,128)S(1)}, f32[3,384]{1,0:T(4,128)S(1)}, u32[]{:S(2)}, u32[]{:S(2)}) collective-permute-start(f32[3,384]{1,0:T(4,128)S(1)} %pad_maximum_fusion.7), channel_id=1, source_target_pairs={{64,0},{128,64},{192,128},{65,1},{129,65},{193,129},{66,2},{130,66... | collective-permute-start | bytes 13832 | tf_op jit(solution)/shard_map/ppermute | solution.py:18
  69.2 15.2 %copy-start.5 = (f32[2,4,64,128]{3,2,0,1:T(8,128)S(1)}, f32[2,4,64,128]{3,2,0,1:T(8,128)}, u32[]{:S(2)}) copy-start(f32[2,4,64,128]{3,2,0,1:T(8,128)} %convolution_bitcast_fusion.4) | copy-start | bytes 786436
  70.1 2.1 %collective-permute-start.2 = (f32[32,16,256]{2,1,0:T(8,128)}, f32[32,16,256]{2,1,0:T(8,128)S(1)}, u32[]{:S(2)}, u32[]{:S(2)}) collective-permute-start(f32[32,16,256]{2,1,0:T(8,128)} %dynamic-slice_bitcast_fusion), channel_id=1, source_target_pairs={{0,1},{1,0},{2,3},{3,2},{4,5},{5,4},{6,7},{7,6},{8,9},{9,8},{10,11... | collective-permute-start | bytes 1572872 | tf_op jit(solution)/shard_map/ppermute | solution.py:255
  70.1 22.7 %copy-start.2 = (f32[1024,128]{1,0:T(8,128)S(1)}, f32[1024,128]{1,0:T(8,128)}, u32[]{:S(2)}) copy-start(f32[1024,128]{1,0:T(8,128)} %copy-done.1) | copy-start | bytes 1572868
  73.1 28.4 %all-to-all-start.1 = ((f32[32,16,256]{2,1,0:T(8,128)}), f32[32,16,256]{2,1,0:T(8,128)S(1)}, u32[]{:S(2)}, u32[]{:S(2)}) async-start(f32[32,16,256]{2,1,0:T(8,128)} %bitcast_add_fusion), calls=%async_computation.1 | async-start | bytes 1048576 | tf_op jit(solution)/shard_map/all_to_all | solution.py:256
  (4 other events, 4.2 us)

commit v9 on v6

--- a/solution.py
+++ b/solution.py
@@ -133,8 +133,31 @@
     return jnp.dot(values, upper, precision=precise, preferred_element_type=jnp.float32)
 
 
+def chain_both(state, adjoint, keep, axis):
+    count, mine = lax.axis_size(axis), lax.axis_index(axis)
+    heads, size = state.shape[0], state[0].size
+    tail = jnp.broadcast_to(keep[:, None], (heads, 128))
+    later = jnp.concatenate([state.reshape(heads, size), tail], axis=1)
+    earlier = jnp.concatenate([adjoint.reshape(heads, size), tail], axis=1)
+    targets = jnp.arange(count)[:, None, None]
+    outgoing = jnp.where(targets > mine, later[None], jnp.where(targets < mine, earlier[None], 0.0))
+    arrived = lax.all_to_all(outgoing, axis, 0, 0, tiled=False)
+    parts = arrived[:, :, :size].reshape((count,) + state.shape)
+    keeps = arrived[:, :, size]
+    totals = []
+    for order in (range(count - 1, -1, -1), range(count)):
+        total = jnp.zeros_like(state)
+        scale = jnp.ones_like(keep)
+        for source in order:
+            near = (source < mine) if order.step < 0 else (source > mine)
+            total = total + jnp.where(near, scale, 0.0)[:, None, None] * parts[source]
+            scale = jnp.where(near, scale * keeps[source], scale)
+        totals.append(total)
+    return totals[0], totals[1]
+
+
 def einsum(spec, *operands):
-    return jnp.einsum(spec, *operands, precision=precise, preferred_element_type=jnp.float32)
+    return jnp.einsum(spec, *operands, precision=lax.Precision.HIGH, preferred_element_type=jnp.float32)
 
 
 def block_forward_all(state, x_all, b_all, c_all, log_all, note_blocks, befores):
@@ -158,12 +181,12 @@
     return (output, state)
 
 
-def reduce_kernel(count, cores, pieces_ref, out_ref, landed, send_sems, recv_sems):
-    seq = lax.axis_index("seq")
-    me = lax.axis_index("chip") * cores + lax.axis_index("core")
+def reduce_kernel(count, pieces_ref, out_ref, landed, send_sems, recv_sems):
+    seq, core = lax.axis_index("seq"), lax.axis_index("core")
+    me = lax.axis_index("chip")
 
     def place(peer):
-        return (seq, peer // cores, peer % cores)
+        return (seq, peer, core)
 
     barrier = pltpu.get_barrier_semaphore()
 
@@ -205,12 +228,10 @@
     out_ref[...] = lax.fori_loop(0, count - 1, accumulate, pieces_ref[me])
 
 
-def head_reduce(partial):
-    cores = lax.axis_size("core")
-    count = lax.axis_size("chip") * cores
-    rows, columns = partial.shape[0] // count, partial.shape[1]
+def chip_reduce(pieces):
+    count, rows, columns = pieces.shape
     return pl.pallas_call(
-        functools.partial(reduce_kernel, count, cores),
+        functools.partial(reduce_kernel, count),
         out_shape=jax.ShapeDtypeStruct((rows, columns), jnp.float32),
         in_specs=[pl.BlockSpec(memory_space=pltpu.VMEM)],
         out_specs=pl.BlockSpec(memory_space=pltpu.VMEM),
@@ -220,7 +241,7 @@
             pltpu.SemaphoreType.DMA((count - 1,)),
         ],
         compiler_params=pltpu.CompilerParams(collective_id=0, has_side_effects=True),
-    )(partial.reshape(count, rows, columns))
+    )(pieces)
 
 
 def local(pre_x, pre_bc, conv_x, conv_bc, log_decay, lengths, grad_out):
@@ -276,8 +297,7 @@
         "thp,ht,tn->hpn", g_rows, entry_rows, v_bc[:, N:], precision=precise,
         preferred_element_type=jnp.float32,
     )
-    state_in = chain_in(local_state, keep, "seq", 1)
-    adjoint_in = chain_in(local_adjoint, keep, "seq", -1)
+    state_in, adjoint_in = chain_both(local_state, local_adjoint, keep, "seq")
 
     def local_forward(x_all, b_all, c_all, log_all):
         return block_forward_all(
@@ -295,7 +315,13 @@
     after_x, after_bc = after_both[:, : grad_u_x.shape[1]], after_both[:, grad_u_x.shape[1] :]
     grad_pre_x = conv_backward(jnp.concatenate([grad_u_x, after_x]), conv_x, note_all[rim_width:])
     whole_bc = conv_backward(jnp.concatenate([grad_u_bc, after_bc]), conv_bc, note_all[rim_width:])
-    grad_pre_bc = head_reduce(whole_bc)
+    chips, cores = lax.axis_size("chip"), lax.axis_size("core")
+    pieces = whole_bc.reshape(chips, cores, tok_rows // (chips * cores), whole_bc.shape[1])
+    core = lax.axis_index("core")
+    mine = lax.dynamic_index_in_dim(pieces, core, 1, keepdims=False)
+    other = lax.dynamic_index_in_dim(pieces, 1 - core, 1, keepdims=False)
+    pair_sum = mine + lax.ppermute(other, "core", [(0, 1), (1, 0)])
+    grad_pre_bc = chip_reduce(pair_sum)
     return (grad_pre_x, grad_pre_bc, grad_log_decay)
 
 

time: 131 us -> 111 us (0.85)
  the two profiles are of different devices: /device:TPU:1 before, /device:TPU:8 now
where the time goes in v9:
time: 111 us; the launch traced here: 110 us
  local copies, waits for them, and re-layouts  26.4 us (24%)
  Pallas kernels  25.7 us (23%)
  other arithmetic  24.8 us (22%)
  matrix products  18.4 us (17%)
  starting transfers between devices  10.1 us (9%)
  between operations  2.7 us (2%)
  waiting for transfers between devices  1.76 us (2%)
    pallas_call x1, Pallas kernels, chip_reduce(): pl.pallas_call(functools.partial(reduce_kernel, count), out_shape=jax.Sha...  25.7 us
    dot_general x11, matrix products, einsum(): jnp.einsum(spec, *operands, precision=lax.Precision.HIGH, preferred_eleme...  15.3 us
    ppermute x2, starting transfers between devices, shifted(): lax.ppermute(value, axis, [(source, source + steps) for source in range(i...  5.39 us
    broadcast_in_dim x4, local copies, waits for them, and re-layouts, block_forward_all(): state = through[:, block, None, None] * state + chunk[:, block]  5.31 us
    unnamed x100, local copies, waits for them, and re-layouts  4.85 us
    all_to_all x1, starting transfers between devices, chain_both(): arrived = lax.all_to_all(outgoing, axis, 0, 0, tiled=False)  4.62 us
    reduce_sum x2, other arithmetic, block_forward_all(): state = through[:, block, None, None] * state + chunk[:, block]  3.59 us
    add x2, other arithmetic, conv_backward(): result + weights[k][None, :] * extended[lag:lag + count] * linked[:, None]  3.42 us
  transfers between devices with their start and end apart: 4, of which 1 were waited for; matrix products, arithmetic and copies ran while one was open for 26% of the time, Pallas kernels for 0%

profile of v9, /device:TPU:8, one launch (start us, length us, event | category | flops | bytes accessed | tf_op | source)
XLA Modules:
  0.0 109.8 jit_solution(13884427344322128938)
XLA Ops:
  0.6 0.7 slice.259
  1.4 0.7 slice.260
  2.1 3.5 %collective-permute-start = (bf16[3,384]{1,0:T(4,128)(2,1)S(1)}, bf16[3,384]{1,0:T(4,128)(2,1)S(1)}, u32[]{:S(2)}, u32[]{:S(2)}) collective-permute-start(bf16[3,384]{1,0:T(4,128)(2,1)S(1)} %pad_maximum_fusion.8), channel_id=1, source_target_pairs={{0,64},{64,128},{128,192},{1,65},{65,129},{129,193},{2,66},{66,130... | collective-permute-start | bytes 6920 | tf_op jit(solution)/shard_map/ppermute | solution.py:23
  5.6 0.8 reduce-window.9
  8.2 1.4 %fusion.19 = f32[2,1024]{1,0:T(2,128)S(1)} fusion(f32[2,1024]{1,0:T(2,128)} %param.11), kind=kOutput, calls=%fused_computation.30 | convolution fusion | flops 26214400 | bytes 16384 | tf_op jit(solution)/shard_map/dot_general | solution.py:133
  9.6 0.7 reshape.472
  11.6 2.0 %fusion.122 = (f32[1024]{0:T(1024)}, f32[1024]{0:T(1024)S(1)}, f32[1024]{0:T(1024)S(1)}, f32[1024]{0:T(1024)}, f32[1024]{0:T(1024)}, /*index=5*/f32[1024]{0:T(1024)S(1)}, f32[1024]{0:T(1024)S(1)}, f32[1024]{0:T(1024)S(1)}) fusion(s32[1030]{0:T(1024)S(1)} %broadcast_add_fusion, s32[]{:T(128)} %bitcast.9, s32[]{:T(128)} %bitcast.15), kind=kLoop, calls=%fused_computation.214 | loop fusion | flops 16384 | bytes 61448 | tf_op jit(solution)/shard_map/convert_element_type | solution.py:102
  13.6 0.8 slice_bitcast_fusion.7
  14.5 0.8 fusion.145
  15.3 0.7 compare_convert_fusion.4
  16.5 0.8 slice_reduce_fusion.8
  17.4 1.4 %compare_and_fusion = (pred[4,256,256]{1,2,0:T(8,128)(4,1)}, f32[4,256,256]{1,2,0:T(8,128)}) fusion(s32[4,256]{1,0:T(4,128)S(1)} %reshape.473, pred[256,256]{0,1:T(8,128)(4,1)S(1)} %iota_compare_fusion.4), kind=kLoop, calls=%fused_computation.57 | loop fusion | flops 786432 | bytes 1380352 | tf_op jit(solution)/shard_map/jvp()/and | solution.py:170
  20.8 1.3 %fusion.66 = (f32[1024,128]{1,0:T(8,128)S(1)}, f32[1024,128]{1,0:T(8,128)}) fusion(f32[1027,128]{1,0:T(8,128)S(1)} %maximum_convert_fusion.1, f32[128]{0:T(128)S(1)} %get-tuple-element.68, f32[1024]{0:T(1024)S(1)} %get-tuple-element.53, f32[128]{0:T(128)S(1)} %get-tuple-element.69, f32[1024]{0:T(1024)S(1)} %get-tuple-element.54, ...), kind=kLoop, calls=%fused_computation.101 | loop fusion | flops 1835008 | bytes 3160064 | tf_op jit(solution)/shard_map/jit(silu)/mul | solution.py:270
  22.1 1.0 copy.182
  24.2 1.2 %copy.220 = f32[4,256,2,64]{1,3,0,2:T(8,128)} copy(f32[4,256,2,64]{3,2,1,0:T(2,128)S(1)} %reshape.494) | data formatting | bytes 1048576 | tf_op jit(solution)/shard_map/transpose | solution.py:272
  25.5 1.0 fusion.37
  26.6 1.0 copy-done.4
  29.2 0.9 select_select_fusion
  30.1 4.6 %all-to-all-start = ((f32[4,2,8320]{2,1,0:T(2,128)}), f32[4,2,8320]{2,1,0:T(2,128)S(1)}, u32[]{:S(2)}, u32[]{:S(2)}) async-start(f32[4,2,8320]{2,1,0:T(2,128)} %select_select_fusion), calls=%async_computation | async-start | bytes 532480 | tf_op jit(solution)/shard_map/all_to_all | solution.py:144
  35.1 0.7 fusion.143
  35.8 1.5 %squeeze.89 = f32[1,2,8192]{2,1,0:T(2,128)} reshape(f32[2,1,64,128]{3,2,0,1:T(8,128)} %get-tuple-element.41) | data formatting | bytes 131072 | tf_op jit(solution)/shard_map/jvp()/squeeze | solution.py:179
  40.0 4.5 %fusion.17 = (f32[2,4,256]{2,1,0:T(4,128)}, f32[2,4,256]{2,1,0:T(4,128)}, f32[4,256,256]{1,2,0:T(8,128)}, f32[2,4,256,256]{2,3,1,0:T(8,128)}) fusion(f32[4,256,256]{1,2,0:T(8,128)S(1)} %copy-done.7, f32[2,4,256]{2,1,0:T(4,128)S(1)} %bitcast.348, f32[4,256,256]{1,2,0:T(8,128)S(1)} %fusion.146, pred[4,256,256]{1,2,0:T(8,128)(4,1)S(1)} %copy-done.14, ...), kind=kOutput, calls=%fused_computation.24 | convolution fusion | flops 207351808 | bytes 6316032 | tf_op jit(solution)/shard_map/transpose(jvp(hbij,hbjp->hbip))/dot_general | solution.py:160
  44.5 1.1 %convolution_bitcast_fusion.4 = f32[2,4,64,128]{3,2,0,1:T(8,128)} fusion(f32[4,256,128,1]{2,1,3,0:T(8,128)S(1)} %bitcast.336, f32[4,2,256]{2,1,0:T(2,128)S(1)} %copy-done.17, bf16[4,256,2,64]{1,0,3,2:T(4,128)(2,1)S(1)} %reshape.474), kind=kOutput, calls=%fused_computation.27 | convolution fusion | flops 100925440 | bytes 1056768 | tf_op jit(solution)/shard_map/transpose(jvp(bin,hbpn->hbip))/dot_general | solution.py:160
  45.9 1.8 %multiply_reduce_fusion.1 = (f32[2]{0:T(128)}, f32[1,2,64,128]{3,1,2,0:T(2,128)S(1)}) fusion(f32[1,2,8192]{2,1,0:T(2,128)S(1)} %copy-done.16, f32[1,2,8192]{2,1,0:T(2,128)} %squeeze.90, f32[1,2,8192]{2,1,0:T(2,128)S(1)} %copy-done.15, f32[4,2,8320]{2,1,0:T(2,128)S(1)} %all-to-all-done, f32[2]{0:T(128)S(1)} %get-tuple-element.72, ...), kind=kLoop, calls=%fused_computation.166 | loop fusion | flops 360446 | bytes 524376 | tf_op jit(solution)/shard_map/transpose(jvp())/reduce_sum | solution.py:179
  47.7 1.4 %multiply_add_fusion = (f32[2,1,64,128]{3,2,0,1:T(8,128)S(1)}, f32[2,1,64,128]{3,2,0,1:T(8,128)S(1)}, f32[2,1,64,128]{3,2,0,1:T(8,128)}, f32[2,1,64,128]{3,2,0,1:T(8,128)}) fusion(f32[2]{0:T(128)} %get-tuple-element.18, f32[2,4,64,128]{3,2,0,1:T(8,128)S(1)} %convolution_bitcast_fusion.3, f32[2]{0:T(128)} %get-tuple-element.17, f32[2]{0:T(128)} %get-tuple-element.16, ...), kind=kLoop, calls=%fused_computation.167 | loop fusion | flops 212992 | bytes 720948 | tf_op jit(solution)/shard_map/jvp()/add | solution.py:179
  49.1 1.6 %fusion.89 = (f32[2,64,128]{2,1,0:T(8,128)}, f32[2,64,128]{2,1,0:T(8,128)}) fusion(f32[1,2,64,128]{3,1,2,0:T(2,128)S(1)} %get-tuple-element.38, f32[1,2,64,128]{3,1,2,0:T(2,128)S(1)} %get-tuple-element.37, f32[1,2,64,128]{3,1,2,0:T(2,128)S(1)} %get-tuple-element.39, f32[1,2,64,128]{3,1,2,0:T(2,128)S(1)} %get-tuple-element.40, f32[2]{0:T(128)S(1)} %get-tuple-element.72, ...), kind=kLoop, calls=%fused_computation.132 | loop fusion | flops 262144 | bytes 458816 | tf_op jit(solution)/shard_map/add | solution.py:153
  50.9 1.4 %convolution_bitcast_fusion.2 = f32[4,256,128]{2,1,0:T(8,128)} fusion(f32[4,256,2,64]{1,3,2,0:T(8,128)S(1)} %copy.194, f32[2,4,256]{2,0,1:T(2,128)S(1)} %copy-done.19, f32[2,1,64,128]{3,2,0,1:T(8,128)S(1)} %get-tuple-element.19, f32[2,1,64,128]{3,2,0,1:T(8,128)S(1)} %get-tuple-element.20, f32[2,1,64,128]{3,2,0,1:T(8,128)S(1)} %get-tuple-element.21, ...), kind=kOutput, calls=%fused_computation.20 | convolution fusion | flops 100990976 | bytes 1318912 | tf_op jit(solution)/shard_map/transpose(jvp(hbjp,bjn->hbpn))/dot_general | solution.py:160
  52.3 1.8 %fusion.60 = (f32[2,4,256]{2,0,1:T(2,128)}, f32[4,2,64,256]{3,2,1,0:T(8,128)}) fusion(f32[4,256,2,64]{1,3,2,0:T(8,128)S(1)} %copy.194, f32[4,256,128,1]{2,1,3,0:T(8,128)S(1)} %bitcast.333, f32[2,1,64,128]{3,2,0,1:T(8,128)S(1)} %get-tuple-element.19, f32[2,1,64,128]{3,2,0,1:T(8,128)S(1)} %get-tuple-element.20, f32[2,1,64,128]{3,2,0,1:T(8,128)S(1)} %get-tuple-element.21, ...), kind=kOutput, calls=%fused_computation.90 | convolution fusion | flops 101120000 | bytes 1843200 | tf_op jit(solution)/shard_map/transpose(jvp(hbjp,bjn->hbpn))/dot_general | solution.py:160
  54.1 1.4 %copy.201 = f32[2,1]{1,0:T(2,128)} copy(f32[2,1]{0,1:T(1,128)} %bitcast.363) | data formatting | bytes 16 | tf_op jit(solution)/shard_map/transpose(jvp())/broadcast_in_dim | solution.py:179
  55.5 1.8 %fusion.101 = (f32[2]{0:T(128)}, f32[2]{0:T(128)}, f32[2]{0:T(128)}) fusion(f32[2,64,128]{2,1,0:T(8,128)} %get-tuple-element.45, f32[2]{0:T(128)S(1)} %copy-done.28, f32[2,64,128]{2,1,0:T(8,128)} %get-tuple-element.44, f32[2]{0:T(128)} %get-tuple-element.16, f32[2,4,64,128]{3,2,0,1:T(8,128)} %copy-done.1, f32[2]{0:T(128)} %get-tuple-element.18, ...), kind=kLoop, calls=%fused_computation.163 | loop fusion | flops 229370 | bytes 393264 | tf_op jit(solution)/shard_map/transpose(jvp())/reduce_sum | solution.py:179
  57.3 1.3 %copy.203 = f32[2,1]{1,0:T(2,128)} copy(f32[2,1]{0,1:T(1,128)} %bitcast.362) | data formatting | bytes 16 | tf_op jit(solution)/shard_map/transpose(jvp())/broadcast_in_dim | solution.py:179
  58.5 1.3 %copy.202 = f32[2,1]{1,0:T(2,128)} copy(f32[2,1]{0,1:T(1,128)} %bitcast.361) | data formatting | bytes 16 | tf_op jit(solution)/shard_map/transpose(jvp())/broadcast_in_dim | solution.py:179
  59.8 1.3 %copy.204 = f32[2,1]{1,0:T(2,128)} copy(f32[2,1]{0,1:T(1,128)} %bitcast.360) | data formatting | bytes 16 | tf_op jit(solution)/shard_map/transpose(jvp())/broadcast_in_dim | solution.py:179
  61.1 1.5 %convolution_bitcast_fusion.1 = f32[4,256,128]{2,1,0:T(8,128)S(1)} fusion(f32[4,2,256]{2,1,0:T(2,128)} %copy.184, bf16[4,256,2,64]{1,0,3,2:T(4,128)(2,1)S(1)} %reshape.474, f32[2,1,64,128]{3,2,0,1:T(8,128)S(1)} %get-tuple-element.23, f32[2,1,64,128]{3,2,0,1:T(8,128)S(1)} %get-tuple-element.24, f32[2,1,64,128]{3,2,0,1:T(8,128)} %get-tuple-element.25, ...), kind=kOutput, calls=%fused_computation.19 | convolution fusion | flops 101122048 | bytes 1056768 | tf_op jit(solution)/shard_map/transpose(jvp(bin,hbpn->hbip))/dot_general | solution.py:160
  62.7 2.3 %convolution_add_fusion = f32[4,256,128]{2,1,0:T(8,128)S(1)} fusion(f32[4,256,128]{2,1,0:T(8,128)S(1)} %convolution_bitcast_fusion.1, f32[4,256,256]{1,2,0:T(8,128)} %get-tuple-element.5, f32[4,256,128]{2,1,0:T(8,128)S(1)} %bitcast.334), kind=kOutput, calls=%fused_computation.15 | convolution fusion | flops 201457664 | bytes 2621440 | tf_op jit(solution)/shard_map/transpose(jvp(bin,bjn->bij))/dot_general | solution.py:160
  66.6 0.7 copy-done.5
  67.4 0.8 fusion.12
  69.3 1.3 %multiply_multiply_fusion = f32[1024,128]{1,0:T(8,128)S(1)} fusion(f32[1024,128]{1,0:T(8,128)S(1)} %reshape.493, f32[1024,128]{1,0:T(8,128)} %get-tuple-element.30), kind=kLoop, calls=%fused_computation.98 | loop fusion | flops 1048576 | bytes 1572864 | tf_op jit(solution)/shard_map/mul | solution.py:312
  70.6 0.7 pad_maximum_fusion.7
  71.3 1.9 %collective-permute-start.1 = (f32[3,384]{1,0:T(4,128)S(1)}, f32[3,384]{1,0:T(4,128)S(1)}, u32[]{:S(2)}, u32[]{:S(2)}) collective-permute-start(f32[3,384]{1,0:T(4,128)S(1)} %pad_maximum_fusion.7), channel_id=1, source_target_pairs={{64,0},{128,64},{192,128},{65,1},{129,65},{193,129},{66,2},{130,66... | collective-permute-start | bytes 13832 | tf_op jit(solution)/shard_map/ppermute | solution.py:23
  73.2 0.8 multiply_bitcast_fusion
  74.0 0.9 fusion.127
  75.1 1.8 %collective-permute-done.1 = f32[3,384]{1,0:T(4,128)S(1)} collective-permute-done((f32[3,384]{1,0:T(4,128)S(1)}, f32[3,384]{1,0:T(4,128)S(1)}, u32[]{:S(2)}, u32[]{:S(2)}) %collective-permute-start.1) | collective-permute-done | bytes 4640 | tf_op jit(solution)/shard_map/ppermute | solution.py:23
  76.9 2.1 %fusion.25 = f32[1024,256]{1,0:T(8,128)S(1)} fusion(f32[3,256]{1,0:T(4,128)S(1)} %slice.361, f32[1024,256]{1,0:T(8,128)S(1)} %maximum_multiply_fusion, f32[1024]{0:T(1024)} %get-tuple-element.51, f32[1024]{0:T(1024)} %get-tuple-element.52, f32[1024]{0:T(1024)S(1)} %copy-done.20, f32[256]{0:T(256)} %bitcast.355, f32[256]{0:T(256)} %bitcast.357, ...), kind=kLoop, calls=%fused_computation.37 | loop fusion | flops 3407872 | bytes 2116608 | tf_op jit(solution)/shard_map/add | solution.py:102
  80.6 1.3 %fusion.46 = f32[1024,128]{1,0:T(8,128)} fusion(f32[3,128]{1,0:T(4,128)S(1)} %slice.353, f32[1024,128]{1,0:T(8,128)S(1)} %multiply_multiply_fusion, f32[1024]{0:T(1024)S(1)} %copy-done.21, f32[1024]{0:T(1024)S(1)} %copy-done.22, f32[1024]{0:T(1024)S(1)} %copy-done.20, f32[128]{0:T(128)S(1)} %copy-done.41, f32[128]{0:T(128)S(1)} %copy-done.43, ...), kind=kLoop, calls=%fused_computation.69 | loop fusion | flops 1703936 | bytes 1064448 | tf_op jit(solution)/shard_map/add | solution.py:102
  81.9 0.9 bitcast_add_fusion.pieces_ref
  82.8 25.7 %shard_map.94 = f32[16,256]{1,0:T(8,128)} custom-call(f32[32,16,256]{2,1,0:T(8,128)} %bitcast_add_fusion.pieces_ref), custom_call_target="tpu_custom_call" | custom-call | tf_op jit(solution)/shard_map/pallas_call | solution.py:233
  108.5 1.3 %copy.297 = f32[16,256]{1,0:T(8,128)} copy(f32[16,256]{1,0:T(8,128)} %shard_map.94) | data formatting | bytes 32768
  (157 shorter events, 15.1 us)
Async XLA Ops:
  0.6 20.1 %copy-start.12 = (bf16[1024,128]{1,0:T(8,128)(2,1)S(1)}, bf16[1024,128]{1,0:T(8,128)(2,1)}, u32[]{:S(2)}) copy-start(bf16[1024,128]{1,0:T(8,128)(2,1)} %param.7) | copy-start | bytes 786436
  0.6 19.7 %copy-start.13 = (bf16[1024,128]{1,0:T(8,128)(2,1)S(1)}, bf16[1024,128]{1,0:T(8,128)(2,1)}, u32[]{:S(2)}) copy-start(bf16[1024,128]{1,0:T(8,128)(2,1)} %param.13) | copy-start | bytes 786436
  2.1 18.6 %collective-permute-start = (bf16[3,384]{1,0:T(4,128)(2,1)S(1)}, bf16[3,384]{1,0:T(4,128)(2,1)S(1)}, u32[]{:S(2)}, u32[]{:S(2)}) collective-permute-start(bf16[3,384]{1,0:T(4,128)(2,1)S(1)} %pad_maximum_fusion.8), channel_id=1, source_target_pairs={{0,64},{64,128},{128,192},{1,65},{65,129},{129,193},{2,66},{66,130... | collective-permute-start | bytes 6920 | tf_op jit(solution)/shard_map/ppermute | solution.py:23
  14.4 7.6 %copy-start.36 = (f32[128]{0:T(128)}, f32[128]{0:T(128)S(1)}, u32[]{:S(2)}) copy-start(f32[128]{0:T(128)S(1)} %get-tuple-element.66) | copy-start | bytes 1540
  14.4 7.6 %copy-start.38 = (f32[128]{0:T(128)}, f32[128]{0:T(128)S(1)}, u32[]{:S(2)}) copy-start(f32[128]{0:T(128)S(1)} %get-tuple-element.67) | copy-start | bytes 1540
  14.4 7.6 %copy-start.40 = (f32[128]{0:T(128)}, f32[128]{0:T(128)S(1)}, u32[]{:S(2)}) copy-start(f32[128]{0:T(128)S(1)} %get-tuple-element.68) | copy-start | bytes 1540
  14.4 7.6 %copy-start.42 = (f32[128]{0:T(128)}, f32[128]{0:T(128)S(1)}, u32[]{:S(2)}) copy-start(f32[128]{0:T(128)S(1)} %get-tuple-element.69) | copy-start | bytes 1540
  15.3 10.2 %copy-start.30 = (f32[1,256]{1,0:T(1,128)}, f32[1,256]{1,0:T(1,128)S(1)}, u32[]{:S(2)}) copy-start(f32[1,256]{1,0:T(1,128)S(1)} %get-tuple-element.62) | copy-start | bytes 3076
  15.3 10.2 %copy-start.31 = (f32[1,256]{1,0:T(1,128)}, f32[1,256]{1,0:T(1,128)S(1)}, u32[]{:S(2)}) copy-start(f32[1,256]{1,0:T(1,128)S(1)} %get-tuple-element.63) | copy-start | bytes 3076
  15.3 10.2 %copy-start.32 = (f32[1,256]{1,0:T(1,128)}, f32[1,256]{1,0:T(1,128)S(1)}, u32[]{:S(2)}) copy-start(f32[1,256]{1,0:T(1,128)S(1)} %get-tuple-element.64) | copy-start | bytes 3076
  15.3 10.2 %copy-start.33 = (f32[1,256]{1,0:T(1,128)}, f32[1,256]{1,0:T(1,128)S(1)}, u32[]{:S(2)}) copy-start(f32[1,256]{1,0:T(1,128)S(1)} %get-tuple-element.65) | copy-start | bytes 3076
  16.1 6.0 %copy-start.34 = (f32[4]{0:T(128)}, f32[4]{0:T(128)S(1)}, u32[]{:S(2)}) copy-start(f32[4]{0:T(128)S(1)} %get-tuple-element.27) | copy-start | bytes 52
  16.1 4.6 %copy-start.44 = (f32[4,256]{1,0:T(4,128)}, f32[4,256]{1,0:T(4,128)S(1)}, u32[]{:S(2)}) copy-start(f32[4,256]{1,0:T(4,128)S(1)} %get-tuple-element.61) | copy-start | bytes 12292
  16.5 5.6 %copy-start.23 = (f32[2,4]{1,0:T(2,128)}, f32[2,4]{1,0:T(2,128)S(1)}, u32[]{:S(2)}) copy-start(f32[2,4]{1,0:T(2,128)S(1)} %slice_reduce_fusion) | copy-start | bytes 100
  20.3 14.3 %copy-start.18 = (f32[2,4,256]{2,0,1:T(2,128)}, f32[2,4,256]{2,0,1:T(2,128)S(1)}, u32[]{:S(2)}) copy-start(f32[2,4,256]{2,0,1:T(2,128)S(1)} %copy.195) | copy-start | bytes 24580
  23.1 2.3 %copy-start.10 = (bf16[1024,256]{1,0:T(8,128)(2,1)S(1)}, bf16[1024,256]{1,0:T(8,128)(2,1)}, u32[]{:S(2)}) copy-start(bf16[1024,256]{1,0:T(8,128)(2,1)} %param.8) | copy-start | bytes 1572868
  30.1 15.6 %all-to-all-start = ((f32[4,2,8320]{2,1,0:T(2,128)}), f32[4,2,8320]{2,1,0:T(2,128)S(1)}, u32[]{:S(2)}, u32[]{:S(2)}) async-start(f32[4,2,8320]{2,1,0:T(2,128)} %select_select_fusion), calls=%async_computation | async-start | bytes 532480 | tf_op jit(solution)/shard_map/all_to_all | solution.py:144
  35.1 12.6 %copy-start.1 = (f32[2,4,64,128]{3,2,0,1:T(8,128)}, f32[2,4,64,128]{3,2,0,1:T(8,128)S(1)}, u32[]{:S(2)}) copy-start(f32[2,4,64,128]{3,2,0,1:T(8,128)S(1)} %convolution_bitcast_fusion.3) | copy-start | bytes 786436
  38.6 1.4 %copy-start.14 = (pred[4,256,256]{1,2,0:T(8,128)(4,1)S(1)}, pred[4,256,256]{1,2,0:T(8,128)(4,1)}, u32[]{:S(2)}) copy-start(pred[4,256,256]{1,2,0:T(8,128)(4,1)} %get-tuple-element.46) | copy-start | bytes 786436
  40.0 4.5 %copy-start.17 = (f32[4,2,256]{2,1,0:T(2,128)S(1)}, f32[4,2,256]{2,1,0:T(2,128)}, u32[]{:S(2)}) copy-start(f32[4,2,256]{2,1,0:T(2,128)} %copy.184) | copy-start | bytes 24580
  40.0 5.8 %copy-start.15 = (f32[1,2,8192]{2,1,0:T(2,128)S(1)}, f32[1,2,8192]{2,1,0:T(2,128)}, u32[]{:S(2)}) copy-start(f32[1,2,8192]{2,1,0:T(2,128)} %squeeze.89) | copy-start | bytes 196612
  40.0 5.8 %copy-start.16 = (f32[1,2,8192]{2,1,0:T(2,128)S(1)}, f32[1,2,8192]{2,1,0:T(2,128)}, u32[]{:S(2)}) copy-start(f32[1,2,8192]{2,1,0:T(2,128)} %squeeze.91) | copy-start | bytes 196612
  45.6 5.1 %copy-start.6 = (f32[2,4,64,128]{3,2,0,1:T(8,128)S(1)}, f32[2,4,64,128]{3,2,0,1:T(8,128)}, u32[]{:S(2)}) copy-start(f32[2,4,64,128]{3,2,0,1:T(8,128)} %convolution_bitcast_fusion.4) | copy-start | bytes 786436
  45.6 5.1 %copy-start.27 = (f32[2]{0:T(128)S(1)}, f32[2]{0:T(128)}, u32[]{:S(2)}) copy-start(f32[2]{0:T(128)} %get-tuple-element.17) | copy-start | bytes 28
  45.6 5.1 %copy-start.29 = (f32[2]{0:T(128)S(1)}, f32[2]{0:T(128)}, u32[]{:S(2)}) copy-start(f32[2]{0:T(128)} %get-tuple-element.18) | copy-start | bytes 28
  45.6 5.1 %copy-start.35 = (f32[2]{0:T(128)S(1)}, f32[2]{0:T(128)}, u32[]{:S(2)}) copy-start(f32[2]{0:T(128)} %get-tuple-element.15) | copy-start | bytes 28
  45.6 5.2 %copy-start.19 = (f32[2,4,256]{2,0,1:T(2,128)S(1)}, f32[2,4,256]{2,0,1:T(2,128)}, u32[]{:S(2)}) copy-start(f32[2,4,256]{2,0,1:T(2,128)} %copy-done.18) | copy-start | bytes 24580
  49.1 6.4 %copy-start.28 = (f32[2]{0:T(128)S(1)}, f32[2]{0:T(128)}, u32[]{:S(2)}) copy-start(f32[2]{0:T(128)} %get-tuple-element.17) | copy-start | bytes 28
  54.1 10.9 %copy-start = (f32[4,256,256]{1,2,0:T(8,128)S(1)}, f32[4,256,256]{1,2,0:T(8,128)}, u32[]{:S(2)}) copy-start(f32[4,256,256]{1,2,0:T(8,128)} %get-tuple-element.5) | copy-start | bytes 3145732
  61.1 3.8 %copy-start.2 = (f32[4,256,128]{2,1,0:T(8,128)S(1)}, f32[4,256,128]{2,1,0:T(8,128)}, u32[]{:S(2)}) copy-start(f32[4,256,128]{2,1,0:T(8,128)} %convolution_bitcast_fusion.2) | copy-start | bytes 1572868
  65.6 1.8 %copy-start.5 = (f32[2,4,256,256]{2,3,1,0:T(8,128)S(1)}, f32[2,4,256,256]{2,3,1,0:T(8,128)}, u32[]{:S(2)}) copy-start(f32[2,4,256,256]{2,3,1,0:T(8,128)} %get-tuple-element.33) | copy-start | bytes 6291460
  65.6 1.8 %copy-start.25 = (f32[4,256,2]{1,2,0:T(2,128)S(1)}, f32[4,256,2]{1,2,0:T(2,128)}, u32[]{:S(2)}) copy-start(f32[4,256,2]{1,2,0:T(2,128)} %copy.187) | copy-start | bytes 24580
  68.1 8.7 %copy-start.20 = (f32[1024]{0:T(1024)S(1)}, f32[1024]{0:T(1024)}, u32[]{:S(2)}) copy-start(f32[1024]{0:T(1024)} %get-tuple-element.48) | copy-start | bytes 12292
  69.3 9.9 %copy-start.8 = (f32[2,1,64,128]{3,2,0,1:T(8,128)S(1)}, f32[2,1,64,128]{3,2,0,1:T(8,128)}, u32[]{:S(2)}) copy-start(f32[2,1,64,128]{3,2,0,1:T(8,128)} %get-tuple-element.25) | copy-start | bytes 196612
  69.3 9.9 %copy-start.9 = (f32[2,1,64,128]{3,2,0,1:T(8,128)S(1)}, f32[2,1,64,128]{3,2,0,1:T(8,128)}, u32[]{:S(2)}) copy-start(f32[2,1,64,128]{3,2,0,1:T(8,128)} %get-tuple-element.26) | copy-start | bytes 196612
  71.3 5.5 %collective-permute-start.1 = (f32[3,384]{1,0:T(4,128)S(1)}, f32[3,384]{1,0:T(4,128)S(1)}, u32[]{:S(2)}, u32[]{:S(2)}) collective-permute-start(f32[3,384]{1,0:T(4,128)S(1)} %pad_maximum_fusion.7), channel_id=1, source_target_pairs={{64,0},{128,64},{192,128},{65,1},{129,65},{193,129},{66,2},{130,66... | collective-permute-start | bytes 13832 | tf_op jit(solution)/shard_map/ppermute | solution.py:23
  76.8 2.9 %copy-start.24 = (f32[2,4]{1,0:T(2,128)S(1)}, f32[2,4]{1,0:T(2,128)}, u32[]{:S(2)}) copy-start(f32[2,4]{1,0:T(2,128)} %copy-done.23) | copy-start | bytes 100
  76.8 2.9 %copy-start.26 = (f32[2,4,256]{2,0,1:T(2,128)S(1)}, f32[2,4,256]{2,0,1:T(2,128)}, u32[]{:S(2)}) copy-start(f32[2,4,256]{2,0,1:T(2,128)} %get-tuple-element.80) | copy-start | bytes 24580
  76.8 2.9 %copy-start.45 = (f32[4,256]{1,0:T(4,128)S(1)}, f32[4,256]{1,0:T(4,128)}, u32[]{:S(2)}) copy-start(f32[4,256]{1,0:T(4,128)} %copy-done.44) | copy-start | bytes 12292
  76.8 2.9 %copy-start.46 = (f32[2,4,256]{2,1,0:T(4,128)S(1)}, f32[2,4,256]{2,1,0:T(4,128)}, u32[]{:S(2)}) copy-start(f32[2,4,256]{2,1,0:T(4,128)} %get-tuple-element.3) | copy-start | bytes 24580
  76.8 2.9 %copy-start.47 = (f32[2,4,256]{2,1,0:T(4,128)S(1)}, f32[2,4,256]{2,1,0:T(4,128)}, u32[]{:S(2)}) copy-start(f32[2,4,256]{2,1,0:T(4,128)} %get-tuple-element.4) | copy-start | bytes 24580
  76.9 3.8 %copy-start.21 = (f32[1024]{0:T(1024)S(1)}, f32[1024]{0:T(1024)}, u32[]{:S(2)}) copy-start(f32[1024]{0:T(1024)} %get-tuple-element.51) | copy-start | bytes 12292
  76.9 3.7 %copy-start.22 = (f32[1024]{0:T(1024)S(1)}, f32[1024]{0:T(1024)}, u32[]{:S(2)}) copy-start(f32[1024]{0:T(1024)} %get-tuple-element.52) | copy-start | bytes 12292
  76.9 3.7 %copy-start.37 = (f32[128]{0:T(128)S(1)}, f32[128]{0:T(128)}, u32[]{:S(2)}) copy-start(f32[128]{0:T(128)} %copy-done.36) | copy-start | bytes 1540
  76.9 3.7 %copy-start.39 = (f32[128]{0:T(128)S(1)}, f32[128]{0:T(128)}, u32[]{:S(2)}) copy-start(f32[128]{0:T(128)} %copy-done.38) | copy-start | bytes 1540
  76.9 3.7 %copy-start.41 = (f32[128]{0:T(128)S(1)}, f32[128]{0:T(128)}, u32[]{:S(2)}) copy-start(f32[128]{0:T(128)} %copy-done.40) | copy-start | bytes 1540
  76.9 3.7 %copy-start.43 = (f32[128]{0:T(128)S(1)}, f32[128]{0:T(128)}, u32[]{:S(2)}) copy-start(f32[128]{0:T(128)} %copy-done.42) | copy-start | bytes 1540
  79.1 2.8 %collective-permute-start.2 = (f32[32,16,256]{2,1,0:T(8,128)S(1)}, f32[32,16,256]{2,1,0:T(8,128)S(1)}, u32[]{:S(2)}, u32[]{:S(2)}) collective-permute-start(f32[32,16,256]{2,1,0:T(8,128)S(1)} %dynamic-slice_bitcast_fusion), channel_id=1, source_target_pairs={{0,1},{1,0},{2,3},{3,2},{4,5},{5,4},{6,7},{7,6},{8,9},{9,8},{10,11... | collective-permute-start | bytes 1572872 | tf_op jit(solution)/shard_map/ppermute | solution.py:323
  (4 other events, 4.7 us)

commit v10 on v8

--- a/solution.py
+++ b/solution.py
@@ -1,6 +1,8 @@
 import jax
 import jax.numpy as jnp
 from jax import lax
+from jax.experimental import pallas as pl
+from jax.experimental.pallas import tpu as pltpu
 from jax.sharding import PartitionSpec as P
 
 P_SIZE = 64
@@ -176,6 +178,36 @@
     return (output, state)
 
 
+def conv_silu_kernel(ext_x, ext_bc, taps_x, taps_bc, links, u_x, v_x, u_bc, v_bc):
+    rows = u_x.shape[0]
+    tile = 128
+    for ext, taps, u, v in ((ext_x, taps_x, u_x, v_x), (ext_bc, taps_bc, u_bc, v_bc)):
+        for start in range(0, rows, tile):
+            total = jnp.zeros((tile, u.shape[1]), jnp.float32)
+            for k in range(taps.shape[0]):
+                total = total + taps[k : k + 1, :] * ext[start + k : start + k + tile, :] * links[
+                    start : start + tile, k : k + 1
+                ]
+            u[start : start + tile, :] = total
+            v[start : start + tile, :] = total / (1.0 + jnp.exp(-total))
+
+
+def conv_silu(ext_x, ext_bc, taps_x, taps_bc, links):
+    rows = links.shape[0]
+    shapes = [
+        jax.ShapeDtypeStruct((rows, ext_x.shape[1]), jnp.float32),
+        jax.ShapeDtypeStruct((rows, ext_x.shape[1]), jnp.float32),
+        jax.ShapeDtypeStruct((rows, ext_bc.shape[1]), jnp.float32),
+        jax.ShapeDtypeStruct((rows, ext_bc.shape[1]), jnp.float32),
+    ]
+    return pl.pallas_call(
+        conv_silu_kernel,
+        out_shape=shapes,
+        in_specs=[pl.BlockSpec(memory_space=pltpu.VMEM)] * 5,
+        out_specs=[pl.BlockSpec(memory_space=pltpu.VMEM)] * 4,
+    )(ext_x, ext_bc, taps_x, taps_bc, links)
+
+
 def local(pre_x, pre_bc, conv_x, conv_bc, log_decay, lengths, grad_out):
     tok_rows = pre_x.shape[0]
     head_count = log_decay.shape[0]
@@ -189,18 +221,16 @@
         jnp.concatenate([pre_x[tok_rows - rim_width :], pre_bc[tok_rows - rim_width :]], axis=1), "seq", 1
     )
     before_x, before_bc = before_both[:, : pre_x.shape[1]], before_both[:, pre_x.shape[1] :]
-    u_x = conv_forward(
+    links = jnp.stack(
+        [note_all[k : k + tok_rows] == note_ids for k in range(K)], axis=1
+    ).astype(jnp.float32)
+    u_x, v_x, u_bc, v_bc = conv_silu(
         jnp.concatenate([before_x, pre_x]).astype(jnp.float32),
+        jnp.concatenate([before_bc, pre_bc]).astype(jnp.float32),
         conv_x,
-        note_all[: tok_rows + rim_width],
-    )
-    u_bc = conv_forward(
-        jnp.concatenate([before_bc, pre_bc]).astype(jnp.float32),
         conv_bc,
-        note_all[: tok_rows + rim_width],
-    )
-    v_x = jax.nn.silu(u_x)
-    v_bc = jax.nn.silu(u_bc)
+        links,
+    )
     x_heads = v_x.reshape(block_count, BLOCK, head_count, P_SIZE).transpose(2, 0, 1, 3)
     b_blocks = v_bc[:, :N].reshape(block_count, BLOCK, N)
     c_blocks = v_bc[:, N:].reshape(block_count, BLOCK, N)

time: 104 us -> 109 us (1.048)
  Pallas kernels: 0 us -> 4.73 us
  waiting for transfers between devices: 12.4 us -> 10.9 us
  matrix products: 17.9 us -> 19.2 us
    pallas_call x0 -> x1, Pallas kernels: none -> 4.73 us  [conv_silu(): pl.pallas_call(conv_silu_kernel, out_shape=shapes, in_specs=[pl.BlockSpec...]
    mul x2 -> x0, other arithmetic: 2.29 us -> none  [the longest x1 1.27 us: local(): v_x = jax.nn.silu(u_x)]
    pallas_call x0 -> x1, local copies, waits for them, and re-layouts: none -> 2.04 us  [conv_silu(): pl.pallas_call(conv_silu_kernel, out_shape=shapes, in_specs=[pl.BlockSpec...]
    unnamed x97 -> x79, local copies, waits for them, and re-layouts: 4.53 us -> 2.84 us
    ppermute x1, waiting for transfers between devices: 2.12 us -> 0.72 us  [local(): pair_sum = mine + lax.ppermute(other, 'core', [(0, 1), (1, 0)])]
    slice x1, local copies, waits for them, and re-layouts: 0.07 us -> 1.39 us  [local(): v_bc[:, N:]]
    dot_general x11, matrix products: 14 us -> 15.2 us  [einsum(): jnp.einsum(spec, *operands, precision=lax.Precision.HIGH, preferred_eleme...]
  transfers between devices with their start and end apart: 5 -> 5, of which waited for: 3 -> 3; matrix products, arithmetic and copies ran while one was open for 33% -> 32% of each run, Pallas kernels for 0% -> 0%
where the time goes in v10:
time: 109 us; the launch traced here: 107 us
  local copies, waits for them, and re-layouts  24.8 us (23%)
  other arithmetic  23.2 us (21%)
  starting transfers between devices  21.3 us (20%)
  matrix products  19.2 us (18%)
  waiting for transfers between devices  10.9 us (10%)
  Pallas kernels  4.73 us (4%)
  between operations  2.58 us (2%)
    dot_general x11, matrix products, einsum(): jnp.einsum(spec, *operands, precision=lax.Precision.HIGH, preferred_eleme...  15.2 us
    all_to_all x1, starting transfers between devices, local(): grad_pre_bc = lax.all_to_all(pair_sum, 'chip', 0, 0, tiled=False).sum(0)  11.3 us
    all_to_all x1, waiting for transfers between devices, local(): grad_pre_bc = lax.all_to_all(pair_sum, 'chip', 0, 0, tiled=False).sum(0)  6.6 us
    ppermute x2, starting transfers between devices, shifted(): lax.ppermute(value, axis, [(source, source + steps) for source in range(i...  5.4 us
    pallas_call x1, Pallas kernels, conv_silu(): pl.pallas_call(conv_silu_kernel, out_shape=shapes, in_specs=[pl.BlockSpec...  4.73 us
    all_to_all x1, starting transfers between devices, chain_both(): arrived = lax.all_to_all(outgoing, axis, 0, 0, tiled=False)  4.62 us
    ppermute x2, waiting for transfers between devices, shifted(): lax.ppermute(value, axis, [(source, source + steps) for source in range(i...  3.57 us
    add x2, other arithmetic, conv_backward(): result + weights[k][None, :] * extended[lag:lag + count] * linked[:, None]  3.24 us
  transfers between devices with their start and end apart: 5, of which 3 were waited for; matrix products, arithmetic and copies ran while one was open for 32% of the time, Pallas kernels for 0%

profile of v10, /device:TPU:8, one launch (start us, length us, event | category | flops | bytes accessed | tf_op | source)
XLA Modules:
  0.0 106.7 jit_solution(16111072611979412968)
XLA Ops:
  0.6 0.7 slice.209
  2.1 3.5 %collective-permute-start = (bf16[3,384]{1,0:T(4,128)(2,1)S(1)}, bf16[3,384]{1,0:T(4,128)(2,1)S(1)}, u32[]{:S(2)}, u32[]{:S(2)}) collective-permute-start(bf16[3,384]{1,0:T(4,128)(2,1)S(1)} %pad_maximum_fusion.8), channel_id=1, source_target_pairs={{0,64},{64,128},{128,192},{1,65},{65,129},{129,193},{2,66},{66,130... | collective-permute-start | bytes 6920 | tf_op jit(solution)/shard_map/ppermute | solution.py:20
  5.6 0.8 reduce-window.9
  8.2 1.4 %fusion.19 = f32[2,1024]{1,0:T(2,128)S(1)} fusion(f32[2,1024]{1,0:T(2,128)} %param.11), kind=kOutput, calls=%fused_computation.30 | convolution fusion | flops 26214400 | bytes 16384 | tf_op jit(solution)/shard_map/dot_general | solution.py:130
  9.6 0.7 reshape.465
  11.6 2.0 %fusion.105 = (f32[1024]{0:T(1024)}, f32[1024]{0:T(1024)S(1)}, f32[1024]{0:T(1024)S(1)}, f32[1024]{0:T(1024)}, f32[1024]{0:T(1024)}, /*index=5*/pred[1024]{0:T(1...) fusion(s32[1030]{0:T(1024)S(1)} %broadcast_add_fusion, s32[]{:T(128)} %bitcast.6, s32[]{:T(128)} %bitcast.8), kind=kLoop, calls=%fused_computation.188 | loop fusion | flops 13312 | bytes 52232 | tf_op jit(solution)/shard_map/convert_element_type | solution.py:99
  13.6 0.8 compare_convert_fusion.4
  14.8 0.8 slice_reduce_fusion.8
  15.8 1.4 %compare_and_fusion = (pred[4,256,256]{1,2,0:T(8,128)(4,1)}, f32[4,256,256]{1,2,0:T(8,128)}) fusion(s32[4,256]{1,0:T(4,128)S(1)} %reshape.466, pred[256,256]{0,1:T(8,128)(4,1)S(1)} %iota_compare_fusion.4), kind=kLoop, calls=%fused_computation.45 | loop fusion | flops 786432 | bytes 1380352 | tf_op jit(solution)/shard_map/jvp()/and | solution.py:167
  18.7 1.0 copy.206.links
  19.7 0.9 maximum_convert_fusion.1.ext_x
  20.6 1.1 %maximum_convert_fusion.ext_bc = f32[1027,256]{1,0:T(8,128)} fusion(bf16[1024,256]{1,0:T(8,128)(2,1)S(1)} %copy-done.13, bf16[3,256]{1,0:T(4,128)(2,1)S(1)} %slice.261), kind=kLoop, calls=%fused_computation.50 | loop fusion | flops 1051648 | bytes 1577472 | tf_op jit(solution)/shard_map/convert_element_type | solution.py:229
  21.7 4.7 %shard_map.94 = (f32[1024,128]{1,0:T(8,128)}, f32[1024,128]{1,0:T(8,128)}, f32[1024,256]{1,0:T(8,128)}, f32[1024,256]{1,0:T(8,128)}) custom-call(f32[1027,128]{1,0:T(8,128)} %maximum_convert_fusion.1.ext_x, f32[1027,256]{1,0:T(8,128)} %maximum_convert_fusion.ext_bc, f32[4,128]{1,0:T(4,128)} %taps_x.1, f32[4,256]{1,0:T(4,128)} %taps_bc.1, f32[1024,4]{1,0:T(8,128)} %copy.206.links), custom_call_target="tpu_custom_call" | custom-call | tf_op jit(solution)/shard_map/pallas_call | solution.py:203
  26.4 2.0 %copy.207 = f32[1024,128]{0,1:T(8,128)} copy(f32[1024,128]{1,0:T(8,128)} %get-tuple-element.7) | data formatting | bytes 1048576 | tf_op jit(solution)/shard_map/pallas_call | solution.py:203
  28.4 1.6 %reshape.487 = f32[4,256,2,64]{3,2,1,0:T(2,128)S(1)} reshape(f32[1024,128]{1,0:T(8,128)} %get-tuple-element.7) | data formatting | bytes 1048576 | tf_op jit(solution)/shard_map/reshape | solution.py:234
  30.6 1.2 %copy.243 = f32[4,256,2,64]{1,3,0,2:T(8,128)} copy(f32[4,256,2,64]{3,2,1,0:T(2,128)S(1)} %reshape.487) | data formatting | bytes 1048576 | tf_op jit(solution)/shard_map/transpose | solution.py:234
  31.8 1.4 %fusion.123 = (f32[1024,128]{1,0:T(8,128)S(1)}, f32[1024,128]{1,0:T(8,128)S(1)}) fusion(f32[1024,256]{1,0:T(8,128)} %get-tuple-element.8), kind=kLoop, calls=%fused_computation.241 | loop fusion | bytes 2097152 | tf_op jit(solution)/shard_map/slice | solution.py:259
  34.9 0.9 select_select_fusion
  35.8 4.6 %all-to-all-start = ((f32[4,2,8320]{2,1,0:T(2,128)}), f32[4,2,8320]{2,1,0:T(2,128)S(1)}, u32[]{:S(2)}, u32[]{:S(2)}) async-start(f32[4,2,8320]{2,1,0:T(2,128)} %select_select_fusion), calls=%async_computation | async-start | bytes 532480 | tf_op jit(solution)/shard_map/all_to_all | solution.py:141
  43.4 5.7 %fusion.17 = (f32[2,4,256]{2,1,0:T(4,128)}, f32[2,4,256]{2,1,0:T(4,128)}, f32[4,256,256]{1,2,0:T(8,128)S(1)}, f32[2,4,256,256]{2,3,1,0:T(8,128)}) fusion(f32[4,256,256]{1,2,0:T(8,128)} %get-tuple-element.51, f32[2,4,256]{2,1,0:T(4,128)S(1)} %bitcast.345, f32[4,256,256]{1,2,0:T(8,128)S(1)} %fusion.127, pred[4,256,256]{1,2,0:T(8,128)(4,1)} %get-tuple-element.50, ...), kind=kOutput, calls=%fused_computation.24 | convolution fusion | flops 207351808 | bytes 6316032 | tf_op jit(solution)/shard_map/transpose(jvp(hbij,hbjp->hbip))/dot_general | solution.py:157
  49.1 1.1 %convolution_bitcast_fusion.4 = f32[2,4,64,128]{3,2,0,1:T(8,128)} fusion(f32[4,256,128,1]{2,1,3,0:T(8,128)S(1)} %bitcast.333, f32[4,2,256]{2,1,0:T(2,128)S(1)} %copy.209, bf16[4,256,2,64]{1,0,3,2:T(4,128)(2,1)S(1)} %reshape.467), kind=kOutput, calls=%fused_computation.27 | convolution fusion | flops 100925440 | bytes 1056768 | tf_op jit(solution)/shard_map/transpose(jvp(bin,hbpn->hbip))/dot_general | solution.py:157
  50.5 1.9 %multiply_reduce_fusion.1 = (f32[2]{0:T(128)}, f32[1,2,64,128]{3,1,2,0:T(2,128)S(1)}) fusion(f32[1,2,8192]{2,1,0:T(2,128)} %squeeze.91, f32[1,2,8192]{2,1,0:T(2,128)} %squeeze.90, f32[1,2,8192]{2,1,0:T(2,128)} %squeeze.89, f32[4,2,8320]{2,1,0:T(2,128)S(1)} %all-to-all-done, f32[2]{0:T(128)S(1)} %get-tuple-element.76, f32[2]{0:T(128)S(1)} %get-tuple-element.77, ...), kind=kLoop, calls=%fused_computation.142 | loop fusion | flops 360446 | bytes 524376 | tf_op jit(solution)/shard_map/transpose(jvp())/reduce_sum | solution.py:176
  52.4 0.8 multiply_add_fusion
  53.2 1.1 %multiply_add_fusion.3 = (f32[2,1,64,128]{3,2,0,1:T(8,128)S(1)}, f32[2,1,64,128]{3,2,0,1:T(8,128)S(1)}, f32[2,1,64,128]{3,2,0,1:T(8,128)S(1)}, f32[2,1,64,128]{3,2,0,1:T(8,128)S(1)}) fusion(f32[2,4,64,128]{3,2,0,1:T(8,128)} %convolution_bitcast_fusion.4, f32[2]{0:T(128)} %get-tuple-element.25, f32[2]{0:T(128)} %get-tuple-element.26, ...), kind=kLoop, calls=%fused_computation.146 | loop fusion | flops 212992 | bytes 720948 | tf_op jit(solution)/shard_map/transpose(jvp())/add_any | solution.py:176
  54.3 1.3 %convolution_bitcast_fusion.2 = f32[4,256,128]{2,1,0:T(8,128)S(1)} fusion(f32[4,256,2,64]{1,3,2,0:T(8,128)S(1)} %copy.219, f32[2,4,256]{2,0,1:T(2,128)} %copy-done.18, f32[2,1,64,128]{3,2,0,1:T(8,128)S(1)} %get-tuple-element.27, f32[2,1,64,128]{3,2,0,1:T(8,128)S(1)} %get-tuple-element.28, f32[2,1,64,128]{3,2,0,1:T(8,128)S(1)} %get-tuple-element.29, ...), kind=kOutput, calls=%fused_computation.20 | convolution fusion | flops 100990976 | bytes 1318912 | tf_op jit(solution)/shard_map/transpose(jvp(hbjp,bjn->hbpn))/dot_general | solution.py:157
  55.6 1.0 fusion.47
  57.3 1.0 convolution_add_fusion
  59.4 1.2 %copy-done.4 = f32[2,4,256,256]{2,3,1,0:T(8,128)S(1)} copy-done((f32[2,4,256,256]{2,3,1,0:T(8,128)S(1)}, f32[2,4,256,256]{2,3,1,0:T(8,128)}, u32[]{:S(2)}) %copy-start.4) | copy-done | bytes 2097176
  60.6 1.6 %fusion.12 = f32[4,256,2,64]{1,3,2,0:T(8,128)} fusion(f32[2,4,256,256]{2,3,1,0:T(8,128)S(1)} %copy-done.4, f32[4,2,64,256]{3,2,1,0:T(8,128)S(1)} %get-tuple-element.85, bf16[2,4,256,64]{2,1,3,0:T(4,128)(2,1)S(1)} %bitcast.337, f32[4,256,2]{1,2,0:T(2,128)S(1)} %copy-done.23), kind=kOutput, calls=%fused_computation.21 | convolution fusion | flops 201588736 | bytes 3416064 | tf_op jit(solution)/shard_map/transpose(jvp(hbij,hbjp->hbip))/dot_general | solution.py:157
  62.2 1.5 %copy.240 = f32[4,256,2,64]{3,2,1,0:T(2,128)S(1)} copy(f32[4,256,2,64]{1,3,2,0:T(8,128)} %fusion.12) | data formatting | bytes 1048576 | tf_op jit(solution)/shard_map/reshape | solution.py:272
  63.6 1.4 %reshape.486 = f32[1024,128]{1,0:T(8,128)} reshape(f32[4,256,2,64]{3,2,1,0:T(2,128)S(1)} %copy.240) | data formatting | bytes 1048576 | tf_op jit(solution)/shard_map/reshape | solution.py:272
  65.0 1.4 %multiply_multiply_fusion = f32[1024,128]{1,0:T(8,128)S(1)} fusion(f32[1024,128]{1,0:T(8,128)} %reshape.486, f32[1024,128]{1,0:T(8,128)} %get-tuple-element.9), kind=kLoop, calls=%fused_computation.76 | loop fusion | flops 1048576 | bytes 1572864 | tf_op jit(solution)/shard_map/mul | solution.py:274
  66.5 1.9 %collective-permute-start.1 = (f32[3,384]{1,0:T(4,128)S(1)}, f32[3,384]{1,0:T(4,128)S(1)}, u32[]{:S(2)}, u32[]{:S(2)}) collective-permute-start(f32[3,384]{1,0:T(4,128)S(1)} %pad_maximum_fusion.7), channel_id=1, source_target_pairs={{64,0},{128,64},{192,128},{65,1},{129,65},{193,129},{66,2},{130,66... | collective-permute-start | bytes 13832 | tf_op jit(solution)/shard_map/ppermute | solution.py:20
  68.4 3.6 %collective-permute-done.1 = f32[3,384]{1,0:T(4,128)S(1)} collective-permute-done((f32[3,384]{1,0:T(4,128)S(1)}, f32[3,384]{1,0:T(4,128)S(1)}, u32[]{:S(2)}, u32[]{:S(2)}) %collective-permute-start.1) | collective-permute-done | bytes 4640 | tf_op jit(solution)/shard_map/ppermute | solution.py:20
  72.6 1.3 %fusion.25 = f32[1024,256]{1,0:T(8,128)S(1)} fusion(f32[3,256]{1,0:T(4,128)S(1)} %slice.293, f32[1024,256]{1,0:T(8,128)S(1)} %maximum_multiply_fusion, f32[256]{0:T(256)S(1)} %bitcast.350, f32[1024]{0:T(1024)S(1)} %copy-done.20, f32[256]{0:T(256)S(1)} %bitcast.351, f32[1024]{0:T(1024)S(1)} %copy-done.21, f32[256]{0:T(256)S(1)} %bitcast.349, ...), kind=kLoop, calls=%fused_computation.37 | loop fusion | flops 3407872 | bytes 2116608 | tf_op jit(solution)/shard_map/add | solution.py:99
  73.9 0.8 dynamic-slice_bitcast_fusion
  74.7 1.4 %slice_bitcast_fusion.7 = (f32[128]{0:T(128)}, f32[128]{0:T(128)}, f32[128]{0:T(128)}, f32[128]{0:T(128)}) fusion(f32[4,128]{1,0:T(4,128)} %taps_x.1), kind=kLoop, calls=%fused_computation.231 | loop fusion | bytes 4096 | tf_op jit(solution)/shard_map/mul | solution.py:99
  76.8 0.9 bitcast_add_fusion
  77.7 11.3 %all-to-all-start.1 = ((f32[32,16,256]{2,1,0:T(8,128)}), f32[32,16,256]{2,1,0:T(8,128)S(1)}, u32[]{:S(2)}, u32[]{:S(2)}) async-start(f32[32,16,256]{2,1,0:T(8,128)} %bitcast_add_fusion), calls=%async_computation.1 | async-start | bytes 1048576 | tf_op jit(solution)/shard_map/all_to_all | solution.py:286
  89.1 1.0 fusion.75
  90.1 0.8 copy.224
  90.8 0.9 fusion.87
  92.0 0.8 multiply_bitcast_fusion
  92.8 0.9 fusion.110
  93.8 1.3 %fusion.18 = f32[2,4,256]{2,0,1:T(2,128)S(1)} fusion(f32[4,256,128,1]{2,1,3,0:T(8,128)S(1)} %bitcast.335, bf16[4,256,2,64]{1,0,3,2:T(4,128)(2,1)S(1)} %reshape.467, f32[2,1,64,128]{3,2,0,1:T(8,128)} %copy-done.9, f32[2,1,64,128]{3,2,0,1:T(8,128)} %copy-done.10, f32[2,1,64,128]{3,2,0,1:T(8,128)} %copy-done.11, f32[2,1,64,128]{3,2,0,1:T(8,128)} %copy-done.12), kind=kOutput, calls=%fused_computation.25 | convolution fusion | flops 101251072 | bytes 1056768 | tf_op jit(solution)/shard_map/jvp(bin,hbpn->hbip)/dot_general | solution.py:157
  95.2 1.0 convolution_bitcast_fusion.7
  97.5 2.0 %fusion.39 = f32[1024,128]{1,0:T(8,128)} fusion(f32[3,128]{1,0:T(4,128)S(1)} %slice.285, f32[1024,128]{1,0:T(8,128)S(1)} %copy-done.2, f32[128]{0:T(128)S(1)} %copy-done.36, f32[1024]{0:T(1024)} %get-tuple-element.55, f32[128]{0:T(128)S(1)} %copy-done.37, f32[1024]{0:T(1024)} %get-tuple-element.56, f32[128]{0:T(128)S(1)} %copy-done.35, ...), kind=kLoop, calls=%fused_computation.57 | loop fusion | flops 1703936 | bytes 1064448 | tf_op jit(solution)/shard_map/add | solution.py:99
  99.5 6.6 %all-to-all-done.1 = f32[32,16,256]{2,1,0:T(8,128)S(1)} async-done(((f32[32,16,256]{2,1,0:T(8,128)}), f32[32,16,256]{2,1,0:T(8,128)S(1)}, u32[]{:S(2)}, u32[]{:S(2)}) %all-to-all-start.1) | async-done | bytes 524320 | tf_op jit(solution)/shard_map/all_to_all | solution.py:286
  (143 shorter events, 15.3 us)
Async XLA Ops:
  0.6 17.7 %copy-start.15 = (bf16[1024,128]{1,0:T(8,128)(2,1)S(1)}, bf16[1024,128]{1,0:T(8,128)(2,1)}, u32[]{:S(2)}) copy-start(bf16[1024,128]{1,0:T(8,128)(2,1)} %param.13) | copy-start | bytes 786436
  2.1 17.6 %collective-permute-start = (bf16[3,384]{1,0:T(4,128)(2,1)S(1)}, bf16[3,384]{1,0:T(4,128)(2,1)S(1)}, u32[]{:S(2)}, u32[]{:S(2)}) collective-permute-start(bf16[3,384]{1,0:T(4,128)(2,1)S(1)} %pad_maximum_fusion.8), channel_id=1, source_target_pairs={{0,64},{64,128},{128,192},{1,65},{65,129},{129,193},{2,66},{66,130... | collective-permute-start | bytes 6920 | tf_op jit(solution)/shard_map/ppermute | solution.py:20
  8.2 11.5 %copy-start.14 = (bf16[1024,128]{1,0:T(8,128)(2,1)S(1)}, bf16[1024,128]{1,0:T(8,128)(2,1)}, u32[]{:S(2)}) copy-start(bf16[1024,128]{1,0:T(8,128)(2,1)} %param.7) | copy-start | bytes 786436
  13.6 7.0 %copy-start.13 = (bf16[1024,256]{1,0:T(8,128)(2,1)S(1)}, bf16[1024,256]{1,0:T(8,128)(2,1)}, u32[]{:S(2)}) copy-start(bf16[1024,256]{1,0:T(8,128)(2,1)} %param.8) | copy-start | bytes 1572868
  14.4 3.1 %copy-start.32 = (f32[4]{0:T(128)}, f32[4]{0:T(128)S(1)}, u32[]{:S(2)}) copy-start(f32[4]{0:T(128)S(1)} %get-tuple-element.35) | copy-start | bytes 52
  14.5 1.2 %copy-start.33 = (f32[4,256]{1,0:T(4,128)}, f32[4,256]{1,0:T(4,128)S(1)}, u32[]{:S(2)}) copy-start(f32[4,256]{1,0:T(4,128)S(1)} %get-tuple-element.69) | copy-start | bytes 12292
  14.8 3.5 %copy-start.22 = (f32[2,4]{1,0:T(2,128)}, f32[2,4]{1,0:T(2,128)S(1)}, u32[]{:S(2)}) copy-start(f32[2,4]{1,0:T(2,128)S(1)} %slice_reduce_fusion) | copy-start | bytes 100
  17.7 31.4 %copy-start.16 = (f32[4,2,256]{2,1,0:T(2,128)}, f32[4,2,256]{2,1,0:T(2,128)S(1)}, u32[]{:S(2)}) copy-start(f32[4,2,256]{2,1,0:T(2,128)S(1)} %copy.209) | copy-start | bytes 24580
  18.3 22.1 %copy-start.18 = (f32[2,4,256]{2,0,1:T(2,128)}, f32[2,4,256]{2,0,1:T(2,128)S(1)}, u32[]{:S(2)}) copy-start(f32[2,4,256]{2,0,1:T(2,128)S(1)} %copy.220) | copy-start | bytes 24580
  31.8 1.5 %copy-start = (f32[1024,256]{1,0:T(8,128)S(1)}, f32[1024,256]{1,0:T(8,128)}, u32[]{:S(2)}) copy-start(f32[1024,256]{1,0:T(8,128)} %get-tuple-element.8) | copy-start | bytes 3145732
  31.8 2.2 %copy-start.3 = (f32[1024,128]{0,1:T(8,128)S(1)}, f32[1024,128]{0,1:T(8,128)}, u32[]{:S(2)}) copy-start(f32[1024,128]{0,1:T(8,128)} %copy.207) | copy-start | bytes 1572868
  35.8 14.4 %all-to-all-start = ((f32[4,2,8320]{2,1,0:T(2,128)}), f32[4,2,8320]{2,1,0:T(2,128)S(1)}, u32[]{:S(2)}, u32[]{:S(2)}) async-start(f32[4,2,8320]{2,1,0:T(2,128)} %select_select_fusion), calls=%async_computation | async-start | bytes 532480 | tf_op jit(solution)/shard_map/all_to_all | solution.py:141
  50.4 6.2 %copy-start.25 = (f32[2]{0:T(128)}, f32[2]{0:T(128)S(1)}, u32[]{:S(2)}) copy-start(f32[2]{0:T(128)S(1)} %get-tuple-element.74) | copy-start | bytes 28
  50.4 6.2 %copy-start.26 = (f32[2]{0:T(128)}, f32[2]{0:T(128)S(1)}, u32[]{:S(2)}) copy-start(f32[2]{0:T(128)S(1)} %get-tuple-element.75) | copy-start | bytes 28
  50.4 6.2 %copy-start.27 = (f32[2]{0:T(128)}, f32[2]{0:T(128)S(1)}, u32[]{:S(2)}) copy-start(f32[2]{0:T(128)S(1)} %get-tuple-element.76) | copy-start | bytes 28
  50.4 6.2 %copy-start.28 = (f32[2]{0:T(128)}, f32[2]{0:T(128)S(1)}, u32[]{:S(2)}) copy-start(f32[2]{0:T(128)S(1)} %get-tuple-element.77) | copy-start | bytes 28
  50.4 6.2 %copy-start.29 = (f32[2]{0:T(128)}, f32[2]{0:T(128)S(1)}, u32[]{:S(2)}) copy-start(f32[2]{0:T(128)S(1)} %get-tuple-element.80) | copy-start | bytes 28
  50.4 6.2 %copy-start.30 = (f32[2]{0:T(128)}, f32[2]{0:T(128)S(1)}, u32[]{:S(2)}) copy-start(f32[2]{0:T(128)S(1)} %get-tuple-element.81) | copy-start | bytes 28
  50.5 6.2 %copy-start.7 = (f32[1,2,64,128]{3,1,2,0:T(2,128)}, f32[1,2,64,128]{3,1,2,0:T(2,128)S(1)}, u32[]{:S(2)}) copy-start(f32[1,2,64,128]{3,1,2,0:T(2,128)S(1)} %get-tuple-element.44) | copy-start | bytes 196612
  52.4 4.3 %copy-start.8 = (f32[1,2,64,128]{3,1,2,0:T(2,128)}, f32[1,2,64,128]{3,1,2,0:T(2,128)S(1)}, u32[]{:S(2)}) copy-start(f32[1,2,64,128]{3,1,2,0:T(2,128)S(1)} %get-tuple-element.41) | copy-start | bytes 196612
  53.2 4.1 %copy-start.9 = (f32[2,1,64,128]{3,2,0,1:T(8,128)}, f32[2,1,64,128]{3,2,0,1:T(8,128)S(1)}, u32[]{:S(2)}) copy-start(f32[2,1,64,128]{3,2,0,1:T(8,128)S(1)} %get-tuple-element.31) | copy-start | bytes 196612
  53.2 4.1 %copy-start.10 = (f32[2,1,64,128]{3,2,0,1:T(8,128)}, f32[2,1,64,128]{3,2,0,1:T(8,128)S(1)}, u32[]{:S(2)}) copy-start(f32[2,1,64,128]{3,2,0,1:T(8,128)S(1)} %get-tuple-element.32) | copy-start | bytes 196612
  53.2 4.1 %copy-start.11 = (f32[2,1,64,128]{3,2,0,1:T(8,128)}, f32[2,1,64,128]{3,2,0,1:T(8,128)S(1)}, u32[]{:S(2)}) copy-start(f32[2,1,64,128]{3,2,0,1:T(8,128)S(1)} %get-tuple-element.33) | copy-start | bytes 196612
  53.2 4.1 %copy-start.12 = (f32[2,1,64,128]{3,2,0,1:T(8,128)}, f32[2,1,64,128]{3,2,0,1:T(8,128)S(1)}, u32[]{:S(2)}) copy-start(f32[2,1,64,128]{3,2,0,1:T(8,128)S(1)} %get-tuple-element.34) | copy-start | bytes 196612
  53.2 3.5 %copy-start.17 = (f32[4,2,256]{2,1,0:T(2,128)S(1)}, f32[4,2,256]{2,1,0:T(2,128)}, u32[]{:S(2)}) copy-start(f32[4,2,256]{2,1,0:T(2,128)} %copy-done.16) | copy-start | bytes 24580
  57.3 1.7 %copy-start.6 = (f32[1024,256]{1,0:T(8,128)S(1)}, f32[1024,256]{1,0:T(8,128)}, u32[]{:S(2)}) copy-start(f32[1024,256]{1,0:T(8,128)} %get-tuple-element.10) | copy-start | bytes 3145732
  59.0 1.6 %copy-start.4 = (f32[2,4,256,256]{2,3,1,0:T(8,128)S(1)}, f32[2,4,256,256]{2,3,1,0:T(8,128)}, u32[]{:S(2)}) copy-start(f32[2,4,256,256]{2,3,1,0:T(8,128)} %get-tuple-element.37) | copy-start | bytes 6291460
  59.0 1.6 %copy-start.23 = (f32[4,256,2]{1,2,0:T(2,128)S(1)}, f32[4,256,2]{1,2,0:T(2,128)}, u32[]{:S(2)}) copy-start(f32[4,256,2]{1,2,0:T(2,128)} %copy.212) | copy-start | bytes 24580
  62.1 6.2 %copy-start.24 = (f32[4,256]{1,0:T(4,128)S(1)}, f32[4,256]{1,0:T(4,128)}, u32[]{:S(2)}) copy-start(f32[4,256]{1,0:T(4,128)} %taps_bc.1) | copy-start | bytes 12292
  62.1 10.4 %copy-start.19 = (f32[1024]{0:T(1024)S(1)}, f32[1024]{0:T(1024)}, u32[]{:S(2)}) copy-start(f32[1024]{0:T(1024)} %get-tuple-element.52) | copy-start | bytes 12292
  62.2 10.4 %copy-start.20 = (f32[1024]{0:T(1024)S(1)}, f32[1024]{0:T(1024)}, u32[]{:S(2)}) copy-start(f32[1024]{0:T(1024)} %get-tuple-element.55) | copy-start | bytes 12292
  62.2 10.4 %copy-start.21 = (f32[1024]{0:T(1024)S(1)}, f32[1024]{0:T(1024)}, u32[]{:S(2)}) copy-start(f32[1024]{0:T(1024)} %get-tuple-element.56) | copy-start | bytes 12292
  66.4 5.6 %copy-start.1 = (f32[1024,128]{1,0:T(8,128)}, f32[1024,128]{1,0:T(8,128)S(1)}, u32[]{:S(2)}) copy-start(f32[1024,128]{1,0:T(8,128)S(1)} %multiply_multiply_fusion) | copy-start | bytes 1572868
  66.5 5.5 %collective-permute-start.1 = (f32[3,384]{1,0:T(4,128)S(1)}, f32[3,384]{1,0:T(4,128)S(1)}, u32[]{:S(2)}, u32[]{:S(2)}) collective-permute-start(f32[3,384]{1,0:T(4,128)S(1)} %pad_maximum_fusion.7), channel_id=1, source_target_pairs={{64,0},{128,64},{192,128},{65,1},{129,65},{193,129},{66,2},{130,66... | collective-permute-start | bytes 13832 | tf_op jit(solution)/shard_map/ppermute | solution.py:20
  72.0 0.6 copy-start.31
  73.9 15.2 %copy-start.5 = (f32[2,4,64,128]{3,2,0,1:T(8,128)S(1)}, f32[2,4,64,128]{3,2,0,1:T(8,128)}, u32[]{:S(2)}) copy-start(f32[2,4,64,128]{3,2,0,1:T(8,128)} %convolution_bitcast_fusion.4) | copy-start | bytes 786436
  74.7 2.1 %collective-permute-start.2 = (f32[32,16,256]{2,1,0:T(8,128)}, f32[32,16,256]{2,1,0:T(8,128)S(1)}, u32[]{:S(2)}, u32[]{:S(2)}) collective-permute-start(f32[32,16,256]{2,1,0:T(8,128)} %dynamic-slice_bitcast_fusion), channel_id=1, source_target_pairs={{0,1},{1,0},{2,3},{3,2},{4,5},{5,4},{6,7},{7,6},{8,9},{9,8},{10,11... | collective-permute-start | bytes 1572872 | tf_op jit(solution)/shard_map/ppermute | solution.py:285
  76.1 21.4 %copy-start.2 = (f32[1024,128]{1,0:T(8,128)S(1)}, f32[1024,128]{1,0:T(8,128)}, u32[]{:S(2)}) copy-start(f32[1024,128]{1,0:T(8,128)} %copy-done.1) | copy-start | bytes 1572868
  77.7 19.8 %copy-start.34 = (f32[128]{0:T(128)S(1)}, f32[128]{0:T(128)}, u32[]{:S(2)}) copy-start(f32[128]{0:T(128)} %get-tuple-element.70) | copy-start | bytes 1540
  77.7 19.8 %copy-start.35 = (f32[128]{0:T(128)S(1)}, f32[128]{0:T(128)}, u32[]{:S(2)}) copy-start(f32[128]{0:T(128)} %get-tuple-element.71) | copy-start | bytes 1540
  77.7 19.8 %copy-start.36 = (f32[128]{0:T(128)S(1)}, f32[128]{0:T(128)}, u32[]{:S(2)}) copy-start(f32[128]{0:T(128)} %get-tuple-element.72) | copy-start | bytes 1540
  77.7 19.8 %copy-start.37 = (f32[128]{0:T(128)S(1)}, f32[128]{0:T(128)}, u32[]{:S(2)}) copy-start(f32[128]{0:T(128)} %get-tuple-element.73) | copy-start | bytes 1540
  77.7 28.4 %all-to-all-start.1 = ((f32[32,16,256]{2,1,0:T(8,128)}), f32[32,16,256]{2,1,0:T(8,128)S(1)}, u32[]{:S(2)}, u32[]{:S(2)}) async-start(f32[32,16,256]{2,1,0:T(8,128)} %bitcast_add_fusion), calls=%async_computation.1 | async-start | bytes 1048576 | tf_op jit(solution)/shard_map/all_to_all | solution.py:286

commit v11 on v8

--- a/solution.py
+++ b/solution.py
@@ -137,17 +137,17 @@
     targets = jnp.arange(count)[:, None, None]
     outgoing = jnp.where(targets > mine, later[None], jnp.where(targets < mine, earlier[None], 0.0))
     arrived = lax.all_to_all(outgoing, axis, 0, 0, tiled=False)
-    parts = arrived[:, :, :size].reshape((count,) + state.shape)
     keeps = arrived[:, :, size]
     totals = []
     for order in (range(count - 1, -1, -1), range(count)):
-        total = jnp.zeros_like(state)
+        weights = [None] * count
         scale = jnp.ones_like(keep)
         for source in order:
             near = (source < mine) if order.step < 0 else (source > mine)
-            total = total + jnp.where(near, scale, 0.0)[:, None, None] * parts[source]
+            weights[source] = jnp.where(near, scale, 0.0)
             scale = jnp.where(near, scale * keeps[source], scale)
-        totals.append(total)
+        combined = jnp.sum(jnp.stack(weights)[:, :, None] * arrived, axis=0)
+        totals.append(combined[:, :size].reshape(state.shape))
     return totals[0], totals[1]
 
 

time: 104 us -> 96.3 us (0.926)
  local copies, waits for them, and re-layouts: 24.2 us -> 19.3 us
  matrix products: 17.9 us -> 14.3 us
  waiting for transfers between devices: 12.4 us -> 13.7 us
    all_to_all x1, waiting for transfers between devices: 6.69 us -> 9.74 us  [local(): grad_pre_bc = lax.all_to_all(pair_sum, 'chip', 0, 0, tiled=False).sum(0)]
    dot_general x11, matrix products: 14 us -> 11.2 us  [einsum(): jnp.einsum(spec, *operands, precision=lax.Precision.HIGH, preferred_eleme...]
    squeeze x3 -> x0, local copies, waits for them, and re-layouts: 2.81 us -> none  [block_forward_all(): state = through[:, block, None, None] * state + chunk[:, block]]
    add x2 -> x0, other arithmetic: 1.74 us -> none  [the longest x1 1 us: chain_both(): total = total + jnp.where(near, scale, 0.0)[:, None, None] * parts[source]]
    unnamed x0 -> x2, other arithmetic: none -> 1.38 us
    ppermute x1, waiting for transfers between devices: 2.12 us -> 0.8 us  [local(): pair_sum = mine + lax.ppermute(other, 'core', [(0, 1), (1, 0)])]
    reshape x1, local copies, waits for them, and re-layouts: 0.1 us -> 1.32 us  [block_forward_all(): cumul[..., -1:] - cumul]
    add_any x1 -> x0, other arithmetic: 1.08 us -> none  [block_forward_all(): state = through[:, block, None, None] * state + chunk[:, block]]
  transfers between devices with their start and end apart: 5 -> 5, of which waited for: 3 -> 3; matrix products, arithmetic and copies ran while one was open for 33% -> 28% of each run, Pallas kernels for 0% -> 0%
where the time goes in v11:
time: 96.3 us; the launch traced here: 94.6 us
  other arithmetic  22.7 us (24%)
  starting transfers between devices  21.8 us (23%)
  local copies, waits for them, and re-layouts  19.3 us (20%)
  matrix products  14.3 us (15%)
  waiting for transfers between devices  13.7 us (14%)
  between operations  2.83 us (3%)
    all_to_all x1, starting transfers between devices, local(): grad_pre_bc = lax.all_to_all(pair_sum, 'chip', 0, 0, tiled=False).sum(0)  11.3 us
    dot_general x11, matrix products, einsum(): jnp.einsum(spec, *operands, precision=lax.Precision.HIGH, preferred_eleme...  11.2 us
    all_to_all x1, waiting for transfers between devices, local(): grad_pre_bc = lax.all_to_all(pair_sum, 'chip', 0, 0, tiled=False).sum(0)  9.74 us
    ppermute x2, starting transfers between devices, shifted(): lax.ppermute(value, axis, [(source, source + steps) for source in range(i...  5.83 us
    all_to_all x1, starting transfers between devices, chain_both(): arrived = lax.all_to_all(outgoing, axis, 0, 0, tiled=False)  4.62 us
    unnamed x114, local copies, waits for them, and re-layouts  3.93 us
    add x2, other arithmetic, conv_backward(): result + weights[k][None, :] * extended[lag:lag + count] * linked[:, None]  3.37 us
    ppermute x2, waiting for transfers between devices, shifted(): lax.ppermute(value, axis, [(source, source + steps) for source in range(i...  3.16 us
  transfers between devices with their start and end apart: 5, of which 3 were waited for; matrix products, arithmetic and copies ran while one was open for 28% of the time, Pallas kernels for 0%

profile of v11, /device:TPU:8, one launch (start us, length us, event | category | flops | bytes accessed | tf_op | source)
XLA Modules:
  0.0 94.6 jit_solution(8882696915691520954)
XLA Ops:
  0.6 0.7 slice.240
  1.4 0.7 slice.241
  2.1 3.5 %collective-permute-start = (bf16[3,384]{1,0:T(4,128)(2,1)S(1)}, bf16[3,384]{1,0:T(4,128)(2,1)S(1)}, u32[]{:S(2)}, u32[]{:S(2)}) collective-permute-start(bf16[3,384]{1,0:T(4,128)(2,1)S(1)} %pad_maximum_fusion.8), channel_id=1, source_target_pairs={{0,64},{64,128},{128,192},{1,65},{65,129},{129,193},{2,66},{66,130... | collective-permute-start | bytes 6920 | tf_op jit(solution)/shard_map/ppermute | solution.py:18
  5.6 0.8 reduce-window.9
  6.4 0.7 bitcast_subtract_fusion.1
  8.2 1.4 %fusion.19 = f32[2,1024]{1,0:T(2,128)S(1)} fusion(f32[2,1024]{1,0:T(2,128)} %param.11), kind=kOutput, calls=%fused_computation.30 | convolution fusion | flops 26214400 | bytes 16384 | tf_op jit(solution)/shard_map/dot_general | solution.py:128
  9.6 0.7 reshape.402
  11.6 2.0 %fusion.120 = (f32[1024]{0:T(1024)}, f32[1024]{0:T(1024)S(1)}, f32[1024]{0:T(1024)S(1)}, f32[1024]{0:T(1024)}, f32[1024]{0:T(1024)}, /*index=5*/f32[1024]{0:T(1024)S(1)}, f32[1024]{0:T(1024)S(1)}, f32[1024]{0:T(1024)S(1)}) fusion(s32[1030]{0:T(1024)S(1)} %broadcast_add_fusion, s32[]{:T(128)} %bitcast.9, s32[]{:T(128)} %bitcast.15), kind=kLoop, calls=%fused_computation.206 | loop fusion | flops 16384 | bytes 61448 | tf_op jit(solution)/shard_map/convert_element_type | solution.py:97
  13.6 0.8 slice_bitcast_fusion.11
  14.5 0.8 fusion.140
  15.3 0.7 compare_convert_fusion.4
  16.5 0.8 slice_reduce_fusion.8
  17.3 1.4 %compare_and_fusion = (pred[4,256,256]{1,2,0:T(8,128)(4,1)}, f32[4,256,256]{1,2,0:T(8,128)}) fusion(s32[4,256]{1,0:T(4,128)S(1)} %reshape.403, pred[256,256]{0,1:T(8,128)(4,1)S(1)} %iota_compare_fusion.4), kind=kLoop, calls=%fused_computation.57 | loop fusion | flops 786432 | bytes 1380352 | tf_op jit(solution)/shard_map/jvp()/and | solution.py:165
  20.2 1.3 %fusion.66 = (f32[1024,128]{1,0:T(8,128)S(1)}, f32[1024,128]{1,0:T(8,128)}) fusion(f32[1027,128]{1,0:T(8,128)S(1)} %maximum_convert_fusion.1, f32[128]{0:T(128)S(1)} %get-tuple-element.73, f32[1024]{0:T(1024)S(1)} %get-tuple-element.58, f32[128]{0:T(128)S(1)} %get-tuple-element.74, f32[1024]{0:T(1024)S(1)} %get-tuple-element.59, ...), kind=kLoop, calls=%fused_computation.101 | loop fusion | flops 1835008 | bytes 3160064 | tf_op jit(solution)/shard_map/jit(silu)/mul | solution.py:202
  21.5 1.0 %copy.200 = f32[1024,128]{0,1:T(8,128)} copy(f32[1024,128]{1,0:T(8,128)S(1)} %get-tuple-element.30) | data formatting | bytes 1048576 | tf_op jit(solution)/shard_map/jit(silu)/mul | solution.py:202
  23.6 1.2 %copy.240 = f32[4,256,2,64]{1,3,0,2:T(8,128)} copy(f32[4,256,2,64]{3,2,1,0:T(2,128)S(1)} %reshape.426) | data formatting | bytes 1048576 | tf_op jit(solution)/shard_map/transpose | solution.py:204
  24.9 1.0 %fusion.37 = (f32[1024,256]{1,0:T(8,128)S(1)}, f32[1024,256]{1,0:T(8,128)S(1)}) fusion(f32[1027,256]{1,0:T(8,128)S(1)} %maximum_convert_fusion, f32[256]{0:T(256)S(1)} %bitcast.360, f32[1024]{0:T(1024)S(1)} %get-tuple-element.58, f32[256]{0:T(256)S(1)} %bitcast.362, f32[1024]{0:T(1024)S(1)} %get-tuple-element.59, f32[256]{0:T(256)S(1)} %bitcast.358, ...), kind=kLoop, calls=%fused_computation.56 | loop fusion | flops 3670016 | bytes 6307840 | tf_op jit(solution)/shard_map/jit(silu)/mul | solution.py:203
  26.0 1.0 %copy-done.1 = f32[1024,128]{0,1:T(8,128)S(1)} copy-done((f32[1024,128]{0,1:T(8,128)S(1)}, f32[1024,128]{0,1:T(8,128)}, u32[]{:S(2)}) %copy-start.1) | copy-done | bytes 524312
  27.0 0.7 convolution_bitcast_fusion.6
  27.6 0.7 convolution_bitcast_fusion.5
  28.6 0.9 select_select_fusion
  29.4 4.6 %all-to-all-start = ((f32[4,2,8320]{2,1,0:T(2,128)}), f32[4,2,8320]{2,1,0:T(2,128)S(1)}, u32[]{:S(2)}, u32[]{:S(2)}) async-start(f32[4,2,8320]{2,1,0:T(2,128)} %select_select_fusion), calls=%async_computation | async-start | bytes 532480 | tf_op jit(solution)/shard_map/all_to_all | solution.py:139
  34.6 0.6 copy-done.7
  35.4 4.5 %fusion.17 = (f32[2,4,256]{2,1,0:T(4,128)}, f32[2,4,256]{2,1,0:T(4,128)}, f32[4,256,256]{1,2,0:T(8,128)}, f32[2,4,256,256]{2,3,1,0:T(8,128)}) fusion(f32[4,256,256]{1,2,0:T(8,128)S(1)} %copy-done.7, f32[2,4,256]{2,1,0:T(4,128)S(1)} %bitcast.354, f32[4,256,256]{1,2,0:T(8,128)S(1)} %fusion.141, pred[4,256,256]{1,2,0:T(8,128)(4,1)S(1)} %copy-done.18, ...), kind=kOutput, calls=%fused_computation.24 | convolution fusion | flops 207351808 | bytes 6316032 | tf_op jit(solution)/shard_map/transpose(jvp(hbij,hbjp->hbip))/dot_general | solution.py:155
  41.0 0.7 slice_bitcast_fusion.1
  42.2 0.7 fusion.125
  44.0 0.7 slice_bitcast_fusion.3
  45.3 1.0 %convolution_add_fusion = f32[4,256,128]{2,1,0:T(8,128)S(1)} fusion(f32[4,256,128]{2,1,0:T(8,128)S(1)} %convolution_bitcast_fusion.1, f32[4,256,256]{1,2,0:T(8,128)S(1)} %copy-done, f32[4,256,128]{2,1,0:T(8,128)S(1)} %bitcast.336), kind=kOutput, calls=%fused_computation.15 | convolution fusion | flops 201457664 | bytes 2621440 | tf_op jit(solution)/shard_map/transpose(jvp(bin,bjn->bij))/dot_general | solution.py:155
  48.6 0.8 fusion.12
  49.9 1.4 %reshape.425 = f32[1024,128]{1,0:T(8,128)} reshape(f32[4,256,2,64]{3,2,1,0:T(2,128)S(1)} %copy.237) | data formatting | bytes 1048576 | tf_op jit(solution)/shard_map/reshape | solution.py:242
  51.3 1.4 %multiply_multiply_fusion = f32[1024,128]{1,0:T(8,128)S(1)} fusion(f32[1024,128]{1,0:T(8,128)} %reshape.425, f32[1024,128]{1,0:T(8,128)} %get-tuple-element.31), kind=kLoop, calls=%fused_computation.98 | loop fusion | flops 1048576 | bytes 1572864 | tf_op jit(solution)/shard_map/mul | solution.py:244
  52.7 0.7 pad_maximum_fusion.7
  53.4 2.3 %collective-permute-start.1 = (f32[3,384]{1,0:T(4,128)S(1)}, f32[3,384]{1,0:T(4,128)S(1)}, u32[]{:S(2)}, u32[]{:S(2)}) collective-permute-start(f32[3,384]{1,0:T(4,128)S(1)} %pad_maximum_fusion.7), channel_id=1, source_target_pairs={{64,0},{128,64},{192,128},{65,1},{129,65},{193,129},{66,2},{130,66... | collective-permute-start | bytes 13832 | tf_op jit(solution)/shard_map/ppermute | solution.py:18
  55.8 3.2 %collective-permute-done.1 = f32[3,384]{1,0:T(4,128)S(1)} collective-permute-done((f32[3,384]{1,0:T(4,128)S(1)}, f32[3,384]{1,0:T(4,128)S(1)}, u32[]{:S(2)}, u32[]{:S(2)}) %collective-permute-start.1) | collective-permute-done | bytes 4640 | tf_op jit(solution)/shard_map/ppermute | solution.py:18
  59.5 2.1 %fusion.25 = f32[1024,256]{1,0:T(8,128)S(1)} fusion(f32[3,256]{1,0:T(4,128)S(1)} %slice.338, f32[1024,256]{1,0:T(8,128)S(1)} %maximum_multiply_fusion, f32[1024]{0:T(1024)S(1)} %copy-done.20, f32[1024]{0:T(1024)} %get-tuple-element.57, f32[1024]{0:T(1024)S(1)} %copy-done.19, f32[256]{0:T(256)} %bitcast.361, f32[256]{0:T(256)} %bitcast.363, f32[256]{0:T(256)} %bitcast.359, ...), kind=kLoop, calls=%fused_computation.37 | loop fusion | flops 3407872 | bytes 2116608 | tf_op jit(solution)/shard_map/add | solution.py:97
  61.7 0.8 dynamic-slice_bitcast_fusion
  62.5 1.3 %copy.227 = f32[2,4,1]{2,1,0:T(4,128)} copy(f32[2,4,1]{1,0,2:T(2,128)} %bitcast.365) | data formatting | bytes 64 | tf_op jit(solution)/shard_map/transpose(jvp())/reshape | solution.py:161
  63.8 0.8 collective-permute-done.2
  64.6 0.9 bitcast_add_fusion
  65.6 11.3 %all-to-all-start.1 = ((f32[32,16,256]{2,1,0:T(8,128)}), f32[32,16,256]{2,1,0:T(8,128)S(1)}, u32[]{:S(2)}, u32[]{:S(2)}) async-start(f32[32,16,256]{2,1,0:T(8,128)} %bitcast_add_fusion), calls=%async_computation.1 | async-start | bytes 1048576 | tf_op jit(solution)/shard_map/all_to_all | solution.py:256
  77.0 0.9 fusion.98
  78.0 1.5 %fusion.92 = (f32[2]{0:T(128)S(1)}, f32[2]{0:T(128)S(1)}) fusion(f32[1,2,64,128]{3,2,1,0:T(8,128)} %get-tuple-element.44, f32[1,2,64,128]{3,2,1,0:T(8,128)} %get-tuple-element.48, f32[1,2,64,128]{3,2,1,0:T(8,128)} %get-tuple-element.43, f32[2,8320]{1,0:T(2,128)} %copy-done.13, f32[2,8320]{1,0:T(2,128)} %copy-done.12, f32[2]{0:T(128)} %get-tuple-element.19, ...), kind=kLoop, calls=%fused_computation.139 | loop fusion | flops 262140 | bytes 524336 | tf_op jit(solution)/shard_map/transpose(jvp())/reduce_sum | solution.py:174
  79.8 0.7 multiply_bitcast_fusion
  80.6 1.4 %fusion.18 = f32[2,4,256]{2,0,1:T(2,128)S(1)} fusion(f32[4,256,128,1]{2,1,3,0:T(8,128)S(1)} %bitcast.340, bf16[4,256,2,64]{1,0,3,2:T(4,128)(2,1)S(1)} %reshape.404, f32[2,1,64,128]{3,2,0,1:T(8,128)} %copy-done.8, f32[2,1,64,128]{3,2,0,1:T(8,128)} %copy-done.9, f32[2,1,64,128]{3,2,0,1:T(8,128)} %copy-done.10, f32[2,1,64,128]{3,2,0,1:T(8,128)} %bitcast.350), kind=kOutput, calls=%fused_computation.25 | convolution fusion | flops 101251072 | bytes 1056768 | tf_op jit(solution)/shard_map/jvp(bin,hbpn->hbip)/dot_general | solution.py:155
  82.3 0.6 copy.260
  83.0 1.3 %fusion.46 = f32[1024,128]{1,0:T(8,128)} fusion(f32[3,128]{1,0:T(4,128)S(1)} %slice-done, f32[1024,128]{1,0:T(8,128)S(1)} %multiply_multiply_fusion, f32[1024]{0:T(1024)S(1)} %copy-done.20, f32[1024]{0:T(1024)S(1)} %copy-done.21, f32[1024]{0:T(1024)S(1)} %copy-done.19, f32[128]{0:T(128)S(1)} %copy-done.46, f32[128]{0:T(128)S(1)} %copy-done.48, ...), kind=kLoop, calls=%fused_computation.69 | loop fusion | flops 1703936 | bytes 1064448 | tf_op jit(solution)/shard_map/add | solution.py:97
  84.2 9.7 %all-to-all-done.1 = f32[32,16,256]{2,1,0:T(8,128)S(1)} async-done(((f32[32,16,256]{2,1,0:T(8,128)}), f32[32,16,256]{2,1,0:T(8,128)S(1)}, u32[]{:S(2)}, u32[]{:S(2)}) %all-to-all-start.1) | async-done | bytes 524320 | tf_op jit(solution)/shard_map/all_to_all | solution.py:256
  94.0 0.6 reduce_sum.128
  (173 shorter events, 12.5 us)
Async XLA Ops:
  0.6 19.5 %copy-start.16 = (bf16[1024,128]{1,0:T(8,128)(2,1)S(1)}, bf16[1024,128]{1,0:T(8,128)(2,1)}, u32[]{:S(2)}) copy-start(bf16[1024,128]{1,0:T(8,128)(2,1)} %param.7) | copy-start | bytes 786436
  0.6 19.1 %copy-start.17 = (bf16[1024,128]{1,0:T(8,128)(2,1)S(1)}, bf16[1024,128]{1,0:T(8,128)(2,1)}, u32[]{:S(2)}) copy-start(bf16[1024,128]{1,0:T(8,128)(2,1)} %param.13) | copy-start | bytes 786436
  2.1 18.0 %collective-permute-start = (bf16[3,384]{1,0:T(4,128)(2,1)S(1)}, bf16[3,384]{1,0:T(4,128)(2,1)S(1)}, u32[]{:S(2)}, u32[]{:S(2)}) collective-permute-start(bf16[3,384]{1,0:T(4,128)(2,1)S(1)} %pad_maximum_fusion.8), channel_id=1, source_target_pairs={{0,64},{64,128},{128,192},{1,65},{65,129},{129,193},{2,66},{66,130... | collective-permute-start | bytes 6920 | tf_op jit(solution)/shard_map/ppermute | solution.py:18
  14.4 7.0 %copy-start.41 = (f32[128]{0:T(128)}, f32[128]{0:T(128)S(1)}, u32[]{:S(2)}) copy-start(f32[128]{0:T(128)S(1)} %get-tuple-element.71) | copy-start | bytes 1540
  14.4 7.0 %copy-start.43 = (f32[128]{0:T(128)}, f32[128]{0:T(128)S(1)}, u32[]{:S(2)}) copy-start(f32[128]{0:T(128)S(1)} %get-tuple-element.72) | copy-start | bytes 1540
  14.4 7.0 %copy-start.45 = (f32[128]{0:T(128)}, f32[128]{0:T(128)S(1)}, u32[]{:S(2)}) copy-start(f32[128]{0:T(128)S(1)} %get-tuple-element.73) | copy-start | bytes 1540
  14.4 7.0 %copy-start.47 = (f32[128]{0:T(128)}, f32[128]{0:T(128)S(1)}, u32[]{:S(2)}) copy-start(f32[128]{0:T(128)S(1)} %get-tuple-element.74) | copy-start | bytes 1540
  15.3 9.6 %copy-start.33 = (f32[1,256]{1,0:T(1,128)}, f32[1,256]{1,0:T(1,128)S(1)}, u32[]{:S(2)}) copy-start(f32[1,256]{1,0:T(1,128)S(1)} %get-tuple-element.67) | copy-start | bytes 3076
  15.3 9.6 %copy-start.34 = (f32[1,256]{1,0:T(1,128)}, f32[1,256]{1,0:T(1,128)S(1)}, u32[]{:S(2)}) copy-start(f32[1,256]{1,0:T(1,128)S(1)} %get-tuple-element.68) | copy-start | bytes 3076
  15.3 9.6 %copy-start.35 = (f32[1,256]{1,0:T(1,128)}, f32[1,256]{1,0:T(1,128)S(1)}, u32[]{:S(2)}) copy-start(f32[1,256]{1,0:T(1,128)S(1)} %get-tuple-element.69) | copy-start | bytes 3076
  15.3 9.6 %copy-start.36 = (f32[1,256]{1,0:T(1,128)}, f32[1,256]{1,0:T(1,128)S(1)}, u32[]{:S(2)}) copy-start(f32[1,256]{1,0:T(1,128)S(1)} %get-tuple-element.70) | copy-start | bytes 3076
  16.1 3.1 %copy-start.40 = (f32[4]{0:T(128)}, f32[4]{0:T(128)S(1)}, u32[]{:S(2)}) copy-start(f32[4]{0:T(128)S(1)} %get-tuple-element.28) | copy-start | bytes 52
  16.1 3.0 %copy-start.50 = (f32[4,256]{1,0:T(4,128)}, f32[4,256]{1,0:T(4,128)S(1)}, u32[]{:S(2)}) copy-start(f32[4,256]{1,0:T(4,128)S(1)} %get-tuple-element.66) | copy-start | bytes 12292
  16.1 26.0 %copy-start.22 = (f32[4,256]{1,0:T(4,128)}, f32[4,256]{1,0:T(4,128)S(1)}, u32[]{:S(2)}) copy-start(f32[4,256]{1,0:T(4,128)S(1)} %get-tuple-element.65) | copy-start | bytes 12292
  16.5 25.7 %copy-start.27 = (f32[2,4]{1,0:T(2,128)}, f32[2,4]{1,0:T(2,128)S(1)}, u32[]{:S(2)}) copy-start(f32[2,4]{1,0:T(2,128)S(1)} %slice_reduce_fusion) | copy-start | bytes 100
  17.3 23.7 %copy-start.29 = (f32[2]{0:T(128)}, f32[2]{0:T(128)S(1)}, u32[]{:S(2)}) copy-start(f32[2]{0:T(128)S(1)} %get-tuple-element.20) | copy-start | bytes 28
  17.3 23.7 %copy-start.31 = (f32[2]{0:T(128)}, f32[2]{0:T(128)S(1)}, u32[]{:S(2)}) copy-start(f32[2]{0:T(128)S(1)} %get-tuple-element.21) | copy-start | bytes 28
  28.3 6.3 %copy-start.18 = (pred[4,256,256]{1,2,0:T(8,128)(4,1)S(1)}, pred[4,256,256]{1,2,0:T(8,128)(4,1)}, u32[]{:S(2)}) copy-start(pred[4,256,256]{1,2,0:T(8,128)(4,1)} %get-tuple-element.49) | copy-start | bytes 786436
  29.4 10.9 %all-to-all-start = ((f32[4,2,8320]{2,1,0:T(2,128)}), f32[4,2,8320]{2,1,0:T(2,128)S(1)}, u32[]{:S(2)}, u32[]{:S(2)}) async-start(f32[4,2,8320]{2,1,0:T(2,128)} %select_select_fusion), calls=%async_computation | async-start | bytes 532480 | tf_op jit(solution)/shard_map/all_to_all | solution.py:139
  35.4 5.6 %copy-start.38 = (f32[2]{0:T(128)S(1)}, f32[2]{0:T(128)}, u32[]{:S(2)}) copy-start(f32[2]{0:T(128)} %get-tuple-element.18) | copy-start | bytes 28
  40.3 3.0 %copy-start.5 = (f32[2,4,64,128]{3,2,0,1:T(8,128)}, f32[2,4,64,128]{3,2,0,1:T(8,128)S(1)}, u32[]{:S(2)}) copy-start(f32[2,4,64,128]{3,2,0,1:T(8,128)S(1)} %convolution_bitcast_fusion.4) | copy-start | bytes 786436
  41.0 3.0 %copy-start.12 = (f32[2,8320]{1,0:T(2,128)}, f32[2,8320]{1,0:T(2,128)S(1)}, u32[]{:S(2)}) copy-start(f32[2,8320]{1,0:T(2,128)S(1)} %get-tuple-element.8) | copy-start | bytes 199684
  41.0 3.0 %copy-start.13 = (f32[2,8320]{1,0:T(2,128)}, f32[2,8320]{1,0:T(2,128)S(1)}, u32[]{:S(2)}) copy-start(f32[2,8320]{1,0:T(2,128)S(1)} %get-tuple-element.9) | copy-start | bytes 199684
  42.9 2.4 %copy-start = (f32[4,256,256]{1,2,0:T(8,128)S(1)}, f32[4,256,256]{1,2,0:T(8,128)}, u32[]{:S(2)}) copy-start(f32[4,256,256]{1,2,0:T(8,128)} %get-tuple-element.5) | copy-start | bytes 3145732
  43.9 2.4 %copy-start.11 = (f32[1,2,64,128]{3,2,1,0:T(8,128)}, f32[1,2,64,128]{3,2,1,0:T(8,128)S(1)}, u32[]{:S(2)}) copy-start(f32[1,2,64,128]{3,2,1,0:T(8,128)S(1)} %copy.328) | copy-start | bytes 196612
  44.7 2.3 %copy-start.8 = (f32[2,1,64,128]{3,2,0,1:T(8,128)}, f32[2,1,64,128]{3,2,0,1:T(8,128)S(1)}, u32[]{:S(2)}) copy-start(f32[2,1,64,128]{3,2,0,1:T(8,128)S(1)} %get-tuple-element.45) | copy-start | bytes 196612
  44.7 2.3 %copy-start.9 = (f32[2,1,64,128]{3,2,0,1:T(8,128)}, f32[2,1,64,128]{3,2,0,1:T(8,128)S(1)}, u32[]{:S(2)}) copy-start(f32[2,1,64,128]{3,2,0,1:T(8,128)S(1)} %get-tuple-element.46) | copy-start | bytes 196612
  44.7 2.3 %copy-start.10 = (f32[2,1,64,128]{3,2,0,1:T(8,128)}, f32[2,1,64,128]{3,2,0,1:T(8,128)S(1)}, u32[]{:S(2)}) copy-start(f32[2,1,64,128]{3,2,0,1:T(8,128)S(1)} %get-tuple-element.47) | copy-start | bytes 196612
  49.4 10.2 %copy-start.19 = (f32[1024]{0:T(1024)S(1)}, f32[1024]{0:T(1024)}, u32[]{:S(2)}) copy-start(f32[1024]{0:T(1024)} %get-tuple-element.53) | copy-start | bytes 12292
  49.4 10.2 %copy-start.20 = (f32[1024]{0:T(1024)S(1)}, f32[1024]{0:T(1024)}, u32[]{:S(2)}) copy-start(f32[1024]{0:T(1024)} %get-tuple-element.56) | copy-start | bytes 12292
  53.4 5.5 %collective-permute-start.1 = (f32[3,384]{1,0:T(4,128)S(1)}, f32[3,384]{1,0:T(4,128)S(1)}, u32[]{:S(2)}, u32[]{:S(2)}) collective-permute-start(f32[3,384]{1,0:T(4,128)S(1)} %pad_maximum_fusion.7), channel_id=1, source_target_pairs={{64,0},{128,64},{192,128},{65,1},{129,65},{193,129},{66,2},{130,66... | collective-permute-start | bytes 13832 | tf_op jit(solution)/shard_map/ppermute | solution.py:18
  61.6 15.3 %copy-start.4 = (f32[2,4,64,128]{3,2,0,1:T(8,128)S(1)}, f32[2,4,64,128]{3,2,0,1:T(8,128)}, u32[]{:S(2)}) copy-start(f32[2,4,64,128]{3,2,0,1:T(8,128)} %copy-done.3) | copy-start | bytes 786436
  61.6 15.3 %copy-start.6 = (f32[2,4,64,128]{3,2,0,1:T(8,128)S(1)}, f32[2,4,64,128]{3,2,0,1:T(8,128)}, u32[]{:S(2)}) copy-start(f32[2,4,64,128]{3,2,0,1:T(8,128)} %copy-done.5) | copy-start | bytes 786436
  62.5 2.1 %collective-permute-start.2 = (f32[32,16,256]{2,1,0:T(8,128)}, f32[32,16,256]{2,1,0:T(8,128)S(1)}, u32[]{:S(2)}, u32[]{:S(2)}) collective-permute-start(f32[32,16,256]{2,1,0:T(8,128)} %dynamic-slice_bitcast_fusion), channel_id=1, source_target_pairs={{0,1},{1,0},{2,3},{3,2},{4,5},{5,4},{6,7},{7,6},{8,9},{9,8},{10,11... | collective-permute-start | bytes 1572872 | tf_op jit(solution)/shard_map/ppermute | solution.py:255
  65.5 16.5 %copy-start.23 = (f32[4,256]{1,0:T(4,128)S(1)}, f32[4,256]{1,0:T(4,128)}, u32[]{:S(2)}) copy-start(f32[4,256]{1,0:T(4,128)} %copy-done.22) | copy-start | bytes 12292
  65.5 16.5 %copy-start.26 = (f32[2,4,256]{2,0,1:T(2,128)S(1)}, f32[2,4,256]{2,0,1:T(2,128)}, u32[]{:S(2)}) copy-start(f32[2,4,256]{2,0,1:T(2,128)} %copy-done.25) | copy-start | bytes 24580
  65.5 16.5 %copy-start.28 = (f32[2,4]{1,0:T(2,128)S(1)}, f32[2,4]{1,0:T(2,128)}, u32[]{:S(2)}) copy-start(f32[2,4]{1,0:T(2,128)} %copy-done.27) | copy-start | bytes 100
  65.5 16.5 %copy-start.49 = (f32[2,4,1]{2,1,0:T(4,128)S(1)}, f32[2,4,1]{2,1,0:T(4,128)}, u32[]{:S(2)}) copy-start(f32[2,4,1]{2,1,0:T(4,128)} %copy.227) | copy-start | bytes 100
  65.5 16.5 %copy-start.51 = (f32[4,256]{1,0:T(4,128)S(1)}, f32[4,256]{1,0:T(4,128)}, u32[]{:S(2)}) copy-start(f32[4,256]{1,0:T(4,128)} %copy-done.50) | copy-start | bytes 12292
  65.5 16.5 %copy-start.52 = (f32[2,4,256]{2,1,0:T(4,128)S(1)}, f32[2,4,256]{2,1,0:T(4,128)}, u32[]{:S(2)}) copy-start(f32[2,4,256]{2,1,0:T(4,128)} %get-tuple-element.3) | copy-start | bytes 24580
  65.5 16.5 %copy-start.53 = (f32[2,4,256]{2,1,0:T(4,128)S(1)}, f32[2,4,256]{2,1,0:T(4,128)}, u32[]{:S(2)}) copy-start(f32[2,4,256]{2,1,0:T(4,128)} %get-tuple-element.4) | copy-start | bytes 24580
  65.5 17.4 %copy-start.21 = (f32[1024]{0:T(1024)S(1)}, f32[1024]{0:T(1024)}, u32[]{:S(2)}) copy-start(f32[1024]{0:T(1024)} %get-tuple-element.57) | copy-start | bytes 12292
  65.6 17.4 %slice-start = ((f32[3,384]{1,0:T(4,128)}), f32[3,128]{1,0:T(4,128)S(1)}, s32[]{:S(2)}) async-start(f32[3,384]{1,0:T(4,128)} %copy-done.37), calls=%async_computation.2 | async-start | bytes 4096 | tf_op jit(solution)/shard_map/slice | solution.py:247
  65.6 17.4 %copy-start.42 = (f32[128]{0:T(128)S(1)}, f32[128]{0:T(128)}, u32[]{:S(2)}) copy-start(f32[128]{0:T(128)} %copy-done.41) | copy-start | bytes 1540
  65.6 17.4 %copy-start.44 = (f32[128]{0:T(128)S(1)}, f32[128]{0:T(128)}, u32[]{:S(2)}) copy-start(f32[128]{0:T(128)} %copy-done.43) | copy-start | bytes 1540
  65.6 17.4 %copy-start.46 = (f32[128]{0:T(128)S(1)}, f32[128]{0:T(128)}, u32[]{:S(2)}) copy-start(f32[128]{0:T(128)} %copy-done.45) | copy-start | bytes 1540
  65.6 17.4 %copy-start.48 = (f32[128]{0:T(128)S(1)}, f32[128]{0:T(128)}, u32[]{:S(2)}) copy-start(f32[128]{0:T(128)} %copy-done.47) | copy-start | bytes 1540
  65.6 28.4 %all-to-all-start.1 = ((f32[32,16,256]{2,1,0:T(8,128)}), f32[32,16,256]{2,1,0:T(8,128)S(1)}, u32[]{:S(2)}, u32[]{:S(2)}) async-start(f32[32,16,256]{2,1,0:T(8,128)} %bitcast_add_fusion), calls=%async_computation.1 | async-start | bytes 1048576 | tf_op jit(solution)/shard_map/all_to_all | solution.py:256
  (12 other events, 18.6 us)

commit v12 on v11

--- a/solution.py
+++ b/solution.py
@@ -217,16 +217,20 @@
     log_rows = log_decay.astype(jnp.float32)
     x_rows = v_x.reshape(tok_rows, head_count, P_SIZE)
     g_rows = grad_out.astype(jnp.float32).reshape(tok_rows, head_count, P_SIZE)
-    shard_cumul = running_sum(log_rows)
+    block_cumul = running_sum(log_blocks)
+    offsets = [jnp.zeros_like(block_cumul[:, 0, -1])]
+    for block in range(block_count - 1):
+        offsets.append(offsets[-1] + block_cumul[:, block, -1])
+    shard_cumul = (block_cumul + jnp.stack(offsets, axis=1)[:, :, None]).reshape(head_count, tok_rows)
     keep = jnp.exp(shard_cumul[:, -1]) * (note_ids[-1] == note_before)
     leave_rows = jnp.exp(shard_cumul[:, -1:] - shard_cumul) * (note_ids == note_ids[-1])
     entry_rows = jnp.exp(shard_cumul) * (note_ids == note_before)
     local_state = jnp.einsum(
-        "thp,ht,tn->hpn", x_rows, leave_rows, v_bc[:, :N], precision=precise,
+        "thp,ht,tn->hpn", x_rows, leave_rows, v_bc[:, :N], precision=lax.Precision.HIGH,
         preferred_element_type=jnp.float32,
     )
     local_adjoint = jnp.einsum(
-        "thp,ht,tn->hpn", g_rows, entry_rows, v_bc[:, N:], precision=precise,
+        "thp,ht,tn->hpn", g_rows, entry_rows, v_bc[:, N:], precision=lax.Precision.HIGH,
         preferred_element_type=jnp.float32,
     )
     state_in, adjoint_in = chain_both(local_state, local_adjoint, keep, "seq")

time: 96.3 us -> 94.9 us (0.985)
  matrix products: 14.3 us -> 12.4 us
    dot_general x3 -> x2, matrix products: 1.8 us -> 0.44 us  [running_sum(): jnp.dot(values, upper, precision=precise, preferred_element_type=jnp.floa...]
    unnamed x114 -> x116, local copies, waits for them, and re-layouts: 3.93 us -> 4.02 us
where the time goes in v12:
time: 94.9 us; the launch traced here: 93.2 us
  other arithmetic  22.7 us (24%)
  starting transfers between devices  21.8 us (23%)
  local copies, waits for them, and re-layouts  19.7 us (21%)
  waiting for transfers between devices  13.7 us (14%)
  matrix products  12.4 us (13%)
  between operations  2.87 us (3%)
    all_to_all x1, starting transfers between devices, local(): grad_pre_bc = lax.all_to_all(pair_sum, 'chip', 0, 0, tiled=False).sum(0)  11.3 us
    dot_general x11, matrix products, einsum(): jnp.einsum(spec, *operands, precision=lax.Precision.HIGH, preferred_eleme...  11.2 us
    all_to_all x1, waiting for transfers between devices, local(): grad_pre_bc = lax.all_to_all(pair_sum, 'chip', 0, 0, tiled=False).sum(0)  9.71 us
    ppermute x2, starting transfers between devices, shifted(): lax.ppermute(value, axis, [(source, source + steps) for source in range(i...  5.85 us
    all_to_all x1, starting transfers between devices, chain_both(): arrived = lax.all_to_all(outgoing, axis, 0, 0, tiled=False)  4.62 us
    unnamed x116, local copies, waits for them, and re-layouts  4.02 us
    add x2, other arithmetic, conv_backward(): result + weights[k][None, :] * extended[lag:lag + count] * linked[:, None]  3.38 us
    ppermute x2, waiting for transfers between devices, shifted(): lax.ppermute(value, axis, [(source, source + steps) for source in range(i...  3.13 us
  transfers between devices with their start and end apart: 5, of which 3 were waited for; matrix products, arithmetic and copies ran while one was open for 28% of the time, Pallas kernels for 0%

profile of v12, /device:TPU:8, one launch (start us, length us, event | category | flops | bytes accessed | tf_op | source)
XLA Modules:
  0.0 93.2 jit_solution(4426178319807763533)
XLA Ops:
  0.6 0.7 slice.249
  1.4 0.7 slice.250
  2.1 3.5 %collective-permute-start = (bf16[3,384]{1,0:T(4,128)(2,1)S(1)}, bf16[3,384]{1,0:T(4,128)(2,1)S(1)}, u32[]{:S(2)}, u32[]{:S(2)}) collective-permute-start(bf16[3,384]{1,0:T(4,128)(2,1)S(1)} %pad_maximum_fusion.8), channel_id=1, source_target_pairs={{0,64},{64,128},{128,192},{1,65},{65,129},{129,193},{2,66},{66,130... | collective-permute-start | bytes 6920 | tf_op jit(solution)/shard_map/ppermute | solution.py:18
  5.6 0.8 reduce-window.9
  6.4 0.7 bitcast_subtract_fusion.1
  8.2 0.7 compare_convert_fusion.4
  9.0 0.7 reshape.439
  11.6 2.0 %fusion.118 = (f32[1024]{0:T(1024)}, f32[1024]{0:T(1024)S(1)}, f32[1024]{0:T(1024)S(1)}, f32[1024]{0:T(1024)}, f32[1024]{0:T(1024)}, /*index=5*/f32[1024]{0:T(1024)S(1)}, f32[1024]{0:T(1024)S(1)}, f32[1024]{0:T(1024)S(1)}) fusion(s32[1030]{0:T(1024)S(1)} %broadcast_add_fusion, s32[]{:T(128)} %bitcast.11, s32[]{:T(128)} %bitcast.17), kind=kLoop, calls=%fused_computation.204 | loop fusion | flops 16384 | bytes 61448 | tf_op jit(solution)/shard_map/convert_element_type | solution.py:97
  13.6 0.8 slice_bitcast_fusion.11
  14.4 0.8 fusion.138
  15.4 0.8 slice_reduce_fusion.11
  16.6 1.4 %compare_and_fusion = (pred[4,256,256]{1,2,0:T(8,128)(4,1)}, f32[4,256,256]{1,2,0:T(8,128)}) fusion(s32[4,256]{1,0:T(4,128)S(1)} %reshape.443, pred[256,256]{0,1:T(8,128)(4,1)S(1)} %iota_compare_fusion), kind=kLoop, calls=%fused_computation.54 | loop fusion | flops 786432 | bytes 1380352 | tf_op jit(solution)/shard_map/jvp()/and | solution.py:165
  19.3 1.3 %fusion.64 = (f32[1024,128]{1,0:T(8,128)S(1)}, f32[1024,128]{1,0:T(8,128)}) fusion(f32[1027,128]{1,0:T(8,128)S(1)} %maximum_convert_fusion.1, f32[128]{0:T(128)S(1)} %get-tuple-element.76, f32[1024]{0:T(1024)S(1)} %get-tuple-element.61, f32[128]{0:T(128)S(1)} %get-tuple-element.77, f32[1024]{0:T(1024)S(1)} %get-tuple-element.62, ...), kind=kLoop, calls=%fused_computation.98 | loop fusion | flops 1835008 | bytes 3160064 | tf_op jit(solution)/shard_map/jit(silu)/mul | solution.py:202
  20.5 1.0 %copy.212 = f32[1024,128]{0,1:T(8,128)} copy(f32[1024,128]{1,0:T(8,128)S(1)} %get-tuple-element.33) | data formatting | bytes 1048576 | tf_op jit(solution)/shard_map/jit(silu)/mul | solution.py:202
  21.5 0.6 reshape.466
  22.6 1.2 %copy.254 = f32[4,256,2,64]{1,3,0,2:T(8,128)} copy(f32[4,256,2,64]{3,2,1,0:T(2,128)S(1)} %reshape.466) | data formatting | bytes 1048576 | tf_op jit(solution)/shard_map/transpose | solution.py:204
  24.0 1.0 %fusion.35 = (f32[1024,256]{1,0:T(8,128)S(1)}, f32[1024,256]{1,0:T(8,128)S(1)}) fusion(f32[1027,256]{1,0:T(8,128)S(1)} %maximum_convert_fusion, f32[256]{0:T(256)S(1)} %bitcast.376, f32[1024]{0:T(1024)S(1)} %get-tuple-element.61, f32[256]{0:T(256)S(1)} %bitcast.378, f32[1024]{0:T(1024)S(1)} %get-tuple-element.62, f32[256]{0:T(256)S(1)} %bitcast.374, ...), kind=kLoop, calls=%fused_computation.53 | loop fusion | flops 3670016 | bytes 6307840 | tf_op jit(solution)/shard_map/jit(silu)/mul | solution.py:203
  25.1 1.0 %copy-done.1 = f32[1024,128]{0,1:T(8,128)S(1)} copy-done((f32[1024,128]{0,1:T(8,128)S(1)}, f32[1024,128]{0,1:T(8,128)}, u32[]{:S(2)}) %copy-start.1) | copy-done | bytes 524312
  27.1 0.9 select_select_fusion
  28.0 4.6 %all-to-all-start = ((f32[4,2,8320]{2,1,0:T(2,128)}), f32[4,2,8320]{2,1,0:T(2,128)S(1)}, u32[]{:S(2)}, u32[]{:S(2)}) async-start(f32[4,2,8320]{2,1,0:T(2,128)} %select_select_fusion), calls=%async_computation | async-start | bytes 532480 | tf_op jit(solution)/shard_map/all_to_all | solution.py:139
  33.2 0.6 copy-done.7
  34.0 4.5 %fusion.16 = (f32[2,4,256]{2,1,0:T(4,128)}, f32[2,4,256]{2,1,0:T(4,128)}, f32[4,256,256]{1,2,0:T(8,128)}, f32[2,4,256,256]{2,3,1,0:T(8,128)}) fusion(f32[4,256,256]{1,2,0:T(8,128)S(1)} %copy-done.7, f32[2,4,256]{2,1,0:T(4,128)S(1)} %bitcast.368, f32[4,256,256]{1,2,0:T(8,128)S(1)} %fusion.139, pred[4,256,256]{1,2,0:T(8,128)(4,1)S(1)} %copy-done.18, ...), kind=kOutput, calls=%fused_computation.22 | convolution fusion | flops 207351808 | bytes 6316032 | tf_op jit(solution)/shard_map/transpose(jvp(hbij,hbjp->hbip))/dot_general | solution.py:155
  39.6 0.7 slice_bitcast_fusion.1
  40.7 0.7 fusion.123
  41.8 0.6 convolution_bitcast_fusion.2
  42.5 0.7 slice_bitcast_fusion.3
  43.2 0.6 convolution_bitcast_fusion.1
  43.8 1.0 %convolution_add_fusion = f32[4,256,128]{2,1,0:T(8,128)S(1)} fusion(f32[4,256,128]{2,1,0:T(8,128)S(1)} %convolution_bitcast_fusion.1, f32[4,256,256]{1,2,0:T(8,128)S(1)} %copy-done, f32[4,256,128]{2,1,0:T(8,128)S(1)} %bitcast.349), kind=kOutput, calls=%fused_computation.13 | convolution fusion | flops 201457664 | bytes 2621440 | tf_op jit(solution)/shard_map/transpose(jvp(bin,bjn->bij))/dot_general | solution.py:155
  47.1 0.8 fusion.11
  48.5 1.4 %reshape.465 = f32[1024,128]{1,0:T(8,128)} reshape(f32[4,256,2,64]{3,2,1,0:T(2,128)S(1)} %copy.251) | data formatting | bytes 1048576 | tf_op jit(solution)/shard_map/reshape | solution.py:246
  49.9 1.4 %multiply_multiply_fusion = f32[1024,128]{1,0:T(8,128)S(1)} fusion(f32[1024,128]{1,0:T(8,128)} %reshape.465, f32[1024,128]{1,0:T(8,128)} %get-tuple-element.34), kind=kLoop, calls=%fused_computation.95 | loop fusion | flops 1048576 | bytes 1572864 | tf_op jit(solution)/shard_map/mul | solution.py:248
  51.3 0.7 pad_maximum_fusion.7
  52.0 2.4 %collective-permute-start.1 = (f32[3,384]{1,0:T(4,128)S(1)}, f32[3,384]{1,0:T(4,128)S(1)}, u32[]{:S(2)}, u32[]{:S(2)}) collective-permute-start(f32[3,384]{1,0:T(4,128)S(1)} %pad_maximum_fusion.7), channel_id=1, source_target_pairs={{64,0},{128,64},{192,128},{65,1},{129,65},{193,129},{66,2},{130,66... | collective-permute-start | bytes 13832 | tf_op jit(solution)/shard_map/ppermute | solution.py:18
  54.3 3.1 %collective-permute-done.1 = f32[3,384]{1,0:T(4,128)S(1)} collective-permute-done((f32[3,384]{1,0:T(4,128)S(1)}, f32[3,384]{1,0:T(4,128)S(1)}, u32[]{:S(2)}, u32[]{:S(2)}) %collective-permute-start.1) | collective-permute-done | bytes 4640 | tf_op jit(solution)/shard_map/ppermute | solution.py:18
  58.1 2.1 %fusion.23 = f32[1024,256]{1,0:T(8,128)S(1)} fusion(f32[3,256]{1,0:T(4,128)S(1)} %slice.353, f32[1024,256]{1,0:T(8,128)S(1)} %maximum_multiply_fusion, f32[1024]{0:T(1024)S(1)} %copy-done.20, f32[1024]{0:T(1024)} %get-tuple-element.60, f32[1024]{0:T(1024)S(1)} %copy-done.19, f32[256]{0:T(256)} %bitcast.377, f32[256]{0:T(256)} %bitcast.379, f32[256]{0:T(256)} %bitcast.375, ...), kind=kLoop, calls=%fused_computation.34 | loop fusion | flops 3407872 | bytes 2116608 | tf_op jit(solution)/shard_map/add | solution.py:97
  60.2 0.8 dynamic-slice_bitcast_fusion
  61.1 1.3 %copy.241 = f32[2,4,1]{2,1,0:T(4,128)} copy(f32[2,4,1]{1,0,2:T(2,128)} %bitcast.382) | data formatting | bytes 64 | tf_op jit(solution)/shard_map/transpose(jvp())/reshape | solution.py:161
  62.4 0.8 collective-permute-done.2
  63.2 0.9 bitcast_add_fusion
  64.2 11.3 %all-to-all-start.1 = ((f32[32,16,256]{2,1,0:T(8,128)}), f32[32,16,256]{2,1,0:T(8,128)S(1)}, u32[]{:S(2)}, u32[]{:S(2)}) async-start(f32[32,16,256]{2,1,0:T(8,128)} %bitcast_add_fusion), calls=%async_computation.1 | async-start | bytes 1048576 | tf_op jit(solution)/shard_map/all_to_all | solution.py:260
  75.5 0.9 fusion.96
  76.6 1.5 %fusion.90 = (f32[2]{0:T(128)S(1)}, f32[2]{0:T(128)S(1)}) fusion(f32[1,2,64,128]{3,2,1,0:T(8,128)} %get-tuple-element.47, f32[1,2,64,128]{3,2,1,0:T(8,128)} %get-tuple-element.51, f32[1,2,64,128]{3,2,1,0:T(8,128)} %get-tuple-element.46, f32[2,8320]{1,0:T(2,128)} %copy-done.13, f32[2,8320]{1,0:T(2,128)} %copy-done.12, f32[2]{0:T(128)} %get-tuple-element.20, ...), kind=kLoop, calls=%fused_computation.136 | loop fusion | flops 262140 | bytes 524336 | tf_op jit(solution)/shard_map/transpose(jvp())/reduce_sum | solution.py:174
  78.3 0.8 multiply_bitcast_fusion
  79.2 1.4 %fusion.17 = f32[2,4,256]{2,0,1:T(2,128)S(1)} fusion(f32[4,256,128,1]{2,1,3,0:T(8,128)S(1)} %bitcast.353, bf16[4,256,2,64]{1,0,3,2:T(4,128)(2,1)S(1)} %reshape.444, f32[2,1,64,128]{3,2,0,1:T(8,128)} %copy-done.8, f32[2,1,64,128]{3,2,0,1:T(8,128)} %copy-done.9, f32[2,1,64,128]{3,2,0,1:T(8,128)} %copy-done.10, f32[2,1,64,128]{3,2,0,1:T(8,128)} %bitcast.363), kind=kOutput, calls=%fused_computation.23 | convolution fusion | flops 101251072 | bytes 1056768 | tf_op jit(solution)/shard_map/jvp(bin,hbpn->hbip)/dot_general | solution.py:155
  80.9 0.6 copy.276
  81.6 1.3 %fusion.44 = f32[1024,128]{1,0:T(8,128)} fusion(f32[3,128]{1,0:T(4,128)S(1)} %slice-done, f32[1024,128]{1,0:T(8,128)S(1)} %multiply_multiply_fusion, f32[1024]{0:T(1024)S(1)} %copy-done.20, f32[1024]{0:T(1024)S(1)} %copy-done.21, f32[1024]{0:T(1024)S(1)} %copy-done.19, f32[128]{0:T(128)S(1)} %copy-done.46, f32[128]{0:T(128)S(1)} %copy-done.48, ...), kind=kLoop, calls=%fused_computation.66 | loop fusion | flops 1703936 | bytes 1064448 | tf_op jit(solution)/shard_map/add | solution.py:97
  82.8 9.7 %all-to-all-done.1 = f32[32,16,256]{2,1,0:T(8,128)S(1)} async-done(((f32[32,16,256]{2,1,0:T(8,128)}), f32[32,16,256]{2,1,0:T(8,128)S(1)}, u32[]{:S(2)}, u32[]{:S(2)}) %all-to-all-start.1) | async-done | bytes 524320 | tf_op jit(solution)/shard_map/all_to_all | solution.py:260
  92.5 0.6 reduce_sum.128
  (181 shorter events, 12.0 us)
Async XLA Ops:
  0.6 18.6 %copy-start.16 = (bf16[1024,128]{1,0:T(8,128)(2,1)S(1)}, bf16[1024,128]{1,0:T(8,128)(2,1)}, u32[]{:S(2)}) copy-start(bf16[1024,128]{1,0:T(8,128)(2,1)} %param.7) | copy-start | bytes 786436
  0.6 18.2 %copy-start.17 = (bf16[1024,128]{1,0:T(8,128)(2,1)S(1)}, bf16[1024,128]{1,0:T(8,128)(2,1)}, u32[]{:S(2)}) copy-start(bf16[1024,128]{1,0:T(8,128)(2,1)} %param.13) | copy-start | bytes 786436
  2.1 17.1 %collective-permute-start = (bf16[3,384]{1,0:T(4,128)(2,1)S(1)}, bf16[3,384]{1,0:T(4,128)(2,1)S(1)}, u32[]{:S(2)}, u32[]{:S(2)}) collective-permute-start(bf16[3,384]{1,0:T(4,128)(2,1)S(1)} %pad_maximum_fusion.8), channel_id=1, source_target_pairs={{0,64},{64,128},{128,192},{1,65},{65,129},{129,193},{2,66},{66,130... | collective-permute-start | bytes 6920 | tf_op jit(solution)/shard_map/ppermute | solution.py:18
  8.9 6.4 %copy-start.40 = (f32[4]{0:T(128)}, f32[4]{0:T(128)S(1)}, u32[]{:S(2)}) copy-start(f32[4]{0:T(128)S(1)} %get-tuple-element.31) | copy-start | bytes 52
  9.0 6.3 %copy-start.50 = (f32[4,256]{1,0:T(4,128)}, f32[4,256]{1,0:T(4,128)S(1)}, u32[]{:S(2)}) copy-start(f32[4,256]{1,0:T(4,128)S(1)} %get-tuple-element.69) | copy-start | bytes 12292
  9.0 31.7 %copy-start.22 = (f32[4,256]{1,0:T(4,128)}, f32[4,256]{1,0:T(4,128)S(1)}, u32[]{:S(2)}) copy-start(f32[4,256]{1,0:T(4,128)S(1)} %get-tuple-element.68) | copy-start | bytes 12292
  10.1 30.6 %copy-start.27 = (f32[2,4]{1,0:T(2,128)}, f32[2,4]{1,0:T(2,128)S(1)}, u32[]{:S(2)}) copy-start(f32[2,4]{1,0:T(2,128)S(1)} %slice_reduce_fusion) | copy-start | bytes 100
  14.4 6.1 %copy-start.41 = (f32[128]{0:T(128)}, f32[128]{0:T(128)S(1)}, u32[]{:S(2)}) copy-start(f32[128]{0:T(128)S(1)} %get-tuple-element.74) | copy-start | bytes 1540
  14.4 6.1 %copy-start.43 = (f32[128]{0:T(128)}, f32[128]{0:T(128)S(1)}, u32[]{:S(2)}) copy-start(f32[128]{0:T(128)S(1)} %get-tuple-element.75) | copy-start | bytes 1540
  14.4 6.1 %copy-start.45 = (f32[128]{0:T(128)}, f32[128]{0:T(128)S(1)}, u32[]{:S(2)}) copy-start(f32[128]{0:T(128)S(1)} %get-tuple-element.76) | copy-start | bytes 1540
  14.4 6.1 %copy-start.47 = (f32[128]{0:T(128)}, f32[128]{0:T(128)S(1)}, u32[]{:S(2)}) copy-start(f32[128]{0:T(128)S(1)} %get-tuple-element.77) | copy-start | bytes 1540
  15.3 8.6 %copy-start.33 = (f32[1,256]{1,0:T(1,128)}, f32[1,256]{1,0:T(1,128)S(1)}, u32[]{:S(2)}) copy-start(f32[1,256]{1,0:T(1,128)S(1)} %get-tuple-element.70) | copy-start | bytes 3076
  15.3 8.6 %copy-start.34 = (f32[1,256]{1,0:T(1,128)}, f32[1,256]{1,0:T(1,128)S(1)}, u32[]{:S(2)}) copy-start(f32[1,256]{1,0:T(1,128)S(1)} %get-tuple-element.71) | copy-start | bytes 3076
  15.3 8.6 %copy-start.35 = (f32[1,256]{1,0:T(1,128)}, f32[1,256]{1,0:T(1,128)S(1)}, u32[]{:S(2)}) copy-start(f32[1,256]{1,0:T(1,128)S(1)} %get-tuple-element.72) | copy-start | bytes 3076
  15.3 8.6 %copy-start.36 = (f32[1,256]{1,0:T(1,128)}, f32[1,256]{1,0:T(1,128)S(1)}, u32[]{:S(2)}) copy-start(f32[1,256]{1,0:T(1,128)S(1)} %get-tuple-element.73) | copy-start | bytes 3076
  16.1 23.4 %copy-start.29 = (f32[2]{0:T(128)}, f32[2]{0:T(128)S(1)}, u32[]{:S(2)}) copy-start(f32[2]{0:T(128)S(1)} %get-tuple-element.21) | copy-start | bytes 28
  16.1 23.4 %copy-start.31 = (f32[2]{0:T(128)}, f32[2]{0:T(128)S(1)}, u32[]{:S(2)}) copy-start(f32[2]{0:T(128)S(1)} %get-tuple-element.22) | copy-start | bytes 28
  26.9 6.3 %copy-start.18 = (pred[4,256,256]{1,2,0:T(8,128)(4,1)S(1)}, pred[4,256,256]{1,2,0:T(8,128)(4,1)}, u32[]{:S(2)}) copy-start(pred[4,256,256]{1,2,0:T(8,128)(4,1)} %get-tuple-element.52) | copy-start | bytes 786436
  28.0 10.8 %all-to-all-start = ((f32[4,2,8320]{2,1,0:T(2,128)}), f32[4,2,8320]{2,1,0:T(2,128)S(1)}, u32[]{:S(2)}, u32[]{:S(2)}) async-start(f32[4,2,8320]{2,1,0:T(2,128)} %select_select_fusion), calls=%async_computation | async-start | bytes 532480 | tf_op jit(solution)/shard_map/all_to_all | solution.py:139
  34.0 5.6 %copy-start.38 = (f32[2]{0:T(128)S(1)}, f32[2]{0:T(128)}, u32[]{:S(2)}) copy-start(f32[2]{0:T(128)} %get-tuple-element.19) | copy-start | bytes 28
  38.8 3.0 %copy-start.5 = (f32[2,4,64,128]{3,2,0,1:T(8,128)}, f32[2,4,64,128]{3,2,0,1:T(8,128)S(1)}, u32[]{:S(2)}) copy-start(f32[2,4,64,128]{3,2,0,1:T(8,128)S(1)} %convolution_bitcast_fusion.4) | copy-start | bytes 786436
  39.5 2.9 %copy-start.12 = (f32[2,8320]{1,0:T(2,128)}, f32[2,8320]{1,0:T(2,128)S(1)}, u32[]{:S(2)}) copy-start(f32[2,8320]{1,0:T(2,128)S(1)} %get-tuple-element.8) | copy-start | bytes 199684
  39.5 2.9 %copy-start.13 = (f32[2,8320]{1,0:T(2,128)}, f32[2,8320]{1,0:T(2,128)S(1)}, u32[]{:S(2)}) copy-start(f32[2,8320]{1,0:T(2,128)S(1)} %get-tuple-element.9) | copy-start | bytes 199684
  41.4 2.4 %copy-start = (f32[4,256,256]{1,2,0:T(8,128)S(1)}, f32[4,256,256]{1,2,0:T(8,128)}, u32[]{:S(2)}) copy-start(f32[4,256,256]{1,2,0:T(8,128)} %get-tuple-element.5) | copy-start | bytes 3145732
  42.5 2.4 %copy-start.11 = (f32[1,2,64,128]{3,2,1,0:T(8,128)}, f32[1,2,64,128]{3,2,1,0:T(8,128)S(1)}, u32[]{:S(2)}) copy-start(f32[1,2,64,128]{3,2,1,0:T(8,128)S(1)} %copy.344) | copy-start | bytes 196612
  43.2 2.3 %copy-start.8 = (f32[2,1,64,128]{3,2,0,1:T(8,128)}, f32[2,1,64,128]{3,2,0,1:T(8,128)S(1)}, u32[]{:S(2)}) copy-start(f32[2,1,64,128]{3,2,0,1:T(8,128)S(1)} %get-tuple-element.48) | copy-start | bytes 196612
  43.2 2.3 %copy-start.9 = (f32[2,1,64,128]{3,2,0,1:T(8,128)}, f32[2,1,64,128]{3,2,0,1:T(8,128)S(1)}, u32[]{:S(2)}) copy-start(f32[2,1,64,128]{3,2,0,1:T(8,128)S(1)} %get-tuple-element.49) | copy-start | bytes 196612
  43.2 2.3 %copy-start.10 = (f32[2,1,64,128]{3,2,0,1:T(8,128)}, f32[2,1,64,128]{3,2,0,1:T(8,128)S(1)}, u32[]{:S(2)}) copy-start(f32[2,1,64,128]{3,2,0,1:T(8,128)S(1)} %get-tuple-element.50) | copy-start | bytes 196612
  47.9 10.2 %copy-start.19 = (f32[1024]{0:T(1024)S(1)}, f32[1024]{0:T(1024)}, u32[]{:S(2)}) copy-start(f32[1024]{0:T(1024)} %get-tuple-element.56) | copy-start | bytes 12292
  47.9 10.2 %copy-start.20 = (f32[1024]{0:T(1024)S(1)}, f32[1024]{0:T(1024)}, u32[]{:S(2)}) copy-start(f32[1024]{0:T(1024)} %get-tuple-element.59) | copy-start | bytes 12292
  52.0 5.5 %collective-permute-start.1 = (f32[3,384]{1,0:T(4,128)S(1)}, f32[3,384]{1,0:T(4,128)S(1)}, u32[]{:S(2)}, u32[]{:S(2)}) collective-permute-start(f32[3,384]{1,0:T(4,128)S(1)} %pad_maximum_fusion.7), channel_id=1, source_target_pairs={{64,0},{128,64},{192,128},{65,1},{129,65},{193,129},{66,2},{130,66... | collective-permute-start | bytes 13832 | tf_op jit(solution)/shard_map/ppermute | solution.py:18
  60.2 15.3 %copy-start.4 = (f32[2,4,64,128]{3,2,0,1:T(8,128)S(1)}, f32[2,4,64,128]{3,2,0,1:T(8,128)}, u32[]{:S(2)}) copy-start(f32[2,4,64,128]{3,2,0,1:T(8,128)} %copy-done.3) | copy-start | bytes 786436
  60.2 15.3 %copy-start.6 = (f32[2,4,64,128]{3,2,0,1:T(8,128)S(1)}, f32[2,4,64,128]{3,2,0,1:T(8,128)}, u32[]{:S(2)}) copy-start(f32[2,4,64,128]{3,2,0,1:T(8,128)} %copy-done.5) | copy-start | bytes 786436
  61.1 2.1 %collective-permute-start.2 = (f32[32,16,256]{2,1,0:T(8,128)}, f32[32,16,256]{2,1,0:T(8,128)S(1)}, u32[]{:S(2)}, u32[]{:S(2)}) collective-permute-start(f32[32,16,256]{2,1,0:T(8,128)} %dynamic-slice_bitcast_fusion), channel_id=1, source_target_pairs={{0,1},{1,0},{2,3},{3,2},{4,5},{5,4},{6,7},{7,6},{8,9},{9,8},{10,11... | collective-permute-start | bytes 1572872 | tf_op jit(solution)/shard_map/ppermute | solution.py:259
  64.1 16.5 %copy-start.23 = (f32[4,256]{1,0:T(4,128)S(1)}, f32[4,256]{1,0:T(4,128)}, u32[]{:S(2)}) copy-start(f32[4,256]{1,0:T(4,128)} %copy-done.22) | copy-start | bytes 12292
  64.1 16.5 %copy-start.26 = (f32[2,4,256]{2,0,1:T(2,128)S(1)}, f32[2,4,256]{2,0,1:T(2,128)}, u32[]{:S(2)}) copy-start(f32[2,4,256]{2,0,1:T(2,128)} %copy-done.25) | copy-start | bytes 24580
  64.1 16.5 %copy-start.28 = (f32[2,4]{1,0:T(2,128)S(1)}, f32[2,4]{1,0:T(2,128)}, u32[]{:S(2)}) copy-start(f32[2,4]{1,0:T(2,128)} %copy-done.27) | copy-start | bytes 100
  64.1 16.5 %copy-start.49 = (f32[2,4,1]{2,1,0:T(4,128)S(1)}, f32[2,4,1]{2,1,0:T(4,128)}, u32[]{:S(2)}) copy-start(f32[2,4,1]{2,1,0:T(4,128)} %copy.241) | copy-start | bytes 100
  64.1 16.5 %copy-start.51 = (f32[4,256]{1,0:T(4,128)S(1)}, f32[4,256]{1,0:T(4,128)}, u32[]{:S(2)}) copy-start(f32[4,256]{1,0:T(4,128)} %copy-done.50) | copy-start | bytes 12292
  64.1 16.5 %copy-start.52 = (f32[2,4,256]{2,1,0:T(4,128)S(1)}, f32[2,4,256]{2,1,0:T(4,128)}, u32[]{:S(2)}) copy-start(f32[2,4,256]{2,1,0:T(4,128)} %get-tuple-element.3) | copy-start | bytes 24580
  64.1 16.5 %copy-start.53 = (f32[2,4,256]{2,1,0:T(4,128)S(1)}, f32[2,4,256]{2,1,0:T(4,128)}, u32[]{:S(2)}) copy-start(f32[2,4,256]{2,1,0:T(4,128)} %get-tuple-element.4) | copy-start | bytes 24580
  64.1 17.4 %copy-start.21 = (f32[1024]{0:T(1024)S(1)}, f32[1024]{0:T(1024)}, u32[]{:S(2)}) copy-start(f32[1024]{0:T(1024)} %get-tuple-element.60) | copy-start | bytes 12292
  64.1 17.4 %slice-start = ((f32[3,384]{1,0:T(4,128)}), f32[3,128]{1,0:T(4,128)S(1)}, s32[]{:S(2)}) async-start(f32[3,384]{1,0:T(4,128)} %copy-done.37), calls=%async_computation.2 | async-start | bytes 4096 | tf_op jit(solution)/shard_map/slice | solution.py:251
  64.1 17.4 %copy-start.42 = (f32[128]{0:T(128)S(1)}, f32[128]{0:T(128)}, u32[]{:S(2)}) copy-start(f32[128]{0:T(128)} %copy-done.41) | copy-start | bytes 1540
  64.1 17.4 %copy-start.44 = (f32[128]{0:T(128)S(1)}, f32[128]{0:T(128)}, u32[]{:S(2)}) copy-start(f32[128]{0:T(128)} %copy-done.43) | copy-start | bytes 1540
  64.2 17.4 %copy-start.46 = (f32[128]{0:T(128)S(1)}, f32[128]{0:T(128)}, u32[]{:S(2)}) copy-start(f32[128]{0:T(128)} %copy-done.45) | copy-start | bytes 1540
  64.2 17.4 %copy-start.48 = (f32[128]{0:T(128)S(1)}, f32[128]{0:T(128)}, u32[]{:S(2)}) copy-start(f32[128]{0:T(128)} %copy-done.47) | copy-start | bytes 1540
  64.2 28.4 %all-to-all-start.1 = ((f32[32,16,256]{2,1,0:T(8,128)}), f32[32,16,256]{2,1,0:T(8,128)S(1)}, u32[]{:S(2)}, u32[]{:S(2)}) async-start(f32[32,16,256]{2,1,0:T(8,128)} %bitcast_add_fusion), calls=%async_computation.1 | async-start | bytes 1048576 | tf_op jit(solution)/shard_map/all_to_all | solution.py:260
  (12 other events, 19.1 us)

commit v13 on v12

--- a/solution.py
+++ b/solution.py
@@ -247,8 +247,8 @@
     grad_v_bc = jnp.concatenate([grad_b.reshape(tok_rows, N), grad_c.reshape(tok_rows, N)], axis=1)
     grad_u_x = grad_v_x * silu_slope(u_x)
     grad_u_bc = grad_v_bc * silu_slope(u_bc)
-    after_both = shifted(jnp.concatenate([grad_u_x[:rim_width], grad_u_bc[:rim_width]], axis=1), "seq", -1)
-    after_x, after_bc = after_both[:, : grad_u_x.shape[1]], after_both[:, grad_u_x.shape[1] :]
+    after_bc = shifted(grad_u_bc[:rim_width], "seq", -1)
+    after_x = shifted(grad_u_x[:rim_width], "seq", -1)
     grad_pre_x = conv_backward(jnp.concatenate([grad_u_x, after_x]), conv_x, note_all[rim_width:])
     whole_bc = conv_backward(jnp.concatenate([grad_u_bc, after_bc]), conv_bc, note_all[rim_width:])
     chips, cores = lax.axis_size("chip"), lax.axis_size("core")

time: 94.9 us -> 94.1 us (level)
  local copies, waits for them, and re-layouts: 19.7 us -> 14.9 us
  starting transfers between devices: 21.8 us -> 24.7 us
  matrix products: 12.4 us -> 14.8 us
  waiting for transfers between devices: 13.7 us -> 11.4 us
    all_to_all x1, waiting for transfers between devices: 9.71 us -> 6.32 us  [local(): grad_pre_bc = lax.all_to_all(pair_sum, 'chip', 0, 0, tiled=False).sum(0)]
    ppermute x2 -> x3, starting transfers between devices: 5.85 us -> 8.65 us  [shifted(): lax.ppermute(value, axis, [(source, source + steps) for source in range(i...]
    reshape x2 -> x0, local copies, waits for them, and re-layouts: 1.95 us -> none  [local(): grad_x_heads.transpose(1, 2, 0, 3).reshape(tok_rows, head_count * P_SIZE)]
    ppermute x2 -> x3, waiting for transfers between devices: 3.13 us -> 5.07 us  [shifted(): lax.ppermute(value, axis, [(source, source + steps) for source in range(i...]
    dot_general x11, matrix products: 11.2 us -> 12.6 us  [einsum(): jnp.einsum(spec, *operands, precision=lax.Precision.HIGH, preferred_eleme...]
    mul x1, other arithmetic: 0.08 us -> 1.35 us  [block_forward_all(): jnp.exp(cumul[..., -1:] - cumul) * (note_blocks == note_blocks[:, -1:])]
    broadcast_in_dim x4, local copies, waits for them, and re-layouts: 0.38 us -> 1.63 us  [block_forward_all(): state = through[:, block, None, None] * state + chunk[:, block]]
    mul x1, other arithmetic: 1.39 us -> 0.19 us  [local(): grad_u_x = grad_v_x * silu_slope(u_x)]
  transfers between devices with their start and end apart: 5 -> 6, of which waited for: 3 -> 3; matrix products, arithmetic and copies ran while one was open for 28% -> 36% of each run, Pallas kernels for 0% -> 0%
where the time goes in v13:
time: 94.1 us; the launch traced here: 92.3 us
  starting transfers between devices  24.7 us (26%)
  other arithmetic  23.5 us (25%)
  local copies, waits for them, and re-layouts  14.9 us (16%)
  matrix products  14.8 us (16%)
  waiting for transfers between devices  11.4 us (12%)
  between operations  2.99 us (3%)
    dot_general x11, matrix products, einsum(): jnp.einsum(spec, *operands, precision=lax.Precision.HIGH, preferred_eleme...  12.6 us
    all_to_all x1, starting transfers between devices, local(): grad_pre_bc = lax.all_to_all(pair_sum, 'chip', 0, 0, tiled=False).sum(0)  11.3 us
    ppermute x3, starting transfers between devices, shifted(): lax.ppermute(value, axis, [(source, source + steps) for source in range(i...  8.65 us
    all_to_all x1, waiting for transfers between devices, local(): grad_pre_bc = lax.all_to_all(pair_sum, 'chip', 0, 0, tiled=False).sum(0)  6.32 us
    ppermute x3, waiting for transfers between devices, shifted(): lax.ppermute(value, axis, [(source, source + steps) for source in range(i...  5.07 us
    all_to_all x1, starting transfers between devices, chain_both(): arrived = lax.all_to_all(outgoing, axis, 0, 0, tiled=False)  4.62 us
    reduce_sum x2, other arithmetic, block_forward_all(): state = through[:, block, None, None] * state + chunk[:, block]  3.24 us
    unnamed x119, local copies, waits for them, and re-layouts  3.01 us
  transfers between devices with their start and end apart: 6, of which 3 were waited for; matrix products, arithmetic and copies ran while one was open for 36% of the time, Pallas kernels for 0%

profile of v13, /device:TPU:8, one launch (start us, length us, event | category | flops | bytes accessed | tf_op | source)
XLA Modules:
  0.0 92.3 jit_solution(362703447402734624)
XLA Ops:
  0.7 0.8 slice.244
  1.4 0.7 slice.243
  2.1 3.5 %collective-permute-start = (bf16[3,384]{1,0:T(4,128)(2,1)S(1)}, bf16[3,384]{1,0:T(4,128)(2,1)S(1)}, u32[]{:S(2)}, u32[]{:S(2)}) collective-permute-start(bf16[3,384]{1,0:T(4,128)(2,1)S(1)} %pad_maximum_fusion.7), channel_id=1, source_target_pairs={{0,64},{64,128},{128,192},{1,65},{65,129},{129,193},{2,66},{66,130... | collective-permute-start | bytes 6920 | tf_op jit(solution)/shard_map/ppermute | solution.py:18
  5.6 0.8 reduce-window.9
  6.5 0.7 bitcast_subtract_fusion.1
  7.7 0.6 fusion.140
  8.3 2.0 %fusion.121 = (f32[1024]{0:T(1024)}, f32[1024]{0:T(1024)S(1)}, f32[1024]{0:T(1024)S(1)}, f32[1024]{0:T(1024)}, f32[1024]{0:T(1024)}, /*index=5*/f32[1024]{0:T(1024)S(1)}, f32[1024]{0:T(1024)S(1)}, f32[1024]{0:T(1024)S(1)}) fusion(s32[1030]{0:T(1024)S(1)} %broadcast_add_fusion, s32[]{:T(128)} %bitcast.11, s32[]{:T(128)} %bitcast.17), kind=kLoop, calls=%fused_computation.208 | loop fusion | flops 16384 | bytes 61448 | tf_op jit(solution)/shard_map/convert_element_type | solution.py:97
  11.6 0.7 compare_convert_fusion.4
  12.4 0.7 reshape.439
  14.1 0.8 fusion.141
  15.0 0.8 slice_bitcast_fusion.11
  15.8 0.7 slice_reduce_fusion.8
  16.6 1.4 %compare_and_fusion = (pred[4,256,256]{1,2,0:T(8,128)(4,1)}, f32[4,256,256]{1,2,0:T(8,128)}) fusion(s32[4,256]{1,0:T(4,128)S(1)} %reshape.443, pred[256,256]{0,1:T(8,128)(4,1)S(1)} %iota_compare_fusion), kind=kLoop, calls=%fused_computation.54 | loop fusion | flops 786432 | bytes 1380352 | tf_op jit(solution)/shard_map/jvp()/and | solution.py:165
  18.4 0.6 pad.56.clone
  19.6 1.8 %fusion.35 = (f32[1024,256]{1,0:T(8,128)S(1)}, f32[1024,256]{1,0:T(8,128)}) fusion(f32[1027,256]{1,0:T(8,128)S(1)} %maximum_convert_fusion, f32[256]{0:T(256)S(1)} %bitcast.385, f32[1024]{0:T(1024)S(1)} %get-tuple-element.79, f32[256]{0:T(256)S(1)} %bitcast.387, f32[1024]{0:T(1024)S(1)} %get-tuple-element.80, f32[256]{0:T(256)S(1)} %bitcast.383, ...), kind=kLoop, calls=%fused_computation.53 | loop fusion | flops 3670016 | bytes 6307840 | tf_op jit(solution)/shard_map/jit(silu)/mul | solution.py:203
  21.7 1.4 %fusion.65 = (f32[1024,128]{0,1:T(8,128)S(1)}, f32[1024,128]{0,1:T(8,128)}) fusion(f32[1027,128]{0,1:T(8,128)S(1)} %maximum_convert_fusion.1, f32[128]{0:T(128)S(1)} %get-tuple-element.94, f32[1024]{0:T(1024)S(1)} %get-tuple-element.79, f32[128]{0:T(128)S(1)} %get-tuple-element.95, f32[1024]{0:T(1024)S(1)} %get-tuple-element.80, ...), kind=kLoop, calls=%fused_computation.101 | loop fusion | flops 1835008 | bytes 3160064 | tf_op jit(solution)/shard_map/jit(silu)/mul | solution.py:202
  23.7 1.4 %convolution_bitcast_fusion.5 = f32[1,2,64,128]{3,2,1,0:T(8,128)S(1)} fusion(bf16[1024,2,64]{0,2,1:T(8,128)(2,1)} %bitcast.366, f32[2,1024]{1,0:T(2,128)S(1)} %get-tuple-element.83, f32[1024,256]{1,0:T(8,128)S(1)} %get-tuple-element.53), kind=kOutput, calls=%fused_computation.26 | convolution fusion | flops 100925440 | bytes 860160 | tf_op jit(solution)/shard_map/thp,ht,tn->hpn/dot_general | solution.py:232
  25.4 0.9 select_select_fusion
  26.2 4.6 %all-to-all-start = ((f32[4,2,8320]{2,1,0:T(2,128)}), f32[4,2,8320]{2,1,0:T(2,128)S(1)}, u32[]{:S(2)}, u32[]{:S(2)}) async-start(f32[4,2,8320]{2,1,0:T(2,128)} %select_select_fusion), calls=%async_computation | async-start | bytes 532480 | tf_op jit(solution)/shard_map/all_to_all | solution.py:139
  31.5 5.1 %fusion.16 = (f32[2,4,256]{2,1,0:T(4,128)}, f32[2,4,256]{2,1,0:T(4,128)}, f32[4,256,256]{1,2,0:T(8,128)S(1)}, f32[2,4,256,256]{2,3,1,0:T(8,128)}) fusion(f32[4,256,256]{1,2,0:T(8,128)} %get-tuple-element.71, f32[2,4,256]{2,1,0:T(4,128)S(1)} %bitcast.377, f32[4,256,256]{1,2,0:T(8,128)S(1)} %fusion.142, pred[4,256,256]{1,2,0:T(8,128)(4,1)S(1)} %copy-done.18, ...), kind=kOutput, calls=%fused_computation.22 | convolution fusion | flops 207351808 | bytes 6316032 | tf_op jit(solution)/shard_map/transpose(jvp(hbij,hbjp->hbip))/dot_general | solution.py:155
  37.7 0.7 slice_bitcast_fusion.1
  38.9 0.7 fusion.126
  40.1 0.6 convolution_bitcast_fusion.2
  40.8 0.7 slice_bitcast_fusion.3
  42.2 0.6 convolution_bitcast_fusion.1
  42.8 1.0 %convolution_add_fusion = f32[4,256,128]{2,1,0:T(8,128)S(1)} fusion(f32[4,256,128]{2,1,0:T(8,128)S(1)} %convolution_bitcast_fusion.1, f32[4,256,256]{1,2,0:T(8,128)S(1)} %get-tuple-element.23, f32[4,256,128]{2,1,0:T(8,128)S(1)} %bitcast.356), kind=kOutput, calls=%fused_computation.13 | convolution fusion | flops 201457664 | bytes 2621440 | tf_op jit(solution)/shard_map/transpose(jvp(bin,bjn->bij))/dot_general | solution.py:155
  44.3 2.7 %collective-permute-start.2 = (f32[3,256]{1,0:T(4,128)S(1)}, f32[3,256]{1,0:T(4,128)S(1)}, u32[]{:S(2)}, u32[]{:S(2)}) collective-permute-start(f32[3,256]{1,0:T(4,128)S(1)} %slice.343), channel_id=1, source_target_pairs={{64,0},{128,64},{192,128},{65,1},{129,65},{193,129},{66,2},{130,66... | collective-permute-start | bytes 9224 | tf_op jit(solution)/shard_map/ppermute | solution.py:18
  46.9 2.8 %collective-permute-done.2 = f32[3,256]{1,0:T(4,128)S(1)} collective-permute-done((f32[3,256]{1,0:T(4,128)S(1)}, f32[3,256]{1,0:T(4,128)S(1)}, u32[]{:S(2)}, u32[]{:S(2)}) %collective-permute-start.2) | collective-permute-done | bytes 3104 | tf_op jit(solution)/shard_map/ppermute | solution.py:18
  49.8 0.6 copy-done.48
  50.4 2.3 %fusion.23 = f32[1024,256]{1,0:T(8,128)S(1)} fusion(f32[3,256]{1,0:T(4,128)} %copy-done.48, f32[1024,256]{1,0:T(8,128)S(1)} %maximum_multiply_fusion, f32[1024]{0:T(1024)S(1)} %copy-done.20, f32[1024]{0:T(1024)} %get-tuple-element.78, f32[1024]{0:T(1024)S(1)} %copy-done.19, f32[256]{0:T(256)} %bitcast.386, f32[256]{0:T(256)} %bitcast.388, f32[256]{0:T(256)} %bitcast.384, ...), kind=kLoop, calls=%fused_computation.34 | loop fusion | flops 3407872 | bytes 2116608 | tf_op jit(solution)/shard_map/add | solution.py:97
  52.9 1.4 %fusion.102 = f32[4,256,2]{1,0,2:T(4,128)} fusion(f32[256,2,4]{0,2,1:T(4,128)S(1)} %get-tuple-element.105, f32[4,256]{1,0:T(4,128)} %copy-done.22, f32[4,2]{0,1:T(2,128)} %bitcast.380), kind=kLoop, calls=%fused_computation.174 | loop fusion | flops 4096 | bytes 20512 | tf_op jit(solution)/shard_map/jvp()/mul | solution.py:161
  54.2 1.3 %copy.220 = f32[4,256,2]{1,2,0:T(2,128)} copy(f32[4,256,2]{1,0,2:T(4,128)} %fusion.102) | data formatting | bytes 16384 | tf_op jit(solution)/shard_map/jvp()/mul | solution.py:161
  55.5 1.7 %fusion.99 = (f32[2]{0:T(128)}, f32[2]{0:T(128)}) fusion(f32[2,4,64,128]{3,2,0,1:T(8,128)} %copy-done.3, f32[2]{0:T(128)} %copy-done.29, f32[1,2,64,128]{3,1,2,0:T(2,128)S(1)} %slice_bitcast_fusion.7, f32[2]{0:T(128)} %copy-done.38, f32[2,4,64,128]{3,2,0,1:T(8,128)} %copy-done.4, f32[1,2,64,128]{3,1,2,0:T(2,128)S(1)} %slice_bitcast_fusion.6, ...), kind=kLoop, calls=%fused_computation.153 | loop fusion | flops 196604 | bytes 393264 | tf_op jit(solution)/shard_map/transpose(jvp())/reduce_sum | solution.py:174
  57.2 0.7 copy.233
  57.9 0.7 copy.234
  58.7 1.5 %fusion.93 = (f32[2]{0:T(128)S(1)}, f32[2]{0:T(128)S(1)}) fusion(f32[1,2,64,128]{3,2,1,0:T(8,128)} %get-tuple-element.65, f32[1,2,64,128]{3,2,1,0:T(8,128)} %get-tuple-element.69, f32[1,2,64,128]{3,2,1,0:T(8,128)} %get-tuple-element.64, f32[2,8320]{1,0:T(2,128)} %copy-done.13, f32[2,8320]{1,0:T(2,128)} %copy-done.14, f32[2]{0:T(128)} %get-tuple-element.37, ...), kind=kLoop, calls=%fused_computation.141 | loop fusion | flops 262140 | bytes 524336 | tf_op jit(solution)/shard_map/transpose(jvp())/reduce_sum | solution.py:174
  60.4 0.8 multiply_bitcast_fusion
  61.3 0.8 copy.238
  62.0 0.9 bitcast_add_fusion
  62.9 11.3 %all-to-all-start.1 = ((f32[32,16,256]{2,1,0:T(8,128)}), f32[32,16,256]{2,1,0:T(8,128)S(1)}, u32[]{:S(2)}, u32[]{:S(2)}) async-start(f32[32,16,256]{2,1,0:T(8,128)} %bitcast_add_fusion), calls=%async_computation.1 | async-start | bytes 1048576 | tf_op jit(solution)/shard_map/all_to_all | solution.py:260
  74.2 2.4 %fusion.11 = f32[4,256,2,64]{1,3,2,0:T(8,128)S(1)} fusion(f32[2,4,256,256]{2,3,1,0:T(8,128)} %get-tuple-element.55, f32[4,2,64,256]{3,2,1,0:T(8,128)S(1)} %get-tuple-element.107, bf16[2,4,256,64]{2,1,3,0:T(4,128)(2,1)S(1)} %bitcast.362, f32[4,256,2]{1,2,0:T(2,128)S(1)} %copy-done.24), kind=kOutput, calls=%fused_computation.19 | convolution fusion | flops 201588736 | bytes 3416064 | tf_op jit(solution)/shard_map/transpose(jvp(hbij,hbjp->hbip))/dot_general | solution.py:155
  77.5 2.5 %collective-permute-start.1 = (f32[3,128]{0,1:T(8,128)S(1)}, f32[3,128]{0,1:T(8,128)S(1)}, u32[]{:S(2)}, u32[]{:S(2)}) collective-permute-start(f32[3,128]{0,1:T(8,128)S(1)} %slice.330), channel_id=1, source_target_pairs={{64,0},{128,64},{192,128},{65,1},{129,65},{193,129},{66,2},{130,66... | collective-permute-start | bytes 4616 | tf_op jit(solution)/shard_map/ppermute | solution.py:18
  80.8 0.6 copy.271
  81.4 2.2 %collective-permute-done.1 = f32[3,128]{0,1:T(8,128)S(1)} collective-permute-done((f32[3,128]{0,1:T(8,128)S(1)}, f32[3,128]{0,1:T(8,128)S(1)}, u32[]{:S(2)}, u32[]{:S(2)}) %collective-permute-start.1) | collective-permute-done | bytes 1568 | tf_op jit(solution)/shard_map/ppermute | solution.py:18
  83.7 0.6 fusion.41
  84.3 1.0 %copy.240 = f32[1024,128]{1,0:T(8,128)} copy(f32[1024,128]{0,1:T(8,128)S(1)} %fusion.41) | data formatting | bytes 1048576
  85.3 6.3 %all-to-all-done.1 = f32[32,16,256]{2,1,0:T(8,128)S(1)} async-done(((f32[32,16,256]{2,1,0:T(8,128)}), f32[32,16,256]{2,1,0:T(8,128)S(1)}, u32[]{:S(2)}, u32[]{:S(2)}) %all-to-all-start.1) | async-done | bytes 524320 | tf_op jit(solution)/shard_map/all_to_all | solution.py:260
  91.6 0.6 reduce_sum.128
  (179 shorter events, 9.1 us)
Async XLA Ops:
  0.6 18.7 %copy-start.15 = (bf16[1024,256]{1,0:T(8,128)(2,1)S(1)}, bf16[1024,256]{1,0:T(8,128)(2,1)}, u32[]{:S(2)}) copy-start(bf16[1024,256]{1,0:T(8,128)(2,1)} %param.8) | copy-start | bytes 1572868
  0.6 17.4 %copy-start.16 = (bf16[1024,128]{1,0:T(8,128)(2,1)S(1)}, bf16[1024,128]{1,0:T(8,128)(2,1)}, u32[]{:S(2)}) copy-start(bf16[1024,128]{1,0:T(8,128)(2,1)} %param.7) | copy-start | bytes 786436
  0.7 17.6 %copy-start.17 = (bf16[1024,128]{1,0:T(8,128)(2,1)S(1)}, bf16[1024,128]{1,0:T(8,128)(2,1)}, u32[]{:S(2)}) copy-start(bf16[1024,128]{1,0:T(8,128)(2,1)} %param.13) | copy-start | bytes 786436
  2.1 17.1 %collective-permute-start = (bf16[3,384]{1,0:T(4,128)(2,1)S(1)}, bf16[3,384]{1,0:T(4,128)(2,1)S(1)}, u32[]{:S(2)}, u32[]{:S(2)}) collective-permute-start(bf16[3,384]{1,0:T(4,128)(2,1)S(1)} %pad_maximum_fusion.7), channel_id=1, source_target_pairs={{0,64},{64,128},{128,192},{1,65},{65,129},{129,193},{2,66},{66,130... | collective-permute-start | bytes 6920 | tf_op jit(solution)/shard_map/ppermute | solution.py:18
  12.3 7.2 %copy-start.39 = (f32[4]{0:T(128)}, f32[4]{0:T(128)S(1)}, u32[]{:S(2)}) copy-start(f32[4]{0:T(128)S(1)} %get-tuple-element.51) | copy-start | bytes 52
  12.4 26.6 %copy-start.22 = (f32[4,256]{1,0:T(4,128)}, f32[4,256]{1,0:T(4,128)S(1)}, u32[]{:S(2)}) copy-start(f32[4,256]{1,0:T(4,128)S(1)} %get-tuple-element.86) | copy-start | bytes 12292
  13.6 25.3 %copy-start.27 = (f32[2,4]{1,0:T(2,128)}, f32[2,4]{1,0:T(2,128)S(1)}, u32[]{:S(2)}) copy-start(f32[2,4]{1,0:T(2,128)S(1)} %slice_reduce_fusion) | copy-start | bytes 100
  14.9 4.7 %copy-start.33 = (f32[1,256]{1,0:T(1,128)}, f32[1,256]{1,0:T(1,128)S(1)}, u32[]{:S(2)}) copy-start(f32[1,256]{1,0:T(1,128)S(1)} %get-tuple-element.88) | copy-start | bytes 3076
  14.9 4.7 %copy-start.34 = (f32[1,256]{1,0:T(1,128)}, f32[1,256]{1,0:T(1,128)S(1)}, u32[]{:S(2)}) copy-start(f32[1,256]{1,0:T(1,128)S(1)} %get-tuple-element.89) | copy-start | bytes 3076
  14.9 4.7 %copy-start.35 = (f32[1,256]{1,0:T(1,128)}, f32[1,256]{1,0:T(1,128)S(1)}, u32[]{:S(2)}) copy-start(f32[1,256]{1,0:T(1,128)S(1)} %get-tuple-element.90) | copy-start | bytes 3076
  15.0 4.7 %copy-start.36 = (f32[1,256]{1,0:T(1,128)}, f32[1,256]{1,0:T(1,128)S(1)}, u32[]{:S(2)}) copy-start(f32[1,256]{1,0:T(1,128)S(1)} %get-tuple-element.91) | copy-start | bytes 3076
  15.8 5.9 %copy-start.40 = (f32[128]{0:T(128)}, f32[128]{0:T(128)S(1)}, u32[]{:S(2)}) copy-start(f32[128]{0:T(128)S(1)} %get-tuple-element.92) | copy-start | bytes 1540
  15.8 5.9 %copy-start.42 = (f32[128]{0:T(128)}, f32[128]{0:T(128)S(1)}, u32[]{:S(2)}) copy-start(f32[128]{0:T(128)S(1)} %get-tuple-element.93) | copy-start | bytes 1540
  15.8 5.9 %copy-start.44 = (f32[128]{0:T(128)}, f32[128]{0:T(128)S(1)}, u32[]{:S(2)}) copy-start(f32[128]{0:T(128)S(1)} %get-tuple-element.94) | copy-start | bytes 1540
  15.8 5.9 %copy-start.46 = (f32[128]{0:T(128)}, f32[128]{0:T(128)S(1)}, u32[]{:S(2)}) copy-start(f32[128]{0:T(128)S(1)} %get-tuple-element.95) | copy-start | bytes 1540
  16.6 21.1 %copy-start.29 = (f32[2]{0:T(128)}, f32[2]{0:T(128)S(1)}, u32[]{:S(2)}) copy-start(f32[2]{0:T(128)S(1)} %get-tuple-element.38) | copy-start | bytes 28
  16.6 21.1 %copy-start.31 = (f32[2]{0:T(128)}, f32[2]{0:T(128)S(1)}, u32[]{:S(2)}) copy-start(f32[2]{0:T(128)S(1)} %get-tuple-element.39) | copy-start | bytes 28
  16.6 21.1 %copy-start.38 = (f32[2]{0:T(128)}, f32[2]{0:T(128)S(1)}, u32[]{:S(2)}) copy-start(f32[2]{0:T(128)S(1)} %get-tuple-element.40) | copy-start | bytes 28
  23.7 7.7 %copy-start.18 = (pred[4,256,256]{1,2,0:T(8,128)(4,1)S(1)}, pred[4,256,256]{1,2,0:T(8,128)(4,1)}, u32[]{:S(2)}) copy-start(pred[4,256,256]{1,2,0:T(8,128)(4,1)} %get-tuple-element.70) | copy-start | bytes 786436
  26.2 10.7 %all-to-all-start = ((f32[4,2,8320]{2,1,0:T(2,128)}), f32[4,2,8320]{2,1,0:T(2,128)S(1)}, u32[]{:S(2)}, u32[]{:S(2)}) async-start(f32[4,2,8320]{2,1,0:T(2,128)} %select_select_fusion), calls=%async_computation | async-start | bytes 532480 | tf_op jit(solution)/shard_map/all_to_all | solution.py:139
  31.4 5.7 %copy-start.51 = (f32[4]{0:T(128)S(1)}, f32[4]{0:T(128)}, u32[]{:S(2)}) copy-start(f32[4]{0:T(128)} %pad.56.clone) | copy-start | bytes 52
  37.6 3.1 %copy-start.13 = (f32[2,8320]{1,0:T(2,128)}, f32[2,8320]{1,0:T(2,128)S(1)}, u32[]{:S(2)}) copy-start(f32[2,8320]{1,0:T(2,128)S(1)} %get-tuple-element.26) | copy-start | bytes 199684
  38.4 2.4 %copy-start.30 = (f32[2]{0:T(128)S(1)}, f32[2]{0:T(128)}, u32[]{:S(2)}) copy-start(f32[2]{0:T(128)} %copy-done.29) | copy-start | bytes 28
  38.4 2.4 %copy-start.32 = (f32[2]{0:T(128)S(1)}, f32[2]{0:T(128)}, u32[]{:S(2)}) copy-start(f32[2]{0:T(128)} %copy-done.31) | copy-start | bytes 28
  38.4 2.4 %copy-start.37 = (f32[2]{0:T(128)S(1)}, f32[2]{0:T(128)}, u32[]{:S(2)}) copy-start(f32[2]{0:T(128)} %get-tuple-element.37) | copy-start | bytes 28
  43.8 6.5 %copy-start.19 = (f32[1024]{0:T(1024)S(1)}, f32[1024]{0:T(1024)}, u32[]{:S(2)}) copy-start(f32[1024]{0:T(1024)} %get-tuple-element.74) | copy-start | bytes 12292
  43.8 6.5 %copy-start.20 = (f32[1024]{0:T(1024)S(1)}, f32[1024]{0:T(1024)}, u32[]{:S(2)}) copy-start(f32[1024]{0:T(1024)} %get-tuple-element.77) | copy-start | bytes 12292
  44.3 5.5 %collective-permute-start.2 = (f32[3,256]{1,0:T(4,128)S(1)}, f32[3,256]{1,0:T(4,128)S(1)}, u32[]{:S(2)}, u32[]{:S(2)}) collective-permute-start(f32[3,256]{1,0:T(4,128)S(1)} %slice.343), channel_id=1, source_target_pairs={{64,0},{128,64},{192,128},{65,1},{129,65},{193,129},{66,2},{130,66... | collective-permute-start | bytes 9224 | tf_op jit(solution)/shard_map/ppermute | solution.py:18
  52.8 9.2 %collective-permute-start.3 = (f32[32,16,256]{2,1,0:T(8,128)S(1)}, f32[32,16,256]{2,1,0:T(8,128)S(1)}, u32[]{:S(2)}, u32[]{:S(2)}) collective-permute-start(f32[32,16,256]{2,1,0:T(8,128)S(1)} %dynamic-slice_bitcast_fusion), channel_id=1, source_target_pairs={{0,1},{1,0},{2,3},{3,2},{4,5},{5,4},{6,7},{7,6},{8,9},{9,8},{10,11... | collective-permute-start | bytes 1572872 | tf_op jit(solution)/shard_map/ppermute | solution.py:259
  57.2 17.0 %copy-start.24 = (f32[4,256,2]{1,2,0:T(2,128)S(1)}, f32[4,256,2]{1,2,0:T(2,128)}, u32[]{:S(2)}) copy-start(f32[4,256,2]{1,2,0:T(2,128)} %copy.220) | copy-start | bytes 24580
  62.9 28.7 %all-to-all-start.1 = ((f32[32,16,256]{2,1,0:T(8,128)}), f32[32,16,256]{2,1,0:T(8,128)S(1)}, u32[]{:S(2)}, u32[]{:S(2)}) async-start(f32[32,16,256]{2,1,0:T(8,128)} %bitcast_add_fusion), calls=%async_computation.1 | async-start | bytes 1048576 | tf_op jit(solution)/shard_map/all_to_all | solution.py:260
  74.2 3.0 %copy-start.2 = (f32[1024,128]{0,1:T(8,128)S(1)}, f32[1024,128]{0,1:T(8,128)}, u32[]{:S(2)}) copy-start(f32[1024,128]{0,1:T(8,128)} %get-tuple-element.48) | copy-start | bytes 1572868
  76.7 3.3 %copy-start.6 = (f32[2,1,64,128]{3,2,0,1:T(8,128)S(1)}, f32[2,1,64,128]{3,2,0,1:T(8,128)}, u32[]{:S(2)}) copy-start(f32[2,1,64,128]{3,2,0,1:T(8,128)} %copy-done.5) | copy-start | bytes 196612
  76.7 3.3 %copy-start.8 = (f32[2,1,64,128]{3,2,0,1:T(8,128)S(1)}, f32[2,1,64,128]{3,2,0,1:T(8,128)}, u32[]{:S(2)}) copy-start(f32[2,1,64,128]{3,2,0,1:T(8,128)} %copy-done.7) | copy-start | bytes 196612
  76.7 3.3 %copy-start.10 = (f32[2,1,64,128]{3,2,0,1:T(8,128)S(1)}, f32[2,1,64,128]{3,2,0,1:T(8,128)}, u32[]{:S(2)}) copy-start(f32[2,1,64,128]{3,2,0,1:T(8,128)} %copy-done.9) | copy-start | bytes 196612
  76.7 3.3 %copy-start.12 = (f32[1,2,64,128]{3,2,1,0:T(8,128)S(1)}, f32[1,2,64,128]{3,2,1,0:T(8,128)}, u32[]{:S(2)}) copy-start(f32[1,2,64,128]{3,2,1,0:T(8,128)} %copy-done.11) | copy-start | bytes 196612
  77.0 3.4 %copy-start.23 = (f32[4,256]{1,0:T(4,128)S(1)}, f32[4,256]{1,0:T(4,128)}, u32[]{:S(2)}) copy-start(f32[4,256]{1,0:T(4,128)} %copy-done.22) | copy-start | bytes 12292
  77.1 3.4 %copy-start.26 = (f32[2,4,256]{2,0,1:T(2,128)S(1)}, f32[2,4,256]{2,0,1:T(2,128)}, u32[]{:S(2)}) copy-start(f32[2,4,256]{2,0,1:T(2,128)} %copy-done.25) | copy-start | bytes 24580
  77.1 3.4 %copy-start.28 = (f32[2,4]{1,0:T(2,128)S(1)}, f32[2,4]{1,0:T(2,128)}, u32[]{:S(2)}) copy-start(f32[2,4]{1,0:T(2,128)} %copy-done.27) | copy-start | bytes 100
  77.1 3.4 %copy-start.50 = (f32[4,256]{1,0:T(4,128)S(1)}, f32[4,256]{1,0:T(4,128)}, u32[]{:S(2)}) copy-start(f32[4,256]{1,0:T(4,128)} %copy-done.49) | copy-start | bytes 12292
  77.1 3.4 %copy-start.52 = (f32[2,4,256]{2,1,0:T(4,128)S(1)}, f32[2,4,256]{2,1,0:T(4,128)}, u32[]{:S(2)}) copy-start(f32[2,4,256]{2,1,0:T(4,128)} %get-tuple-element.21) | copy-start | bytes 24580
  77.1 3.4 %copy-start.53 = (f32[2,4,256]{2,1,0:T(4,128)S(1)}, f32[2,4,256]{2,1,0:T(4,128)}, u32[]{:S(2)}) copy-start(f32[2,4,256]{2,1,0:T(4,128)} %get-tuple-element.22) | copy-start | bytes 24580
  77.1 6.5 %copy-start.21 = (f32[1024]{0:T(1024)S(1)}, f32[1024]{0:T(1024)}, u32[]{:S(2)}) copy-start(f32[1024]{0:T(1024)} %get-tuple-element.78) | copy-start | bytes 12292
  77.1 6.5 %copy-start.41 = (f32[128]{0:T(128)S(1)}, f32[128]{0:T(128)}, u32[]{:S(2)}) copy-start(f32[128]{0:T(128)} %copy-done.40) | copy-start | bytes 1540
  77.1 6.5 %copy-start.43 = (f32[128]{0:T(128)S(1)}, f32[128]{0:T(128)}, u32[]{:S(2)}) copy-start(f32[128]{0:T(128)} %copy-done.42) | copy-start | bytes 1540
  77.1 6.5 %copy-start.45 = (f32[128]{0:T(128)S(1)}, f32[128]{0:T(128)}, u32[]{:S(2)}) copy-start(f32[128]{0:T(128)} %copy-done.44) | copy-start | bytes 1540
  77.1 6.5 %copy-start.47 = (f32[128]{0:T(128)S(1)}, f32[128]{0:T(128)}, u32[]{:S(2)}) copy-start(f32[128]{0:T(128)} %copy-done.46) | copy-start | bytes 1540
  77.5 6.2 %collective-permute-start.1 = (f32[3,128]{0,1:T(8,128)S(1)}, f32[3,128]{0,1:T(8,128)S(1)}, u32[]{:S(2)}, u32[]{:S(2)}) collective-permute-start(f32[3,128]{0,1:T(8,128)S(1)} %slice.330), channel_id=1, source_target_pairs={{64,0},{128,64},{192,128},{65,1},{129,65},{193,129},{66,2},{130,66... | collective-permute-start | bytes 4616 | tf_op jit(solution)/shard_map/ppermute | solution.py:18
  (12 other events, 13.6 us)

commit v14 on v13

--- a/solution.py
+++ b/solution.py
@@ -250,7 +250,15 @@
     after_bc = shifted(grad_u_bc[:rim_width], "seq", -1)
     after_x = shifted(grad_u_x[:rim_width], "seq", -1)
     grad_pre_x = conv_backward(jnp.concatenate([grad_u_x, after_x]), conv_x, note_all[rim_width:])
-    whole_bc = conv_backward(jnp.concatenate([grad_u_bc, after_bc]), conv_bc, note_all[rim_width:])
+    bulk_bc = conv_backward(
+        jnp.concatenate([grad_u_bc, jnp.zeros_like(after_bc)]), conv_bc, note_all[rim_width:]
+    )
+    tail_bc = conv_backward(
+        jnp.concatenate([grad_u_bc[tok_rows - rim_width :], after_bc]),
+        conv_bc,
+        note_all[tok_rows : tok_rows + 2 * rim_width],
+    )
+    whole_bc = jnp.concatenate([bulk_bc[: tok_rows - rim_width], tail_bc])
     chips, cores = lax.axis_size("chip"), lax.axis_size("core")
     pieces = whole_bc.reshape(chips, cores, tok_rows // (chips * cores), whole_bc.shape[1])
     core = lax.axis_index("core")

time: 94.1 us -> 87.6 us (0.931)
  other arithmetic: 23.5 us -> 19.8 us
  local copies, waits for them, and re-layouts: 14.9 us -> 12.7 us
    add x2 -> x3, other arithmetic: 2.96 us -> 1.18 us  [conv_backward(): result + weights[k][None, :] * extended[lag:lag + count] * linked[:, None]]
    reduce_sum x2, other arithmetic: 3.24 us -> 1.55 us  [block_forward_all(): state = through[:, block, None, None] * state + chunk[:, block]]
    mul x2, local copies, waits for them, and re-layouts: 1.3 us -> 0.01 us  [block_forward_all(): jnp.exp(cumul[..., -1:] - cumul) * (note_blocks == note_blocks[:, -1:])]
    mul x1, other arithmetic: 1.35 us -> 0.08 us  [block_forward_all(): jnp.exp(cumul[..., -1:] - cumul) * (note_blocks == note_blocks[:, -1:])]
    broadcast_in_dim x4, local copies, waits for them, and re-layouts: 1.63 us -> 0.37 us  [block_forward_all(): state = through[:, block, None, None] * state + chunk[:, block]]
    add x1, other arithmetic: 0.88 us -> 1.91 us  [local(): pair_sum = mine + lax.ppermute(other, 'core', [(0, 1), (1, 0)])]
    convert_element_type x1 -> x2, other arithmetic: 1.98 us -> 2.62 us  [conv_backward(): weights[k][None, :] * extended[lag:lag + count] * linked[:, None]]
    unnamed x119 -> x157, local copies, waits for them, and re-layouts: 3.01 us -> 2.48 us
  transfers between devices with their start and end apart: 6 -> 6, of which waited for: 3 -> 3; matrix products, arithmetic and copies ran while one was open for 36% -> 33% of each run, Pallas kernels for 0% -> 0%
where the time goes in v14:
time: 87.6 us; the launch traced here: 85.9 us
  starting transfers between devices  24.4 us (28%)
  other arithmetic  19.8 us (23%)
  matrix products  14.9 us (17%)
  local copies, waits for them, and re-layouts  12.7 us (14%)
  waiting for transfers between devices  10.9 us (12%)
  between operations  3.25 us (4%)
    dot_general x11, matrix products, einsum(): jnp.einsum(spec, *operands, precision=lax.Precision.HIGH, preferred_eleme...  12.6 us
    all_to_all x1, starting transfers between devices, local(): grad_pre_bc = lax.all_to_all(pair_sum, 'chip', 0, 0, tiled=False).sum(0)  11.3 us
    ppermute x3, starting transfers between devices, shifted(): lax.ppermute(value, axis, [(source, source + steps) for source in range(i...  8.45 us
    all_to_all x1, waiting for transfers between devices, local(): grad_pre_bc = lax.all_to_all(pair_sum, 'chip', 0, 0, tiled=False).sum(0)  6.38 us
    all_to_all x1, starting transfers between devices, chain_both(): arrived = lax.all_to_all(outgoing, axis, 0, 0, tiled=False)  4.62 us
    ppermute x3, waiting for transfers between devices, shifted(): lax.ppermute(value, axis, [(source, source + steps) for source in range(i...  4.53 us
    convert_element_type x2, other arithmetic, conv_backward(): weights[k][None, :] * extended[lag:lag + count] * linked[:, None]  2.62 us
    unnamed x157, local copies, waits for them, and re-layouts  2.48 us
  transfers between devices with their start and end apart: 6, of which 3 were waited for; matrix products, arithmetic and copies ran while one was open for 33% of the time, Pallas kernels for 0%

profile of v14, /device:TPU:8, one launch (start us, length us, event | category | flops | bytes accessed | tf_op | source)
XLA Modules:
  0.0 85.9 jit_solution(7534220648916757519)
XLA Ops:
  0.7 0.8 slice.281
  1.4 0.7 slice.280
  2.1 3.5 %collective-permute-start = (bf16[3,384]{1,0:T(4,128)(2,1)S(1)}, bf16[3,384]{1,0:T(4,128)(2,1)S(1)}, u32[]{:S(2)}, u32[]{:S(2)}) collective-permute-start(bf16[3,384]{1,0:T(4,128)(2,1)S(1)} %pad_maximum_fusion.8), channel_id=1, source_target_pairs={{0,64},{64,128},{128,192},{1,65},{65,129},{129,193},{2,66},{66,130... | collective-permute-start | bytes 6920 | tf_op jit(solution)/shard_map/ppermute | solution.py:18
  5.6 0.8 reduce-window.9
  6.5 0.7 bitcast_subtract_fusion.1
  7.7 0.6 fusion.144
  8.3 2.0 %fusion.124 = (f32[1024]{0:T(1024)}, f32[1024]{0:T(1024)S(1)}, f32[1024]{0:T(1024)S(1)}, f32[1024]{0:T(1024)}, f32[1024]{0:T(1024)}, /*index=5*/f32[1024]{0:T(1024)S(1)}, f32[1024]{0:T(1024)S(1)}, f32[1024]{0:T(1024)S(1)}) fusion(s32[1030]{0:T(1024)S(1)} %broadcast_add_fusion, s32[]{:T(128)} %bitcast.11, s32[]{:T(128)} %bitcast.17), kind=kLoop, calls=%fused_computation.219 | loop fusion | flops 16384 | bytes 61448 | tf_op jit(solution)/shard_map/convert_element_type | solution.py:97
  11.6 0.7 compare_convert_fusion.7
  12.4 0.7 reshape.446
  13.6 0.6 compare_convert_fusion.6
  14.7 0.8 fusion.145
  15.6 0.8 slice_bitcast_fusion.11
  16.5 0.7 slice_reduce_fusion.8
  17.2 1.3 %compare_and_fusion = (pred[4,256,256]{1,2,0:T(8,128)(4,1)}, f32[4,256,256]{1,2,0:T(8,128)}) fusion(s32[4,256]{1,0:T(4,128)S(1)} %reshape.450, pred[256,256]{0,1:T(8,128)(4,1)S(1)} %iota_compare_fusion), kind=kLoop, calls=%fused_computation.51 | loop fusion | flops 786432 | bytes 1380352 | tf_op jit(solution)/shard_map/jvp()/and | solution.py:165
  19.0 0.6 pad.59.clone
  20.2 1.8 %fusion.30 = (f32[1024,256]{1,0:T(8,128)S(1)}, f32[1024,256]{1,0:T(8,128)}) fusion(f32[1027,256]{1,0:T(8,128)S(1)} %maximum_convert_fusion, f32[256]{0:T(256)S(1)} %bitcast.393, f32[1024]{0:T(1024)S(1)} %get-tuple-element.87, f32[256]{0:T(256)S(1)} %bitcast.396, f32[1024]{0:T(1024)S(1)} %get-tuple-element.88, f32[256]{0:T(256)S(1)} %bitcast.390, ...), kind=kLoop, calls=%fused_computation.50 | loop fusion | flops 3670016 | bytes 6307840 | tf_op jit(solution)/shard_map/jit(silu)/mul | solution.py:203
  22.2 1.4 %fusion.60 = (f32[1024,128]{0,1:T(8,128)S(1)}, f32[1024,128]{0,1:T(8,128)}) fusion(f32[1027,128]{0,1:T(8,128)S(1)} %maximum_convert_fusion.1, f32[128]{0:T(128)S(1)} %get-tuple-element.102, f32[1024]{0:T(1024)S(1)} %get-tuple-element.87, f32[128]{0:T(128)S(1)} %get-tuple-element.103, f32[1024]{0:T(1024)S(1)} %get-tuple-element.88, ...), kind=kLoop, calls=%fused_computation.101 | loop fusion | flops 1835008 | bytes 3160064 | tf_op jit(solution)/shard_map/jit(silu)/mul | solution.py:202
  24.2 1.4 %convolution_bitcast_fusion.5 = f32[1,2,64,128]{3,2,1,0:T(8,128)S(1)} fusion(bf16[1024,2,64]{0,2,1:T(8,128)(2,1)} %bitcast.369, f32[2,1024]{1,0:T(2,128)S(1)} %get-tuple-element.91, f32[1024,256]{1,0:T(8,128)S(1)} %get-tuple-element.53), kind=kOutput, calls=%fused_computation.24 | convolution fusion | flops 100925440 | bytes 860160 | tf_op jit(solution)/shard_map/thp,ht,tn->hpn/dot_general | solution.py:232
  25.9 0.9 %select_select_fusion = f32[4,2,8320]{2,1,0:T(2,128)} fusion(pred[4]{0:T(512)(128)(4,1)S(1)} %get-tuple-element.117, pred[4]{0:T(512)(128)(4,1)S(1)} %get-tuple-element.116, f32[2,8320]{1,0:T(2,128)S(1)} %get-tuple-element.109, f32[2,8320]{1,0:T(2,128)S(1)} %get-tuple-element.108), kind=kLoop, calls=%fused_computation.107 | loop fusion | flops 133120 | bytes 399368 | tf_op jit(solution)/shard_map/jit(_where)/select_n | solution.py:138
  26.8 4.6 %all-to-all-start = ((f32[4,2,8320]{2,1,0:T(2,128)}), f32[4,2,8320]{2,1,0:T(2,128)S(1)}, u32[]{:S(2)}, u32[]{:S(2)}) async-start(f32[4,2,8320]{2,1,0:T(2,128)} %select_select_fusion), calls=%async_computation | async-start | bytes 532480 | tf_op jit(solution)/shard_map/all_to_all | solution.py:139
  31.4 0.6 fusion.146
  32.0 5.1 %fusion.16 = (f32[2,4,256]{2,1,0:T(4,128)}, f32[2,4,256]{2,1,0:T(4,128)}, f32[4,256,256]{1,2,0:T(8,128)S(1)}, f32[2,4,256,256]{2,3,1,0:T(8,128)}) fusion(f32[4,256,256]{1,2,0:T(8,128)} %get-tuple-element.76, f32[2,4,256]{2,1,0:T(4,128)S(1)} %bitcast.380, f32[4,256,256]{1,2,0:T(8,128)S(1)} %fusion.146, pred[4,256,256]{1,2,0:T(8,128)(4,1)S(1)} %copy-done.22, ...), kind=kOutput, calls=%fused_computation.20 | convolution fusion | flops 207351808 | bytes 6316032 | tf_op jit(solution)/shard_map/transpose(jvp(hbij,hbjp->hbip))/dot_general | solution.py:155
  38.2 0.7 slice_bitcast_fusion.1
  38.9 0.5 fusion.53
  39.5 0.7 fusion.129
  40.2 0.4 convolution_bitcast_fusion.3
  40.6 0.6 convolution_bitcast_fusion.2
  41.3 0.7 slice_bitcast_fusion.3
  42.0 0.6 convolution_add_fusion.1
  42.7 0.6 convolution_bitcast_fusion.1
  43.3 1.0 %convolution_add_fusion = f32[4,256,128]{2,1,0:T(8,128)S(1)} fusion(f32[4,256,128]{2,1,0:T(8,128)S(1)} %convolution_bitcast_fusion.1, f32[4,256,256]{1,2,0:T(8,128)S(1)} %get-tuple-element.23, f32[4,256,128]{2,1,0:T(8,128)S(1)} %bitcast.359), kind=kOutput, calls=%fused_computation.11 | convolution fusion | flops 201457664 | bytes 2621440 | tf_op jit(solution)/shard_map/transpose(jvp(bin,bjn->bij))/dot_general | solution.py:155
  45.1 2.5 %collective-permute-start.2 = (f32[3,256]{1,0:T(4,128)S(1)}, f32[3,256]{1,0:T(4,128)S(1)}, u32[]{:S(2)}, u32[]{:S(2)}) collective-permute-start(f32[3,256]{1,0:T(4,128)S(1)} %get-tuple-element.59), channel_id=1, source_target_pairs={{64,0},{128,64},{192,128},{65,1},{129,65},{193,129},{66,2},{130,66... | collective-permute-start | bytes 9224 | tf_op jit(solution)/shard_map/ppermute | solution.py:18
  47.6 0.5 fusion.18
  48.3 2.3 %collective-permute-done.2 = f32[3,256]{1,0:T(4,128)S(1)} collective-permute-done((f32[3,256]{1,0:T(4,128)S(1)}, f32[3,256]{1,0:T(4,128)S(1)}, u32[]{:S(2)}, u32[]{:S(2)}) %collective-permute-start.2) | collective-permute-done | bytes 3104 | tf_op jit(solution)/shard_map/ppermute | solution.py:18
  50.7 0.8 dynamic-slice_bitcast_fusion
  52.2 1.4 %fusion.88 = (f32[2]{0:T(128)S(1)}, f32[2]{0:T(128)S(1)}) fusion(f32[1,2,64,128]{3,2,1,0:T(8,128)S(1)} %copy-done.27, f32[1,2,64,128]{3,2,1,0:T(8,128)} %get-tuple-element.74, f32[1,2,64,128]{3,2,1,0:T(8,128)S(1)} %copy-done.26, f32[2,8320]{1,0:T(2,128)S(1)} %copy-done.16, f32[2,8320]{1,0:T(2,128)S(1)} %copy-done.18, f32[2]{0:T(128)S(1)} %copy-done.52, ...), kind=kLoop, calls=%fused_computation.141 | loop fusion | flops 262140 | bytes 524336 | tf_op jit(solution)/shard_map/transpose(jvp())/reduce_sum | solution.py:174
  53.9 0.7 copy.238
  54.6 1.9 %bitcast_add_fusion = f32[32,16,256]{2,1,0:T(8,128)} fusion(f32[32,16,256]{2,1,0:T(8,128)} %collective-permute-done.3, f32[32,2,16,256]{3,2,1,0:T(8,128)S(1)} %bitcast.368, s32[]{:T(128)S(6)} %select_n.242), kind=kLoop, calls=%fused_computation.89 | loop fusion | flops 131072 | bytes 1572868 | tf_op jit(solution)/shard_map/add | solution.py:267
  56.5 11.3 %all-to-all-start.1 = ((f32[32,16,256]{2,1,0:T(8,128)}), f32[32,16,256]{2,1,0:T(8,128)S(1)}, u32[]{:S(2)}, u32[]{:S(2)}) async-start(f32[32,16,256]{2,1,0:T(8,128)} %bitcast_add_fusion), calls=%async_computation.1 | async-start | bytes 1048576 | tf_op jit(solution)/shard_map/all_to_all | solution.py:268
  67.9 2.4 %fusion.11 = f32[4,256,2,64]{1,3,2,0:T(8,128)S(1)} fusion(f32[2,4,256,256]{2,3,1,0:T(8,128)} %get-tuple-element.55, f32[4,2,64,256]{3,2,1,0:T(8,128)S(1)} %get-tuple-element.115, bf16[2,4,256,64]{2,1,3,0:T(4,128)(2,1)S(1)} %bitcast.365, f32[4,256,2]{1,2,0:T(2,128)S(1)} %copy.220), kind=kOutput, calls=%fused_computation.17 | convolution fusion | flops 201588736 | bytes 3416064 | tf_op jit(solution)/shard_map/transpose(jvp(hbij,hbjp->hbip))/dot_general | solution.py:155
  71.1 2.5 %collective-permute-start.1 = (f32[3,128]{0,1:T(8,128)S(1)}, f32[3,128]{0,1:T(8,128)S(1)}, u32[]{:S(2)}, u32[]{:S(2)}) collective-permute-start(f32[3,128]{0,1:T(8,128)S(1)} %slice.375), channel_id=1, source_target_pairs={{64,0},{128,64},{192,128},{65,1},{129,65},{193,129},{66,2},{130,66... | collective-permute-start | bytes 4616 | tf_op jit(solution)/shard_map/ppermute | solution.py:18
  73.6 0.4 fusion.17
  74.3 0.6 copy.271
  75.0 2.3 %collective-permute-done.1 = f32[3,128]{0,1:T(8,128)S(1)} collective-permute-done((f32[3,128]{0,1:T(8,128)S(1)}, f32[3,128]{0,1:T(8,128)S(1)}, u32[]{:S(2)}, u32[]{:S(2)}) %collective-permute-start.1) | collective-permute-done | bytes 1568 | tf_op jit(solution)/shard_map/ppermute | solution.py:18
  77.3 0.6 fusion.36
  77.9 1.0 %copy.240 = f32[1024,128]{1,0:T(8,128)} copy(f32[1024,128]{0,1:T(8,128)S(1)} %fusion.36) | data formatting | bytes 1048576
  78.9 6.4 %all-to-all-done.1 = f32[32,16,256]{2,1,0:T(8,128)S(1)} async-done(((f32[32,16,256]{2,1,0:T(8,128)}), f32[32,16,256]{2,1,0:T(8,128)S(1)}, u32[]{:S(2)}, u32[]{:S(2)}) %all-to-all-start.1) | async-done | bytes 524320 | tf_op jit(solution)/shard_map/all_to_all | solution.py:268
  85.3 0.6 reduce_sum.128
  (221 shorter events, 7.5 us)
Async XLA Ops:
  0.6 19.2 %copy-start.19 = (bf16[1024,256]{1,0:T(8,128)(2,1)S(1)}, bf16[1024,256]{1,0:T(8,128)(2,1)}, u32[]{:S(2)}) copy-start(bf16[1024,256]{1,0:T(8,128)(2,1)} %param.8) | copy-start | bytes 1572868
  0.6 18.0 %copy-start.20 = (bf16[1024,128]{1,0:T(8,128)(2,1)S(1)}, bf16[1024,128]{1,0:T(8,128)(2,1)}, u32[]{:S(2)}) copy-start(bf16[1024,128]{1,0:T(8,128)(2,1)} %param.7) | copy-start | bytes 786436
  0.7 18.2 %copy-start.21 = (bf16[1024,128]{1,0:T(8,128)(2,1)S(1)}, bf16[1024,128]{1,0:T(8,128)(2,1)}, u32[]{:S(2)}) copy-start(bf16[1024,128]{1,0:T(8,128)(2,1)} %param.13) | copy-start | bytes 786436
  2.1 17.7 %collective-permute-start = (bf16[3,384]{1,0:T(4,128)(2,1)S(1)}, bf16[3,384]{1,0:T(4,128)(2,1)S(1)}, u32[]{:S(2)}, u32[]{:S(2)}) collective-permute-start(bf16[3,384]{1,0:T(4,128)(2,1)S(1)} %pad_maximum_fusion.8), channel_id=1, source_target_pairs={{0,64},{64,128},{128,192},{1,65},{65,129},{129,193},{2,66},{66,130... | collective-permute-start | bytes 6920 | tf_op jit(solution)/shard_map/ppermute | solution.py:18
  12.3 6.3 %copy-start.55 = (f32[4]{0:T(128)}, f32[4]{0:T(128)S(1)}, u32[]{:S(2)}) copy-start(f32[4]{0:T(128)S(1)} %get-tuple-element.51) | copy-start | bytes 52
  12.4 27.1 %copy-start.31 = (f32[4,256]{1,0:T(4,128)}, f32[4,256]{1,0:T(4,128)S(1)}, u32[]{:S(2)}) copy-start(f32[4,256]{1,0:T(4,128)S(1)} %get-tuple-element.94) | copy-start | bytes 12292
  13.6 25.8 %copy-start.35 = (f32[2,4]{1,0:T(2,128)}, f32[2,4]{1,0:T(2,128)S(1)}, u32[]{:S(2)}) copy-start(f32[2,4]{1,0:T(2,128)S(1)} %slice_reduce_fusion) | copy-start | bytes 100
  15.6 4.6 %copy-start.37 = (f32[1,256]{1,0:T(1,128)}, f32[1,256]{1,0:T(1,128)S(1)}, u32[]{:S(2)}) copy-start(f32[1,256]{1,0:T(1,128)S(1)} %get-tuple-element.96) | copy-start | bytes 3076
  15.6 4.6 %copy-start.39 = (f32[1,256]{1,0:T(1,128)}, f32[1,256]{1,0:T(1,128)S(1)}, u32[]{:S(2)}) copy-start(f32[1,256]{1,0:T(1,128)S(1)} %get-tuple-element.97) | copy-start | bytes 3076
  15.6 4.6 %copy-start.41 = (f32[1,256]{1,0:T(1,128)}, f32[1,256]{1,0:T(1,128)S(1)}, u32[]{:S(2)}) copy-start(f32[1,256]{1,0:T(1,128)S(1)} %get-tuple-element.98) | copy-start | bytes 3076
  15.6 4.6 %copy-start.43 = (f32[1,256]{1,0:T(1,128)}, f32[1,256]{1,0:T(1,128)S(1)}, u32[]{:S(2)}) copy-start(f32[1,256]{1,0:T(1,128)S(1)} %get-tuple-element.99) | copy-start | bytes 3076
  16.4 5.7 %copy-start.57 = (f32[128]{0:T(128)}, f32[128]{0:T(128)S(1)}, u32[]{:S(2)}) copy-start(f32[128]{0:T(128)S(1)} %get-tuple-element.100) | copy-start | bytes 1540
  16.4 5.8 %copy-start.59 = (f32[128]{0:T(128)}, f32[128]{0:T(128)S(1)}, u32[]{:S(2)}) copy-start(f32[128]{0:T(128)S(1)} %get-tuple-element.101) | copy-start | bytes 1540
  16.4 5.8 %copy-start.61 = (f32[128]{0:T(128)}, f32[128]{0:T(128)S(1)}, u32[]{:S(2)}) copy-start(f32[128]{0:T(128)S(1)} %get-tuple-element.102) | copy-start | bytes 1540
  16.4 5.8 %copy-start.63 = (f32[128]{0:T(128)}, f32[128]{0:T(128)S(1)}, u32[]{:S(2)}) copy-start(f32[128]{0:T(128)S(1)} %get-tuple-element.103) | copy-start | bytes 1540
  17.2 21.0 %copy-start.45 = (f32[2]{0:T(128)}, f32[2]{0:T(128)S(1)}, u32[]{:S(2)}) copy-start(f32[2]{0:T(128)S(1)} %get-tuple-element.38) | copy-start | bytes 28
  17.2 21.0 %copy-start.48 = (f32[2]{0:T(128)}, f32[2]{0:T(128)S(1)}, u32[]{:S(2)}) copy-start(f32[2]{0:T(128)S(1)} %get-tuple-element.39) | copy-start | bytes 28
  17.2 21.0 %copy-start.53 = (f32[2]{0:T(128)}, f32[2]{0:T(128)S(1)}, u32[]{:S(2)}) copy-start(f32[2]{0:T(128)S(1)} %get-tuple-element.40) | copy-start | bytes 28
  24.2 7.7 %copy-start.22 = (pred[4,256,256]{1,2,0:T(8,128)(4,1)S(1)}, pred[4,256,256]{1,2,0:T(8,128)(4,1)}, u32[]{:S(2)}) copy-start(pred[4,256,256]{1,2,0:T(8,128)(4,1)} %get-tuple-element.75) | copy-start | bytes 786436
  26.8 10.7 %all-to-all-start = ((f32[4,2,8320]{2,1,0:T(2,128)}), f32[4,2,8320]{2,1,0:T(2,128)S(1)}, u32[]{:S(2)}, u32[]{:S(2)}) async-start(f32[4,2,8320]{2,1,0:T(2,128)} %select_select_fusion), calls=%async_computation | async-start | bytes 532480 | tf_op jit(solution)/shard_map/all_to_all | solution.py:139
  32.0 5.7 %copy-start.70 = (f32[4]{0:T(128)S(1)}, f32[4]{0:T(128)}, u32[]{:S(2)}) copy-start(f32[4]{0:T(128)} %pad.59.clone) | copy-start | bytes 52
  45.1 5.5 %collective-permute-start.2 = (f32[3,256]{1,0:T(4,128)S(1)}, f32[3,256]{1,0:T(4,128)S(1)}, u32[]{:S(2)}, u32[]{:S(2)}) collective-permute-start(f32[3,256]{1,0:T(4,128)S(1)} %get-tuple-element.59), channel_id=1, source_target_pairs={{64,0},{128,64},{192,128},{65,1},{129,65},{193,129},{66,2},{130,66... | collective-permute-start | bytes 9224 | tf_op jit(solution)/shard_map/ppermute | solution.py:18
  48.1 3.4 %copy-start.32 = (f32[4,256]{1,0:T(4,128)S(1)}, f32[4,256]{1,0:T(4,128)}, u32[]{:S(2)}) copy-start(f32[4,256]{1,0:T(4,128)} %copy-done.31) | copy-start | bytes 12292
  48.2 3.4 %copy-start.36 = (f32[2,4]{1,0:T(2,128)S(1)}, f32[2,4]{1,0:T(2,128)}, u32[]{:S(2)}) copy-start(f32[2,4]{1,0:T(2,128)} %copy-done.35) | copy-start | bytes 100
  48.2 3.5 %copy-start.4 = (f32[2,4,64,128]{3,2,0,1:T(8,128)S(1)}, f32[2,4,64,128]{3,2,0,1:T(8,128)}, u32[]{:S(2)}) copy-start(f32[2,4,64,128]{3,2,0,1:T(8,128)} %copy-done.3) | copy-start | bytes 786436
  48.2 3.5 %copy-start.6 = (f32[2,4,64,128]{3,2,0,1:T(8,128)S(1)}, f32[2,4,64,128]{3,2,0,1:T(8,128)}, u32[]{:S(2)}) copy-start(f32[2,4,64,128]{3,2,0,1:T(8,128)} %copy-done.5) | copy-start | bytes 786436
  48.2 3.5 %copy-start.47 = (f32[2]{0:T(128)S(1)}, f32[2]{0:T(128)}, u32[]{:S(2)}) copy-start(f32[2]{0:T(128)} %copy-done.45) | copy-start | bytes 28
  48.2 3.5 %copy-start.50 = (f32[2]{0:T(128)S(1)}, f32[2]{0:T(128)}, u32[]{:S(2)}) copy-start(f32[2]{0:T(128)} %copy-done.48) | copy-start | bytes 28
  48.2 3.5 %copy-start.52 = (f32[2]{0:T(128)S(1)}, f32[2]{0:T(128)}, u32[]{:S(2)}) copy-start(f32[2]{0:T(128)} %get-tuple-element.37) | copy-start | bytes 28
  48.2 3.5 %copy-start.54 = (f32[2]{0:T(128)S(1)}, f32[2]{0:T(128)}, u32[]{:S(2)}) copy-start(f32[2]{0:T(128)} %copy-done.53) | copy-start | bytes 28
  48.2 3.9 %copy-start.16 = (f32[2,8320]{1,0:T(2,128)S(1)}, f32[2,8320]{1,0:T(2,128)}, u32[]{:S(2)}) copy-start(f32[2,8320]{1,0:T(2,128)} %copy-done.15) | copy-start | bytes 199684
  48.2 3.9 %copy-start.18 = (f32[2,8320]{1,0:T(2,128)S(1)}, f32[2,8320]{1,0:T(2,128)}, u32[]{:S(2)}) copy-start(f32[2,8320]{1,0:T(2,128)} %copy-done.17) | copy-start | bytes 199684
  48.2 3.9 %copy-start.23 = (f32[1,2,64,128]{3,2,1,0:T(8,128)S(1)}, f32[1,2,64,128]{3,2,1,0:T(8,128)}, u32[]{:S(2)}) copy-start(f32[1,2,64,128]{3,2,1,0:T(8,128)} %get-tuple-element.63) | copy-start | bytes 196612
  48.3 3.9 %copy-start.24 = (f32[1,2,64,128]{3,2,1,0:T(8,128)S(1)}, f32[1,2,64,128]{3,2,1,0:T(8,128)}, u32[]{:S(2)}) copy-start(f32[1,2,64,128]{3,2,1,0:T(8,128)} %get-tuple-element.64) | copy-start | bytes 196612
  48.3 3.9 %copy-start.25 = (f32[1,2,64,128]{3,2,1,0:T(8,128)S(1)}, f32[1,2,64,128]{3,2,1,0:T(8,128)}, u32[]{:S(2)}) copy-start(f32[1,2,64,128]{3,2,1,0:T(8,128)} %get-tuple-element.68) | copy-start | bytes 196612
  48.3 3.9 %copy-start.26 = (f32[1,2,64,128]{3,2,1,0:T(8,128)S(1)}, f32[1,2,64,128]{3,2,1,0:T(8,128)}, u32[]{:S(2)}) copy-start(f32[1,2,64,128]{3,2,1,0:T(8,128)} %get-tuple-element.69) | copy-start | bytes 196612
  48.3 3.9 %copy-start.27 = (f32[1,2,64,128]{3,2,1,0:T(8,128)S(1)}, f32[1,2,64,128]{3,2,1,0:T(8,128)}, u32[]{:S(2)}) copy-start(f32[1,2,64,128]{3,2,1,0:T(8,128)} %get-tuple-element.70) | copy-start | bytes 196612
  48.3 5.4 %copy-start.56 = (f32[4]{0:T(128)S(1)}, f32[4]{0:T(128)}, u32[]{:S(2)}) copy-start(f32[4]{0:T(128)} %copy-done.55) | copy-start | bytes 52
  51.6 3.1 %collective-permute-start.3 = (f32[32,16,256]{2,1,0:T(8,128)}, f32[32,16,256]{2,1,0:T(8,128)}, u32[]{:S(2)}, u32[]{:S(2)}) collective-permute-start(f32[32,16,256]{2,1,0:T(8,128)} %dynamic-slice_bitcast_fusion), channel_id=1, source_target_pairs={{0,1},{1,0},{2,3},{3,2},{4,5},{5,4},{6,7},{7,6},{8,9},{9,8},{10,11... | collective-permute-start | bytes 1572872 | tf_op jit(solution)/shard_map/ppermute | solution.py:267
  56.5 28.7 %all-to-all-start.1 = ((f32[32,16,256]{2,1,0:T(8,128)}), f32[32,16,256]{2,1,0:T(8,128)S(1)}, u32[]{:S(2)}, u32[]{:S(2)}) async-start(f32[32,16,256]{2,1,0:T(8,128)} %bitcast_add_fusion), calls=%async_computation.1 | async-start | bytes 1048576 | tf_op jit(solution)/shard_map/all_to_all | solution.py:268
  70.7 3.4 %copy-start.34 = (f32[2,4,256]{2,0,1:T(2,128)S(1)}, f32[2,4,256]{2,0,1:T(2,128)}, u32[]{:S(2)}) copy-start(f32[2,4,256]{2,0,1:T(2,128)} %copy-done.33) | copy-start | bytes 24580
  70.7 3.4 %copy-start.66 = (f32[4,256]{1,0:T(4,128)S(1)}, f32[4,256]{1,0:T(4,128)}, u32[]{:S(2)}) copy-start(f32[4,256]{1,0:T(4,128)} %copy-done.65) | copy-start | bytes 12292
  70.7 3.4 %copy-start.71 = (f32[2,4,256]{2,1,0:T(4,128)S(1)}, f32[2,4,256]{2,1,0:T(4,128)}, u32[]{:S(2)}) copy-start(f32[2,4,256]{2,1,0:T(4,128)} %get-tuple-element.21) | copy-start | bytes 24580
  70.7 6.5 %copy-start.58 = (f32[128]{0:T(128)S(1)}, f32[128]{0:T(128)}, u32[]{:S(2)}) copy-start(f32[128]{0:T(128)} %copy-done.57) | copy-start | bytes 1540
  70.7 6.5 %copy-start.60 = (f32[128]{0:T(128)S(1)}, f32[128]{0:T(128)}, u32[]{:S(2)}) copy-start(f32[128]{0:T(128)} %copy-done.59) | copy-start | bytes 1540
  70.7 6.5 %copy-start.62 = (f32[128]{0:T(128)S(1)}, f32[128]{0:T(128)}, u32[]{:S(2)}) copy-start(f32[128]{0:T(128)} %copy-done.61) | copy-start | bytes 1540
  70.8 6.5 %copy-start.64 = (f32[128]{0:T(128)S(1)}, f32[128]{0:T(128)}, u32[]{:S(2)}) copy-start(f32[128]{0:T(128)} %copy-done.63) | copy-start | bytes 1540
  71.1 6.2 %collective-permute-start.1 = (f32[3,128]{0,1:T(8,128)S(1)}, f32[3,128]{0,1:T(8,128)S(1)}, u32[]{:S(2)}, u32[]{:S(2)}) collective-permute-start(f32[3,128]{0,1:T(8,128)S(1)} %slice.375), channel_id=1, source_target_pairs={{64,0},{128,64},{192,128},{65,1},{129,65},{193,129},{66,2},{130,66... | collective-permute-start | bytes 4616 | tf_op jit(solution)/shard_map/ppermute | solution.py:18
  (31 other events, 72.1 us)

commit v15 on v14

--- a/solution.py
+++ b/solution.py
@@ -249,7 +249,15 @@
     grad_u_bc = grad_v_bc * silu_slope(u_bc)
     after_bc = shifted(grad_u_bc[:rim_width], "seq", -1)
     after_x = shifted(grad_u_x[:rim_width], "seq", -1)
-    grad_pre_x = conv_backward(jnp.concatenate([grad_u_x, after_x]), conv_x, note_all[rim_width:])
+    bulk_x = conv_backward(
+        jnp.concatenate([grad_u_x, jnp.zeros_like(after_x)]), conv_x, note_all[rim_width:]
+    )
+    tail_x = conv_backward(
+        jnp.concatenate([grad_u_x[tok_rows - rim_width :], after_x]),
+        conv_x,
+        note_all[tok_rows : tok_rows + 2 * rim_width],
+    )
+    grad_pre_x = jnp.concatenate([bulk_x[: tok_rows - rim_width], tail_x])
     bulk_bc = conv_backward(
         jnp.concatenate([grad_u_bc, jnp.zeros_like(after_bc)]), conv_bc, note_all[rim_width:]
     )

time: 87.6 us -> 100 us (1.14)
  local copies, waits for them, and re-layouts: 12.7 us -> 22.1 us
  waiting for transfers between devices: 10.9 us -> 14.6 us
    all_to_all x1, waiting for transfers between devices: 6.38 us -> 14.6 us  [local(): grad_pre_bc = lax.all_to_all(pair_sum, 'chip', 0, 0, tiled=False).sum(0)]
    ppermute x3, waiting for transfers between devices: 4.53 us -> 0.01 us  [shifted(): lax.ppermute(value, axis, [(source, source + steps) for source in range(i...]
    broadcast_in_dim x4, local copies, waits for them, and re-layouts: 0.37 us -> 2.63 us  [block_forward_all(): state = through[:, block, None, None] * state + chunk[:, block]]
    reshape x0 -> x2, local copies, waits for them, and re-layouts: none -> 1.95 us  [local(): grad_x_heads.transpose(1, 2, 0, 3).reshape(tok_rows, head_count * P_SIZE)]
    slice x1 -> x2, local copies, waits for them, and re-layouts: 0.24 us -> 1.86 us  [conv_backward(): extended[lag:lag + count]]
    add x3 -> x4, other arithmetic: 1.18 us -> 2.72 us  [conv_backward(): result + weights[k][None, :] * extended[lag:lag + count] * linked[:, None]]
    transpose x0 -> x1, local copies, waits for them, and re-layouts: none -> 1.18 us  [local(): v_x.reshape(block_count, BLOCK, head_count, P_SIZE).transpose(2, 0, 1, 3)]
    add x1, other arithmetic: 1.91 us -> 0.89 us  [local(): pair_sum = mine + lax.ppermute(other, 'core', [(0, 1), (1, 0)])]
  transfers between devices with their start and end apart: 6 -> 6, of which waited for: 3 -> 1; matrix products, arithmetic and copies ran while one was open for 33% -> 31% of each run, Pallas kernels for 0% -> 0%
where the time goes in v15:
time: 100 us; the launch traced here: 98.1 us
  starting transfers between devices  24.1 us (24%)
  local copies, waits for them, and re-layouts  22.1 us (22%)
  other arithmetic  19.4 us (19%)
  matrix products  14.7 us (15%)
  waiting for transfers between devices  14.6 us (15%)
  between operations  3.17 us (3%)
    all_to_all x1, waiting for transfers between devices, local(): grad_pre_bc = lax.all_to_all(pair_sum, 'chip', 0, 0, tiled=False).sum(0)  14.6 us
    dot_general x11, matrix products, einsum(): jnp.einsum(spec, *operands, precision=lax.Precision.HIGH, preferred_eleme...  13.4 us
    all_to_all x1, starting transfers between devices, local(): grad_pre_bc = lax.all_to_all(pair_sum, 'chip', 0, 0, tiled=False).sum(0)  11.3 us
    ppermute x3, starting transfers between devices, shifted(): lax.ppermute(value, axis, [(source, source + steps) for source in range(i...  8.03 us
    all_to_all x1, starting transfers between devices, chain_both(): arrived = lax.all_to_all(outgoing, axis, 0, 0, tiled=False)  4.62 us
    unnamed x150, local copies, waits for them, and re-layouts  3.01 us
    add x4, other arithmetic, conv_backward(): result + weights[k][None, :] * extended[lag:lag + count] * linked[:, None]  2.72 us
    convert_element_type x2, other arithmetic, conv_backward(): weights[k][None, :] * extended[lag:lag + count] * linked[:, None]  2.64 us
  transfers between devices with their start and end apart: 6, of which 1 were waited for; matrix products, arithmetic and copies ran while one was open for 31% of the time, Pallas kernels for 0%

profile of v15, /device:TPU:8, one launch (start us, length us, event | category | flops | bytes accessed | tf_op | source)
XLA Modules:
  0.0 98.1 jit_solution(16799842212797900924)
XLA Ops:
  0.6 0.7 slice.305
  1.4 0.7 slice.306
  2.1 3.5 %collective-permute-start = (bf16[3,384]{1,0:T(4,128)(2,1)S(1)}, bf16[3,384]{1,0:T(4,128)(2,1)S(1)}, u32[]{:S(2)}, u32[]{:S(2)}) collective-permute-start(bf16[3,384]{1,0:T(4,128)(2,1)S(1)} %pad_maximum_fusion.9), channel_id=1, source_target_pairs={{0,64},{64,128},{128,192},{1,65},{65,129},{129,193},{2,66},{66,130... | collective-permute-start | bytes 6920 | tf_op jit(solution)/shard_map/ppermute | solution.py:18
  5.6 0.8 reduce-window.9
  6.4 0.7 bitcast_subtract_fusion.1
  7.8 0.7 compare_convert_fusion.6
  8.9 0.7 compare_convert_fusion.7
  9.7 0.7 reshape.446
  12.2 2.0 %fusion.116 = (f32[1024]{0:T(1024)}, f32[1024]{0:T(1024)S(1)}, f32[1024]{0:T(1024)S(1)}, f32[1024]{0:T(1024)}, f32[1024]{0:T(1024)}, /*index=5*/f32[1024]{0:T(1024)S(1)}, f32[1024]{0:T(1024)S(1)}, f32[1024]{0:T(1024)S(1)}) fusion(s32[1030]{0:T(1024)S(1)} %broadcast_add_fusion, s32[]{:T(128)} %bitcast.11, s32[]{:T(128)} %bitcast.17), kind=kLoop, calls=%fused_computation.215 | loop fusion | flops 16384 | bytes 61448 | tf_op jit(solution)/shard_map/convert_element_type | solution.py:97
  14.3 0.8 slice_bitcast_fusion.11
  15.1 0.8 fusion.138
  16.7 1.4 %compare_and_fusion = (pred[4,256,256]{1,2,0:T(8,128)(4,1)}, f32[4,256,256]{1,2,0:T(8,128)}) fusion(s32[4,256]{1,0:T(4,128)S(1)} %reshape.450, pred[256,256]{0,1:T(8,128)(4,1)S(1)} %iota_compare_fusion), kind=kLoop, calls=%fused_computation.51 | loop fusion | flops 786432 | bytes 1380352 | tf_op jit(solution)/shard_map/jvp()/and | solution.py:165
  18.4 0.6 copy.252
  19.4 1.3 %fusion.54 = (f32[1024,128]{1,0:T(8,128)S(1)}, f32[1024,128]{1,0:T(8,128)}) fusion(f32[1027,128]{1,0:T(8,128)S(1)} %maximum_convert_fusion.1, f32[128]{0:T(128)S(1)} %get-tuple-element.104, f32[1024]{0:T(1024)S(1)} %get-tuple-element.86, f32[128]{0:T(128)S(1)} %get-tuple-element.105, f32[1024]{0:T(1024)S(1)} %get-tuple-element.87, ...), kind=kLoop, calls=%fused_computation.95 | loop fusion | flops 1835008 | bytes 3160064 | tf_op jit(solution)/shard_map/jit(silu)/mul | solution.py:202
  20.7 1.0 %copy.243 = f32[1024,128]{0,1:T(8,128)} copy(f32[1024,128]{1,0:T(8,128)S(1)} %get-tuple-element.44) | data formatting | bytes 1048576 | tf_op jit(solution)/shard_map/jit(silu)/mul | solution.py:202
  21.7 0.6 reshape.473
  22.8 1.2 %copy.285 = f32[4,256,2,64]{1,3,0,2:T(8,128)} copy(f32[4,256,2,64]{3,2,1,0:T(2,128)S(1)} %reshape.473) | data formatting | bytes 1048576 | tf_op jit(solution)/shard_map/transpose | solution.py:204
  24.2 1.0 %fusion.30 = (f32[1024,256]{1,0:T(8,128)S(1)}, f32[1024,256]{1,0:T(8,128)S(1)}) fusion(f32[1027,256]{1,0:T(8,128)S(1)} %maximum_convert_fusion, f32[256]{0:T(256)S(1)} %bitcast.387, f32[1024]{0:T(1024)S(1)} %get-tuple-element.86, f32[256]{0:T(256)S(1)} %bitcast.390, f32[1024]{0:T(1024)S(1)} %get-tuple-element.87, f32[256]{0:T(256)S(1)} %bitcast.384, ...), kind=kLoop, calls=%fused_computation.50 | loop fusion | flops 3670016 | bytes 6307840 | tf_op jit(solution)/shard_map/jit(silu)/mul | solution.py:203
  25.3 1.0 copy-done.7
  27.3 0.9 select_select_fusion
  28.2 4.6 %all-to-all-start = ((f32[4,2,8320]{2,1,0:T(2,128)}), f32[4,2,8320]{2,1,0:T(2,128)S(1)}, u32[]{:S(2)}, u32[]{:S(2)}) async-start(f32[4,2,8320]{2,1,0:T(2,128)} %select_select_fusion), calls=%async_computation | async-start | bytes 532480 | tf_op jit(solution)/shard_map/all_to_all | solution.py:139
  33.4 0.6 copy-done.9
  34.2 4.5 %fusion.16 = (f32[2,4,256]{2,1,0:T(4,128)}, f32[2,4,256]{2,1,0:T(4,128)}, f32[4,256,256]{1,2,0:T(8,128)}, f32[2,4,256,256]{2,3,1,0:T(8,128)}) fusion(f32[4,256,256]{1,2,0:T(8,128)S(1)} %copy-done.9, f32[2,4,256]{2,1,0:T(4,128)S(1)} %bitcast.371, f32[4,256,256]{1,2,0:T(8,128)S(1)} %fusion.139, pred[4,256,256]{1,2,0:T(8,128)(4,1)S(1)} %copy-done.22, ...), kind=kOutput, calls=%fused_computation.20 | convolution fusion | flops 207351808 | bytes 6316032 | tf_op jit(solution)/shard_map/transpose(jvp(hbij,hbjp->hbip))/dot_general | solution.py:155
  39.8 1.2 %fusion.48 = (f32[2,4,256]{2,0,1:T(2,128)S(1)}, f32[4,2,64,256]{3,2,1,0:T(8,128)}) fusion(f32[4,256,2,64]{1,3,2,0:T(8,128)S(1)} %copy.259, f32[4,256,128,1]{2,1,3,0:T(8,128)S(1)} %bitcast.350, f32[2,1,64,128]{3,2,0,1:T(8,128)S(1)} %get-tuple-element.67, f32[2,1,64,128]{3,2,0,1:T(8,128)S(1)} %get-tuple-element.68, ...), kind=kOutput, calls=%fused_computation.83 | convolution fusion | flops 101120000 | bytes 1843200 | tf_op jit(solution)/shard_map/transpose(jvp(hbjp,bjn->hbpn))/dot_general | solution.py:155
  41.0 0.7 fusion.121
  42.9 0.8 fusion.86
  43.7 0.7 slice_bitcast_fusion.3
  44.4 0.6 convolution_bitcast_fusion.1
  45.1 1.0 %convolution_add_fusion = f32[4,256,128]{2,1,0:T(8,128)S(1)} fusion(f32[4,256,128]{2,1,0:T(8,128)S(1)} %convolution_bitcast_fusion.1, f32[4,256,256]{1,2,0:T(8,128)S(1)} %copy-done, f32[4,256,128]{2,1,0:T(8,128)S(1)} %bitcast.352), kind=kOutput, calls=%fused_computation.11 | convolution fusion | flops 201457664 | bytes 2621440 | tf_op jit(solution)/shard_map/transpose(jvp(bin,bjn->bij))/dot_general | solution.py:155
  47.8 1.8 %pad_slice_fusion.2 = (f32[1024,256]{1,0:T(8,128)}, f32[1024,256]{1,0:T(8,128)}, f32[1024,256]{1,0:T(8,128)}) fusion(f32[1024,256]{1,0:T(8,128)S(1)} %maximum_multiply_fusion), kind=kLoop, calls=%fused_computation.54 | loop fusion | bytes 4194304 | tf_op jit(solution)/shard_map/slice | solution.py:97
  49.5 0.7 copy.268
  50.2 0.7 copy.267
  51.4 0.7 copy.269
  52.1 0.6 copy.266
  52.7 2.6 %collective-permute-start.2 = (f32[3,256]{1,0:T(4,128)}, f32[3,256]{1,0:T(4,128)}, u32[]{:S(2)}, u32[]{:S(2)}) collective-permute-start(f32[3,256]{1,0:T(4,128)} %get-tuple-element.56), channel_id=1, source_target_pairs={{64,0},{128,64},{192,128},{65,1},{129,65},{193,129},{66,2},{130,66... | collective-permute-start | bytes 9224 | tf_op jit(solution)/shard_map/ppermute | solution.py:18
  55.3 3.2 %fusion.11 = f32[4,256,2,64]{1,3,2,0:T(8,128)} fusion(f32[2,4,256,256]{2,3,1,0:T(8,128)} %get-tuple-element.52, f32[4,2,64,256]{3,2,1,0:T(8,128)S(1)} %copy-done.6, bf16[2,4,256,64]{2,1,3,0:T(4,128)(2,1)S(1)} %bitcast.358, f32[4,256,2]{1,2,0:T(2,128)S(1)} %copy-done.28), kind=kOutput, calls=%fused_computation.17 | convolution fusion | flops 201588736 | bytes 3416064 | tf_op jit(solution)/shard_map/transpose(jvp(hbij,hbjp->hbip))/dot_general | solution.py:155
  58.6 1.3 %fusion.18 = f32[1021,256]{1,0:T(8,128)S(1)} fusion(f32[1024,256]{1,0:T(8,128)S(1)} %maximum_multiply_fusion, f32[1024,256]{1,0:T(8,128)S(1)} %copy-done.3, f32[1024,256]{1,0:T(8,128)S(1)} %copy-done.2, f32[1024,256]{1,0:T(8,128)S(1)} %copy-done.1, f32[256]{0:T(256)} %bitcast.388, f32[1021]{0:T(1024)S(1)} %bitcast.376, f32[256]{0:T(256)} %bitcast.391, ...), kind=kLoop, calls=%fused_computation.28 | loop fusion | flops 2613760 | bytes 5243868 | tf_op jit(solution)/shard_map/add | solution.py:97
  60.0 1.4 %copy.272 = f32[2,4,1]{2,1,0:T(4,128)} copy(f32[2,4,1]{1,0,2:T(2,128)} %bitcast.395) | data formatting | bytes 64 | tf_op jit(solution)/shard_map/transpose(jvp())/reshape | solution.py:161
  61.4 0.7 copy.270
  62.6 1.4 %reshape.472 = f32[1024,128]{1,0:T(8,128)} reshape(f32[4,256,2,64]{3,2,1,0:T(2,128)S(1)} %copy.282) | data formatting | bytes 1048576 | tf_op jit(solution)/shard_map/reshape | solution.py:246
  64.0 0.9 fusion.109
  65.5 1.9 %collective-permute-start.1 = (f32[3,128]{1,0:T(4,128)S(1)}, f32[3,128]{1,0:T(4,128)S(1)}, u32[]{:S(2)}, u32[]{:S(2)}) collective-permute-start(f32[3,128]{1,0:T(4,128)S(1)} %get-tuple-element.64), channel_id=1, source_target_pairs={{64,0},{128,64},{192,128},{65,1},{129,65},{193,129},{66,2},{130,66... | collective-permute-start | bytes 4616 | tf_op jit(solution)/shard_map/ppermute | solution.py:18
  67.9 0.9 bitcast_add_fusion
  68.8 11.3 %all-to-all-start.1 = ((f32[32,16,256]{2,1,0:T(8,128)}), f32[32,16,256]{2,1,0:T(8,128)S(1)}, u32[]{:S(2)}, u32[]{:S(2)}) async-start(f32[32,16,256]{2,1,0:T(8,128)} %bitcast_add_fusion), calls=%async_computation.1 | async-start | bytes 1048576 | tf_op jit(solution)/shard_map/all_to_all | solution.py:276
  81.2 0.6 copy.307
  82.0 0.8 pad_maximum_fusion.1
  82.8 14.6 %all-to-all-done.1 = f32[32,16,256]{2,1,0:T(8,128)S(1)} async-done(((f32[32,16,256]{2,1,0:T(8,128)}), f32[32,16,256]{2,1,0:T(8,128)S(1)}, u32[]{:S(2)}, u32[]{:S(2)}) %all-to-all-start.1) | async-done | bytes 524320 | tf_op jit(solution)/shard_map/all_to_all | solution.py:276
  97.4 0.6 reduce_sum.128
  (221 shorter events, 12.4 us)
Async XLA Ops:
  0.6 18.7 %copy-start.20 = (bf16[1024,128]{1,0:T(8,128)(2,1)S(1)}, bf16[1024,128]{1,0:T(8,128)(2,1)}, u32[]{:S(2)}) copy-start(bf16[1024,128]{1,0:T(8,128)(2,1)} %param.7) | copy-start | bytes 786436
  0.6 18.3 %copy-start.21 = (bf16[1024,128]{1,0:T(8,128)(2,1)S(1)}, bf16[1024,128]{1,0:T(8,128)(2,1)}, u32[]{:S(2)}) copy-start(bf16[1024,128]{1,0:T(8,128)(2,1)} %param.13) | copy-start | bytes 786436
  2.1 17.2 %collective-permute-start = (bf16[3,384]{1,0:T(4,128)(2,1)S(1)}, bf16[3,384]{1,0:T(4,128)(2,1)S(1)}, u32[]{:S(2)}, u32[]{:S(2)}) collective-permute-start(bf16[3,384]{1,0:T(4,128)(2,1)S(1)} %pad_maximum_fusion.9), channel_id=1, source_target_pairs={{0,64},{64,128},{128,192},{1,65},{65,129},{129,193},{2,66},{66,130... | collective-permute-start | bytes 6920 | tf_op jit(solution)/shard_map/ppermute | solution.py:18
  9.6 8.6 %copy-start.57 = (f32[4]{0:T(128)}, f32[4]{0:T(128)S(1)}, u32[]{:S(2)}) copy-start(f32[4]{0:T(128)S(1)} %get-tuple-element.48) | copy-start | bytes 52
  9.7 6.6 %copy-start.61 = (f32[4,256]{1,0:T(4,128)}, f32[4,256]{1,0:T(4,128)S(1)}, u32[]{:S(2)}) copy-start(f32[4,256]{1,0:T(4,128)S(1)} %get-tuple-element.97) | copy-start | bytes 12292
  9.7 31.4 %copy-start.26 = (f32[4,256]{1,0:T(4,128)}, f32[4,256]{1,0:T(4,128)S(1)}, u32[]{:S(2)}) copy-start(f32[4,256]{1,0:T(4,128)S(1)} %get-tuple-element.96) | copy-start | bytes 12292
  10.8 30.3 %copy-start.31 = (f32[2,4]{1,0:T(2,128)}, f32[2,4]{1,0:T(2,128)S(1)}, u32[]{:S(2)}) copy-start(f32[2,4]{1,0:T(2,128)S(1)} %slice_reduce_fusion) | copy-start | bytes 100
  15.1 5.6 %copy-start.46 = (f32[128]{0:T(128)}, f32[128]{0:T(128)S(1)}, u32[]{:S(2)}) copy-start(f32[128]{0:T(128)S(1)} %get-tuple-element.102) | copy-start | bytes 1540
  15.1 5.6 %copy-start.48 = (f32[128]{0:T(128)}, f32[128]{0:T(128)S(1)}, u32[]{:S(2)}) copy-start(f32[128]{0:T(128)S(1)} %get-tuple-element.103) | copy-start | bytes 1540
  15.1 5.6 %copy-start.50 = (f32[128]{0:T(128)}, f32[128]{0:T(128)S(1)}, u32[]{:S(2)}) copy-start(f32[128]{0:T(128)S(1)} %get-tuple-element.104) | copy-start | bytes 1540
  15.1 5.6 %copy-start.52 = (f32[128]{0:T(128)}, f32[128]{0:T(128)S(1)}, u32[]{:S(2)}) copy-start(f32[128]{0:T(128)S(1)} %get-tuple-element.105) | copy-start | bytes 1540
  16.0 8.2 %copy-start.34 = (f32[1,256]{1,0:T(1,128)}, f32[1,256]{1,0:T(1,128)S(1)}, u32[]{:S(2)}) copy-start(f32[1,256]{1,0:T(1,128)S(1)} %get-tuple-element.98) | copy-start | bytes 3076
  16.0 8.2 %copy-start.35 = (f32[1,256]{1,0:T(1,128)}, f32[1,256]{1,0:T(1,128)S(1)}, u32[]{:S(2)}) copy-start(f32[1,256]{1,0:T(1,128)S(1)} %get-tuple-element.99) | copy-start | bytes 3076
  16.0 8.2 %copy-start.36 = (f32[1,256]{1,0:T(1,128)}, f32[1,256]{1,0:T(1,128)S(1)}, u32[]{:S(2)}) copy-start(f32[1,256]{1,0:T(1,128)S(1)} %get-tuple-element.100) | copy-start | bytes 3076
  16.0 8.2 %copy-start.37 = (f32[1,256]{1,0:T(1,128)}, f32[1,256]{1,0:T(1,128)S(1)}, u32[]{:S(2)}) copy-start(f32[1,256]{1,0:T(1,128)S(1)} %get-tuple-element.101) | copy-start | bytes 3076
  16.2 26.6 %copy-start.38 = (f32[2]{0:T(128)}, f32[2]{0:T(128)S(1)}, u32[]{:S(2)}) copy-start(f32[2]{0:T(128)S(1)} %get-tuple-element.35) | copy-start | bytes 28
  16.2 26.6 %copy-start.40 = (f32[2]{0:T(128)}, f32[2]{0:T(128)S(1)}, u32[]{:S(2)}) copy-start(f32[2]{0:T(128)S(1)} %get-tuple-element.36) | copy-start | bytes 28
  16.2 26.6 %copy-start.42 = (f32[2]{0:T(128)}, f32[2]{0:T(128)S(1)}, u32[]{:S(2)}) copy-start(f32[2]{0:T(128)S(1)} %get-tuple-element.34) | copy-start | bytes 28
  16.2 26.6 %copy-start.44 = (f32[2]{0:T(128)}, f32[2]{0:T(128)S(1)}, u32[]{:S(2)}) copy-start(f32[2]{0:T(128)S(1)} %get-tuple-element.37) | copy-start | bytes 28
  27.1 6.3 %copy-start.22 = (pred[4,256,256]{1,2,0:T(8,128)(4,1)S(1)}, pred[4,256,256]{1,2,0:T(8,128)(4,1)}, u32[]{:S(2)}) copy-start(pred[4,256,256]{1,2,0:T(8,128)(4,1)} %get-tuple-element.77) | copy-start | bytes 786436
  28.2 10.8 %all-to-all-start = ((f32[4,2,8320]{2,1,0:T(2,128)}), f32[4,2,8320]{2,1,0:T(2,128)S(1)}, u32[]{:S(2)}, u32[]{:S(2)}) async-start(f32[4,2,8320]{2,1,0:T(2,128)} %select_select_fusion), calls=%async_computation | async-start | bytes 532480 | tf_op jit(solution)/shard_map/all_to_all | solution.py:139
  39.7 3.1 %copy-start.14 = (f32[2,8320]{1,0:T(2,128)}, f32[2,8320]{1,0:T(2,128)S(1)}, u32[]{:S(2)}) copy-start(f32[2,8320]{1,0:T(2,128)S(1)} %get-tuple-element.23) | copy-start | bytes 199684
  42.2 2.9 %copy-start = (f32[4,256,256]{1,2,0:T(8,128)S(1)}, f32[4,256,256]{1,2,0:T(8,128)}, u32[]{:S(2)}) copy-start(f32[4,256,256]{1,2,0:T(8,128)} %get-tuple-element.20) | copy-start | bytes 3145732
  42.8 3.3 %copy-start.12 = (f32[1,2,64,128]{3,2,1,0:T(8,128)}, f32[1,2,64,128]{3,2,1,0:T(8,128)S(1)}, u32[]{:S(2)}) copy-start(f32[1,2,64,128]{3,2,1,0:T(8,128)S(1)} %copy.375) | copy-start | bytes 196612
  47.7 2.5 %copy-start.67 = (f32[2]{0:T(128)S(1)}, f32[2]{0:T(128)}, u32[]{:S(2)}) copy-start(f32[2]{0:T(128)} %get-tuple-element.21) | copy-start | bytes 28
  47.7 3.2 %copy-start.15 = (f32[2,8320]{1,0:T(2,128)S(1)}, f32[2,8320]{1,0:T(2,128)}, u32[]{:S(2)}) copy-start(f32[2,8320]{1,0:T(2,128)} %copy-done.14) | copy-start | bytes 199684
  47.7 3.2 %copy-start.17 = (f32[2,8320]{1,0:T(2,128)S(1)}, f32[2,8320]{1,0:T(2,128)}, u32[]{:S(2)}) copy-start(f32[2,8320]{1,0:T(2,128)} %copy-done.16) | copy-start | bytes 199684
  47.7 3.2 %copy-start.39 = (f32[2]{0:T(128)S(1)}, f32[2]{0:T(128)}, u32[]{:S(2)}) copy-start(f32[2]{0:T(128)} %copy-done.38) | copy-start | bytes 28
  47.7 3.2 %copy-start.41 = (f32[2]{0:T(128)S(1)}, f32[2]{0:T(128)}, u32[]{:S(2)}) copy-start(f32[2]{0:T(128)} %copy-done.40) | copy-start | bytes 28
  47.7 3.2 %copy-start.43 = (f32[2]{0:T(128)S(1)}, f32[2]{0:T(128)}, u32[]{:S(2)}) copy-start(f32[2]{0:T(128)} %copy-done.42) | copy-start | bytes 28
  47.7 3.2 %copy-start.45 = (f32[2]{0:T(128)S(1)}, f32[2]{0:T(128)}, u32[]{:S(2)}) copy-start(f32[2]{0:T(128)} %copy-done.44) | copy-start | bytes 28
  47.8 7.6 %copy-start.6 = (f32[4,2,64,256]{3,2,1,0:T(8,128)S(1)}, f32[4,2,64,256]{3,2,1,0:T(8,128)}, u32[]{:S(2)}) copy-start(f32[4,2,64,256]{3,2,1,0:T(8,128)} %get-tuple-element.117) | copy-start | bytes 1572868
  47.8 7.6 %copy-start.28 = (f32[4,256,2]{1,2,0:T(2,128)S(1)}, f32[4,256,2]{1,2,0:T(2,128)}, u32[]{:S(2)}) copy-start(f32[4,256,2]{1,2,0:T(2,128)} %copy.252) | copy-start | bytes 24580
  49.5 9.0 %copy-start.23 = (f32[1024]{0:T(1024)S(1)}, f32[1024]{0:T(1024)}, u32[]{:S(2)}) copy-start(f32[1024]{0:T(1024)} %get-tuple-element.81) | copy-start | bytes 12292
  49.5 9.0 %copy-start.24 = (f32[1024]{0:T(1024)S(1)}, f32[1024]{0:T(1024)}, u32[]{:S(2)}) copy-start(f32[1024]{0:T(1024)} %get-tuple-element.84) | copy-start | bytes 12292
  52.7 5.8 %copy-start.1 = (f32[1024,256]{1,0:T(8,128)S(1)}, f32[1024,256]{1,0:T(8,128)}, u32[]{:S(2)}) copy-start(f32[1024,256]{1,0:T(8,128)} %get-tuple-element.53) | copy-start | bytes 3145732
  52.7 5.8 %copy-start.2 = (f32[1024,256]{1,0:T(8,128)S(1)}, f32[1024,256]{1,0:T(8,128)}, u32[]{:S(2)}) copy-start(f32[1024,256]{1,0:T(8,128)} %get-tuple-element.54) | copy-start | bytes 3145732
  52.7 5.8 %copy-start.3 = (f32[1024,256]{1,0:T(8,128)S(1)}, f32[1024,256]{1,0:T(8,128)}, u32[]{:S(2)}) copy-start(f32[1024,256]{1,0:T(8,128)} %get-tuple-element.55) | copy-start | bytes 3145732
  52.7 11.3 %collective-permute-start.2 = (f32[3,256]{1,0:T(4,128)}, f32[3,256]{1,0:T(4,128)}, u32[]{:S(2)}, u32[]{:S(2)}) collective-permute-start(f32[3,256]{1,0:T(4,128)} %get-tuple-element.56), channel_id=1, source_target_pairs={{64,0},{128,64},{192,128},{65,1},{129,65},{193,129},{66,2},{130,66... | collective-permute-start | bytes 9224 | tf_op jit(solution)/shard_map/ppermute | solution.py:18
  58.6 3.5 %copy-start.8 = (f32[4,256,2,64]{1,3,2,0:T(8,128)S(1)}, f32[4,256,2,64]{1,3,2,0:T(8,128)}, u32[]{:S(2)}) copy-start(f32[4,256,2,64]{1,3,2,0:T(8,128)} %fusion.11) | copy-start | bytes 1572868
  65.1 2.8 %collective-permute-start.3 = (f32[32,16,256]{2,1,0:T(8,128)S(1)}, f32[32,16,256]{2,1,0:T(8,128)S(1)}, u32[]{:S(2)}, u32[]{:S(2)}) collective-permute-start(f32[32,16,256]{2,1,0:T(8,128)S(1)} %dynamic-slice_bitcast_fusion), channel_id=1, source_target_pairs={{0,1},{1,0},{2,3},{3,2},{4,5},{5,4},{6,7},{7,6},{8,9},{9,8},{10,11... | collective-permute-start | bytes 1572872 | tf_op jit(solution)/shard_map/ppermute | solution.py:275
  65.5 16.4 %collective-permute-start.1 = (f32[3,128]{1,0:T(4,128)S(1)}, f32[3,128]{1,0:T(4,128)S(1)}, u32[]{:S(2)}, u32[]{:S(2)}) collective-permute-start(f32[3,128]{1,0:T(4,128)S(1)} %get-tuple-element.64), channel_id=1, source_target_pairs={{64,0},{128,64},{192,128},{65,1},{129,65},{193,129},{66,2},{130,66... | collective-permute-start | bytes 4616 | tf_op jit(solution)/shard_map/ppermute | solution.py:18
  67.8 12.5 %copy-start.25 = (f32[1024]{0:T(1024)S(1)}, f32[1024]{0:T(1024)}, u32[]{:S(2)}) copy-start(f32[1024]{0:T(1024)} %get-tuple-element.85) | copy-start | bytes 12292
  67.9 12.5 %copy-start.47 = (f32[128]{0:T(128)S(1)}, f32[128]{0:T(128)}, u32[]{:S(2)}) copy-start(f32[128]{0:T(128)} %copy-done.46) | copy-start | bytes 1540
  67.9 12.5 %copy-start.49 = (f32[128]{0:T(128)S(1)}, f32[128]{0:T(128)}, u32[]{:S(2)}) copy-start(f32[128]{0:T(128)} %copy-done.48) | copy-start | bytes 1540
  67.9 12.5 %copy-start.51 = (f32[128]{0:T(128)S(1)}, f32[128]{0:T(128)}, u32[]{:S(2)}) copy-start(f32[128]{0:T(128)} %copy-done.50) | copy-start | bytes 1540
  67.9 12.5 %copy-start.53 = (f32[128]{0:T(128)S(1)}, f32[128]{0:T(128)}, u32[]{:S(2)}) copy-start(f32[128]{0:T(128)} %copy-done.52) | copy-start | bytes 1540
  68.8 28.7 %all-to-all-start.1 = ((f32[32,16,256]{2,1,0:T(8,128)}), f32[32,16,256]{2,1,0:T(8,128)S(1)}, u32[]{:S(2)}, u32[]{:S(2)}) async-start(f32[32,16,256]{2,1,0:T(8,128)} %bitcast_add_fusion), calls=%async_computation.1 | async-start | bytes 1048576 | tf_op jit(solution)/shard_map/all_to_all | solution.py:276
  (29 other events, 39.5 us)

commit v16 on v14

--- a/solution.py
+++ b/solution.py
@@ -253,18 +253,21 @@
     bulk_bc = conv_backward(
         jnp.concatenate([grad_u_bc, jnp.zeros_like(after_bc)]), conv_bc, note_all[rim_width:]
     )
-    tail_bc = conv_backward(
-        jnp.concatenate([grad_u_bc[tok_rows - rim_width :], after_bc]),
+    rim_bc = conv_backward(
+        jnp.concatenate([jnp.zeros_like(after_bc), after_bc]),
         conv_bc,
         note_all[tok_rows : tok_rows + 2 * rim_width],
     )
-    whole_bc = jnp.concatenate([bulk_bc[: tok_rows - rim_width], tail_bc])
     chips, cores = lax.axis_size("chip"), lax.axis_size("core")
-    pieces = whole_bc.reshape(chips, cores, tok_rows // (chips * cores), whole_bc.shape[1])
+    share = tok_rows // (chips * cores)
+    pieces = bulk_bc.reshape(chips, cores, share, bulk_bc.shape[1])
     core = lax.axis_index("core")
     mine = lax.dynamic_index_in_dim(pieces, core, 1, keepdims=False)
     other = lax.dynamic_index_in_dim(pieces, 1 - core, 1, keepdims=False)
     pair_sum = mine + lax.ppermute(other, "core", [(0, 1), (1, 0)])
+    rim_pair = rim_bc + lax.ppermute(rim_bc, "core", [(source, cores - 1) for source in range(cores - 1)])
+    rim_pair = jnp.where(core == cores - 1, rim_pair, 0.0)
+    pair_sum = pair_sum.at[chips - 1, share - rim_width :].add(rim_pair)
     grad_pre_bc = lax.all_to_all(pair_sum, "chip", 0, 0, tiled=False).sum(0)
     return (grad_pre_x, grad_pre_bc, grad_log_decay)
 

time: 87.6 us -> 89.9 us (1.026)
  local copies, waits for them, and re-layouts: 12.7 us -> 14.7 us
  starting transfers between devices: 24.4 us -> 25.7 us
  waiting for transfers between devices: 10.9 us -> 9.61 us
  other arithmetic: 19.8 us -> 20.7 us
    scatter-add x0 -> x1, local copies, waits for them, and re-layouts: none -> 1.3 us  [local(): pair_sum = pair_sum.at[chips - 1, share - rim_width:].add(rim_pair)]
    ppermute x0 -> x1, starting transfers between devices: none -> 1.28 us  [local(): lax.ppermute(rim_bc, 'core', [(source, cores - 1) for source in range(cor...]
    unnamed x3, other arithmetic: 1.46 us -> 0.25 us
    add x3, other arithmetic: 1.18 us -> 2.25 us  [conv_backward(): result + weights[k][None, :] * extended[lag:lag + count] * linked[:, None]]
    unnamed x157 -> x137, local copies, waits for them, and re-layouts: 2.48 us -> 2.57 us
  transfers between devices with their start and end apart: 6 -> 7, of which waited for: 3 -> 3; matrix products, arithmetic and copies ran while one was open for 33% -> 34% of each run, Pallas kernels for 0% -> 0%
where the time goes in v16:
time: 89.9 us; the launch traced here: 88.7 us
  starting transfers between devices  25.7 us (29%)
  other arithmetic  20.7 us (23%)
  matrix products  14.9 us (17%)
  local copies, waits for them, and re-layouts  14.7 us (16%)
  waiting for transfers between devices  9.61 us (11%)
  between operations  3.13 us (3%)
    dot_general x11, matrix products, einsum(): jnp.einsum(spec, *operands, precision=lax.Precision.HIGH, preferred_eleme...  12.7 us
    all_to_all x1, starting transfers between devices, local(): grad_pre_bc = lax.all_to_all(pair_sum, 'chip', 0, 0, tiled=False).sum(0)  11.3 us
    ppermute x3, starting transfers between devices, shifted(): lax.ppermute(value, axis, [(source, source + steps) for source in range(i...  8.39 us
    all_to_all x1, waiting for transfers between devices, local(): grad_pre_bc = lax.all_to_all(pair_sum, 'chip', 0, 0, tiled=False).sum(0)  5.76 us
    all_to_all x1, starting transfers between devices, chain_both(): arrived = lax.all_to_all(outgoing, axis, 0, 0, tiled=False)  4.62 us
    ppermute x3, waiting for transfers between devices, shifted(): lax.ppermute(value, axis, [(source, source + steps) for source in range(i...  3.84 us
    convert_element_type x2, other arithmetic, conv_backward(): weights[k][None, :] * extended[lag:lag + count] * linked[:, None]  2.61 us
    unnamed x137, local copies, waits for them, and re-layouts  2.57 us
  transfers between devices with their start and end apart: 7, of which 3 were waited for; matrix products, arithmetic and copies ran while one was open for 34% of the time, Pallas kernels for 0%

profile of v16, /device:TPU:8, one launch (start us, length us, event | category | flops | bytes accessed | tf_op | source)
XLA Modules:
  0.0 88.7 jit_solution(5637663113816073944)
XLA Ops:
  0.7 0.8 slice.303
  1.4 0.7 slice.302
  2.1 3.5 %collective-permute-start = (bf16[3,384]{1,0:T(4,128)(2,1)S(1)}, bf16[3,384]{1,0:T(4,128)(2,1)S(1)}, u32[]{:S(2)}, u32[]{:S(2)}) collective-permute-start(bf16[3,384]{1,0:T(4,128)(2,1)S(1)} %pad_maximum_fusion.6), channel_id=1, source_target_pairs={{0,64},{64,128},{128,192},{1,65},{65,129},{129,193},{2,66},{66,130... | collective-permute-start | bytes 6920 | tf_op jit(solution)/shard_map/ppermute | solution.py:18
  5.6 0.8 reduce-window.9
  6.5 0.7 bitcast_subtract_fusion.1
  7.7 0.6 fusion.138
  8.3 2.0 %fusion.119 = (f32[1024]{0:T(1024)}, f32[1024]{0:T(1024)S(1)}, f32[1024]{0:T(1024)S(1)}, f32[1024]{0:T(1024)}, f32[1024]{0:T(1024)}, /*index=5*/f32[1024]{0:T(1024)S(1)}, f32[1024]{0:T(1024)S(1)}, f32[1024]{0:T(1024)S(1)}) fusion(s32[1030]{0:T(1024)S(1)} %broadcast_add_fusion, s32[]{:T(128)} %bitcast.11, s32[]{:T(128)} %bitcast.17), kind=kLoop, calls=%fused_computation.208 | loop fusion | flops 16384 | bytes 61448 | tf_op jit(solution)/shard_map/convert_element_type | solution.py:97
  11.5 0.7 compare_convert_fusion.7
  12.3 0.7 reshape.485
  13.6 0.6 compare_convert_fusion.6
  14.7 0.8 fusion.139
  15.6 0.8 slice_bitcast_fusion.11
  16.5 0.7 slice_reduce_fusion.8
  17.2 1.4 %compare_and_fusion = (pred[4,256,256]{1,2,0:T(8,128)(4,1)}, f32[4,256,256]{1,2,0:T(8,128)}) fusion(s32[4,256]{1,0:T(4,128)S(1)} %reshape.489, pred[256,256]{0,1:T(8,128)(4,1)S(1)} %iota_compare_fusion), kind=kLoop, calls=%fused_computation.44 | loop fusion | flops 786432 | bytes 1380352 | tf_op jit(solution)/shard_map/jvp()/and | solution.py:165
  18.6 0.6 broadcast_multiply_fusion
  19.1 0.5 multiply_bitcast_fusion.1
  20.5 0.6 copy.232
  21.4 1.8 %fusion.26 = (f32[1024,256]{1,0:T(8,128)S(1)}, f32[1024,256]{1,0:T(8,128)}) fusion(f32[1027,256]{1,0:T(8,128)S(1)} %maximum_convert_fusion, f32[256]{0:T(256)S(1)} %bitcast.398, f32[1024]{0:T(1024)S(1)} %get-tuple-element.94, f32[256]{0:T(256)S(1)} %bitcast.392, f32[1024]{0:T(1024)S(1)} %get-tuple-element.95, f32[256]{0:T(256)S(1)} %bitcast.388, ...), kind=kLoop, calls=%fused_computation.43 | loop fusion | flops 3670016 | bytes 6307840 | tf_op jit(solution)/shard_map/jit(silu)/mul | solution.py:203
  23.5 1.4 %fusion.56 = (f32[1024,128]{0,1:T(8,128)S(1)}, f32[1024,128]{0,1:T(8,128)}) fusion(f32[1027,128]{0,1:T(8,128)S(1)} %maximum_convert_fusion.1, f32[128]{0:T(128)S(1)} %get-tuple-element.109, f32[1024]{0:T(1024)S(1)} %get-tuple-element.94, f32[128]{0:T(128)S(1)} %get-tuple-element.110, f32[1024]{0:T(1024)S(1)} %get-tuple-element.95, ...), kind=kLoop, calls=%fused_computation.91 | loop fusion | flops 1835008 | bytes 3160064 | tf_op jit(solution)/shard_map/jit(silu)/mul | solution.py:202
  25.5 1.4 %convolution_bitcast_fusion.5 = f32[1,2,64,128]{3,2,1,0:T(8,128)S(1)} fusion(bf16[1024,2,64]{0,2,1:T(8,128)(2,1)} %bitcast.370, f32[2,1024]{1,0:T(2,128)S(1)} %get-tuple-element.98, f32[1024,256]{1,0:T(8,128)S(1)} %get-tuple-element.65), kind=kOutput, calls=%fused_computation.24 | convolution fusion | flops 100925440 | bytes 860160 | tf_op jit(solution)/shard_map/thp,ht,tn->hpn/dot_general | solution.py:232
  27.2 0.9 select_select_fusion
  28.1 4.6 %all-to-all-start = ((f32[4,2,8320]{2,1,0:T(2,128)}), f32[4,2,8320]{2,1,0:T(2,128)S(1)}, u32[]{:S(2)}, u32[]{:S(2)}) async-start(f32[4,2,8320]{2,1,0:T(2,128)} %select_select_fusion), calls=%async_computation | async-start | bytes 532480 | tf_op jit(solution)/shard_map/all_to_all | solution.py:139
  32.7 0.6 fusion.140
  33.3 5.1 %fusion.16 = (f32[2,4,256]{2,1,0:T(4,128)}, f32[2,4,256]{2,1,0:T(4,128)}, f32[4,256,256]{1,2,0:T(8,128)S(1)}, f32[2,4,256,256]{2,3,1,0:T(8,128)}) fusion(f32[4,256,256]{1,2,0:T(8,128)} %get-tuple-element.83, f32[2,4,256]{2,1,0:T(4,128)S(1)} %bitcast.381, f32[4,256,256]{1,2,0:T(8,128)S(1)} %fusion.140, pred[4,256,256]{1,2,0:T(8,128)(4,1)S(1)} %copy-done.12, ...), kind=kOutput, calls=%fused_computation.20 | convolution fusion | flops 207351808 | bytes 6316032 | tf_op jit(solution)/shard_map/transpose(jvp(hbij,hbjp->hbip))/dot_general | solution.py:155
  40.2 0.8 fusion.124
  41.4 0.6 convolution_bitcast_fusion.2
  42.2 0.6 convolution_add_fusion.1
  42.8 0.6 convolution_bitcast_fusion.1
  43.4 1.0 %convolution_add_fusion = f32[4,256,128]{2,1,0:T(8,128)S(1)} fusion(f32[4,256,128]{2,1,0:T(8,128)S(1)} %convolution_bitcast_fusion.1, f32[4,256,256]{1,2,0:T(8,128)S(1)} %get-tuple-element.35, f32[4,256,128]{2,1,0:T(8,128)S(1)} %bitcast.362), kind=kOutput, calls=%fused_computation.11 | convolution fusion | flops 201457664 | bytes 2621440 | tf_op jit(solution)/shard_map/transpose(jvp(bin,bjn->bij))/dot_general | solution.py:155
  45.2 1.6 %multiply_add_fusion = f32[1024,256]{1,0:T(8,128)} fusion(f32[1024,256]{1,0:T(8,128)S(1)} %maximum_multiply_fusion, f32[1024]{0:T(1024)S(1)} %copy-done.16, f32[1024]{0:T(1024)S(1)} %copy-done.17, f32[1024]{0:T(1024)S(1)} %copy-done.15, f32[256]{0:T(256)S(1)} %bitcast.399, f32[256]{0:T(256)S(1)} %bitcast.393, f32[256]{0:T(256)S(1)} %bitcast.389, ...), kind=kLoop, calls=%fused_computation.38 | loop fusion | flops 2621440 | bytes 2113536 | tf_op jit(solution)/shard_map/add | solution.py:97
  46.7 1.1 %dynamic-slice_bitcast_fusion = f32[32,16,256]{2,1,0:T(8,128)S(1)} fusion(f32[32,2,16,256]{3,2,1,0:T(8,128)} %bitcast.49, s32[]{:T(128)S(6)} %select_n.251), kind=kLoop, calls=%fused_computation.87 | loop fusion | bytes 1048580 | tf_op jit(solution)/shard_map/jit(dynamic_index_in_dim)/squeeze | solution.py:266
  49.0 2.4 %collective-permute-start.3 = (f32[3,256]{1,0:T(4,128)S(1)}, f32[3,256]{1,0:T(4,128)S(1)}, u32[]{:S(2)}, u32[]{:S(2)}) collective-permute-start(f32[3,256]{1,0:T(4,128)S(1)} %slice.410), channel_id=1, source_target_pairs={{64,0},{128,64},{192,128},{65,1},{129,65},{193,129},{66,2},{130,66... | collective-permute-start | bytes 9224 | tf_op jit(solution)/shard_map/ppermute | solution.py:18
  51.6 0.7 copy.250
  52.3 0.7 copy.252
  52.9 1.6 %collective-permute-done.3 = f32[3,256]{1,0:T(4,128)S(1)} collective-permute-done((f32[3,256]{1,0:T(4,128)S(1)}, f32[3,256]{1,0:T(4,128)S(1)}, u32[]{:S(2)}, u32[]{:S(2)}) %collective-permute-start.3) | collective-permute-done | bytes 3104 | tf_op jit(solution)/shard_map/ppermute | solution.py:18
  54.6 1.3 %collective-permute-start.4 = (f32[3,256]{1,0:T(4,128)S(1)}, f32[3,256]{1,0:T(4,128)S(1)}, u32[]{:S(2)}, u32[]{:S(2)}) collective-permute-start(f32[3,256]{1,0:T(4,128)S(1)} %fusion.112), channel_id=1, source_target_pairs={{0,1},{2,3},{4,5},{6,7},{8,9},{10,11},{12,13},{14,15},{16,17},{18,... | collective-permute-start | bytes 9224 | tf_op jit(solution)/shard_map/ppermute | solution.py:268
  55.9 1.9 %bitcast_add_fusion = f32[32,16,256]{2,1,0:T(8,128)} fusion(f32[32,16,256]{2,1,0:T(8,128)S(1)} %collective-permute-done.2, f32[32,2,16,256]{3,2,1,0:T(8,128)} %bitcast.49, s32[]{:T(128)S(6)} %select_n.250), kind=kLoop, calls=%fused_computation.75 | loop fusion | flops 131072 | bytes 1572868 | tf_op jit(solution)/shard_map/add | solution.py:267
  57.8 0.8 slice_add_fusion
  58.6 1.3 %scatter-add.4 = f32[32,16,256]{2,1,0:T(8,128)} dynamic-update-slice(f32[32,16,256]{2,1,0:T(8,128)} %bitcast_add_fusion, f32[1,3,256]{2,1,0:T(4,128)S(1)} %slice_add_fusion, s32[]{:T(128)} %constant.86.clone.1, s32[]{:T(128)} %constant.87.clone.1, s32[]{:T(128)} %constant.76.clone.1) | dynamic-update-slice | bytes 6148 | tf_op jit(solution)/shard_map/scatter-add | solution.py:270
  59.9 11.3 %all-to-all-start.1 = ((f32[32,16,256]{2,1,0:T(8,128)}), f32[32,16,256]{2,1,0:T(8,128)S(1)}, u32[]{:S(2)}, u32[]{:S(2)}) async-start(f32[32,16,256]{2,1,0:T(8,128)} %scatter-add.4), calls=%async_computation.1 | async-start | bytes 1048576 | tf_op jit(solution)/shard_map/all_to_all | solution.py:271
  71.2 2.4 %fusion.11 = f32[4,256,2,64]{1,3,2,0:T(8,128)S(1)} fusion(f32[2,4,256,256]{2,3,1,0:T(8,128)} %get-tuple-element.67, f32[4,2,64,256]{3,2,1,0:T(8,128)S(1)} %get-tuple-element.122, bf16[2,4,256,64]{2,1,3,0:T(4,128)(2,1)S(1)} %bitcast.368, f32[4,256,2]{1,2,0:T(2,128)} %copy.232), kind=kOutput, calls=%fused_computation.17 | convolution fusion | flops 201588736 | bytes 3416064 | tf_op jit(solution)/shard_map/transpose(jvp(hbij,hbjp->hbip))/dot_general | solution.py:155
  74.5 2.5 %collective-permute-start.1 = (f32[3,128]{0,1:T(8,128)S(1)}, f32[3,128]{0,1:T(8,128)S(1)}, u32[]{:S(2)}, u32[]{:S(2)}) collective-permute-start(f32[3,128]{0,1:T(8,128)S(1)} %slice.396), channel_id=1, source_target_pairs={{64,0},{128,64},{192,128},{65,1},{129,65},{193,129},{66,2},{130,66... | collective-permute-start | bytes 4616 | tf_op jit(solution)/shard_map/ppermute | solution.py:18
  77.7 0.6 copy.287
  78.4 2.3 %collective-permute-done.1 = f32[3,128]{0,1:T(8,128)S(1)} collective-permute-done((f32[3,128]{0,1:T(8,128)S(1)}, f32[3,128]{0,1:T(8,128)S(1)}, u32[]{:S(2)}, u32[]{:S(2)}) %collective-permute-start.1) | collective-permute-done | bytes 1568 | tf_op jit(solution)/shard_map/ppermute | solution.py:18
  80.7 0.6 fusion.32
  81.3 1.0 %copy.254 = f32[1024,128]{1,0:T(8,128)} copy(f32[1024,128]{0,1:T(8,128)S(1)} %fusion.32) | data formatting | bytes 1048576
  82.3 5.8 %all-to-all-done.1 = f32[32,16,256]{2,1,0:T(8,128)S(1)} async-done(((f32[32,16,256]{2,1,0:T(8,128)}), f32[32,16,256]{2,1,0:T(8,128)S(1)}, u32[]{:S(2)}, u32[]{:S(2)}) %all-to-all-start.1) | async-done | bytes 524320 | tf_op jit(solution)/shard_map/all_to_all | solution.py:271
  88.1 0.6 reduce_sum.128
  (204 shorter events, 9.2 us)
Async XLA Ops:
  0.6 20.5 %copy-start.9 = (bf16[1024,256]{1,0:T(8,128)(2,1)S(1)}, bf16[1024,256]{1,0:T(8,128)(2,1)}, u32[]{:S(2)}) copy-start(bf16[1024,256]{1,0:T(8,128)(2,1)} %param.10) | copy-start | bytes 1572868
  0.6 19.2 %copy-start.10 = (bf16[1024,128]{1,0:T(8,128)(2,1)S(1)}, bf16[1024,128]{1,0:T(8,128)(2,1)}, u32[]{:S(2)}) copy-start(bf16[1024,128]{1,0:T(8,128)(2,1)} %param.9) | copy-start | bytes 786436
  0.7 19.4 %copy-start.11 = (bf16[1024,128]{1,0:T(8,128)(2,1)S(1)}, bf16[1024,128]{1,0:T(8,128)(2,1)}, u32[]{:S(2)}) copy-start(bf16[1024,128]{1,0:T(8,128)(2,1)} %param.15) | copy-start | bytes 786436
  2.1 19.0 %collective-permute-start = (bf16[3,384]{1,0:T(4,128)(2,1)S(1)}, bf16[3,384]{1,0:T(4,128)(2,1)S(1)}, u32[]{:S(2)}, u32[]{:S(2)}) collective-permute-start(bf16[3,384]{1,0:T(4,128)(2,1)S(1)} %pad_maximum_fusion.6), channel_id=1, source_target_pairs={{0,64},{64,128},{128,192},{1,65},{65,129},{129,193},{2,66},{66,130... | collective-permute-start | bytes 6920 | tf_op jit(solution)/shard_map/ppermute | solution.py:18
  12.3 4.2 %copy-start.45 = (f32[4]{0:T(128)}, f32[4]{0:T(128)S(1)}, u32[]{:S(2)}) copy-start(f32[4]{0:T(128)S(1)} %get-tuple-element.63) | copy-start | bytes 52
  12.3 27.8 %copy-start.19 = (f32[4,256]{1,0:T(4,128)}, f32[4,256]{1,0:T(4,128)S(1)}, u32[]{:S(2)}) copy-start(f32[4,256]{1,0:T(4,128)S(1)} %get-tuple-element.101) | copy-start | bytes 12292
  13.6 26.6 %copy-start.29 = (f32[2,4]{1,0:T(2,128)}, f32[2,4]{1,0:T(2,128)S(1)}, u32[]{:S(2)}) copy-start(f32[2,4]{1,0:T(2,128)S(1)} %slice_reduce_fusion) | copy-start | bytes 100
  15.6 5.8 %copy-start.23 = (f32[1,256]{1,0:T(1,128)}, f32[1,256]{1,0:T(1,128)S(1)}, u32[]{:S(2)}) copy-start(f32[1,256]{1,0:T(1,128)S(1)} %get-tuple-element.103) | copy-start | bytes 3076
  15.6 5.8 %copy-start.25 = (f32[1,256]{1,0:T(1,128)}, f32[1,256]{1,0:T(1,128)S(1)}, u32[]{:S(2)}) copy-start(f32[1,256]{1,0:T(1,128)S(1)} %get-tuple-element.104) | copy-start | bytes 3076
  15.6 5.8 %copy-start.27 = (f32[1,256]{1,0:T(1,128)}, f32[1,256]{1,0:T(1,128)S(1)}, u32[]{:S(2)}) copy-start(f32[1,256]{1,0:T(1,128)S(1)} %get-tuple-element.106) | copy-start | bytes 3076
  15.6 5.8 %copy-start.32 = (f32[1,256]{1,0:T(1,128)}, f32[1,256]{1,0:T(1,128)S(1)}, u32[]{:S(2)}) copy-start(f32[1,256]{1,0:T(1,128)S(1)} %get-tuple-element.105) | copy-start | bytes 3076
  16.4 7.0 %copy-start.47 = (f32[128]{0:T(128)}, f32[128]{0:T(128)S(1)}, u32[]{:S(2)}) copy-start(f32[128]{0:T(128)S(1)} %get-tuple-element.107) | copy-start | bytes 1540
  16.4 7.0 %copy-start.49 = (f32[128]{0:T(128)}, f32[128]{0:T(128)S(1)}, u32[]{:S(2)}) copy-start(f32[128]{0:T(128)S(1)} %get-tuple-element.108) | copy-start | bytes 1540
  16.4 7.0 %copy-start.51 = (f32[128]{0:T(128)}, f32[128]{0:T(128)S(1)}, u32[]{:S(2)}) copy-start(f32[128]{0:T(128)S(1)} %get-tuple-element.109) | copy-start | bytes 1540
  16.4 7.0 %copy-start.53 = (f32[128]{0:T(128)}, f32[128]{0:T(128)S(1)}, u32[]{:S(2)}) copy-start(f32[128]{0:T(128)S(1)} %get-tuple-element.110) | copy-start | bytes 1540
  17.2 22.3 %copy-start.34 = (f32[2]{0:T(128)}, f32[2]{0:T(128)S(1)}, u32[]{:S(2)}) copy-start(f32[2]{0:T(128)S(1)} %get-tuple-element.50) | copy-start | bytes 28
  17.2 22.3 %copy-start.36 = (f32[2]{0:T(128)}, f32[2]{0:T(128)S(1)}, u32[]{:S(2)}) copy-start(f32[2]{0:T(128)S(1)} %get-tuple-element.51) | copy-start | bytes 28
  17.2 22.3 %copy-start.40 = (f32[2]{0:T(128)}, f32[2]{0:T(128)S(1)}, u32[]{:S(2)}) copy-start(f32[2]{0:T(128)S(1)} %get-tuple-element.52) | copy-start | bytes 28
  20.3 18.1 %copy-start.13 = (f32[4,2,256]{2,1,0:T(2,128)}, f32[4,2,256]{2,1,0:T(2,128)S(1)}, u32[]{:S(2)}) copy-start(f32[4,2,256]{2,1,0:T(2,128)S(1)} %copy.229) | copy-start | bytes 24580
  25.5 7.8 %copy-start.12 = (pred[4,256,256]{1,2,0:T(8,128)(4,1)S(1)}, pred[4,256,256]{1,2,0:T(8,128)(4,1)}, u32[]{:S(2)}) copy-start(pred[4,256,256]{1,2,0:T(8,128)(4,1)} %get-tuple-element.82) | copy-start | bytes 786436
  28.1 10.8 %all-to-all-start = ((f32[4,2,8320]{2,1,0:T(2,128)}), f32[4,2,8320]{2,1,0:T(2,128)S(1)}, u32[]{:S(2)}, u32[]{:S(2)}) async-start(f32[4,2,8320]{2,1,0:T(2,128)} %select_select_fusion), calls=%async_computation | async-start | bytes 532480 | tf_op jit(solution)/shard_map/all_to_all | solution.py:139
  44.9 3.5 %copy-start.4 = (f32[2,4,64,128]{3,2,0,1:T(8,128)S(1)}, f32[2,4,64,128]{3,2,0,1:T(8,128)}, u32[]{:S(2)}) copy-start(f32[2,4,64,128]{3,2,0,1:T(8,128)} %copy-done.3) | copy-start | bytes 786436
  44.9 6.5 %copy-start.30 = (f32[2,4]{1,0:T(2,128)S(1)}, f32[2,4]{1,0:T(2,128)}, u32[]{:S(2)}) copy-start(f32[2,4]{1,0:T(2,128)} %copy-done.29) | copy-start | bytes 100
  45.0 6.5 %copy-start.46 = (f32[4]{0:T(128)S(1)}, f32[4]{0:T(128)}, u32[]{:S(2)}) copy-start(f32[4]{0:T(128)} %copy-done.45) | copy-start | bytes 52
  45.0 7.3 %copy-start.55 = (f32[2,4]{1,0:T(2,128)S(1)}, f32[2,4]{1,0:T(2,128)}, u32[]{:S(2)}) copy-start(f32[2,4]{1,0:T(2,128)} %get-tuple-element.84) | copy-start | bytes 100
  45.0 9.5 %copy-start.38 = (f32[256]{0:T(256)S(1)}, f32[256]{0:T(256)}, u32[]{:S(2)}) copy-start(f32[256]{0:T(256)} %broadcast_multiply_fusion) | copy-start | bytes 3076
  45.0 9.5 %copy-start.42 = (f32[3]{0:T(128)S(1)}, f32[3]{0:T(128)}, u32[]{:S(2)}) copy-start(f32[3]{0:T(128)} %get-tuple-element.86) | copy-start | bytes 40
  45.0 9.5 %copy-start.43 = (f32[3]{0:T(128)S(1)}, f32[3]{0:T(128)}, u32[]{:S(2)}) copy-start(f32[3]{0:T(128)} %get-tuple-element.87) | copy-start | bytes 40
  45.0 9.5 %copy-start.44 = (f32[3]{0:T(128)S(1)}, f32[3]{0:T(128)}, u32[]{:S(2)}) copy-start(f32[3]{0:T(128)} %get-tuple-element.88) | copy-start | bytes 40
  47.8 8.1 %collective-permute-start.2 = (f32[32,16,256]{2,1,0:T(8,128)S(1)}, f32[32,16,256]{2,1,0:T(8,128)S(1)}, u32[]{:S(2)}, u32[]{:S(2)}) collective-permute-start(f32[32,16,256]{2,1,0:T(8,128)S(1)} %dynamic-slice_bitcast_fusion), channel_id=1, source_target_pairs={{0,1},{1,0},{2,3},{3,2},{4,5},{5,4},{6,7},{7,6},{8,9},{9,8},{10,11... | collective-permute-start | bytes 1572872 | tf_op jit(solution)/shard_map/ppermute | solution.py:267
  49.0 5.5 %collective-permute-start.3 = (f32[3,256]{1,0:T(4,128)S(1)}, f32[3,256]{1,0:T(4,128)S(1)}, u32[]{:S(2)}, u32[]{:S(2)}) collective-permute-start(f32[3,256]{1,0:T(4,128)S(1)} %slice.410), channel_id=1, source_target_pairs={{64,0},{128,64},{192,128},{65,1},{129,65},{193,129},{66,2},{130,66... | collective-permute-start | bytes 9224 | tf_op jit(solution)/shard_map/ppermute | solution.py:18
  54.6 3.2 %collective-permute-start.4 = (f32[3,256]{1,0:T(4,128)S(1)}, f32[3,256]{1,0:T(4,128)S(1)}, u32[]{:S(2)}, u32[]{:S(2)}) collective-permute-start(f32[3,256]{1,0:T(4,128)S(1)} %fusion.112), channel_id=1, source_target_pairs={{0,1},{2,3},{4,5},{6,7},{8,9},{10,11},{12,13},{14,15},{16,17},{18,... | collective-permute-start | bytes 9224 | tf_op jit(solution)/shard_map/ppermute | solution.py:268
  59.9 28.2 %all-to-all-start.1 = ((f32[32,16,256]{2,1,0:T(8,128)}), f32[32,16,256]{2,1,0:T(8,128)S(1)}, u32[]{:S(2)}, u32[]{:S(2)}) async-start(f32[32,16,256]{2,1,0:T(8,128)} %scatter-add.4), calls=%async_computation.1 | async-start | bytes 1048576 | tf_op jit(solution)/shard_map/all_to_all | solution.py:271
  73.7 3.3 %copy-start.8 = (f32[1,2,64,128]{3,2,1,0:T(8,128)S(1)}, f32[1,2,64,128]{3,2,1,0:T(8,128)}, u32[]{:S(2)}) copy-start(f32[1,2,64,128]{3,2,1,0:T(8,128)} %copy-done.7) | copy-start | bytes 196612
  74.0 3.4 %copy-start.20 = (f32[4,256]{1,0:T(4,128)S(1)}, f32[4,256]{1,0:T(4,128)}, u32[]{:S(2)}) copy-start(f32[4,256]{1,0:T(4,128)} %copy-done.19) | copy-start | bytes 12292
  74.0 3.4 %copy-start.22 = (f32[2,4,256]{2,0,1:T(2,128)S(1)}, f32[2,4,256]{2,0,1:T(2,128)}, u32[]{:S(2)}) copy-start(f32[2,4,256]{2,0,1:T(2,128)} %copy-done.21) | copy-start | bytes 24580
  74.1 3.4 %copy-start.31 = (f32[2,4]{1,0:T(2,128)S(1)}, f32[2,4]{1,0:T(2,128)}, u32[]{:S(2)}) copy-start(f32[2,4]{1,0:T(2,128)} %copy-done.29) | copy-start | bytes 100
  74.1 3.4 %copy-start.56 = (f32[2,4,1]{2,1,0:T(4,128)S(1)}, f32[2,4,1]{2,1,0:T(4,128)}, u32[]{:S(2)}) copy-start(f32[2,4,1]{2,1,0:T(4,128)} %copy.250) | copy-start | bytes 100
  74.1 3.4 %copy-start.57 = (f32[2,4,1]{2,1,0:T(4,128)S(1)}, f32[2,4,1]{2,1,0:T(4,128)}, u32[]{:S(2)}) copy-start(f32[2,4,1]{2,1,0:T(4,128)} %copy.252) | copy-start | bytes 100
  74.1 3.4 %copy-start.59 = (f32[4,256]{1,0:T(4,128)S(1)}, f32[4,256]{1,0:T(4,128)}, u32[]{:S(2)}) copy-start(f32[4,256]{1,0:T(4,128)} %copy-done.58) | copy-start | bytes 12292
  74.1 3.4 %copy-start.61 = (f32[2,4,256]{2,1,0:T(4,128)S(1)}, f32[2,4,256]{2,1,0:T(4,128)}, u32[]{:S(2)}) copy-start(f32[2,4,256]{2,1,0:T(4,128)} %get-tuple-element.33) | copy-start | bytes 24580
  74.1 3.4 %copy-start.62 = (f32[2,4,256]{2,1,0:T(4,128)S(1)}, f32[2,4,256]{2,1,0:T(4,128)}, u32[]{:S(2)}) copy-start(f32[2,4,256]{2,1,0:T(4,128)} %get-tuple-element.34) | copy-start | bytes 24580
  74.1 6.5 %copy-start.18 = (f32[1024]{0:T(1024)S(1)}, f32[1024]{0:T(1024)}, u32[]{:S(2)}) copy-start(f32[1024]{0:T(1024)} %get-tuple-element.93) | copy-start | bytes 12292
  74.1 6.5 %copy-start.48 = (f32[128]{0:T(128)S(1)}, f32[128]{0:T(128)}, u32[]{:S(2)}) copy-start(f32[128]{0:T(128)} %copy-done.47) | copy-start | bytes 1540
  74.1 6.5 %copy-start.50 = (f32[128]{0:T(128)S(1)}, f32[128]{0:T(128)}, u32[]{:S(2)}) copy-start(f32[128]{0:T(128)} %copy-done.49) | copy-start | bytes 1540
  74.2 6.5 %copy-start.52 = (f32[128]{0:T(128)S(1)}, f32[128]{0:T(128)}, u32[]{:S(2)}) copy-start(f32[128]{0:T(128)} %copy-done.51) | copy-start | bytes 1540
  74.2 6.5 %copy-start.54 = (f32[128]{0:T(128)S(1)}, f32[128]{0:T(128)}, u32[]{:S(2)}) copy-start(f32[128]{0:T(128)} %copy-done.53) | copy-start | bytes 1540
  74.5 6.2 %collective-permute-start.1 = (f32[3,128]{0,1:T(8,128)S(1)}, f32[3,128]{0,1:T(8,128)S(1)}, u32[]{:S(2)}, u32[]{:S(2)}) collective-permute-start(f32[3,128]{0,1:T(8,128)S(1)} %slice.396), channel_id=1, source_target_pairs={{64,0},{128,64},{192,128},{65,1},{129,65},{193,129},{66,2},{130,66... | collective-permute-start | bytes 4616 | tf_op jit(solution)/shard_map/ppermute | solution.py:18
  (22 other events, 30.9 us)

commit v17 on v14

--- a/solution.py
+++ b/solution.py
@@ -258,7 +258,7 @@
         conv_bc,
         note_all[tok_rows : tok_rows + 2 * rim_width],
     )
-    whole_bc = jnp.concatenate([bulk_bc[: tok_rows - rim_width], tail_bc])
+    whole_bc = lax.dynamic_update_slice_in_dim(bulk_bc, tail_bc, tok_rows - rim_width, 0)
     chips, cores = lax.axis_size("chip"), lax.axis_size("core")
     pieces = whole_bc.reshape(chips, cores, tok_rows // (chips * cores), whole_bc.shape[1])
     core = lax.axis_index("core")

time: 87.6 us -> 95.5 us (1.090)
  local copies, waits for them, and re-layouts: 12.7 us -> 17.3 us
  other arithmetic: 19.8 us -> 23.8 us
  waiting for transfers between devices: 10.9 us -> 9.83 us
    dynamic_update_slice x0 -> x1, local copies, waits for them, and re-layouts: none -> 1.31 us  [local(): lax.dynamic_update_slice_in_dim(bulk_bc, tail_bc, tok_rows - rim_width, 0)]
    mul x2, local copies, waits for them, and re-layouts: 0.01 us -> 1.3 us  [block_forward_all(): jnp.exp(cumul[..., -1:] - cumul) * (note_blocks == note_blocks[:, -1:])]
    mul x1, other arithmetic: 0.08 us -> 1.35 us  [block_forward_all(): jnp.exp(cumul[..., -1:] - cumul) * (note_blocks == note_blocks[:, -1:])]
    broadcast_in_dim x4, local copies, waits for them, and re-layouts: 0.37 us -> 1.61 us  [block_forward_all(): state = through[:, block, None, None] * state + chunk[:, block]]
    squeeze x1, local copies, waits for them, and re-layouts: 0.85 us -> 1.95 us  [local(): other = lax.dynamic_index_in_dim(pieces, 1 - core, 1, keepdims=False)]
    add x3, other arithmetic: 1.18 us -> 2.26 us  [conv_backward(): result + weights[k][None, :] * extended[lag:lag + count] * linked[:, None]]
    reduce_sum x2, other arithmetic: 1.55 us -> 2.56 us  [block_forward_all(): state = through[:, block, None, None] * state + chunk[:, block]]
    ppermute x3, waiting for transfers between devices: 4.53 us -> 3.54 us  [shifted(): lax.ppermute(value, axis, [(source, source + steps) for source in range(i...]
  transfers between devices with their start and end apart: 6 -> 6, of which waited for: 3 -> 3; matrix products, arithmetic and copies ran while one was open for 33% -> 37% of each run, Pallas kernels for 0% -> 0%
where the time goes in v17:
time: 95.5 us; the launch traced here: 93.7 us
  starting transfers between devices  24.6 us (26%)
  other arithmetic  23.8 us (25%)
  local copies, waits for them, and re-layouts  17.3 us (18%)
  matrix products  15 us (16%)
  waiting for transfers between devices  9.83 us (10%)
  between operations  3.2 us (3%)
    dot_general x11, matrix products, einsum(): jnp.einsum(spec, *operands, precision=lax.Precision.HIGH, preferred_eleme...  12.7 us
    all_to_all x1, starting transfers between devices, local(): grad_pre_bc = lax.all_to_all(pair_sum, 'chip', 0, 0, tiled=False).sum(0)  11.3 us
    ppermute x3, starting transfers between devices, shifted(): lax.ppermute(value, axis, [(source, source + steps) for source in range(i...  8.66 us
    all_to_all x1, waiting for transfers between devices, local(): grad_pre_bc = lax.all_to_all(pair_sum, 'chip', 0, 0, tiled=False).sum(0)  6.28 us
    all_to_all x1, starting transfers between devices, chain_both(): arrived = lax.all_to_all(outgoing, axis, 0, 0, tiled=False)  4.62 us
    ppermute x3, waiting for transfers between devices, shifted(): lax.ppermute(value, axis, [(source, source + steps) for source in range(i...  3.54 us
    unnamed x161, local copies, waits for them, and re-layouts  2.9 us
    convert_element_type x2, other arithmetic, conv_backward(): weights[k][None, :] * extended[lag:lag + count] * linked[:, None]  2.63 us
  transfers between devices with their start and end apart: 6, of which 3 were waited for; matrix products, arithmetic and copies ran while one was open for 37% of the time, Pallas kernels for 0%

profile of v17, /device:TPU:8, one launch (start us, length us, event | category | flops | bytes accessed | tf_op | source)
XLA Modules:
  0.0 93.7 jit_solution(15690542266318258604)
XLA Ops:
  0.7 0.8 slice.278
  1.4 0.7 slice.277
  2.1 3.5 %collective-permute-start = (bf16[3,384]{1,0:T(4,128)(2,1)S(1)}, bf16[3,384]{1,0:T(4,128)(2,1)S(1)}, u32[]{:S(2)}, u32[]{:S(2)}) collective-permute-start(bf16[3,384]{1,0:T(4,128)(2,1)S(1)} %pad_maximum_fusion.7), channel_id=1, source_target_pairs={{0,64},{64,128},{128,192},{1,65},{65,129},{129,193},{2,66},{66,130... | collective-permute-start | bytes 6920 | tf_op jit(solution)/shard_map/ppermute | solution.py:18
  5.6 0.8 reduce-window.9
  6.5 0.7 bitcast_subtract_fusion.1
  8.3 2.0 %fusion.120 = (f32[1024]{0:T(1024)}, f32[1024]{0:T(1024)S(1)}, f32[1024]{0:T(1024)S(1)}, f32[1024]{0:T(1024)}, f32[1024]{0:T(1024)}, /*index=5*/f32[1024]{0:T(1024)S(1)}, f32[1024]{0:T(1024)S(1)}, f32[1024]{0:T(1024)S(1)}) fusion(s32[1030]{0:T(1024)S(1)} %broadcast_add_fusion, s32[]{:T(128)} %bitcast.11, s32[]{:T(128)} %bitcast.17), kind=kLoop, calls=%fused_computation.209 | loop fusion | flops 16384 | bytes 61448 | tf_op jit(solution)/shard_map/convert_element_type | solution.py:97
  11.5 0.7 compare_convert_fusion.7
  12.3 0.7 reshape.446
  13.6 0.7 compare_convert_fusion.6
  14.7 0.8 fusion.141
  15.6 0.8 slice_bitcast_fusion.11
  16.5 0.7 slice_reduce_fusion.8
  17.2 1.3 %compare_and_fusion = (pred[4,256,256]{1,2,0:T(8,128)(4,1)}, f32[4,256,256]{1,2,0:T(8,128)}) fusion(s32[4,256]{1,0:T(4,128)S(1)} %reshape.450, pred[256,256]{0,1:T(8,128)(4,1)S(1)} %iota_compare_fusion), kind=kLoop, calls=%fused_computation.44 | loop fusion | flops 786432 | bytes 1380352 | tf_op jit(solution)/shard_map/jvp()/and | solution.py:165
  20.0 1.8 %fusion.26 = (f32[1024,256]{1,0:T(8,128)S(1)}, f32[1024,256]{1,0:T(8,128)}) fusion(f32[1027,256]{1,0:T(8,128)S(1)} %maximum_convert_fusion, f32[256]{0:T(256)S(1)} %bitcast.387, f32[1024]{0:T(1024)S(1)} %get-tuple-element.84, f32[256]{0:T(256)S(1)} %bitcast.390, f32[1024]{0:T(1024)S(1)} %get-tuple-element.85, f32[256]{0:T(256)S(1)} %bitcast.384, ...), kind=kLoop, calls=%fused_computation.43 | loop fusion | flops 3670016 | bytes 6307840 | tf_op jit(solution)/shard_map/jit(silu)/mul | solution.py:203
  22.0 1.4 %fusion.56 = (f32[1024,128]{0,1:T(8,128)S(1)}, f32[1024,128]{0,1:T(8,128)}) fusion(f32[1027,128]{0,1:T(8,128)S(1)} %maximum_convert_fusion.1, f32[128]{0:T(128)S(1)} %get-tuple-element.99, f32[1024]{0:T(1024)S(1)} %get-tuple-element.84, f32[128]{0:T(128)S(1)} %get-tuple-element.100, f32[1024]{0:T(1024)S(1)} %get-tuple-element.85, ...), kind=kLoop, calls=%fused_computation.91 | loop fusion | flops 1835008 | bytes 3160064 | tf_op jit(solution)/shard_map/jit(silu)/mul | solution.py:202
  24.1 1.4 %convolution_bitcast_fusion.5 = f32[1,2,64,128]{3,2,1,0:T(8,128)S(1)} fusion(bf16[1024,2,64]{0,2,1:T(8,128)(2,1)} %bitcast.366, f32[2,1024]{1,0:T(2,128)S(1)} %get-tuple-element.88, f32[1024,256]{1,0:T(8,128)S(1)} %get-tuple-element.53), kind=kOutput, calls=%fused_computation.24 | convolution fusion | flops 100925440 | bytes 860160 | tf_op jit(solution)/shard_map/thp,ht,tn->hpn/dot_general | solution.py:232
  25.7 0.9 select_select_fusion
  26.6 4.6 %all-to-all-start = ((f32[4,2,8320]{2,1,0:T(2,128)}), f32[4,2,8320]{2,1,0:T(2,128)S(1)}, u32[]{:S(2)}, u32[]{:S(2)}) async-start(f32[4,2,8320]{2,1,0:T(2,128)} %select_select_fusion), calls=%async_computation | async-start | bytes 532480 | tf_op jit(solution)/shard_map/all_to_all | solution.py:139
  31.8 5.2 %fusion.16 = (f32[2,4,256]{2,1,0:T(4,128)}, f32[2,4,256]{2,1,0:T(4,128)}, f32[4,256,256]{1,2,0:T(8,128)S(1)}, f32[2,4,256,256]{2,3,1,0:T(8,128)}) fusion(f32[4,256,256]{1,2,0:T(8,128)} %get-tuple-element.73, f32[2,4,256]{2,1,0:T(4,128)S(1)} %bitcast.377, f32[4,256,256]{1,2,0:T(8,128)S(1)} %fusion.142, pred[4,256,256]{1,2,0:T(8,128)(4,1)S(1)} %copy-done.23, ...), kind=kOutput, calls=%fused_computation.20 | convolution fusion | flops 207351808 | bytes 6316032 | tf_op jit(solution)/shard_map/transpose(jvp(hbij,hbjp->hbip))/dot_general | solution.py:155
  38.1 0.7 slice_bitcast_fusion.1
  39.4 0.8 fusion.125
  40.6 0.6 convolution_bitcast_fusion.2
  41.3 0.7 slice_bitcast_fusion.3
  42.7 0.6 convolution_bitcast_fusion.1
  43.3 1.0 %convolution_add_fusion = f32[4,256,128]{2,1,0:T(8,128)S(1)} fusion(f32[4,256,128]{2,1,0:T(8,128)S(1)} %convolution_bitcast_fusion.1, f32[4,256,256]{1,2,0:T(8,128)S(1)} %get-tuple-element.23, f32[4,256,128]{2,1,0:T(8,128)S(1)} %bitcast.356), kind=kOutput, calls=%fused_computation.11 | convolution fusion | flops 201457664 | bytes 2621440 | tf_op jit(solution)/shard_map/transpose(jvp(bin,bjn->bij))/dot_general | solution.py:155
  44.9 2.7 %collective-permute-start.2 = (f32[3,256]{1,0:T(4,128)S(1)}, f32[3,256]{1,0:T(4,128)S(1)}, u32[]{:S(2)}, u32[]{:S(2)}) collective-permute-start(f32[3,256]{1,0:T(4,128)S(1)} %get-tuple-element.56), channel_id=1, source_target_pairs={{64,0},{128,64},{192,128},{65,1},{129,65},{193,129},{66,2},{130,66... | collective-permute-start | bytes 9224 | tf_op jit(solution)/shard_map/ppermute | solution.py:18
  47.8 1.6 %multiply_add_fusion = f32[1024,256]{1,0:T(8,128)} fusion(f32[1024,256]{1,0:T(8,128)S(1)} %maximum_multiply_fusion, f32[1024]{0:T(1024)S(1)} %copy-done.34, f32[1024]{0:T(1024)S(1)} %copy-done.36, f32[1024]{0:T(1024)S(1)} %copy-done.32, f32[256]{0:T(256)S(1)} %bitcast.388, f32[256]{0:T(256)S(1)} %bitcast.391, f32[256]{0:T(256)S(1)} %bitcast.385, ...), kind=kLoop, calls=%fused_computation.38 | loop fusion | flops 2621440 | bytes 2113536 | tf_op jit(solution)/shard_map/add | solution.py:97
  49.3 1.2 %collective-permute-done.2 = f32[3,256]{1,0:T(4,128)S(1)} collective-permute-done((f32[3,256]{1,0:T(4,128)S(1)}, f32[3,256]{1,0:T(4,128)S(1)}, u32[]{:S(2)}, u32[]{:S(2)}) %collective-permute-start.2) | collective-permute-done | bytes 3104 | tf_op jit(solution)/shard_map/ppermute | solution.py:18
  50.7 1.3 %dynamic_update_slice.3 = f32[1024,256]{1,0:T(8,128)} dynamic-update-slice(f32[1024,256]{1,0:T(8,128)} %multiply_add_fusion, f32[3,256]{1,0:T(4,128)S(1)} %fusion.113, s32[]{:T(128)} %constant.55.clone.1, s32[]{:T(128)} %constant.26.clone.1) | dynamic-update-slice | bytes 6148 | tf_op jit(solution)/shard_map/dynamic_update_slice | solution.py:261
  52.0 1.9 %dynamic-slice_bitcast_fusion = f32[32,16,256]{2,1,0:T(8,128)} fusion(f32[32,2,16,256]{3,2,1,0:T(8,128)} %bitcast.364, s32[]{:T(128)S(6)} %select_n.243), kind=kLoop, calls=%fused_computation.87 | loop fusion | bytes 1048580 | tf_op jit(solution)/shard_map/jit(dynamic_index_in_dim)/squeeze | solution.py:266
  53.9 1.3 %fusion.93 = f32[4,256,2]{1,0,2:T(4,128)} fusion(f32[256,2,4]{0,2,1:T(4,128)S(1)} %get-tuple-element.110, f32[4,256]{1,0:T(4,128)} %copy-done.38, f32[4,2]{0,1:T(2,128)} %bitcast.380), kind=kLoop, calls=%fused_computation.166 | loop fusion | flops 4096 | bytes 20512 | tf_op jit(solution)/shard_map/jvp()/mul | solution.py:161
  55.3 1.3 %copy.220 = f32[4,256,2]{1,2,0:T(2,128)} copy(f32[4,256,2]{1,0,2:T(4,128)} %fusion.93) | data formatting | bytes 16384 | tf_op jit(solution)/shard_map/jvp()/mul | solution.py:161
  56.6 1.4 %fusion.90 = (f32[2]{0:T(128)}, f32[2]{0:T(128)}) fusion(f32[2,4,64,128]{3,2,0,1:T(8,128)S(1)} %copy-done.5, f32[2]{0:T(128)} %copy-done.53, f32[1,2,64,128]{3,1,2,0:T(2,128)S(1)} %slice_bitcast_fusion.7, f32[2]{0:T(128)} %copy-done.58, f32[2,4,64,128]{3,2,0,1:T(8,128)S(1)} %copy-done.7, f32[1,2,64,128]{3,1,2,0:T(2,128)S(1)} %slice_bitcast_fusion.6, ...), kind=kLoop, calls=%fused_computation.143 | loop fusion | flops 196604 | bytes 393264 | tf_op jit(solution)/shard_map/transpose(jvp())/reduce_sum | solution.py:174
  58.0 0.7 copy.233
  58.7 0.7 copy.234
  59.5 1.2 %fusion.84 = (f32[2]{0:T(128)S(1)}, f32[2]{0:T(128)S(1)}) fusion(f32[1,2,64,128]{3,2,1,0:T(8,128)S(1)} %copy-done.28, f32[1,2,64,128]{3,2,1,0:T(8,128)S(1)} %copy-done.29, f32[1,2,64,128]{3,2,1,0:T(8,128)S(1)} %copy-done.27, f32[2,8320]{1,0:T(2,128)S(1)} %copy-done.17, f32[2,8320]{1,0:T(2,128)S(1)} %copy-done.19, f32[2]{0:T(128)} %get-tuple-element.37, ...), kind=kLoop, calls=%fused_computation.131 | loop fusion | flops 262140 | bytes 524336 | tf_op jit(solution)/shard_map/transpose(jvp())/reduce_sum | solution.py:174
  60.8 0.7 multiply_bitcast_fusion
  61.6 0.8 copy.238
  62.4 1.9 %bitcast_add_fusion = f32[32,16,256]{2,1,0:T(8,128)} fusion(f32[32,16,256]{2,1,0:T(8,128)} %collective-permute-done.3, f32[32,2,16,256]{3,2,1,0:T(8,128)S(1)} %bitcast.365, s32[]{:T(128)S(6)} %select_n.242), kind=kLoop, calls=%fused_computation.79 | loop fusion | flops 131072 | bytes 1572868 | tf_op jit(solution)/shard_map/add | solution.py:267
  64.3 11.3 %all-to-all-start.1 = ((f32[32,16,256]{2,1,0:T(8,128)}), f32[32,16,256]{2,1,0:T(8,128)S(1)}, u32[]{:S(2)}, u32[]{:S(2)}) async-start(f32[32,16,256]{2,1,0:T(8,128)} %bitcast_add_fusion), calls=%async_computation.1 | async-start | bytes 1048576 | tf_op jit(solution)/shard_map/all_to_all | solution.py:268
  75.7 2.4 %fusion.11 = f32[4,256,2,64]{1,3,2,0:T(8,128)S(1)} fusion(f32[2,4,256,256]{2,3,1,0:T(8,128)} %get-tuple-element.55, f32[4,2,64,256]{3,2,1,0:T(8,128)S(1)} %get-tuple-element.112, bf16[2,4,256,64]{2,1,3,0:T(4,128)(2,1)S(1)} %bitcast.362, f32[4,256,2]{1,2,0:T(2,128)S(1)} %copy-done.40), kind=kOutput, calls=%fused_computation.17 | convolution fusion | flops 201588736 | bytes 3416064 | tf_op jit(solution)/shard_map/transpose(jvp(hbij,hbjp->hbip))/dot_general | solution.py:155
  79.0 2.4 %collective-permute-start.1 = (f32[3,128]{0,1:T(8,128)S(1)}, f32[3,128]{0,1:T(8,128)S(1)}, u32[]{:S(2)}, u32[]{:S(2)}) collective-permute-start(f32[3,128]{0,1:T(8,128)S(1)} %slice.371), channel_id=1, source_target_pairs={{64,0},{128,64},{192,128},{65,1},{129,65},{193,129},{66,2},{130,66... | collective-permute-start | bytes 4616 | tf_op jit(solution)/shard_map/ppermute | solution.py:18
  82.2 0.6 copy.271
  82.8 2.3 %collective-permute-done.1 = f32[3,128]{0,1:T(8,128)S(1)} collective-permute-done((f32[3,128]{0,1:T(8,128)S(1)}, f32[3,128]{0,1:T(8,128)S(1)}, u32[]{:S(2)}, u32[]{:S(2)}) %collective-permute-start.1) | collective-permute-done | bytes 1568 | tf_op jit(solution)/shard_map/ppermute | solution.py:18
  85.2 0.6 fusion.32
  85.8 1.0 %copy.240 = f32[1024,128]{1,0:T(8,128)} copy(f32[1024,128]{0,1:T(8,128)S(1)} %fusion.32) | data formatting | bytes 1048576
  86.8 6.3 %all-to-all-done.1 = f32[32,16,256]{2,1,0:T(8,128)S(1)} async-done(((f32[32,16,256]{2,1,0:T(8,128)}), f32[32,16,256]{2,1,0:T(8,128)S(1)}, u32[]{:S(2)}, u32[]{:S(2)}) %all-to-all-start.1) | async-done | bytes 524320 | tf_op jit(solution)/shard_map/all_to_all | solution.py:268
  93.1 0.6 reduce_sum.128
  (224 shorter events, 10.1 us)
Async XLA Ops:
  0.6 19.0 %copy-start.20 = (bf16[1024,256]{1,0:T(8,128)(2,1)S(1)}, bf16[1024,256]{1,0:T(8,128)(2,1)}, u32[]{:S(2)}) copy-start(bf16[1024,256]{1,0:T(8,128)(2,1)} %param.8) | copy-start | bytes 1572868
  0.6 18.0 %copy-start.21 = (bf16[1024,128]{1,0:T(8,128)(2,1)S(1)}, bf16[1024,128]{1,0:T(8,128)(2,1)}, u32[]{:S(2)}) copy-start(bf16[1024,128]{1,0:T(8,128)(2,1)} %param.7) | copy-start | bytes 786436
  0.7 18.2 %copy-start.22 = (bf16[1024,128]{1,0:T(8,128)(2,1)S(1)}, bf16[1024,128]{1,0:T(8,128)(2,1)}, u32[]{:S(2)}) copy-start(bf16[1024,128]{1,0:T(8,128)(2,1)} %param.13) | copy-start | bytes 786436
  2.1 17.1 %collective-permute-start = (bf16[3,384]{1,0:T(4,128)(2,1)S(1)}, bf16[3,384]{1,0:T(4,128)(2,1)S(1)}, u32[]{:S(2)}, u32[]{:S(2)}) collective-permute-start(bf16[3,384]{1,0:T(4,128)(2,1)S(1)} %pad_maximum_fusion.7), channel_id=1, source_target_pairs={{0,64},{64,128},{128,192},{1,65},{65,129},{129,193},{2,66},{66,130... | collective-permute-start | bytes 6920 | tf_op jit(solution)/shard_map/ppermute | solution.py:18
  12.3 6.3 %copy-start.59 = (f32[4]{0:T(128)}, f32[4]{0:T(128)S(1)}, u32[]{:S(2)}) copy-start(f32[4]{0:T(128)S(1)} %get-tuple-element.51) | copy-start | bytes 52
  12.3 27.0 %copy-start.38 = (f32[4,256]{1,0:T(4,128)}, f32[4,256]{1,0:T(4,128)S(1)}, u32[]{:S(2)}) copy-start(f32[4,256]{1,0:T(4,128)S(1)} %get-tuple-element.91) | copy-start | bytes 12292
  13.6 25.8 %copy-start.43 = (f32[2,4]{1,0:T(2,128)}, f32[2,4]{1,0:T(2,128)S(1)}, u32[]{:S(2)}) copy-start(f32[2,4]{1,0:T(2,128)S(1)} %slice_reduce_fusion) | copy-start | bytes 100
  15.6 4.4 %copy-start.45 = (f32[1,256]{1,0:T(1,128)}, f32[1,256]{1,0:T(1,128)S(1)}, u32[]{:S(2)}) copy-start(f32[1,256]{1,0:T(1,128)S(1)} %get-tuple-element.93) | copy-start | bytes 3076
  15.6 4.4 %copy-start.47 = (f32[1,256]{1,0:T(1,128)}, f32[1,256]{1,0:T(1,128)S(1)}, u32[]{:S(2)}) copy-start(f32[1,256]{1,0:T(1,128)S(1)} %get-tuple-element.94) | copy-start | bytes 3076
  15.6 4.4 %copy-start.49 = (f32[1,256]{1,0:T(1,128)}, f32[1,256]{1,0:T(1,128)S(1)}, u32[]{:S(2)}) copy-start(f32[1,256]{1,0:T(1,128)S(1)} %get-tuple-element.95) | copy-start | bytes 3076
  15.6 4.4 %copy-start.51 = (f32[1,256]{1,0:T(1,128)}, f32[1,256]{1,0:T(1,128)S(1)}, u32[]{:S(2)}) copy-start(f32[1,256]{1,0:T(1,128)S(1)} %get-tuple-element.96) | copy-start | bytes 3076
  16.4 5.6 %copy-start.60 = (f32[128]{0:T(128)}, f32[128]{0:T(128)S(1)}, u32[]{:S(2)}) copy-start(f32[128]{0:T(128)S(1)} %get-tuple-element.97) | copy-start | bytes 1540
  16.4 5.6 %copy-start.62 = (f32[128]{0:T(128)}, f32[128]{0:T(128)S(1)}, u32[]{:S(2)}) copy-start(f32[128]{0:T(128)S(1)} %get-tuple-element.98) | copy-start | bytes 1540
  16.4 5.6 %copy-start.64 = (f32[128]{0:T(128)}, f32[128]{0:T(128)S(1)}, u32[]{:S(2)}) copy-start(f32[128]{0:T(128)S(1)} %get-tuple-element.99) | copy-start | bytes 1540
  16.5 5.6 %copy-start.66 = (f32[128]{0:T(128)}, f32[128]{0:T(128)S(1)}, u32[]{:S(2)}) copy-start(f32[128]{0:T(128)S(1)} %get-tuple-element.100) | copy-start | bytes 1540
  17.2 20.9 %copy-start.53 = (f32[2]{0:T(128)}, f32[2]{0:T(128)S(1)}, u32[]{:S(2)}) copy-start(f32[2]{0:T(128)S(1)} %get-tuple-element.38) | copy-start | bytes 28
  17.2 20.9 %copy-start.55 = (f32[2]{0:T(128)}, f32[2]{0:T(128)S(1)}, u32[]{:S(2)}) copy-start(f32[2]{0:T(128)S(1)} %get-tuple-element.39) | copy-start | bytes 28
  17.2 20.9 %copy-start.58 = (f32[2]{0:T(128)}, f32[2]{0:T(128)S(1)}, u32[]{:S(2)}) copy-start(f32[2]{0:T(128)S(1)} %get-tuple-element.40) | copy-start | bytes 28
  19.1 17.9 %copy-start.30 = (f32[4,2,256]{2,1,0:T(2,128)}, f32[4,2,256]{2,1,0:T(2,128)S(1)}, u32[]{:S(2)}) copy-start(f32[4,2,256]{2,1,0:T(2,128)S(1)} %copy.217) | copy-start | bytes 24580
  24.1 7.8 %copy-start.23 = (pred[4,256,256]{1,2,0:T(8,128)(4,1)S(1)}, pred[4,256,256]{1,2,0:T(8,128)(4,1)}, u32[]{:S(2)}) copy-start(pred[4,256,256]{1,2,0:T(8,128)(4,1)} %get-tuple-element.72) | copy-start | bytes 786436
  26.6 10.8 %all-to-all-start = ((f32[4,2,8320]{2,1,0:T(2,128)}), f32[4,2,8320]{2,1,0:T(2,128)S(1)}, u32[]{:S(2)}, u32[]{:S(2)}) async-start(f32[4,2,8320]{2,1,0:T(2,128)} %select_select_fusion), calls=%async_computation | async-start | bytes 532480 | tf_op jit(solution)/shard_map/all_to_all | solution.py:139
  44.4 6.2 %copy-start.70 = (f32[3]{0:T(128)S(1)}, f32[3]{0:T(128)}, u32[]{:S(2)}) copy-start(f32[3]{0:T(128)} %get-tuple-element.76) | copy-start | bytes 40
  44.4 6.2 %copy-start.71 = (f32[3]{0:T(128)S(1)}, f32[3]{0:T(128)}, u32[]{:S(2)}) copy-start(f32[3]{0:T(128)} %get-tuple-element.77) | copy-start | bytes 40
  44.4 6.2 %copy-start.72 = (f32[3]{0:T(128)S(1)}, f32[3]{0:T(128)}, u32[]{:S(2)}) copy-start(f32[3]{0:T(128)} %get-tuple-element.78) | copy-start | bytes 40
  44.8 11.7 %copy-start.5 = (f32[2,4,64,128]{3,2,0,1:T(8,128)S(1)}, f32[2,4,64,128]{3,2,0,1:T(8,128)}, u32[]{:S(2)}) copy-start(f32[2,4,64,128]{3,2,0,1:T(8,128)} %copy-done.4) | copy-start | bytes 786436
  44.8 11.7 %copy-start.7 = (f32[2,4,64,128]{3,2,0,1:T(8,128)S(1)}, f32[2,4,64,128]{3,2,0,1:T(8,128)}, u32[]{:S(2)}) copy-start(f32[2,4,64,128]{3,2,0,1:T(8,128)} %copy-done.6) | copy-start | bytes 786436
  44.9 14.6 %copy-start.17 = (f32[2,8320]{1,0:T(2,128)S(1)}, f32[2,8320]{1,0:T(2,128)}, u32[]{:S(2)}) copy-start(f32[2,8320]{1,0:T(2,128)} %copy-done.16) | copy-start | bytes 199684
  44.9 14.6 %copy-start.19 = (f32[2,8320]{1,0:T(2,128)S(1)}, f32[2,8320]{1,0:T(2,128)}, u32[]{:S(2)}) copy-start(f32[2,8320]{1,0:T(2,128)} %copy-done.18) | copy-start | bytes 199684
  44.9 14.5 %copy-start.24 = (f32[1,2,64,128]{3,2,1,0:T(8,128)S(1)}, f32[1,2,64,128]{3,2,1,0:T(8,128)}, u32[]{:S(2)}) copy-start(f32[1,2,64,128]{3,2,1,0:T(8,128)} %get-tuple-element.60) | copy-start | bytes 196612
  44.9 14.5 %copy-start.25 = (f32[1,2,64,128]{3,2,1,0:T(8,128)S(1)}, f32[1,2,64,128]{3,2,1,0:T(8,128)}, u32[]{:S(2)}) copy-start(f32[1,2,64,128]{3,2,1,0:T(8,128)} %get-tuple-element.61) | copy-start | bytes 196612
  44.9 14.5 %copy-start.26 = (f32[1,2,64,128]{3,2,1,0:T(8,128)S(1)}, f32[1,2,64,128]{3,2,1,0:T(8,128)}, u32[]{:S(2)}) copy-start(f32[1,2,64,128]{3,2,1,0:T(8,128)} %get-tuple-element.65) | copy-start | bytes 196612
  44.9 14.5 %copy-start.27 = (f32[1,2,64,128]{3,2,1,0:T(8,128)S(1)}, f32[1,2,64,128]{3,2,1,0:T(8,128)}, u32[]{:S(2)}) copy-start(f32[1,2,64,128]{3,2,1,0:T(8,128)} %get-tuple-element.66) | copy-start | bytes 196612
  44.9 14.5 %copy-start.28 = (f32[1,2,64,128]{3,2,1,0:T(8,128)S(1)}, f32[1,2,64,128]{3,2,1,0:T(8,128)}, u32[]{:S(2)}) copy-start(f32[1,2,64,128]{3,2,1,0:T(8,128)} %get-tuple-element.67) | copy-start | bytes 196612
  44.9 14.5 %copy-start.29 = (f32[1,2,64,128]{3,2,1,0:T(8,128)S(1)}, f32[1,2,64,128]{3,2,1,0:T(8,128)}, u32[]{:S(2)}) copy-start(f32[1,2,64,128]{3,2,1,0:T(8,128)} %get-tuple-element.71) | copy-start | bytes 196612
  44.9 5.6 %collective-permute-start.2 = (f32[3,256]{1,0:T(4,128)S(1)}, f32[3,256]{1,0:T(4,128)S(1)}, u32[]{:S(2)}, u32[]{:S(2)}) collective-permute-start(f32[3,256]{1,0:T(4,128)S(1)} %get-tuple-element.56), channel_id=1, source_target_pairs={{64,0},{128,64},{192,128},{65,1},{129,65},{193,129},{66,2},{130,66... | collective-permute-start | bytes 9224 | tf_op jit(solution)/shard_map/ppermute | solution.py:18
  52.0 10.4 %copy-start.1 = (f32[1024,256]{1,0:T(8,128)S(1)}, f32[1024,256]{1,0:T(8,128)}, u32[]{:S(2)}) copy-start(f32[1024,256]{1,0:T(8,128)} %dynamic_update_slice.3) | copy-start | bytes 3145732
  53.9 8.5 %collective-permute-start.3 = (f32[32,16,256]{2,1,0:T(8,128)}, f32[32,16,256]{2,1,0:T(8,128)}, u32[]{:S(2)}, u32[]{:S(2)}) collective-permute-start(f32[32,16,256]{2,1,0:T(8,128)} %dynamic-slice_bitcast_fusion), channel_id=1, source_target_pairs={{0,1},{1,0},{2,3},{3,2},{4,5},{5,4},{6,7},{7,6},{8,9},{9,8},{10,11... | collective-permute-start | bytes 1572872 | tf_op jit(solution)/shard_map/ppermute | solution.py:267
  58.0 17.7 %copy-start.40 = (f32[4,256,2]{1,2,0:T(2,128)S(1)}, f32[4,256,2]{1,2,0:T(2,128)}, u32[]{:S(2)}) copy-start(f32[4,256,2]{1,2,0:T(2,128)} %copy.220) | copy-start | bytes 24580
  64.3 28.7 %all-to-all-start.1 = ((f32[32,16,256]{2,1,0:T(8,128)}), f32[32,16,256]{2,1,0:T(8,128)S(1)}, u32[]{:S(2)}, u32[]{:S(2)}) async-start(f32[32,16,256]{2,1,0:T(8,128)} %bitcast_add_fusion), calls=%async_computation.1 | async-start | bytes 1048576 | tf_op jit(solution)/shard_map/all_to_all | solution.py:268
  78.5 3.4 %copy-start.39 = (f32[4,256]{1,0:T(4,128)S(1)}, f32[4,256]{1,0:T(4,128)}, u32[]{:S(2)}) copy-start(f32[4,256]{1,0:T(4,128)} %copy-done.38) | copy-start | bytes 12292
  78.6 6.6 %copy-start.33 = (f32[1024]{0:T(1024)S(1)}, f32[1024]{0:T(1024)}, u32[]{:S(2)}) copy-start(f32[1024]{0:T(1024)} %get-tuple-element.79) | copy-start | bytes 12292
  78.6 6.6 %copy-start.35 = (f32[1024]{0:T(1024)S(1)}, f32[1024]{0:T(1024)}, u32[]{:S(2)}) copy-start(f32[1024]{0:T(1024)} %get-tuple-element.82) | copy-start | bytes 12292
  78.6 6.6 %copy-start.37 = (f32[1024]{0:T(1024)S(1)}, f32[1024]{0:T(1024)}, u32[]{:S(2)}) copy-start(f32[1024]{0:T(1024)} %get-tuple-element.83) | copy-start | bytes 12292
  78.6 6.5 %copy-start.61 = (f32[128]{0:T(128)S(1)}, f32[128]{0:T(128)}, u32[]{:S(2)}) copy-start(f32[128]{0:T(128)} %copy-done.60) | copy-start | bytes 1540
  78.6 6.5 %copy-start.63 = (f32[128]{0:T(128)S(1)}, f32[128]{0:T(128)}, u32[]{:S(2)}) copy-start(f32[128]{0:T(128)} %copy-done.62) | copy-start | bytes 1540
  78.6 6.5 %copy-start.65 = (f32[128]{0:T(128)S(1)}, f32[128]{0:T(128)}, u32[]{:S(2)}) copy-start(f32[128]{0:T(128)} %copy-done.64) | copy-start | bytes 1540
  78.6 6.5 %copy-start.67 = (f32[128]{0:T(128)S(1)}, f32[128]{0:T(128)}, u32[]{:S(2)}) copy-start(f32[128]{0:T(128)} %copy-done.66) | copy-start | bytes 1540
  79.0 6.2 %collective-permute-start.1 = (f32[3,128]{0,1:T(8,128)S(1)}, f32[3,128]{0,1:T(8,128)S(1)}, u32[]{:S(2)}, u32[]{:S(2)}) collective-permute-start(f32[3,128]{0,1:T(8,128)S(1)} %slice.371), channel_id=1, source_target_pairs={{64,0},{128,64},{192,128},{65,1},{129,65},{193,129},{66,2},{130,66... | collective-permute-start | bytes 4616 | tf_op jit(solution)/shard_map/ppermute | solution.py:18
  (33 other events, 82.1 us)

commit v18 on v14

--- a/solution.py
+++ b/solution.py
@@ -262,8 +262,8 @@
     chips, cores = lax.axis_size("chip"), lax.axis_size("core")
     pieces = whole_bc.reshape(chips, cores, tok_rows // (chips * cores), whole_bc.shape[1])
     core = lax.axis_index("core")
-    mine = lax.dynamic_index_in_dim(pieces, core, 1, keepdims=False)
-    other = lax.dynamic_index_in_dim(pieces, 1 - core, 1, keepdims=False)
+    mine = jnp.where(core == 0, pieces[:, 0], pieces[:, 1])
+    other = jnp.where(core == 0, pieces[:, 1], pieces[:, 0])
     pair_sum = mine + lax.ppermute(other, "core", [(0, 1), (1, 0)])
     grad_pre_bc = lax.all_to_all(pair_sum, "chip", 0, 0, tiled=False).sum(0)
     return (grad_pre_x, grad_pre_bc, grad_log_decay)

time: 87.6 us -> 86.6 us (0.989)
  local copies, waits for them, and re-layouts: 12.7 us -> 11.5 us
    add x1, other arithmetic: 1.91 us -> 0.97 us  [local(): pair_sum = mine + lax.ppermute(other, 'core', [(0, 1), (1, 0)])]
    unnamed x157 -> x137, local copies, waits for them, and re-layouts: 2.48 us -> 3.4 us
    select_n x0 -> x1, other arithmetic: none -> 0.89 us  [local(): other = jnp.where(core == 0, pieces[:, 1], pieces[:, 0])]
  transfers between devices with their start and end apart: 6 -> 6, of which waited for: 3 -> 3; matrix products, arithmetic and copies ran while one was open for 33% -> 32% of each run, Pallas kernels for 0% -> 0%
where the time goes in v18:
time: 86.6 us; the launch traced here: 85 us
  starting transfers between devices  24.6 us (28%)
  other arithmetic  20 us (23%)
  matrix products  14.8 us (17%)
  local copies, waits for them, and re-layouts  11.5 us (13%)
  waiting for transfers between devices  11 us (13%)
  between operations  3.05 us (4%)
    dot_general x11, matrix products, einsum(): jnp.einsum(spec, *operands, precision=lax.Precision.HIGH, preferred_eleme...  12.6 us
    all_to_all x1, starting transfers between devices, local(): grad_pre_bc = lax.all_to_all(pair_sum, 'chip', 0, 0, tiled=False).sum(0)  11.3 us
    ppermute x3, starting transfers between devices, shifted(): lax.ppermute(value, axis, [(source, source + steps) for source in range(i...  8.66 us
    all_to_all x1, waiting for transfers between devices, local(): grad_pre_bc = lax.all_to_all(pair_sum, 'chip', 0, 0, tiled=False).sum(0)  6.4 us
    all_to_all x1, starting transfers between devices, chain_both(): arrived = lax.all_to_all(outgoing, axis, 0, 0, tiled=False)  4.62 us
    ppermute x3, waiting for transfers between devices, shifted(): lax.ppermute(value, axis, [(source, source + steps) for source in range(i...  4.58 us
    unnamed x137, local copies, waits for them, and re-layouts  3.4 us
    convert_element_type x2, other arithmetic, conv_backward(): weights[k][None, :] * extended[lag:lag + count] * linked[:, None]  2.62 us
  transfers between devices with their start and end apart: 6, of which 3 were waited for; matrix products, arithmetic and copies ran while one was open for 32% of the time, Pallas kernels for 0%

profile of v18, /device:TPU:8, one launch (start us, length us, event | category | flops | bytes accessed | tf_op | source)
XLA Modules:
  0.0 85.0 jit_solution(3218224936663813001)
XLA Ops:
  0.7 0.8 slice.289
  1.4 0.7 slice.288
  2.1 3.5 %collective-permute-start = (bf16[3,384]{1,0:T(4,128)(2,1)S(1)}, bf16[3,384]{1,0:T(4,128)(2,1)S(1)}, u32[]{:S(2)}, u32[]{:S(2)}) collective-permute-start(bf16[3,384]{1,0:T(4,128)(2,1)S(1)} %pad_maximum_fusion.8), channel_id=1, source_target_pairs={{0,64},{64,128},{128,192},{1,65},{65,129},{129,193},{2,66},{66,130... | collective-permute-start | bytes 6920 | tf_op jit(solution)/shard_map/ppermute | solution.py:18
  5.6 0.8 reduce-window.9
  6.5 0.7 bitcast_subtract_fusion.1
  7.7 0.6 fusion.146
  8.3 2.0 %fusion.126 = (f32[1024]{0:T(1024)}, f32[1024]{0:T(1024)S(1)}, f32[1024]{0:T(1024)S(1)}, f32[1024]{0:T(1024)}, f32[1024]{0:T(1024)}, /*index=5*/f32[1024]{0:T(1024)S(1)}, f32[1024]{0:T(1024)S(1)}, f32[1024]{0:T(1024)S(1)}) fusion(s32[1030]{0:T(1024)S(1)} %broadcast_add_fusion, s32[]{:T(128)} %bitcast.11, s32[]{:T(128)} %bitcast.17), kind=kLoop, calls=%fused_computation.221 | loop fusion | flops 16384 | bytes 61448 | tf_op jit(solution)/shard_map/convert_element_type | solution.py:97
  11.6 0.7 compare_convert_fusion.7
  12.4 0.7 reshape.450
  13.6 0.6 compare_convert_fusion.6
  14.7 0.8 fusion.147
  15.6 0.8 slice_bitcast_fusion.11
  16.5 0.7 slice_reduce_fusion.8
  17.1 1.4 %compare_and_fusion = (pred[4,256,256]{1,2,0:T(8,128)(4,1)}, f32[4,256,256]{1,2,0:T(8,128)}) fusion(s32[4,256]{1,0:T(4,128)S(1)} %reshape.454, pred[256,256]{0,1:T(8,128)(4,1)S(1)} %iota_compare_fusion), kind=kLoop, calls=%fused_computation.51 | loop fusion | flops 786432 | bytes 1380352 | tf_op jit(solution)/shard_map/jvp()/and | solution.py:165
  19.3 0.4 copy-done.1
  20.0 1.8 %fusion.30 = (f32[1024,256]{1,0:T(8,128)S(1)}, f32[1024,256]{1,0:T(8,128)}) fusion(f32[1027,256]{1,0:T(8,128)S(1)} %maximum_convert_fusion, f32[256]{0:T(256)S(1)} %bitcast.407, f32[1024]{0:T(1024)S(1)} %get-tuple-element.87, f32[256]{0:T(256)S(1)} %bitcast.410, f32[1024]{0:T(1024)S(1)} %get-tuple-element.88, f32[256]{0:T(256)S(1)} %bitcast.404, ...), kind=kLoop, calls=%fused_computation.50 | loop fusion | flops 3670016 | bytes 6307840 | tf_op jit(solution)/shard_map/jit(silu)/mul | solution.py:203
  22.1 1.4 %fusion.62 = (f32[1024,128]{0,1:T(8,128)S(1)}, f32[1024,128]{0,1:T(8,128)}) fusion(f32[1027,128]{0,1:T(8,128)S(1)} %maximum_convert_fusion.1, f32[128]{0:T(128)S(1)} %get-tuple-element.102, f32[1024]{0:T(1024)S(1)} %get-tuple-element.87, f32[128]{0:T(128)S(1)} %get-tuple-element.103, f32[1024]{0:T(1024)S(1)} %get-tuple-element.88, ...), kind=kLoop, calls=%fused_computation.103 | loop fusion | flops 1835008 | bytes 3160064 | tf_op jit(solution)/shard_map/jit(silu)/mul | solution.py:202
  24.1 1.4 %convolution_bitcast_fusion.5 = f32[1,2,64,128]{3,2,1,0:T(8,128)S(1)} fusion(bf16[1024,2,64]{0,2,1:T(8,128)(2,1)} %bitcast.383, f32[2,1024]{1,0:T(2,128)S(1)} %get-tuple-element.91, f32[1024,256]{1,0:T(8,128)S(1)} %get-tuple-element.53), kind=kOutput, calls=%fused_computation.24 | convolution fusion | flops 100925440 | bytes 860160 | tf_op jit(solution)/shard_map/thp,ht,tn->hpn/dot_general | solution.py:232
  25.7 0.9 %select_select_fusion = f32[4,2,8320]{2,1,0:T(2,128)} fusion(pred[4]{0:T(512)(128)(4,1)S(1)} %get-tuple-element.117, pred[4]{0:T(512)(128)(4,1)S(1)} %get-tuple-element.116, f32[2,8320]{1,0:T(2,128)S(1)} %get-tuple-element.109, f32[2,8320]{1,0:T(2,128)S(1)} %get-tuple-element.108), kind=kLoop, calls=%fused_computation.109 | loop fusion | flops 133120 | bytes 399368 | tf_op jit(solution)/shard_map/jit(_where)/select_n | solution.py:138
  26.6 4.6 %all-to-all-start = ((f32[4,2,8320]{2,1,0:T(2,128)}), f32[4,2,8320]{2,1,0:T(2,128)S(1)}, u32[]{:S(2)}, u32[]{:S(2)}) async-start(f32[4,2,8320]{2,1,0:T(2,128)} %select_select_fusion), calls=%async_computation | async-start | bytes 532480 | tf_op jit(solution)/shard_map/all_to_all | solution.py:139
  31.2 0.6 fusion.148
  31.8 5.1 %fusion.16 = (f32[2,4,256]{2,1,0:T(4,128)}, f32[2,4,256]{2,1,0:T(4,128)}, f32[4,256,256]{1,2,0:T(8,128)S(1)}, f32[2,4,256,256]{2,3,1,0:T(8,128)}) fusion(f32[4,256,256]{1,2,0:T(8,128)} %get-tuple-element.76, f32[2,4,256]{2,1,0:T(4,128)S(1)} %bitcast.394, f32[4,256,256]{1,2,0:T(8,128)S(1)} %fusion.148, pred[4,256,256]{1,2,0:T(8,128)(4,1)S(1)} %copy-done.16, ...), kind=kOutput, calls=%fused_computation.20 | convolution fusion | flops 207351808 | bytes 6316032 | tf_op jit(solution)/shard_map/transpose(jvp(hbij,hbjp->hbip))/dot_general | solution.py:155
  38.0 0.6 copy-done.11
  38.6 0.7 slice_bitcast_fusion.1
  39.3 0.5 fusion.55
  39.8 0.7 fusion.131
  40.6 0.4 convolution_bitcast_fusion.3
  41.0 0.6 convolution_bitcast_fusion.2
  41.7 0.7 slice_bitcast_fusion.3
  42.4 0.6 convolution_add_fusion.1
  43.0 0.6 convolution_bitcast_fusion.1
  43.6 1.0 %convolution_add_fusion = f32[4,256,128]{2,1,0:T(8,128)S(1)} fusion(f32[4,256,128]{2,1,0:T(8,128)S(1)} %convolution_bitcast_fusion.1, f32[4,256,256]{1,2,0:T(8,128)S(1)} %get-tuple-element.23, f32[4,256,128]{2,1,0:T(8,128)S(1)} %bitcast.373), kind=kOutput, calls=%fused_computation.11 | convolution fusion | flops 201457664 | bytes 2621440 | tf_op jit(solution)/shard_map/transpose(jvp(bin,bjn->bij))/dot_general | solution.py:155
  45.4 2.7 %collective-permute-start.2 = (f32[3,256]{1,0:T(4,128)S(1)}, f32[3,256]{1,0:T(4,128)S(1)}, u32[]{:S(2)}, u32[]{:S(2)}) collective-permute-start(f32[3,256]{1,0:T(4,128)S(1)} %get-tuple-element.59), channel_id=1, source_target_pairs={{64,0},{128,64},{192,128},{65,1},{129,65},{193,129},{66,2},{130,66... | collective-permute-start | bytes 9224 | tf_op jit(solution)/shard_map/ppermute | solution.py:18
  48.2 0.5 fusion.18
  48.8 2.3 %collective-permute-done.2 = f32[3,256]{1,0:T(4,128)S(1)} collective-permute-done((f32[3,256]{1,0:T(4,128)S(1)}, f32[3,256]{1,0:T(4,128)S(1)}, u32[]{:S(2)}, u32[]{:S(2)}) %collective-permute-start.2) | collective-permute-done | bytes 3104 | tf_op jit(solution)/shard_map/ppermute | solution.py:18
  51.2 0.9 %select_bitcast_fusion = f32[32,16,256]{2,1,0:T(8,128)} fusion(f32[32,2,16,256]{3,2,1,0:T(8,128)S(1)} %bitcast.378, pred[]{:T(512)S(6)} %eq.124), kind=kLoop, calls=%fused_computation.99 | loop fusion | flops 131072 | bytes 1572865 | tf_op jit(solution)/shard_map/jit(_where)/select_n | solution.py:266
  52.7 1.5 %fusion.90 = (f32[2]{0:T(128)S(1)}, f32[2]{0:T(128)S(1)}) fusion(f32[1,2,64,128]{3,2,1,0:T(8,128)} %get-tuple-element.70, f32[1,2,64,128]{3,2,1,0:T(8,128)} %get-tuple-element.74, f32[1,2,64,128]{3,2,1,0:T(8,128)} %get-tuple-element.69, f32[2,8320]{1,0:T(2,128)S(1)} %copy-done.10, f32[2,8320]{1,0:T(2,128)S(1)} %copy-done.12, f32[2]{0:T(128)S(1)} %copy-done.42, ...), kind=kLoop, calls=%fused_computation.143 | loop fusion | flops 262140 | bytes 524336 | tf_op jit(solution)/shard_map/transpose(jvp())/reduce_sum | solution.py:174
  54.6 1.0 %fusion.52 = f32[32,16,256]{2,1,0:T(8,128)} fusion(f32[32,16,256]{2,1,0:T(8,128)S(1)} %collective-permute-done.3, f32[32,2,16,256]{3,2,1,0:T(8,128)S(1)} %bitcast.379, pred[]{:T(512)S(6)} %eq.124), kind=kLoop, calls=%fused_computation.87 | loop fusion | flops 262144 | bytes 2097153 | tf_op jit(solution)/shard_map/add | solution.py:267
  55.6 11.3 %all-to-all-start.1 = ((f32[32,16,256]{2,1,0:T(8,128)}), f32[32,16,256]{2,1,0:T(8,128)S(1)}, u32[]{:S(2)}, u32[]{:S(2)}) async-start(f32[32,16,256]{2,1,0:T(8,128)} %fusion.52), calls=%async_computation.1 | async-start | bytes 1048576 | tf_op jit(solution)/shard_map/all_to_all | solution.py:268
  67.0 2.4 %fusion.11 = f32[4,256,2,64]{1,3,2,0:T(8,128)S(1)} fusion(f32[2,4,256,256]{2,3,1,0:T(8,128)} %get-tuple-element.55, f32[4,2,64,256]{3,2,1,0:T(8,128)S(1)} %get-tuple-element.115, bf16[2,4,256,64]{2,1,3,0:T(4,128)(2,1)S(1)} %bitcast.381, f32[4,256,2]{1,2,0:T(2,128)S(1)} %copy.244), kind=kOutput, calls=%fused_computation.17 | convolution fusion | flops 201588736 | bytes 3416064 | tf_op jit(solution)/shard_map/transpose(jvp(hbij,hbjp->hbip))/dot_general | solution.py:155
  70.1 2.5 %collective-permute-start.1 = (f32[3,128]{0,1:T(8,128)S(1)}, f32[3,128]{0,1:T(8,128)S(1)}, u32[]{:S(2)}, u32[]{:S(2)}) collective-permute-start(f32[3,128]{0,1:T(8,128)S(1)} %slice.385), channel_id=1, source_target_pairs={{64,0},{128,64},{192,128},{65,1},{129,65},{193,129},{66,2},{130,66... | collective-permute-start | bytes 4616 | tf_op jit(solution)/shard_map/ppermute | solution.py:18
  72.7 0.4 fusion.17
  73.4 0.6 copy.300
  74.0 2.3 %collective-permute-done.1 = f32[3,128]{0,1:T(8,128)S(1)} collective-permute-done((f32[3,128]{0,1:T(8,128)S(1)}, f32[3,128]{0,1:T(8,128)S(1)}, u32[]{:S(2)}, u32[]{:S(2)}) %collective-permute-start.1) | collective-permute-done | bytes 1568 | tf_op jit(solution)/shard_map/ppermute | solution.py:18
  76.3 0.6 fusion.36
  76.9 1.0 %copy.268 = f32[1024,128]{1,0:T(8,128)} copy(f32[1024,128]{0,1:T(8,128)S(1)} %fusion.36) | data formatting | bytes 1048576
  77.9 6.4 %all-to-all-done.1 = f32[32,16,256]{2,1,0:T(8,128)S(1)} async-done(((f32[32,16,256]{2,1,0:T(8,128)}), f32[32,16,256]{2,1,0:T(8,128)S(1)}, u32[]{:S(2)}, u32[]{:S(2)}) %all-to-all-start.1) | async-done | bytes 524320 | tf_op jit(solution)/shard_map/all_to_all | solution.py:268
  84.3 0.6 reduce_sum.128
  (201 shorter events, 7.5 us)
Async XLA Ops:
  0.6 19.1 %copy-start.13 = (bf16[1024,256]{1,0:T(8,128)(2,1)S(1)}, bf16[1024,256]{1,0:T(8,128)(2,1)}, u32[]{:S(2)}) copy-start(bf16[1024,256]{1,0:T(8,128)(2,1)} %param.8) | copy-start | bytes 1572868
  0.6 18.0 %copy-start.14 = (bf16[1024,128]{1,0:T(8,128)(2,1)S(1)}, bf16[1024,128]{1,0:T(8,128)(2,1)}, u32[]{:S(2)}) copy-start(bf16[1024,128]{1,0:T(8,128)(2,1)} %param.7) | copy-start | bytes 786436
  0.7 18.2 %copy-start.15 = (bf16[1024,128]{1,0:T(8,128)(2,1)S(1)}, bf16[1024,128]{1,0:T(8,128)(2,1)}, u32[]{:S(2)}) copy-start(bf16[1024,128]{1,0:T(8,128)(2,1)} %param.13) | copy-start | bytes 786436
  2.1 17.1 %collective-permute-start = (bf16[3,384]{1,0:T(4,128)(2,1)S(1)}, bf16[3,384]{1,0:T(4,128)(2,1)S(1)}, u32[]{:S(2)}, u32[]{:S(2)}) collective-permute-start(bf16[3,384]{1,0:T(4,128)(2,1)S(1)} %pad_maximum_fusion.8), channel_id=1, source_target_pairs={{0,64},{64,128},{128,192},{1,65},{65,129},{129,193},{2,66},{66,130... | collective-permute-start | bytes 6920 | tf_op jit(solution)/shard_map/ppermute | solution.py:18
  12.3 6.3 %copy-start.45 = (f32[4]{0:T(128)}, f32[4]{0:T(128)S(1)}, u32[]{:S(2)}) copy-start(f32[4]{0:T(128)S(1)} %get-tuple-element.51) | copy-start | bytes 52
  12.3 27.4 %copy-start.21 = (f32[4,256]{1,0:T(4,128)}, f32[4,256]{1,0:T(4,128)S(1)}, u32[]{:S(2)}) copy-start(f32[4,256]{1,0:T(4,128)S(1)} %get-tuple-element.94) | copy-start | bytes 12292
  13.6 26.2 %copy-start.25 = (f32[2,4]{1,0:T(2,128)}, f32[2,4]{1,0:T(2,128)S(1)}, u32[]{:S(2)}) copy-start(f32[2,4]{1,0:T(2,128)S(1)} %slice_reduce_fusion) | copy-start | bytes 100
  15.6 4.4 %copy-start.27 = (f32[1,256]{1,0:T(1,128)}, f32[1,256]{1,0:T(1,128)S(1)}, u32[]{:S(2)}) copy-start(f32[1,256]{1,0:T(1,128)S(1)} %get-tuple-element.96) | copy-start | bytes 3076
  15.6 4.4 %copy-start.29 = (f32[1,256]{1,0:T(1,128)}, f32[1,256]{1,0:T(1,128)S(1)}, u32[]{:S(2)}) copy-start(f32[1,256]{1,0:T(1,128)S(1)} %get-tuple-element.97) | copy-start | bytes 3076
  15.6 4.4 %copy-start.31 = (f32[1,256]{1,0:T(1,128)}, f32[1,256]{1,0:T(1,128)S(1)}, u32[]{:S(2)}) copy-start(f32[1,256]{1,0:T(1,128)S(1)} %get-tuple-element.98) | copy-start | bytes 3076
  15.6 4.4 %copy-start.33 = (f32[1,256]{1,0:T(1,128)}, f32[1,256]{1,0:T(1,128)S(1)}, u32[]{:S(2)}) copy-start(f32[1,256]{1,0:T(1,128)S(1)} %get-tuple-element.99) | copy-start | bytes 3076
  16.4 5.6 %copy-start.47 = (f32[128]{0:T(128)}, f32[128]{0:T(128)S(1)}, u32[]{:S(2)}) copy-start(f32[128]{0:T(128)S(1)} %get-tuple-element.100) | copy-start | bytes 1540
  16.4 5.6 %copy-start.49 = (f32[128]{0:T(128)}, f32[128]{0:T(128)S(1)}, u32[]{:S(2)}) copy-start(f32[128]{0:T(128)S(1)} %get-tuple-element.101) | copy-start | bytes 1540
  16.4 5.6 %copy-start.51 = (f32[128]{0:T(128)}, f32[128]{0:T(128)S(1)}, u32[]{:S(2)}) copy-start(f32[128]{0:T(128)S(1)} %get-tuple-element.102) | copy-start | bytes 1540
  16.4 5.6 %copy-start.53 = (f32[128]{0:T(128)}, f32[128]{0:T(128)S(1)}, u32[]{:S(2)}) copy-start(f32[128]{0:T(128)S(1)} %get-tuple-element.103) | copy-start | bytes 1540
  17.1 21.5 %copy-start.35 = (f32[2]{0:T(128)}, f32[2]{0:T(128)S(1)}, u32[]{:S(2)}) copy-start(f32[2]{0:T(128)S(1)} %get-tuple-element.38) | copy-start | bytes 28
  17.1 21.5 %copy-start.38 = (f32[2]{0:T(128)}, f32[2]{0:T(128)S(1)}, u32[]{:S(2)}) copy-start(f32[2]{0:T(128)S(1)} %get-tuple-element.39) | copy-start | bytes 28
  17.1 21.5 %copy-start.43 = (f32[2]{0:T(128)}, f32[2]{0:T(128)S(1)}, u32[]{:S(2)}) copy-start(f32[2]{0:T(128)S(1)} %get-tuple-element.40) | copy-start | bytes 28
  24.1 7.7 %copy-start.16 = (pred[4,256,256]{1,2,0:T(8,128)(4,1)S(1)}, pred[4,256,256]{1,2,0:T(8,128)(4,1)}, u32[]{:S(2)}) copy-start(pred[4,256,256]{1,2,0:T(8,128)(4,1)} %get-tuple-element.75) | copy-start | bytes 786436
  26.6 10.7 %all-to-all-start = ((f32[4,2,8320]{2,1,0:T(2,128)}), f32[4,2,8320]{2,1,0:T(2,128)S(1)}, u32[]{:S(2)}, u32[]{:S(2)}) async-start(f32[4,2,8320]{2,1,0:T(2,128)} %select_select_fusion), calls=%async_computation | async-start | bytes 532480 | tf_op jit(solution)/shard_map/all_to_all | solution.py:139
  38.0 3.6 %copy-start.9 = (f32[2,8320]{1,0:T(2,128)}, f32[2,8320]{1,0:T(2,128)S(1)}, u32[]{:S(2)}) copy-start(f32[2,8320]{1,0:T(2,128)S(1)} %get-tuple-element.26) | copy-start | bytes 199684
  45.0 3.0 %copy-start.18 = (f32[1024]{0:T(1024)S(1)}, f32[1024]{0:T(1024)}, u32[]{:S(2)}) copy-start(f32[1024]{0:T(1024)} %get-tuple-element.82) | copy-start | bytes 12292
  45.4 5.7 %collective-permute-start.2 = (f32[3,256]{1,0:T(4,128)S(1)}, f32[3,256]{1,0:T(4,128)S(1)}, u32[]{:S(2)}, u32[]{:S(2)}) collective-permute-start(f32[3,256]{1,0:T(4,128)S(1)} %get-tuple-element.59), channel_id=1, source_target_pairs={{64,0},{128,64},{192,128},{65,1},{129,65},{193,129},{66,2},{130,66... | collective-permute-start | bytes 9224 | tf_op jit(solution)/shard_map/ppermute | solution.py:18
  48.7 3.5 %copy-start.22 = (f32[4,256]{1,0:T(4,128)S(1)}, f32[4,256]{1,0:T(4,128)}, u32[]{:S(2)}) copy-start(f32[4,256]{1,0:T(4,128)} %copy-done.21) | copy-start | bytes 12292
  48.7 3.5 %copy-start.26 = (f32[2,4]{1,0:T(2,128)S(1)}, f32[2,4]{1,0:T(2,128)}, u32[]{:S(2)}) copy-start(f32[2,4]{1,0:T(2,128)} %copy-done.25) | copy-start | bytes 100
  48.7 3.5 %copy-start.4 = (f32[2,4,64,128]{3,2,0,1:T(8,128)S(1)}, f32[2,4,64,128]{3,2,0,1:T(8,128)}, u32[]{:S(2)}) copy-start(f32[2,4,64,128]{3,2,0,1:T(8,128)} %copy-done.3) | copy-start | bytes 786436
  48.7 3.5 %copy-start.44 = (f32[2]{0:T(128)S(1)}, f32[2]{0:T(128)}, u32[]{:S(2)}) copy-start(f32[2]{0:T(128)} %copy-done.43) | copy-start | bytes 28
  48.7 3.9 %copy-start.10 = (f32[2,8320]{1,0:T(2,128)S(1)}, f32[2,8320]{1,0:T(2,128)}, u32[]{:S(2)}) copy-start(f32[2,8320]{1,0:T(2,128)} %copy-done.9) | copy-start | bytes 199684
  48.7 3.9 %copy-start.12 = (f32[2,8320]{1,0:T(2,128)S(1)}, f32[2,8320]{1,0:T(2,128)}, u32[]{:S(2)}) copy-start(f32[2,8320]{1,0:T(2,128)} %copy-done.11) | copy-start | bytes 199684
  48.7 3.9 %copy-start.17 = (f32[1,2,64,128]{3,2,1,0:T(8,128)S(1)}, f32[1,2,64,128]{3,2,1,0:T(8,128)}, u32[]{:S(2)}) copy-start(f32[1,2,64,128]{3,2,1,0:T(8,128)} %get-tuple-element.63) | copy-start | bytes 196612
  48.7 3.9 %copy-start.37 = (f32[2]{0:T(128)S(1)}, f32[2]{0:T(128)}, u32[]{:S(2)}) copy-start(f32[2]{0:T(128)} %copy-done.35) | copy-start | bytes 28
  48.7 3.9 %copy-start.40 = (f32[2]{0:T(128)S(1)}, f32[2]{0:T(128)}, u32[]{:S(2)}) copy-start(f32[2]{0:T(128)} %copy-done.38) | copy-start | bytes 28
  48.8 3.9 %copy-start.42 = (f32[2]{0:T(128)S(1)}, f32[2]{0:T(128)}, u32[]{:S(2)}) copy-start(f32[2]{0:T(128)} %get-tuple-element.37) | copy-start | bytes 28
  51.2 3.2 %copy-start.46 = (f32[4]{0:T(128)S(1)}, f32[4]{0:T(128)}, u32[]{:S(2)}) copy-start(f32[4]{0:T(128)} %copy-done.45) | copy-start | bytes 52
  51.2 3.4 %copy-start.55 = (f32[2,4]{1,0:T(2,128)S(1)}, f32[2,4]{1,0:T(2,128)}, u32[]{:S(2)}) copy-start(f32[2,4]{1,0:T(2,128)} %get-tuple-element.77) | copy-start | bytes 100
  52.1 2.5 %collective-permute-start.3 = (f32[32,16,256]{2,1,0:T(8,128)}, f32[32,16,256]{2,1,0:T(8,128)S(1)}, u32[]{:S(2)}, u32[]{:S(2)}) collective-permute-start(f32[32,16,256]{2,1,0:T(8,128)} %select_bitcast_fusion), channel_id=1, source_target_pairs={{0,1},{1,0},{2,3},{3,2},{4,5},{5,4},{6,7},{7,6},{8,9},{9,8},{10,11... | collective-permute-start | bytes 1572872 | tf_op jit(solution)/shard_map/ppermute | solution.py:267
  55.6 28.7 %all-to-all-start.1 = ((f32[32,16,256]{2,1,0:T(8,128)}), f32[32,16,256]{2,1,0:T(8,128)S(1)}, u32[]{:S(2)}, u32[]{:S(2)}) async-start(f32[32,16,256]{2,1,0:T(8,128)} %fusion.52), calls=%async_computation.1 | async-start | bytes 1048576 | tf_op jit(solution)/shard_map/all_to_all | solution.py:268
  69.4 3.3 %copy-start.6 = (f32[2,1,64,128]{3,2,0,1:T(8,128)S(1)}, f32[2,1,64,128]{3,2,0,1:T(8,128)}, u32[]{:S(2)}) copy-start(f32[2,1,64,128]{3,2,0,1:T(8,128)} %copy-done.5) | copy-start | bytes 196612
  69.4 3.3 %copy-start.8 = (f32[1,2,64,128]{3,2,1,0:T(8,128)S(1)}, f32[1,2,64,128]{3,2,1,0:T(8,128)}, u32[]{:S(2)}) copy-start(f32[1,2,64,128]{3,2,1,0:T(8,128)} %copy-done.7) | copy-start | bytes 196612
  69.7 3.4 %copy-start.24 = (f32[2,4,256]{2,0,1:T(2,128)S(1)}, f32[2,4,256]{2,0,1:T(2,128)}, u32[]{:S(2)}) copy-start(f32[2,4,256]{2,0,1:T(2,128)} %copy-done.23) | copy-start | bytes 24580
  69.7 3.4 %copy-start.57 = (f32[4,256]{1,0:T(4,128)S(1)}, f32[4,256]{1,0:T(4,128)}, u32[]{:S(2)}) copy-start(f32[4,256]{1,0:T(4,128)} %copy-done.56) | copy-start | bytes 12292
  69.7 3.4 %copy-start.61 = (f32[2,4,256]{2,1,0:T(4,128)S(1)}, f32[2,4,256]{2,1,0:T(4,128)}, u32[]{:S(2)}) copy-start(f32[2,4,256]{2,1,0:T(4,128)} %get-tuple-element.21) | copy-start | bytes 24580
  69.8 3.4 %copy-start.62 = (f32[2,4,256]{2,1,0:T(4,128)S(1)}, f32[2,4,256]{2,1,0:T(4,128)}, u32[]{:S(2)}) copy-start(f32[2,4,256]{2,1,0:T(4,128)} %get-tuple-element.22) | copy-start | bytes 24580
  69.8 6.5 %copy-start.48 = (f32[128]{0:T(128)S(1)}, f32[128]{0:T(128)}, u32[]{:S(2)}) copy-start(f32[128]{0:T(128)} %copy-done.47) | copy-start | bytes 1540
  69.8 6.5 %copy-start.50 = (f32[128]{0:T(128)S(1)}, f32[128]{0:T(128)}, u32[]{:S(2)}) copy-start(f32[128]{0:T(128)} %copy-done.49) | copy-start | bytes 1540
  69.8 6.5 %copy-start.52 = (f32[128]{0:T(128)S(1)}, f32[128]{0:T(128)}, u32[]{:S(2)}) copy-start(f32[128]{0:T(128)} %copy-done.51) | copy-start | bytes 1540
  69.8 6.5 %copy-start.54 = (f32[128]{0:T(128)S(1)}, f32[128]{0:T(128)}, u32[]{:S(2)}) copy-start(f32[128]{0:T(128)} %copy-done.53) | copy-start | bytes 1540
  70.1 6.2 %collective-permute-start.1 = (f32[3,128]{0,1:T(8,128)S(1)}, f32[3,128]{0,1:T(8,128)S(1)}, u32[]{:S(2)}, u32[]{:S(2)}) collective-permute-start(f32[3,128]{0,1:T(8,128)S(1)} %slice.385), channel_id=1, source_target_pairs={{64,0},{128,64},{192,128},{65,1},{129,65},{193,129},{66,2},{130,66... | collective-permute-start | bytes 4616 | tf_op jit(solution)/shard_map/ppermute | solution.py:18
  (21 other events, 46.8 us)
